TPU v7x, 512 devices: a whole 4x8x8 slice. The times are simulated.
512 devices in a mesh: gx: 32 (over x, y), gy: 16 (over z, core).
Axes of the slice: x: 4, y: 8, z: 8, core: 2. Of those that a mesh axis runs over, the one named last changes fastest.
Arguments:
- enthalpy: float32 [128, 256, 2048], P(None, 'gx', 'gy'), may hold values from -6 to 6
- velocity_init: float32 [2, 256, 2048], P(None, 'gx', 'gy'), may hold values from -0.35 to 0.35
- thickness: float32 [256, 2048], P('gx', 'gy'), may hold values from 0.3 to 3
- surface: float32 [256, 2048], P('gx', 'gy'), may hold values from -24 to 24
- friction: float32 [256, 2048], P('gx', 'gy'), may hold values from 0.3 to 10
- kappa: float32 [129], replicated, may hold values from 0.3 to 10
- surface_enthalpy: float32 [256, 2048], P('gx', 'gy'), may hold values from -6 to 6
- geo_flux: float32 [256, 2048], P('gx', 'gy'), may hold values from 0.2 to 1.5
- ice_mask: int32 [256, 2048], P('gx', 'gy'), may hold values 0 or 1
- grounded: int32 [256, 2048], P('gx', 'gy'), may hold values 0 or 1
- boundary_code: int32 [256, 2048], P('gx', 'gy'), may hold values from 0 to 2, as said below
Outputs:
- enthalpy_new: float32 [128, 256, 2048], P(None, 'gx', 'gy')
- velocity: float32 [2, 256, 2048], P(None, 'gx', 'gy')
Inputs may be any that keep to these rules, and one draw needn't show every extreme that they name: `boundary_code`: 0 marks a free cell, 1 a cell held at rest, 2 a cell whose velocity stays at its given value.
All inputs are finite; a program needn't handle non-finite values. No bound on the sum of `ice_mask` or of `grounded` on one device may be relied on, other than what follows from the above.
Results may differ from a plain program's by a relative error of at most 0.00018.
Values sent between devices are 32-bit elements; how exact they have to be, the bound alone decides.
No kernel may reach another device: no remote copies, remote signals or barrier semaphores. Data moves between devices by JAX's collectives and lax.ppermute only.
A program may use at most 64 MiB of HBM per device.

v0:
```python
import functools

import jax
import jax.numpy as jnp
from jax import lax
from jax.sharding import Mesh
from jax.sharding import PartitionSpec as P

SUBSTEPS = 2
PICARD = 2
KRYLOV = 6
GX_GY = ("gx_0", "gx_1", "gy_0", "gy_1")
GX = ("gx_0", "gx_1")
GY = ("gy_0", "gy_1")


soften = 0.3
shelf_drag = 0.2
strain_floor = 0.01


def with_halo(shard, sides, width):
    for axis, dim in sides:
        size, length = (lax.axis_size(axis), shard.shape[dim])
        up = [(i, (i + 1) % size) for i in range(size - 1)]
        down = [(j, i) for i, j in up]
        last = lax.slice_in_dim(shard, length - width, length, axis=dim)
        first = lax.slice_in_dim(shard, 0, width, axis=dim)
        before = lax.ppermute(last, axis, up)
        after = lax.ppermute(first, axis, down)
        shard = jnp.concatenate([before, shard, after], axis=dim)
    return shard


def one_axis_at_a_time(shard, axes):
    return functools.reduce(lax.psum, axes, shard)


def with_halo_2(shard, sides, width):
    edges = {}
    for axis, dim in sides:
        size, length = (lax.axis_size(axis), shard.shape[dim])
        up = [(i, (i + 1) % size) for i in range(size - 1)]
        last = lax.slice_in_dim(shard, length - width, length, axis=dim)
        first = lax.slice_in_dim(shard, 0, width, axis=dim)
        edges[dim] = (
            lax.ppermute(last, axis, up),
            lax.ppermute(first, axis, [(b, a) for a, b in up]),
        )
    done = []
    for _, dim in sides:
        low, high = edges[dim]
        around = [(width, width) if d in done else (0, 0) for d in range(shard.ndim)]
        shard = jnp.concatenate([jnp.pad(low, around), shard, jnp.pad(high, around)], axis=dim)
        done.append(dim)
    return shard


def upwind_sweep(values, courant, axis):
    length = values.shape[axis]

    def window(array, start_cut, end_cut):
        return lax.slice_in_dim(array, start_cut, length - end_cut, axis=axis)

    face_speed = 0.5 * (window(courant, 1, 2) + window(courant, 2, 1))
    minus_one = window(values, 0, 3)
    here_cell = window(values, 1, 2)
    plus_one = window(values, 2, 1)
    plus_two = window(values, 3, 0)
    positive = jnp.maximum(face_speed, 0.0)
    negative = jnp.minimum(face_speed, 0.0)
    face_flux = positive * (here_cell + 0.25 * (1.0 - positive) * (plus_one - minus_one))
    face_flux = face_flux + negative * (plus_one - 0.25 * (1.0 + negative) * (plus_two - here_cell))
    count = face_flux.shape[axis]
    return lax.slice_in_dim(face_flux, 1, count, axis=axis) - lax.slice_in_dim(
        face_flux, 0, count - 1, axis=axis
    )


def advect(padded, courant_x, courant_y):
    row_count = padded.shape[1]
    col_count = padded.shape[2]
    along_x = upwind_sweep(
        padded[:, :, 2 : col_count - 2], courant_x[None, :, 2 : col_count - 2], 1
    )
    along_y = upwind_sweep(
        padded[:, 2 : row_count - 2, :], courant_y[None, 2 : row_count - 2, :], 2
    )
    return padded[:, 2 : row_count - 2, 2 : col_count - 2] - along_x - along_y


def column_inverses(kappa):
    levels = kappa.shape[0] - 1
    nothing = jnp.zeros((1,), kappa.dtype)
    lower_band = jnp.concatenate([nothing, -kappa[1:levels]])
    upper_band = jnp.concatenate([-kappa[1:levels], nothing])
    floating = 1.0 + kappa[:levels] + kappa[1:]
    bottom = lax.broadcasted_iota(jnp.int32, (levels,), 0) == levels - 1
    on_bed = jnp.where(bottom, floating - kappa[levels], floating)
    identity = jnp.eye(levels, dtype=kappa.dtype)
    inverse_bed = lax.linalg.tridiagonal_solve(lower_band, on_bed, upper_band, identity)
    inverse_shelf = lax.linalg.tridiagonal_solve(lower_band, floating, upper_band, identity)
    return (inverse_bed, inverse_shelf)


def diffuse(moved, inverse_bed, inverse_shelf, kappa, ice_cols, bed_cols, surface_heat, heat_flux):
    levels = moved.shape[0]
    depth_index = lax.broadcasted_iota(jnp.int32, (levels, 1, 1), 0)
    right_side = moved + jnp.where(depth_index == 0, kappa[0] * surface_heat[None], 0.0)
    right_side = right_side + jnp.where(
        depth_index == levels - 1, bed_cols[None] * heat_flux[None], 0.0
    )
    columns = right_side.reshape(levels, -1)
    solved_bed = jnp.dot(inverse_bed, columns, precision=lax.Precision.HIGHEST).reshape(moved.shape)
    solved_shelf = jnp.dot(inverse_shelf, columns, precision=lax.Precision.HIGHEST).reshape(
        moved.shape
    )
    solved = jnp.where(bed_cols[None] > 0.5, solved_bed, solved_shelf)
    return jnp.where(ice_cols[None] > 0.5, solved, moved)


def corner_mean(array):
    return 0.25 * (array[:-1, :-1] + array[1:, :-1] + array[:-1, 1:] + array[1:, 1:])


def diff_rows(array):
    return 0.5 * (array[1:, :-1] - array[:-1, :-1] + (array[1:, 1:] - array[:-1, 1:]))


def diff_cols(array):
    return 0.5 * (array[:-1, 1:] - array[:-1, :-1] + (array[1:, 1:] - array[1:, :-1]))


def back_rows(array):
    return 0.5 * (array[:-1, :-1] + array[:-1, 1:] - array[1:, :-1] - array[1:, 1:])


def back_cols(array):
    return 0.5 * (array[:-1, :-1] + array[1:, :-1] - array[:-1, 1:] - array[1:, 1:])


def strains(padded):
    stretch_x = diff_rows(padded[0])
    stretch_y = diff_cols(padded[1])
    shear_rate = 0.5 * (diff_cols(padded[0]) + diff_rows(padded[1]))
    return (stretch_x, stretch_y, shear_rate)


def viscous_weight(rates, thick_corner, stiff_corner):
    stretch_x, stretch_y, shear_rate = rates
    square = (
        stretch_x * stretch_x
        + stretch_y * stretch_y
        + stretch_x * stretch_y
        + shear_rate * shear_rate
    )
    return 0.5 * stiff_corner * thick_corner * jnp.power(square + strain_floor, -1.0 / 3.0)


def stress_image(rates, weight, center, drag_term):
    stretch_x, stretch_y, shear_rate = rates
    stress_x = weight * (4.0 * stretch_x + 2.0 * stretch_y)
    stress_y = weight * (4.0 * stretch_y + 2.0 * stretch_x)
    shear_stress = 2.0 * weight * shear_rate
    first = back_rows(stress_x) + back_cols(shear_stress) + drag_term * center[0]
    second = back_rows(shear_stress) + back_cols(stress_y) + drag_term * center[1]
    return jnp.stack([first, second])


def apply_field(direction, weight, drag_term, projector):
    padded = with_halo(direction, ((GX, 1), (GY, 2)), 1)
    return projector * stress_image(strains(padded), weight, direction, drag_term)


def paired_sums(residual, imaged):
    return (
        one_axis_at_a_time(jnp.sum(residual * residual), GX_GY),
        one_axis_at_a_time(jnp.sum(residual * imaged), GX_GY),
    )


def shards(
    enthalpy,
    velocity_init,
    thickness,
    surface,
    friction,
    kappa,
    surface_enthalpy,
    geo_flux,
    ice_mask,
    grounded,
    boundary_code,
):
    ice_cols = ice_mask.astype(jnp.float32)
    bed_cols = grounded.astype(jnp.float32)
    inverse_bed, inverse_shelf = column_inverses(kappa)
    levels = enthalpy.shape[0]
    stacked = jnp.concatenate([enthalpy, velocity_init], axis=0)
    padded = with_halo_2(stacked, ((GX, 1), (GY, 2)), 2)
    current = padded[:levels]
    courant = padded[levels:]
    for substep in range(SUBSTEPS):
        if substep > 0:
            current = with_halo_2(current, ((GX, 1), (GY, 2)), 2)
        moved = advect(current, courant[0], courant[1])
        current = diffuse(
            moved, inverse_bed, inverse_shelf, kappa, ice_cols, bed_cols, surface_enthalpy, geo_flux
        )
    stiffness = jnp.exp(-soften * jnp.mean(current, axis=0))
    statics = with_halo(jnp.stack([thickness, stiffness, surface]), ((GX, 1), (GY, 2)), 1)
    thick_corner = corner_mean(statics[0])
    stiff_corner = corner_mean(statics[1])
    heights = statics[2]
    driving = jnp.stack(
        [
            -thickness * 0.5 * (heights[2:, 1:-1] - heights[:-2, 1:-1]),
            -thickness * 0.5 * (heights[1:-1, 2:] - heights[1:-1, :-2]),
        ]
    )
    free_cells = (boundary_code == 0) & (ice_mask == 1)
    held_cells = free_cells | (boundary_code == 2)
    projector = free_cells.astype(jnp.float32)[None]
    drag_term = jnp.where(grounded == 1, friction, 0.0) + shelf_drag
    velocity = jnp.where(held_cells[None], velocity_init, 0.0)
    for picard_step in range(PICARD):
        padded_flow = with_halo(velocity, ((GX, 1), (GY, 2)), 1)
        rates = strains(padded_flow)
        weight = viscous_weight(rates, thick_corner, stiff_corner)
        residual = projector * (driving - stress_image(rates, weight, velocity, drag_term))
        change = jnp.zeros_like(velocity)
        imaged = apply_field(residual, weight, drag_term, projector)
        norm_now, product = paired_sums(residual, imaged)
        step_size = norm_now / product
        direction = residual
        along = imaged
        for krylov_step in range(KRYLOV):
            change = change + step_size * direction
            residual = residual - step_size * along
            if krylov_step + 1 < KRYLOV:
                imaged = apply_field(residual, weight, drag_term, projector)
                norm_next, product = paired_sums(residual, imaged)
                factor = norm_next / norm_now
                step_size = norm_next / (product - factor * norm_next / step_size)
                direction = residual + factor * direction
                along = imaged + factor * along
                norm_now = norm_next
        velocity = velocity + change
    return (current, velocity)


def solution(mesh):
    torus = Mesh(mesh.devices.reshape(4, 8, 8, 2), ("gx_0", "gx_1", "gy_0", "gy_1"))
    placed = (
        P(None, GX, GY),
        P(None, GX, GY),
        P(GX, GY),
        P(GX, GY),
        P(GX, GY),
        P(),
        P(GX, GY),
        P(GX, GY),
        P(GX, GY),
        P(GX, GY),
        P(GX, GY),
    )
    return jax.shard_map(
        shards,
        mesh=torus,
        in_specs=placed,
        out_specs=(P(None, GX, GY), P(None, GX, GY)),
        check_vma=False,
    )
```

profile of v0, /device:TPU:1, one launch (start us, length us, event | category | flops | bytes accessed | tf_op | source)
XLA Modules:
  0.0 1796.9 jit_solution(8222196172101525611)
XLA Ops:
  26.1 254.7 %while.64 = (s32[]{:T(128)}, f32[]{:T(128)}, f32[128]{0:T(128)S(1)}, f32[3,32]{1,0:T(4,128)S(1)}, f32[3,32,128]{2,1,0:T(8,128)S(1)}, /*index=5*/f32[3,32]{1,0:T(...) while((s32[]{:T(128)}, f32[]{:T(128)}, ...), condition=%wide.region_1.2_spmd, body=%wide.region_0.1_spmd.sunk | while | flops 12417 | bytes 104185 | solution.py:101
  90.3 20.5 %fusion.890 = (f32[128]{0:T(128)S(1)}, f32[128]{0:T(128)S(1)}, f32[128]{0:T(128)S(1)}, f32[128]{0:T(128)S(1)}, f32[128]{0:T(128)S(1)}, /*index=5*/f32[128]{0:T(1...) fusion(f32[3,32,128]{2,1,0:T(8,128)S(1)} %get-tuple-element.243, ...), kind=kLoop, calls=%fused_computation.41.clone.1 | loop fusion | flops 12288 | bytes 33664 | tf_op jit(solution)/shard_map/while/body/eval_jaxpr/div | solution.py:101
  175.2 20.5 %fusion.890 = (f32[128]{0:T(128)S(1)}, f32[128]{0:T(128)S(1)}, f32[128]{0:T(128)S(1)}, f32[128]{0:T(128)S(1)}, f32[128]{0:T(128)S(1)}, /*index=5*/f32[128]{0:T(1...) fusion(f32[3,32,128]{2,1,0:T(8,128)S(1)} %get-tuple-element.243, ...), kind=kLoop, calls=%fused_computation.41.clone.1 | loop fusion | flops 12288 | bytes 33664 | tf_op jit(solution)/shard_map/while/body/eval_jaxpr/div | solution.py:101
  260.1 20.5 %fusion.890 = (f32[128]{0:T(128)S(1)}, f32[128]{0:T(128)S(1)}, f32[128]{0:T(128)S(1)}, f32[128]{0:T(128)S(1)}, f32[128]{0:T(128)S(1)}, /*index=5*/f32[128]{0:T(1...) fusion(f32[3,32,128]{2,1,0:T(8,128)S(1)} %get-tuple-element.243, ...), kind=kLoop, calls=%fused_computation.41.clone.1 | loop fusion | flops 12288 | bytes 33664 | tf_op jit(solution)/shard_map/while/body/eval_jaxpr/div | solution.py:101
  285.3 253.7 %while.66 = (s32[]{:T(128)}, f32[]{:T(128)}, f32[128]{0:T(128)S(1)}, f32[3,32]{1,0:T(4,128)S(1)}, f32[3,32,128]{2,1,0:T(8,128)S(1)}, /*index=5*/f32[3,32]{1,0:T(...) while((s32[]{:T(128)}, f32[]{:T(128)}, ...), condition=%wide.region_5.6_spmd, body=%wide.region_4.5_spmd.sunk | while | flops 12417 | bytes 104185 | solution.py:101
  349.5 20.1 %fusion.900 = (f32[128]{0:T(128)S(1)}, f32[128]{0:T(128)S(1)}, f32[128]{0:T(128)S(1)}, f32[128]{0:T(128)S(1)}, f32[128]{0:T(128)S(1)}, /*index=5*/f32[128]{0:T(1...) fusion(f32[3,32,128]{2,1,0:T(8,128)S(1)} %get-tuple-element.268, ...), kind=kLoop, calls=%fused_computation.271.clone.1 | loop fusion | flops 12288 | bytes 33664 | tf_op jit(solution)/shard_map/while/body/eval_jaxpr/div | solution.py:101
  434.0 20.1 %fusion.900 = (f32[128]{0:T(128)S(1)}, f32[128]{0:T(128)S(1)}, f32[128]{0:T(128)S(1)}, f32[128]{0:T(128)S(1)}, f32[128]{0:T(128)S(1)}, /*index=5*/f32[128]{0:T(1...) fusion(f32[3,32,128]{2,1,0:T(8,128)S(1)} %get-tuple-element.268, ...), kind=kLoop, calls=%fused_computation.271.clone.1 | loop fusion | flops 12288 | bytes 33664 | tf_op jit(solution)/shard_map/while/body/eval_jaxpr/div | solution.py:101
  518.6 20.1 %fusion.900 = (f32[128]{0:T(128)S(1)}, f32[128]{0:T(128)S(1)}, f32[128]{0:T(128)S(1)}, f32[128]{0:T(128)S(1)}, f32[128]{0:T(128)S(1)}, /*index=5*/f32[128]{0:T(1...) fusion(f32[3,32,128]{2,1,0:T(8,128)S(1)} %get-tuple-element.268, ...), kind=kLoop, calls=%fused_computation.271.clone.1 | loop fusion | flops 12288 | bytes 33664 | tf_op jit(solution)/shard_map/while/body/eval_jaxpr/div | solution.py:101
  598.5 19.3 %subtract_divide_fusion.31 = (f32[128]{0:T(128)S(1)}, f32[128]{0:T(128)S(1)}, f32[128]{0:T(128)S(1)}, f32[128]{0:T(128)S(1)}, f32[128]{0:T(128)S(1)}, /*index=5*...) fusion(f32[128,128]{1,0:T(8,128)S(1)} %fusion.394, ...), kind=kLoop, calls=%fused_computation.1250 | loop fusion | flops 11904 | bytes 32504 | tf_op jit(solution)/shard_map/eval_jaxpr/div | solution.py:101
  618.3 64.7 %while.65 = (s32[]{:T(128)}, f32[128]{0:T(128)S(1)}, f32[3,32,128]{2,1,0:T(8,128)S(1)}, f32[3,32,128]{2,1,0:T(8,128)S(1)}, f32[3,32]{1,0:T(4,128)S(1)}, /*index=...) while((s32[]{:T(128)}, f32[128]{0:T(128)S(1)}, ...), condition=%wide.region_3.4_spmd, body=%wide.region_2.3_spmd.sunk | while | flops 8226 | bytes 101341 | solution.py:101
  619.7 20.0 %fusion.893 = (f32[128]{0:T(128)S(1)}, f32[128]{0:T(128)S(1)}, f32[128]{0:T(128)S(1)}, f32[128]{0:T(128)S(1)}, f32[128]{0:T(128)S(1)}, /*index=5*/f32[128]{0:T(1...) fusion(f32[3,32,128]{2,1,0:T(8,128)S(1)} %get-tuple-element.255, ...), kind=kLoop, calls=%fused_computation.169.clone.1 | loop fusion | flops 8192 | bytes 33536 | tf_op jit(solution)/shard_map/while/body/eval_jaxpr/sub | solution.py:101
  641.3 20.0 %fusion.893 = (f32[128]{0:T(128)S(1)}, f32[128]{0:T(128)S(1)}, f32[128]{0:T(128)S(1)}, f32[128]{0:T(128)S(1)}, f32[128]{0:T(128)S(1)}, /*index=5*/f32[128]{0:T(1...) fusion(f32[3,32,128]{2,1,0:T(8,128)S(1)} %get-tuple-element.255, ...), kind=kLoop, calls=%fused_computation.169.clone.1 | loop fusion | flops 8192 | bytes 33536 | tf_op jit(solution)/shard_map/while/body/eval_jaxpr/sub | solution.py:101
  662.9 20.0 %fusion.893 = (f32[128]{0:T(128)S(1)}, f32[128]{0:T(128)S(1)}, f32[128]{0:T(128)S(1)}, f32[128]{0:T(128)S(1)}, f32[128]{0:T(128)S(1)}, /*index=5*/f32[128]{0:T(1...) fusion(f32[3,32,128]{2,1,0:T(8,128)S(1)} %get-tuple-element.255, ...), kind=kLoop, calls=%fused_computation.169.clone.1 | loop fusion | flops 8192 | bytes 33536 | tf_op jit(solution)/shard_map/while/body/eval_jaxpr/sub | solution.py:101
  740.1 19.3 %subtract_divide_fusion = (f32[128]{0:T(128)S(1)}, f32[128]{0:T(128)S(1)}, f32[128]{0:T(128)S(1)}, f32[128]{0:T(128)S(1)}, f32[128]{0:T(128)S(1)}, /*index=5*/f3...) fusion(f32[128,128]{1,0:T(8,128)S(1)} %fusion.394, ...), kind=kLoop, calls=%fused_computation.1217 | loop fusion | flops 11904 | bytes 32504 | tf_op jit(solution)/shard_map/eval_jaxpr/div | solution.py:101
  759.9 64.5 %while.67 = (s32[]{:T(128)}, f32[128]{0:T(128)S(1)}, f32[3,32,128]{2,1,0:T(8,128)S(1)}, f32[3,32,128]{2,1,0:T(8,128)S(1)}, f32[3,32]{1,0:T(4,128)S(1)}, /*index=...) while((s32[]{:T(128)}, f32[128]{0:T(128)S(1)}, ...), condition=%wide.region_7.8_spmd, body=%wide.region_6.7_spmd.sunk | while | flops 8226 | bytes 101341 | solution.py:101
  761.3 19.9 %fusion.903 = (f32[128]{0:T(128)S(1)}, f32[128]{0:T(128)S(1)}, f32[128]{0:T(128)S(1)}, f32[128]{0:T(128)S(1)}, f32[128]{0:T(128)S(1)}, /*index=5*/f32[128]{0:T(1...) fusion(f32[3,32,128]{2,1,0:T(8,128)S(1)} %get-tuple-element.279, ...), kind=kLoop, calls=%fused_computation.399.clone.1 | loop fusion | flops 8192 | bytes 33536 | tf_op jit(solution)/shard_map/while/body/eval_jaxpr/sub | solution.py:101
  782.8 19.9 %fusion.903 = (f32[128]{0:T(128)S(1)}, f32[128]{0:T(128)S(1)}, f32[128]{0:T(128)S(1)}, f32[128]{0:T(128)S(1)}, f32[128]{0:T(128)S(1)}, /*index=5*/f32[128]{0:T(1...) fusion(f32[3,32,128]{2,1,0:T(8,128)S(1)} %get-tuple-element.279, ...), kind=kLoop, calls=%fused_computation.399.clone.1 | loop fusion | flops 8192 | bytes 33536 | tf_op jit(solution)/shard_map/while/body/eval_jaxpr/sub | solution.py:101
  804.3 19.9 %fusion.903 = (f32[128]{0:T(128)S(1)}, f32[128]{0:T(128)S(1)}, f32[128]{0:T(128)S(1)}, f32[128]{0:T(128)S(1)}, f32[128]{0:T(128)S(1)}, /*index=5*/f32[128]{0:T(1...) fusion(f32[3,32,128]{2,1,0:T(8,128)S(1)} %get-tuple-element.279, ...), kind=kLoop, calls=%fused_computation.399.clone.1 | loop fusion | flops 8192 | bytes 33536 | tf_op jit(solution)/shard_map/while/body/eval_jaxpr/sub | solution.py:101
  966.4 22.4 %all-reduce.39 = (f32[]{:T(128)}, f32[]{:T(128)}) all-reduce(f32[]{:T(128)} %get-tuple-element.353, f32[]{:T(128)} %get-tuple-element.352), channel_id=1, replica_groups=mesh['gx_0'=4,'gx_1'=8,'gy_0'=8,'gy_1'=2] {'gx_0'}, use_global_device_ids=true, to_apply=%region_10.11 | all-reduce | flops 2 | bytes 16 | tf_op jit(solution)/shard_map/psum | solution.py:36
  1000.1 21.1 %all-reduce.15 = (f32[]{:T(128)}, f32[]{:T(128)}) all-reduce(f32[]{:T(128)} %get-tuple-element.456, f32[]{:T(128)} %get-tuple-element.457), channel_id=1, replica_groups=mesh['gx_0'=4,'gx_1'=8,'gy_0'=8,'gy_1'=2] {'gy_0'}, use_global_device_ids=true, to_apply=%region_12.13 | all-reduce | flops 2 | bytes 16 | tf_op jit(solution)/shard_map/psum | solution.py:36
  1021.2 12.5 all-reduce.51
  1049.5 12.2 all-reduce.38
  1073.1 13.0 all-reduce.14
  1086.0 14.0 all-reduce.50
  1141.5 12.6 all-reduce.13
  1154.1 13.9 all-reduce.49
  1185.7 11.9 all-reduce.36
  1209.0 12.7 all-reduce.12
  1221.7 14.0 all-reduce.48
  1276.6 12.6 all-reduce.11
  1289.3 13.9 all-reduce.47
  1320.9 11.9 all-reduce.34
  1344.2 12.7 all-reduce.10
  1356.9 14.0 all-reduce.46
  1403.1 14.3 all-reduce.33
  1428.8 13.7 all-reduce.9
  1442.5 12.8 all-reduce.45
  1471.1 12.2 all-reduce.32
  1494.6 13.0 all-reduce.8
  1507.6 14.0 all-reduce.44
  1563.1 12.6 all-reduce.7
  1575.7 13.9 all-reduce.43
  1630.6 12.7 all-reduce.6
  1643.3 14.0 all-reduce.42
  1698.2 12.6 all-reduce.5
  1710.8 13.9 all-reduce.41
  1765.7 12.7 all-reduce.4
  1778.4 14.0 all-reduce.40
  (545 shorter events, 582.3 us)
Async XLA Ops:
  2.9 909.5 %collective-permute-start.2 = (f32[130,2,128]{0,2,1:T(8,128)S(1)}, f32[130,2,128]{0,2,1:T(8,128)S(1)}, u32[]{:S(2)}, u32[]{:S(2)}) collective-permute-start(f32[130,2,128]{0,2,1:T(8,128)S(1)} %get-tuple-element.1084), channel_id=1, source_target_pairs={{16,0},{32,16},{48,32},{64,48},{80,64},{96,80},{112,96},{128,112},... | collective-permute-start | bytes 399368 | tf_op jit(solution)/shard_map/ppermute | solution.py:48
  4.2 908.2 %collective-permute-start.1 = (f32[130,2,128]{0,2,1:T(8,128)S(1)}, f32[130,2,128]{0,2,1:T(8,128)S(1)}, u32[]{:S(2)}, u32[]{:S(2)}) collective-permute-start(f32[130,2,128]{0,2,1:T(8,128)S(1)} %get-tuple-element.1083), channel_id=1, source_target_pairs={{0,16},{16,32},{32,48},{48,64},{64,80},{80,96},{96,112},{112,128},... | collective-permute-start | bytes 399368 | tf_op jit(solution)/shard_map/ppermute | solution.py:47
  8.9 902.9 %collective-permute-start = (f32[130,8,2]{0,2,1:T(2,128)S(1)}, f32[130,8,2]{0,2,1:T(2,128)S(1)}, u32[]{:S(2)}, u32[]{:S(2)}) collective-permute-start(f32[130,8,2]{0,2,1:T(2,128)S(1)} %get-tuple-element.1081), channel_id=1, source_target_pairs={{0,1},{1,2},{2,3},{3,4},{4,5},{5,6},{6,7},{7,8},{8,9},{9,10},{10,1... | collective-permute-start | bytes 24968 | tf_op jit(solution)/shard_map/ppermute | solution.py:47
  14.3 892.1 %collective-permute-start.13 = (f32[2,1,128]{2,1,0:T(1,128)S(1)}, f32[2,1,128]{2,1,0:T(1,128)S(1)}, u32[]{:S(2)}, u32[]{:S(2)}) collective-permute-start(f32[2,1,128]{2,1,0:T(1,128)S(1)} %get-tuple-element.1227), channel_id=1, source_target_pairs={{16,0},{32,16},{48,32},{64,48},{80,64},{96,80},{112,96},{128,112},... | collective-permute-start | bytes 3080 | tf_op jit(solution)/shard_map/ppermute | solution.py:30
  15.6 896.2 %collective-permute-start.12 = (f32[2,1,128]{2,1,0:T(1,128)S(1)}, f32[2,1,128]{2,1,0:T(1,128)S(1)}, u32[]{:S(2)}, u32[]{:S(2)}) collective-permute-start(f32[2,1,128]{2,1,0:T(1,128)S(1)} %get-tuple-element.1226), channel_id=1, source_target_pairs={{0,16},{16,32},{32,48},{48,64},{64,80},{80,96},{96,112},{112,128},... | collective-permute-start | bytes 3080 | tf_op jit(solution)/shard_map/ppermute | solution.py:29
  906.4 6.0 collective-permute-start.3
  918.1 12.2 collective-permute-start.6
  920.1 13.9 collective-permute-start.5
  921.4 12.6 collective-permute-start.4
  925.4 8.6 collective-permute-start.7
  928.4 14.5 collective-permute-start.15
  930.3 12.5 collective-permute-start.14
  937.6 5.4 collective-permute-start.9
  943.7 5.6 collective-permute-start.11
  950.7 6.2 collective-permute-start.17
  952.0 5.6 collective-permute-start.16
  957.7 7.0 collective-permute-start.19
  959.6 5.9 collective-permute-start.18
  1035.1 5.6 collective-permute-start.21
  1041.4 6.3 collective-permute-start.23
  1104.6 5.6 collective-permute-start.25
  1110.9 5.6 collective-permute-start.27
  1172.0 5.6 collective-permute-start.29
  1173.3 5.0 collective-permute-start.28
  1178.4 5.6 collective-permute-start.31
  1239.7 5.6 collective-permute-start.33
  1241.0 5.0 collective-permute-start.32
  1246.1 5.8 collective-permute-start.35
  1307.1 5.6 collective-permute-start.37
  1308.4 5.0 collective-permute-start.36
  1313.5 5.6 collective-permute-start.39
  1374.9 5.6 collective-permute-start.41
  1376.2 5.0 collective-permute-start.40
  1381.2 5.6 collective-permute-start.43
  1388.0 5.6 collective-permute-start.45
  1389.3 5.0 collective-permute-start.44
  1394.4 7.0 collective-permute-start.47
  1456.6 5.6 collective-permute-start.49
  1463.0 6.3 collective-permute-start.51
  1526.2 5.6 collective-permute-start.53
  1532.5 5.6 collective-permute-start.55
  1593.6 5.6 collective-permute-start.57
  1599.9 5.6 collective-permute-start.59
  1661.3 5.6 collective-permute-start.61
  1667.7 5.6 collective-permute-start.63
  1728.7 6.6 collective-permute-start.65
  1730.0 5.3 collective-permute-start.64
  1735.4 5.6 collective-permute-start.67
  (32 other events, 1329.7 us)
where the time goes:
time: 1810 us; the launch traced here: 1800 us
  blocking collectives  620 us (34%)
  other arithmetic  382 us (21%)
  loops' own time  360 us (20%)
  starting transfers between devices  198 us (11%)
  between operations  163 us (9%)
  local copies, waits for them, and re-layouts  50.4 us (3%)
  waiting for transfers between devices  21.2 us (1%)
    psum x48, blocking collectives, one_axis_at_a_time(): return functools.reduce(lax.psum, axes, shard)  620 us
    another operation x4, loops' own time, column_inverses(): lax.linalg.tridiagonal_solve(lower_band, on_bed, upper_band, identity)  360 us
    div x9, other arithmetic, column_inverses(): lax.linalg.tridiagonal_solve(lower_band, on_bed, upper_band, identity)  162 us
    sub x6, other arithmetic, column_inverses(): lax.linalg.tridiagonal_solve(lower_band, on_bed, upper_band, identity)  120 us
    ppermute x30, starting transfers between devices, with_halo(): before = lax.ppermute(last, axis, up)  109 us
    broadcast_in_dim x32, other arithmetic, column_inverses(): lax.linalg.tridiagonal_solve(lower_band, on_bed, upper_band, identity)  81.1 us
    ppermute x30, starting transfers between devices, with_halo(): after = lax.ppermute(first, axis, down)  61.8 us
    slice x66, local copies, waits for them, and re-layouts, column_inverses(): lax.linalg.tridiagonal_solve(lower_band, on_bed, upper_band, identity)  41.8 us
  transfers between devices with their start and end apart: 68, of which 28 were waited for; matrix products, arithmetic and copies ran while one was open for 23% of the time, Pallas kernels for 0%

commit v1 on v0

--- a/solution.py
+++ b/solution.py
@@ -3,12 +3,15 @@
 import jax
 import jax.numpy as jnp
 from jax import lax
+from jax.experimental import pallas as pl
+from jax.experimental.pallas import tpu as pltpu
 from jax.sharding import Mesh
 from jax.sharding import PartitionSpec as P
 
 SUBSTEPS = 2
 PICARD = 2
 KRYLOV = 6
+TORUS = (4, 8, 8, 2)
 GX_GY = ("gx_0", "gx_1", "gy_0", "gy_1")
 GX = ("gx_0", "gx_1")
 GY = ("gy_0", "gy_1")
@@ -17,6 +20,12 @@
 soften = 0.3
 shelf_drag = 0.2
 strain_floor = 0.01
+
+MIDDLE = 17.0
+RADIUS = 17.0
+PIVOT_FLOOR = 2e-4
+OWN = 16
+SIDE = 64
 
 
 def with_halo(shard, sides, width):
@@ -89,20 +98,6 @@
     return padded[:, 2 : row_count - 2, 2 : col_count - 2] - along_x - along_y
 
 
-def column_inverses(kappa):
-    levels = kappa.shape[0] - 1
-    nothing = jnp.zeros((1,), kappa.dtype)
-    lower_band = jnp.concatenate([nothing, -kappa[1:levels]])
-    upper_band = jnp.concatenate([-kappa[1:levels], nothing])
-    floating = 1.0 + kappa[:levels] + kappa[1:]
-    bottom = lax.broadcasted_iota(jnp.int32, (levels,), 0) == levels - 1
-    on_bed = jnp.where(bottom, floating - kappa[levels], floating)
-    identity = jnp.eye(levels, dtype=kappa.dtype)
-    inverse_bed = lax.linalg.tridiagonal_solve(lower_band, on_bed, upper_band, identity)
-    inverse_shelf = lax.linalg.tridiagonal_solve(lower_band, floating, upper_band, identity)
-    return (inverse_bed, inverse_shelf)
-
-
 def diffuse(moved, inverse_bed, inverse_shelf, kappa, ice_cols, bed_cols, surface_heat, heat_flux):
     levels = moved.shape[0]
     depth_index = lax.broadcasted_iota(jnp.int32, (levels, 1, 1), 0)
@@ -172,11 +167,348 @@
     return projector * stress_image(strains(padded), weight, direction, drag_term)
 
 
-def paired_sums(residual, imaged):
-    return (
-        one_axis_at_a_time(jnp.sum(residual * residual), GX_GY),
-        one_axis_at_a_time(jnp.sum(residual * imaged), GX_GY),
-    )
+def inverse_kernel(kappa_ref, bed_ref, shelf_ref):
+    levels = kappa_ref.shape[1]
+    above = kappa_ref[0:8, :]
+    below = kappa_ref[8:16, :]
+    lane = lax.broadcasted_iota(jnp.int32, (8, levels), 1)
+    rows = lax.broadcasted_iota(jnp.int32, (levels, levels), 0)
+    cols = lax.broadcasted_iota(jnp.int32, (levels, levels), 1)
+    floating = 1.0 + above + below
+    on_bed = jnp.where(lane == levels - 1, 1.0 + above, floating)
+    for diagonal, out_ref in ((on_bed, bed_ref), (floating, shelf_ref)):
+        low = jnp.where(lane == 0, 0.0, -above)
+        high = jnp.where(lane == levels - 1, 0.0, -below)
+        mid = diagonal
+        right = jnp.where(rows == cols, 1.0, 0.0)
+        step = 1
+        while step < levels:
+            back = levels - step
+            down = -low / pltpu.roll(mid, step, 1)
+            up = -high / pltpu.roll(mid, back, 1)
+            mid = mid + down * pltpu.roll(high, step, 1) + up * pltpu.roll(low, back, 1)
+            low = down * pltpu.roll(low, step, 1)
+            high = up * pltpu.roll(high, back, 1)
+            right = (
+                right
+                + down[0:1] * pltpu.roll(right, step, 1)
+                + up[0:1] * pltpu.roll(right, back, 1)
+            )
+            step *= 2
+        out_ref[...] = right / mid[0:1]
+
+
+def column_inverses(kappa):
+    levels = kappa.shape[0] - 1
+    above = jnp.broadcast_to(kappa[None, :levels], (8, levels))
+    below = jnp.broadcast_to(kappa[None, 1:], (8, levels))
+    shape = jax.ShapeDtypeStruct((levels, levels), kappa.dtype)
+    return pl.pallas_call(inverse_kernel, out_shape=(shape, shape), name="column_inverses")(
+        jnp.concatenate([above, below], axis=0)
+    )
+
+
+def next_row(array):
+    return pltpu.roll(array, array.shape[0] - 1, 0)
+
+
+def next_col(array):
+    return pltpu.roll(array, array.shape[1] - 1, 1)
+
+
+def last_row(array):
+    return pltpu.roll(array, 1, 0)
+
+
+def last_col(array):
+    return pltpu.roll(array, 1, 1)
+
+
+def corner_rates(u, v):
+    u_next = next_col(u)
+    v_next = next_col(v)
+    u_sum, u_diff = (u + u_next, u_next - u)
+    v_sum, v_diff = (v + v_next, v_next - v)
+    along = next_row(u_sum) - u_sum
+    across = v_diff + next_row(v_diff)
+    shear = u_diff + next_row(u_diff) + (next_row(v_sum) - v_sum)
+    return (along, across, shear)
+
+
+def stress_back(rates, half_weight):
+    along, across, shear = rates
+    stress_x = half_weight * (2.0 * along + across)
+    stress_y = half_weight * (2.0 * across + along)
+    stress_s = 0.5 * half_weight * shear
+    x_before = last_col(stress_x)
+    y_before = last_col(stress_y)
+    s_before = last_col(stress_s)
+    x_sum, s_diff = (stress_x + x_before, s_before - stress_s)
+    s_sum, y_diff = (stress_s + s_before, y_before - stress_y)
+    first = last_row(x_sum + s_diff) + (s_diff - x_sum)
+    second = last_row(s_sum + y_diff) + (y_diff - s_sum)
+    return (first, second)
+
+
+def half_weights(rates, corner_product):
+    along, across, shear = rates
+    square = 0.25 * (along * along + across * across + along * across) + 0.0625 * shear * shear
+    return corner_product * jnp.exp(jnp.log(square + strain_floor) * (-1.0 / 3.0))
+
+
+def krylov_basis(u, v, drag, driving, corner_product, own_row, keep):
+    free = drag > 0.0
+    rates = corner_rates(u, v)
+    half_weight = half_weights(rates, corner_product)
+    first, second = stress_back(rates, half_weight)
+    r_u = jnp.where(free, driving[0] - first - drag * u, 0.0)
+    r_v = jnp.where(free, driving[1] - second - drag * v, 0.0)
+
+    def own(array):
+        return array[own_row : own_row + 8, :128]
+
+    basis_u, basis_v = ([r_u], [r_v])
+    own_basis, own_image = ([(own(r_u), own(r_v))], [])
+    keep(0, r_u, r_v)
+    for k in range(KRYLOV):
+        b_u, b_v = (basis_u[k], basis_v[k])
+        first, second = stress_back(corner_rates(b_u, b_v), half_weight)
+        a_u = jnp.where(free, first, 0.0) + drag * b_u
+        a_v = jnp.where(free, second, 0.0) + drag * b_v
+        own_image.append((own(a_u), own(a_v)))
+        if k + 1 < KRYLOV:
+            scale = (1.0 if k == 0 else 2.0) / RADIUS
+            n_u = scale * a_u - (scale * MIDDLE) * b_u
+            n_v = scale * a_v - (scale * MIDDLE) * b_v
+            if k > 0:
+                n_u = n_u - basis_u[k - 1]
+                n_v = n_v - basis_v[k - 1]
+            basis_u.append(n_u)
+            basis_v.append(n_v)
+            own_basis.append((own(n_u), own(n_v)))
+            keep(k + 1, n_u, n_v)
+    products = []
+    for i in range(KRYLOV):
+        for j in range(i, KRYLOV):
+            products.append(
+                own_basis[i][0] * own_image[j][0] + own_basis[i][1] * own_image[j][1]
+            )
+    for i in range(KRYLOV):
+        products.append(own_basis[i][0] * own_basis[0][0] + own_basis[i][1] * own_basis[0][1])
+    return products
+
+
+def write_sums(products, out_ref):
+    count = out_ref.shape[0]
+    lines = [jnp.sum(p, axis=0, keepdims=True) for p in products]
+    lines.append(jnp.zeros((128 - len(lines), 128), jnp.float32))
+    table = jnp.concatenate(lines, axis=0)
+    out_ref[...] = lax.dot_general(
+        jnp.ones((count, 128), jnp.float32),
+        table,
+        (((1,), (1,)), ((), ())),
+        precision=lax.Precision.HIGHEST,
+        preferred_element_type=jnp.float32,
+    )
+
+
+def small_solve(parts):
+    sums = jnp.sum(parts, axis=0, keepdims=True)
+    at = lambda k: sums[:, k : k + 1]
+    full = {}
+    k = 0
+    for i in range(KRYLOV):
+        for j in range(i, KRYLOV):
+            full[i, j] = at(k)
+            k += 1
+    norm = [lax.rsqrt(full[i, i]) for i in range(KRYLOV)]
+    right = [at(k + i) * norm[i] for i in range(KRYLOV)]
+    lower, pivots, least = ({}, [], None)
+    scaled = {}
+    for j in range(KRYLOV):
+        pivot = jnp.ones_like(right[0])
+        for m in range(j):
+            pivot = pivot - scaled[j, m] * lower[j, m]
+        pivots.append(pivot)
+        least = pivot if least is None else jnp.minimum(least, pivot)
+        inverse = 1.0 / pivot
+        for i in range(j + 1, KRYLOV):
+            value = full[j, i] * norm[i] * norm[j]
+            for m in range(j):
+                value = value - scaled[i, m] * lower[j, m]
+            scaled[i, j] = value
+            lower[i, j] = value * inverse
+    forward = []
+    for i in range(KRYLOV):
+        value = right[i]
+        for m in range(i):
+            value = value - lower[i, m] * forward[m]
+        forward.append(value)
+    answer = [None] * KRYLOV
+    for i in reversed(range(KRYLOV)):
+        value = forward[i] / pivots[i]
+        for m in range(i + 1, KRYLOV):
+            value = value - lower[m, i] * answer[m]
+        answer[i] = value
+    return ([a * n for a, n in zip(answer, norm)], least)
+
+
+def first_picard_kernel(
+    place_ref, grid_ref, mine_ref, left_ref, right_ref, basis_ref, fixed_ref, sums_ref
+):
+    rows = mine_ref.shape[1]
+    lane = lax.broadcasted_iota(jnp.int32, (rows, 128), 1)
+    row = lax.broadcasted_iota(jnp.int32, (rows, 128), 0) + (place_ref[0] * 8 - OWN)
+    row_in = (row >= 0) & (row < grid_ref[0] * 8)
+    from_right = lane < SIDE
+    col = place_ref[1] + jnp.where(from_right, 1, -1)
+    side_in = row_in & (col >= 0) & (col < grid_ref[1])
+
+    def field(k):
+        side = jnp.where(from_right, right_ref[k], left_ref[k])
+        return jnp.concatenate(
+            [jnp.where(row_in, mine_ref[k], 0.0), jnp.where(side_in, side, 0.0)], axis=1
+        )
+
+    u, v, drag, thick, stiff, surface = (field(k) for k in range(6))
+    t_sum = thick + next_col(thick)
+    s_sum = stiff + next_col(stiff)
+    corner_product = (1.0 / 64.0) * (t_sum + next_row(t_sum)) * (s_sum + next_row(s_sum))
+    driving = (
+        -thick * 0.5 * (next_row(surface) - last_row(surface)),
+        -thick * 0.5 * (next_col(surface) - last_col(surface)),
+    )
+    kept = slice(OWN - 8, OWN + 16)
+
+    def keep(k, b_u, b_v):
+        basis_ref[2 * k] = b_u[kept]
+        basis_ref[2 * k + 1] = b_v[kept]
+
+    for k, value in enumerate((u, v, drag, corner_product, driving[0], driving[1])):
+        fixed_ref[k] = value[kept]
+    products = krylov_basis(u, v, drag, driving, corner_product, OWN, keep)
+    write_sums(products, sums_ref)
+
+
+def second_picard_kernel(
+    parts_ref, basis_ref, fixed_ref, next_ref, velocity_ref, sums_ref, least_ref
+):
+    answer, least = small_solve(parts_ref[...])
+    u, v = (fixed_ref[0], fixed_ref[1])
+    for k in range(KRYLOV):
+        u = u + answer[k] * basis_ref[2 * k]
+        v = v + answer[k] * basis_ref[2 * k + 1]
+    velocity_ref[0] = u[8:16, :128]
+    velocity_ref[1] = v[8:16, :128]
+    least_ref[...] = jnp.broadcast_to(least, least_ref.shape)
+
+    def keep(k, b_u, b_v):
+        next_ref[2 * k] = b_u[8:16, :128]
+        next_ref[2 * k + 1] = b_v[8:16, :128]
+
+    driving = (fixed_ref[4], fixed_ref[5])
+    products = krylov_basis(u, v, fixed_ref[2], driving, fixed_ref[3], 8, keep)
+    write_sums(products, sums_ref)
+
+
+def last_kernel(parts_ref, basis_ref, velocity_ref, least_ref, out_ref, worst_ref):
+    answer, least = small_solve(parts_ref[...])
+    u, v = (velocity_ref[0], velocity_ref[1])
+    for k in range(KRYLOV):
+        u = u + answer[k] * basis_ref[2 * k]
+        v = v + answer[k] * basis_ref[2 * k + 1]
+    out_ref[0] = u
+    out_ref[1] = v
+    worst_ref[...] = jnp.minimum(least_ref[...], least)
+
+
+def over_all(sums):
+    count = lax.axis_size(GX)
+    part = lax.all_to_all(sums, GY, 0, 0, tiled=True)
+    part = jnp.broadcast_to(jnp.sum(part, axis=0, keepdims=True), (count, 128))
+    return lax.all_to_all(part, GX, 0, 0, tiled=True)
+
+
+def shifted(array, axis, by):
+    size = lax.axis_size(axis)
+    return lax.ppermute(array, axis, [(i, (i + by) % size) for i in range(size)])
+
+
+def momentum(fields):
+    f32 = jnp.float32
+    below = [shifted(fields, GX, by) for by in (2, 1)]
+    above = [shifted(fields, GX, -by) for by in (1, 2)]
+    mine = jnp.concatenate(below + [fields] + above, axis=1)
+    left = shifted(mine, GY, 1)
+    right = shifted(mine, GY, -1)
+    gx, gy = (lax.axis_size(GX), lax.axis_size(GY))
+    place = jnp.stack([lax.axis_index(GX), lax.axis_index(GY)]).astype(jnp.int32)
+    grid = jnp.array([gx, gy], jnp.int32)
+    smem = pl.BlockSpec(memory_space=pltpu.SMEM)
+    vmem = pl.BlockSpec(memory_space=pltpu.VMEM)
+    struct = jax.ShapeDtypeStruct
+    basis, fixed, sums = pl.pallas_call(
+        first_picard_kernel,
+        out_shape=(
+            struct((2 * KRYLOV, 24, 256), f32),
+            struct((6, 24, 256), f32),
+            struct((gy, 128), f32),
+        ),
+        in_specs=[smem, smem, vmem, vmem, vmem],
+        out_specs=(vmem, vmem, vmem),
+        name="first_picard",
+    )(place, grid, mine, left, right)
+    basis, velocity, sums, least = pl.pallas_call(
+        second_picard_kernel,
+        out_shape=(
+            struct((2 * KRYLOV, 8, 128), f32),
+            struct((2, 8, 128), f32),
+            struct((gy, 128), f32),
+            struct((8, 128), f32),
+        ),
+        name="second_picard",
+    )(over_all(sums), basis, fixed)
+    return pl.pallas_call(
+        last_kernel,
+        out_shape=(struct((2, 8, 128), f32), struct((8, 128), f32)),
+        name="last_picard",
+    )(over_all(sums), basis, velocity, least)
+
+
+def plain_picard(velocity, thickness, stiffness, surface, drag_term, projector):
+    statics = with_halo(jnp.stack([thickness, stiffness, surface]), ((GX, 1), (GY, 2)), 1)
+    thick_corner = corner_mean(statics[0])
+    stiff_corner = corner_mean(statics[1])
+    heights = statics[2]
+    driving = jnp.stack(
+        [
+            -thickness * 0.5 * (heights[2:, 1:-1] - heights[:-2, 1:-1]),
+            -thickness * 0.5 * (heights[1:-1, 2:] - heights[1:-1, :-2]),
+        ]
+    )
+
+    def total(array):
+        return one_axis_at_a_time(jnp.sum(array), GX_GY)
+
+    def picard(_, velocity):
+        rates = strains(with_halo(velocity, ((GX, 1), (GY, 2)), 1))
+        weight = viscous_weight(rates, thick_corner, stiff_corner)
+        residual = projector * (driving - stress_image(rates, weight, velocity, drag_term))
+
+        def krylov(_, state):
+            change, residual, direction, norm_now = state
+            imaged = apply_field(direction, weight, drag_term, projector)
+            step_size = norm_now / total(direction * imaged)
+            change = change + step_size * direction
+            residual = residual - step_size * imaged
+            norm_next = total(residual * residual)
+            direction = residual + norm_next / norm_now * direction
+            return (change, residual, direction, norm_next)
+
+        state = (jnp.zeros_like(velocity), residual, residual, total(residual * residual))
+        return velocity + lax.fori_loop(0, KRYLOV, krylov, state)[0]
+
+    return lax.fori_loop(0, PICARD, picard, velocity)
 
 
 def shards(
@@ -208,49 +540,27 @@
             moved, inverse_bed, inverse_shelf, kappa, ice_cols, bed_cols, surface_enthalpy, geo_flux
         )
     stiffness = jnp.exp(-soften * jnp.mean(current, axis=0))
-    statics = with_halo(jnp.stack([thickness, stiffness, surface]), ((GX, 1), (GY, 2)), 1)
-    thick_corner = corner_mean(statics[0])
-    stiff_corner = corner_mean(statics[1])
-    heights = statics[2]
-    driving = jnp.stack(
-        [
-            -thickness * 0.5 * (heights[2:, 1:-1] - heights[:-2, 1:-1]),
-            -thickness * 0.5 * (heights[1:-1, 2:] - heights[1:-1, :-2]),
-        ]
-    )
     free_cells = (boundary_code == 0) & (ice_mask == 1)
     held_cells = free_cells | (boundary_code == 2)
-    projector = free_cells.astype(jnp.float32)[None]
+    projector = free_cells.astype(jnp.float32)
     drag_term = jnp.where(grounded == 1, friction, 0.0) + shelf_drag
     velocity = jnp.where(held_cells[None], velocity_init, 0.0)
-    for picard_step in range(PICARD):
-        padded_flow = with_halo(velocity, ((GX, 1), (GY, 2)), 1)
-        rates = strains(padded_flow)
-        weight = viscous_weight(rates, thick_corner, stiff_corner)
-        residual = projector * (driving - stress_image(rates, weight, velocity, drag_term))
-        change = jnp.zeros_like(velocity)
-        imaged = apply_field(residual, weight, drag_term, projector)
-        norm_now, product = paired_sums(residual, imaged)
-        step_size = norm_now / product
-        direction = residual
-        along = imaged
-        for krylov_step in range(KRYLOV):
-            change = change + step_size * direction
-            residual = residual - step_size * along
-            if krylov_step + 1 < KRYLOV:
-                imaged = apply_field(residual, weight, drag_term, projector)
-                norm_next, product = paired_sums(residual, imaged)
-                factor = norm_next / norm_now
-                step_size = norm_next / (product - factor * norm_next / step_size)
-                direction = residual + factor * direction
-                along = imaged + factor * along
-                norm_now = norm_next
-        velocity = velocity + change
+    fields = jnp.stack(
+        [velocity[0], velocity[1], projector * drag_term, thickness, stiffness, surface]
+    )
+    quick, worst = momentum(fields)
+    velocity = lax.cond(
+        worst[0, 0] > PIVOT_FLOOR,
+        lambda: quick,
+        lambda: plain_picard(
+            velocity, thickness, stiffness, surface, drag_term, projector[None]
+        ),
+    )
     return (current, velocity)
 
 
 def solution(mesh):
-    torus = Mesh(mesh.devices.reshape(4, 8, 8, 2), ("gx_0", "gx_1", "gy_0", "gy_1"))
+    torus = Mesh(mesh.devices.reshape(TORUS), ("gx_0", "gx_1", "gy_0", "gy_1"))
     placed = (
         P(None, GX, GY),
         P(None, GX, GY),

time: 1810 us -> 149 us (0.08)
  blocking collectives: 620 us -> 49.6 us
  other arithmetic: 382 us -> 7.89 us
  loops' own time: 360 us -> 0.02 us
  between operations: 163 us -> 1.9 us
  starting transfers between devices: 198 us -> 46.2 us
  local copies, waits for them, and re-layouts: 50.4 us -> 8.34 us
    psum x48 -> x0, blocking collectives: 620 us -> none  [one_axis_at_a_time(): return functools.reduce(lax.psum, axes, shard)]
    another operation x4 -> x1, loops' own time: 360 us -> 0.02 us  [shards(): lax.cond(worst[0, 0] > PIVOT_FLOOR, lambda: quick, lambda: plain_picard(v...]
    div x9 -> x0, other arithmetic: 162 us -> none  [column_inverses(): lax.linalg.tridiagonal_solve(lower_band, on_bed, upper_band, identity)]
    ppermute x60 -> x6, starting transfers between devices: 171 us -> 16.3 us  [shifted(): lax.ppermute(array, axis, [(i, (i + by) % size) for i in range(size)])]
    sub x16 -> x0, other arithmetic: 120 us -> none  [the longest x6 120 us: column_inverses(): lax.linalg.tridiagonal_solve(lower_band, on_bed, upper_band, identity)]
    broadcast_in_dim x32 -> x0, other arithmetic: 81.1 us -> none  [column_inverses(): lax.linalg.tridiagonal_solve(lower_band, on_bed, upper_band, identity)]
    all_to_all x0 -> x3, blocking collectives: none -> 49.6 us  [the longest x2 31.6 us: over_all(): part = lax.all_to_all(sums, GY, 0, 0, tiled=True)]
    slice x96 -> x3, local copies, waits for them, and re-layouts: 43.5 us -> 1.78 us  [the longest x1 1.19 us: shards(): worst[0, 0] > PIVOT_FLOOR]
  transfers between devices with their start and end apart: 68 -> 15, of which waited for: 28 -> 5; matrix products, arithmetic and copies ran while one was open for 23% -> 2% of each run, Pallas kernels for 0% -> 1%
where the time goes in v1:
time: 149 us; the launch traced here: 148 us
  blocking collectives  49.6 us (33%)
  starting transfers between devices  46.2 us (31%)
  waiting for transfers between devices  17.6 us (12%)
  Pallas kernels  13.1 us (9%)
  local copies, waits for them, and re-layouts  8.34 us (6%)
  other arithmetic  7.89 us (5%)
  matrix products  3.11 us (2%)
  between operations  1.9 us (1%)
    all_to_all x2, blocking collectives, over_all(): part = lax.all_to_all(sums, GY, 0, 0, tiled=True)  31.6 us
    all_to_all x1, blocking collectives, over_all(): return lax.all_to_all(part, GX, 0, 0, tiled=True)  18.1 us
    ppermute x6, starting transfers between devices, shifted(): lax.ppermute(array, axis, [(i, (i + by) % size) for i in range(size)])  16.3 us
    ppermute x4, starting transfers between devices, with_halo_2(): lax.ppermute(last, axis, up)  15.9 us
    ppermute x4, starting transfers between devices, with_halo_2(): lax.ppermute(first, axis, [(b, a) for a, b in up])  10.2 us
    ppermute x6, waiting for transfers between devices, shifted(): lax.ppermute(array, axis, [(i, (i + by) % size) for i in range(size)])  7.94 us
    all_to_all x1, waiting for transfers between devices, over_all(): return lax.all_to_all(part, GX, 0, 0, tiled=True)  7.66 us
    unnamed x44, local copies, waits for them, and re-layouts  5.8 us
  transfers between devices with their start and end apart: 15, of which 5 were waited for; matrix products, arithmetic and copies ran while one was open for 2% of the time, Pallas kernels for 1%

profile of v1, /device:TPU:1, one launch (start us, length us, event | category | flops | bytes accessed | tf_op | source)
XLA Modules:
  0.0 147.8 jit_solution(15583369888142200714)
XLA Ops:
  0.6 0.9 copy.27
  1.6 1.3 copy.28
  3.0 1.3 collective-permute-start.14
  4.3 4.7 %collective-permute-start.13 = (f32[130,2,128]{0,2,1:T(8,128)S(1)}, f32[130,2,128]{0,2,1:T(8,128)S(1)}, u32[]{:S(2)}, u32[]{:S(2)}) collective-permute-start(f32[130,2,128]{0,2,1:T(8,128)S(1)} %get-tuple-element.426), channel_id=1, source_target_pairs={{0,16},{16,32},{32,48},{48,64},{64,80},{80,96},{96,112},{112,128},... | collective-permute-start | bytes 399368 | tf_op jit(solution)/shard_map/ppermute | solution.py:56
  9.0 5.3 %collective-permute-start.12 = (f32[130,8,2]{0,2,1:T(2,128)S(1)}, f32[130,8,2]{0,2,1:T(2,128)S(1)}, u32[]{:S(2)}, u32[]{:S(2)}) collective-permute-start(f32[130,8,2]{0,2,1:T(2,128)S(1)} %get-tuple-element.424), channel_id=1, source_target_pairs={{0,1},{1,2},{2,3},{3,4},{4,5},{5,6},{6,7},{7,8},{8,9},{9,10},{10,1... | collective-permute-start | bytes 24968 | tf_op jit(solution)/shard_map/ppermute | solution.py:56
  14.3 4.7 %collective-permute-start.15 = (f32[130,8,2]{0,2,1:T(2,128)S(1)}, f32[130,8,2]{0,2,1:T(2,128)S(1)}, u32[]{:S(2)}, u32[]{:S(2)}) collective-permute-start(f32[130,8,2]{0,2,1:T(2,128)S(1)} %get-tuple-element.425), channel_id=1, source_target_pairs={{1,0},{2,1},{3,2},{4,3},{5,4},{6,5},{7,6},{8,7},{9,8},{10,9},{11,1... | collective-permute-start | bytes 24968 | tf_op jit(solution)/shard_map/ppermute | solution.py:57
  18.9 0.5 slice.662
  19.6 0.7 convert_multiply_fusion
  20.3 0.6 pad_maximum_fusion.26.kappa_ref
  20.9 2.2 %column_inverses.1 = (f32[128,128]{1,0:T(8,128)}, f32[128,128]{1,0:T(8,128)}) custom-call(f32[16,128]{1,0:T(8,128)} %pad_maximum_fusion.26.kappa_ref), custom_call_target="tpu_custom_call" | custom-call | tf_op jit(solution)/shard_map/column_inverses/pallas_call | solution.py:206
  24.0 1.5 %maximum_reduce_fusion = (f32[8,129]{1,0:T(8,128)S(1)}, f32[8,129]{1,0:T(8,128)S(1)}, f32[8,129]{1,0:T(8,128)S(1)}, f32[8,129]{1,0:T(8,128)S(1)}) fusion(f32[130,12,130]{0,2,1:T(8,128)S(1)} %get-tuple-element.423, f32[130,12,130]{0,2,1:T(8,128)S(1)} %get-tuple-element.422), kind=kLoop, calls=%fused_computation.171 | loop fusion | flops 8256 | bytes 24768 | tf_op jit(solution)/shard_map/max | solution.py:79
  25.5 0.8 fusion.56
  26.3 0.8 fusion.41
  27.3 0.7 copy-done.2
  27.9 0.7 fusion.63
  28.7 0.8 fusion.24
  29.5 1.9 %collective-permute-start.18 = (f32[128,8,2]{0,2,1:T(2,128)S(1)}, f32[128,8,2]{0,2,1:T(2,128)S(1)}, u32[]{:S(2)}, u32[]{:S(2)}) collective-permute-start(f32[128,8,2]{0,2,1:T(2,128)S(1)} %get-tuple-element.430), channel_id=1, source_target_pairs={{0,1},{1,2},{2,3},{3,4},{4,5},{5,6},{6,7},{7,8},{8,9},{9,10},{10,1... | collective-permute-start | bytes 24584 | tf_op jit(solution)/shard_map/ppermute | solution.py:56
  31.4 1.3 collective-permute-start.17
  32.7 4.0 %collective-permute-start.16 = (f32[128,2,128]{0,2,1:T(8,128)S(1)}, f32[128,2,128]{0,2,1:T(8,128)S(1)}, u32[]{:S(2)}, u32[]{:S(2)}) collective-permute-start(f32[128,2,128]{0,2,1:T(8,128)S(1)} %get-tuple-element.432), channel_id=1, source_target_pairs={{0,16},{16,32},{32,48},{48,64},{64,80},{80,96},{96,112},{112,128},... | collective-permute-start | bytes 393224 | tf_op jit(solution)/shard_map/ppermute | solution.py:56
  36.7 3.0 %collective-permute-start.19 = (f32[128,8,2]{0,2,1:T(2,128)S(1)}, f32[128,8,2]{0,2,1:T(2,128)S(1)}, u32[]{:S(2)}, u32[]{:S(2)}) collective-permute-start(f32[128,8,2]{0,2,1:T(2,128)S(1)} %get-tuple-element.431), channel_id=1, source_target_pairs={{1,0},{2,1},{3,2},{4,3},{5,4},{6,5},{7,6},{8,7},{9,8},{10,9},{11,1... | collective-permute-start | bytes 24584 | tf_op jit(solution)/shard_map/ppermute | solution.py:57
  39.7 2.0 %collective-permute-done.19 = f32[128,8,2]{0,2,1:T(2,128)S(1)} collective-permute-done((f32[128,8,2]{0,2,1:T(2,128)S(1)}, f32[128,8,2]{0,2,1:T(2,128)S(1)}, u32[]{:S(2)}, u32[]{:S(2)}) %collective-permute-start.19) | collective-permute-done | bytes 8224 | tf_op jit(solution)/shard_map/ppermute | solution.py:57
  41.8 0.8 fusion.49
  42.6 0.8 fusion.32
  43.6 0.7 fusion.67
  44.3 0.9 fusion.113
  45.2 4.2 %collective-permute-start.20 = (f32[6,8,128]{2,1,0:T(8,128)S(1)}, f32[6,8,128]{2,1,0:T(8,128)S(1)}, u32[]{:S(2)}, u32[]{:S(2)}) collective-permute-start(f32[6,8,128]{2,1,0:T(8,128)S(1)} %constant_dynamic-update-slice_fusion), channel_id=1, source_target_pairs={{0,32},{16,48},{32,64},{48,80},{64,96},{80,112},{96,128},{112,144}... | collective-permute-start | bytes 73736 | tf_op jit(solution)/shard_map/ppermute | solution.py:434
  49.5 4.6 %collective-permute-start.21 = (f32[6,8,128]{2,1,0:T(8,128)S(1)}, f32[6,8,128]{2,1,0:T(8,128)S(1)}, u32[]{:S(2)}, u32[]{:S(2)}) collective-permute-start(f32[6,8,128]{2,1,0:T(8,128)S(1)} %constant_dynamic-update-slice_fusion), channel_id=1, source_target_pairs={{0,16},{16,32},{32,48},{48,64},{64,80},{80,96},{96,112},{112,128},... | collective-permute-start | bytes 73736 | tf_op jit(solution)/shard_map/ppermute | solution.py:434
  54.1 4.0 %collective-permute-start.22 = (f32[6,8,128]{2,1,0:T(8,128)S(1)}, f32[6,8,128]{2,1,0:T(8,128)S(1)}, u32[]{:S(2)}, u32[]{:S(2)}) collective-permute-start(f32[6,8,128]{2,1,0:T(8,128)S(1)} %constant_dynamic-update-slice_fusion), channel_id=1, source_target_pairs={{0,496},{16,0},{32,16},{48,32},{64,48},{80,64},{96,80},{112,96},{1... | collective-permute-start | bytes 73736 | tf_op jit(solution)/shard_map/ppermute | solution.py:434
  58.1 1.9 %collective-permute-start.23 = (f32[6,8,128]{2,1,0:T(8,128)S(1)}, f32[6,8,128]{2,1,0:T(8,128)S(1)}, u32[]{:S(2)}, u32[]{:S(2)}) collective-permute-start(f32[6,8,128]{2,1,0:T(8,128)S(1)} %constant_dynamic-update-slice_fusion), channel_id=1, source_target_pairs={{0,480},{16,496},{32,0},{48,16},{64,32},{80,48},{96,64},{112,80},{... | collective-permute-start | bytes 73736 | tf_op jit(solution)/shard_map/ppermute | solution.py:434
  60.2 4.0 %collective-permute-done.23 = f32[6,8,128]{2,1,0:T(8,128)S(1)} collective-permute-done((f32[6,8,128]{2,1,0:T(8,128)S(1)}, f32[6,8,128]{2,1,0:T(8,128)S(1)}, u32[]{:S(2)}, u32[]{:S(2)}) %collective-permute-start.23) | collective-permute-done | bytes 24608 | tf_op jit(solution)/shard_map/ppermute | solution.py:434
  64.2 1.5 %collective-permute-start.24 = (f32[6,40,128]{2,1,0:T(8,128)S(1)}, f32[6,40,128]{2,1,0:T(8,128)S(1)}, u32[]{:S(2)}, u32[]{:S(2)}) collective-permute-start(f32[6,40,128]{2,1,0:T(8,128)S(1)} %constant_dynamic-update-slice_fusion.5.mine_ref), channel_id=1, source_target_pairs={{0,1},{1,2},{2,3},{3,4},{4,5},{5,6},{6,7},{7,8},{8,9},{9,10},{10,1... | collective-permute-start | bytes 368648 | tf_op jit(solution)/shard_map/ppermute | solution.py:434
  65.7 0.6 pad_add_fusion.place_ref
  66.3 1.2 collective-permute-done.24.left_ref
  67.5 2.7 %collective-permute-done.25.right_ref = f32[6,40,128]{2,1,0:T(8,128)S(1)} collective-permute-done((f32[6,40,128]{2,1,0:T(8,128)S(1)}, f32[6,40,128]{2,1,0:T(8,128)S(1)}, u32[]{:S(2)}, u32[]{:S(2)}) %collective-permute-start.25) | collective-permute-done | bytes 122912 | tf_op jit(solution)/shard_map/ppermute | solution.py:434
  70.3 0.7 copy-done.6
  70.9 3.3 %first_picard.1 = (f32[12,24,256]{2,1,0:T(8,128)}, f32[6,24,256]{2,1,0:T(8,128)}, f32[16,128]{1,0:T(8,128)}) custom-call(s32[2]{0:T(128)} %pad_add_fusion.place_ref, s32[2]{0:T(128)} %constant.169.clone.grid_ref, f32[6,40,128]{2,1,0:T(8,128)} %copy-done.3, f32[6,40,128]{2,1,0:T(8,128)} %copy-done.5, f32[6,40,128]{2,1,0:T(8,128)} %copy-done.6), custom_call_target="tpu_custom_call" | custom-call | tf_op jit(solution)/shard_map/first_picard/pallas_call | solution.py:450
  74.2 19.2 %all_to_all.34 = f32[16,1,128]{2,1,0:T(1,128)S(1)} all-to-all(f32[16,1,128]{2,1,0:T(1,128)} %bitcast.141), channel_id=1, replica_groups=mesh['gx_0'=4,'gx_1'=8,'gy_0'=8,'gy_1'=2] {'gy_0','gy_1'}, dimensions={0} | all-to-all | bytes 16384 | tf_op jit(solution)/shard_map/all_to_all | solution.py:427
  93.4 18.1 %all_to_all.35 = f32[32,1,128]{2,1,0:T(1,128)} all-to-all(f32[32,1,128]{2,1,0:T(1,128)S(1)} %broadcast_in_dim.137), channel_id=1, replica_groups=mesh['gx_0'=4,'gx_1'=8,'gy_0'=8,'gy_1'=2] {'gx_0','gx_1'}, dimensions={0} | all-to-all | bytes 32768 | tf_op jit(solution)/shard_map/all_to_all | solution.py:429
  111.5 4.7 %second_picard.1 = (f32[12,8,128]{2,1,0:T(8,128)}, f32[2,8,128]{2,1,0:T(8,128)}, f32[16,128]{1,0:T(8,128)}, f32[8,128]{1,0:T(8,128)}) custom-call(f32[32,128]{1,0:T(8,128)} %bitcast.140, f32[12,24,256]{2,1,0:T(8,128)} %get-tuple-element.295.basis_ref, f32[6,24,256]{2,1,0:T(8,128)} %get-tuple-element.296.fixed_ref), custom_call_target="tpu_custom_call" | custom-call | tf_op jit(solution)/shard_map/second_picard/pallas_call | solution.py:461
  116.2 12.4 %all_to_all.36 = f32[16,1,128]{2,1,0:T(1,128)S(1)} all-to-all(f32[16,1,128]{2,1,0:T(1,128)} %bitcast.142), channel_id=1, replica_groups=mesh['gx_0'=4,'gx_1'=8,'gy_0'=8,'gy_1'=2] {'gy_0','gy_1'}, dimensions={0} | all-to-all | bytes 16384 | tf_op jit(solution)/shard_map/all_to_all | solution.py:427
  128.6 0.6 broadcast_in_dim.138
  129.2 3.8 %all-to-all-start.3 = ((f32[32,1,128]{2,1,0:T(1,128)}), f32[32,1,128]{2,1,0:T(1,128)S(1)}, u32[]{:S(2)}, u32[]{:S(2)}) async-start(f32[32,1,128]{2,1,0:T(1,128)} %broadcast_in_dim.138), calls=%async_computation.3 | async-start | bytes 32768 | tf_op jit(solution)/shard_map/all_to_all | solution.py:429
  133.1 1.0 copy.33
  134.1 7.7 %all-to-all-done.3 = f32[32,1,128]{2,1,0:T(1,128)S(1)} async-done(((f32[32,1,128]{2,1,0:T(1,128)}), f32[32,1,128]{2,1,0:T(1,128)S(1)}, u32[]{:S(2)}, u32[]{:S(2)}) %all-to-all-start.3) | async-done | bytes 16416 | tf_op jit(solution)/shard_map/all_to_all | solution.py:429
  141.7 0.6 copy-done.8
  142.3 3.0 %last_picard.1 = (f32[2,8,128]{2,1,0:T(8,128)S(1)}, f32[8,128]{1,0:T(8,128)}) custom-call(f32[32,128]{1,0:T(8,128)} %bitcast.139, f32[12,8,128]{2,1,0:T(8,128)} %get-tuple-element.298.basis_ref, f32[2,8,128]{2,1,0:T(8,128)} %get-tuple-element.299.velocity_ref, f32[8,128]{1,0:T(8,128)} %get-tuple-element.300.least_ref), custom_call_target="tpu_custom_call" | custom-call | tf_op jit(solution)/shard_map/last_picard/pallas_call | solution.py:471
  145.3 1.2 slice.679
  147.2 0.6 copy-done
  (80 shorter events, 1.7 us)
Async XLA Ops:
  1.6 17.4 %copy-start.16 = (f32[129]{0:T(256)S(1)}, f32[129]{0:T(256)}, u32[]{:S(2)}) copy-start(f32[129]{0:T(256)} %param.23) | copy-start | bytes 1552
  1.6 18.0 %copy-start.9 = (s32[8,128]{1,0:T(8,128)S(1)}, s32[8,128]{1,0:T(8,128)}, u32[]{:S(2)}) copy-start(s32[8,128]{1,0:T(8,128)} %param.27) | copy-start | bytes 12292
  1.6 17.9 %copy-start.11 = (s32[8,128]{1,0:T(8,128)S(1)}, s32[8,128]{1,0:T(8,128)}, u32[]{:S(2)}) copy-start(s32[8,128]{1,0:T(8,128)} %param.28) | copy-start | bytes 12292
  1.6 17.9 %copy-start.12 = (s32[8,128]{1,0:T(8,128)S(1)}, s32[8,128]{1,0:T(8,128)}, u32[]{:S(2)}) copy-start(s32[8,128]{1,0:T(8,128)} %param.26) | copy-start | bytes 12292
  1.6 18.0 %copy-start.10 = (f32[2,8,128]{2,1,0:T(8,128)S(1)}, f32[2,8,128]{2,1,0:T(8,128)}, u32[]{:S(2)}) copy-start(f32[2,8,128]{2,1,0:T(8,128)} %param.19) | copy-start | bytes 24580
  1.6 18.0 %copy-start.13 = (f32[8,128]{1,0:T(8,128)S(1)}, f32[8,128]{1,0:T(8,128)}, u32[]{:S(2)}) copy-start(f32[8,128]{1,0:T(8,128)} %param.22) | copy-start | bytes 12292
  1.6 18.0 %copy-start.14 = (f32[8,128]{1,0:T(8,128)S(1)}, f32[8,128]{1,0:T(8,128)}, u32[]{:S(2)}) copy-start(f32[8,128]{1,0:T(8,128)} %param.25) | copy-start | bytes 12292
  1.6 18.0 %copy-start.15 = (f32[8,128]{1,0:T(8,128)S(1)}, f32[8,128]{1,0:T(8,128)}, u32[]{:S(2)}) copy-start(f32[8,128]{1,0:T(8,128)} %param.24) | copy-start | bytes 12292
  3.0 20.1 %collective-permute-start.14 = (f32[130,2,128]{0,2,1:T(8,128)S(1)}, f32[130,2,128]{0,2,1:T(8,128)S(1)}, u32[]{:S(2)}, u32[]{:S(2)}) collective-permute-start(f32[130,2,128]{0,2,1:T(8,128)S(1)} %get-tuple-element.427), channel_id=1, source_target_pairs={{16,0},{32,16},{48,32},{64,48},{80,64},{96,80},{112,96},{128,112},... | collective-permute-start | bytes 399368 | tf_op jit(solution)/shard_map/ppermute | solution.py:57
  4.3 18.9 %collective-permute-start.13 = (f32[130,2,128]{0,2,1:T(8,128)S(1)}, f32[130,2,128]{0,2,1:T(8,128)S(1)}, u32[]{:S(2)}, u32[]{:S(2)}) collective-permute-start(f32[130,2,128]{0,2,1:T(8,128)S(1)} %get-tuple-element.426), channel_id=1, source_target_pairs={{0,16},{16,32},{32,48},{48,64},{64,80},{80,96},{96,112},{112,128},... | collective-permute-start | bytes 399368 | tf_op jit(solution)/shard_map/ppermute | solution.py:56
  9.0 14.1 %collective-permute-start.12 = (f32[130,8,2]{0,2,1:T(2,128)S(1)}, f32[130,8,2]{0,2,1:T(2,128)S(1)}, u32[]{:S(2)}, u32[]{:S(2)}) collective-permute-start(f32[130,8,2]{0,2,1:T(2,128)S(1)} %get-tuple-element.424), channel_id=1, source_target_pairs={{0,1},{1,2},{2,3},{3,4},{4,5},{5,6},{6,7},{7,8},{8,9},{9,10},{10,1... | collective-permute-start | bytes 24968 | tf_op jit(solution)/shard_map/ppermute | solution.py:56
  14.3 8.8 %collective-permute-start.15 = (f32[130,8,2]{0,2,1:T(2,128)S(1)}, f32[130,8,2]{0,2,1:T(2,128)S(1)}, u32[]{:S(2)}, u32[]{:S(2)}) collective-permute-start(f32[130,8,2]{0,2,1:T(2,128)S(1)} %get-tuple-element.425), channel_id=1, source_target_pairs={{1,0},{2,1},{3,2},{4,3},{5,4},{6,5},{7,6},{8,7},{9,8},{10,9},{11,1... | collective-permute-start | bytes 24968 | tf_op jit(solution)/shard_map/ppermute | solution.py:57
  27.1 0.8 copy-start.2
  27.1 1.6 %copy-start.1 = (f32[128,128]{1,0:T(8,128)S(1)}, f32[128,128]{1,0:T(8,128)}, u32[]{:S(2)}) copy-start(f32[128,128]{1,0:T(8,128)} %get-tuple-element.293) | copy-start | bytes 196612
  27.9 11.8 %copy-start.4 = (f32[8,128]{1,0:T(8,128)S(1)}, f32[8,128]{1,0:T(8,128)}, u32[]{:S(2)}) copy-start(f32[8,128]{1,0:T(8,128)} %param.20) | copy-start | bytes 12292
  29.5 10.2 %collective-permute-start.18 = (f32[128,8,2]{0,2,1:T(2,128)S(1)}, f32[128,8,2]{0,2,1:T(2,128)S(1)}, u32[]{:S(2)}, u32[]{:S(2)}) collective-permute-start(f32[128,8,2]{0,2,1:T(2,128)S(1)} %get-tuple-element.430), channel_id=1, source_target_pairs={{0,1},{1,2},{2,3},{3,4},{4,5},{5,6},{6,7},{7,8},{8,9},{9,10},{10,1... | collective-permute-start | bytes 24584 | tf_op jit(solution)/shard_map/ppermute | solution.py:56
  31.4 10.3 %collective-permute-start.17 = (f32[128,2,128]{0,2,1:T(8,128)S(1)}, f32[128,2,128]{0,2,1:T(8,128)S(1)}, u32[]{:S(2)}, u32[]{:S(2)}) collective-permute-start(f32[128,2,128]{0,2,1:T(8,128)S(1)} %get-tuple-element.433), channel_id=1, source_target_pairs={{16,0},{32,16},{48,32},{64,48},{80,64},{96,80},{112,96},{128,112},... | collective-permute-start | bytes 393224 | tf_op jit(solution)/shard_map/ppermute | solution.py:57
  32.7 9.0 %collective-permute-start.16 = (f32[128,2,128]{0,2,1:T(8,128)S(1)}, f32[128,2,128]{0,2,1:T(8,128)S(1)}, u32[]{:S(2)}, u32[]{:S(2)}) collective-permute-start(f32[128,2,128]{0,2,1:T(8,128)S(1)} %get-tuple-element.432), channel_id=1, source_target_pairs={{0,16},{16,32},{32,48},{48,64},{64,80},{80,96},{96,112},{112,128},... | collective-permute-start | bytes 393224 | tf_op jit(solution)/shard_map/ppermute | solution.py:56
  36.7 5.0 %collective-permute-start.19 = (f32[128,8,2]{0,2,1:T(2,128)S(1)}, f32[128,8,2]{0,2,1:T(2,128)S(1)}, u32[]{:S(2)}, u32[]{:S(2)}) collective-permute-start(f32[128,8,2]{0,2,1:T(2,128)S(1)} %get-tuple-element.431), channel_id=1, source_target_pairs={{1,0},{2,1},{3,2},{4,3},{5,4},{6,5},{7,6},{8,7},{9,8},{10,9},{11,1... | collective-permute-start | bytes 24584 | tf_op jit(solution)/shard_map/ppermute | solution.py:57
  43.6 1.6 %copy-start.7 = (f32[8,128]{1,0:T(8,128)S(1)}, f32[8,128]{1,0:T(8,128)}, u32[]{:S(2)}) copy-start(f32[8,128]{1,0:T(8,128)} %param.21) | copy-start | bytes 12292
  45.2 14.8 %collective-permute-start.20 = (f32[6,8,128]{2,1,0:T(8,128)S(1)}, f32[6,8,128]{2,1,0:T(8,128)S(1)}, u32[]{:S(2)}, u32[]{:S(2)}) collective-permute-start(f32[6,8,128]{2,1,0:T(8,128)S(1)} %constant_dynamic-update-slice_fusion), channel_id=1, source_target_pairs={{0,32},{16,48},{32,64},{48,80},{64,96},{80,112},{96,128},{112,144}... | collective-permute-start | bytes 73736 | tf_op jit(solution)/shard_map/ppermute | solution.py:434
  49.5 10.6 %collective-permute-start.21 = (f32[6,8,128]{2,1,0:T(8,128)S(1)}, f32[6,8,128]{2,1,0:T(8,128)S(1)}, u32[]{:S(2)}, u32[]{:S(2)}) collective-permute-start(f32[6,8,128]{2,1,0:T(8,128)S(1)} %constant_dynamic-update-slice_fusion), channel_id=1, source_target_pairs={{0,16},{16,32},{32,48},{48,64},{64,80},{80,96},{96,112},{112,128},... | collective-permute-start | bytes 73736 | tf_op jit(solution)/shard_map/ppermute | solution.py:434
  54.1 6.1 %collective-permute-start.22 = (f32[6,8,128]{2,1,0:T(8,128)S(1)}, f32[6,8,128]{2,1,0:T(8,128)S(1)}, u32[]{:S(2)}, u32[]{:S(2)}) collective-permute-start(f32[6,8,128]{2,1,0:T(8,128)S(1)} %constant_dynamic-update-slice_fusion), channel_id=1, source_target_pairs={{0,496},{16,0},{32,16},{48,32},{64,48},{80,64},{96,80},{112,96},{1... | collective-permute-start | bytes 73736 | tf_op jit(solution)/shard_map/ppermute | solution.py:434
  58.1 6.1 %collective-permute-start.23 = (f32[6,8,128]{2,1,0:T(8,128)S(1)}, f32[6,8,128]{2,1,0:T(8,128)S(1)}, u32[]{:S(2)}, u32[]{:S(2)}) collective-permute-start(f32[6,8,128]{2,1,0:T(8,128)S(1)} %constant_dynamic-update-slice_fusion), channel_id=1, source_target_pairs={{0,480},{16,496},{32,0},{48,16},{64,32},{80,48},{96,64},{112,80},{... | collective-permute-start | bytes 73736 | tf_op jit(solution)/shard_map/ppermute | solution.py:434
  64.2 6.1 %copy-start.3 = (f32[6,40,128]{2,1,0:T(8,128)}, f32[6,40,128]{2,1,0:T(8,128)S(1)}, u32[]{:S(2)}) copy-start(f32[6,40,128]{2,1,0:T(8,128)S(1)} %constant_dynamic-update-slice_fusion.5.mine_ref) | copy-start | bytes 368644
  64.2 3.4 %collective-permute-start.24 = (f32[6,40,128]{2,1,0:T(8,128)S(1)}, f32[6,40,128]{2,1,0:T(8,128)S(1)}, u32[]{:S(2)}, u32[]{:S(2)}) collective-permute-start(f32[6,40,128]{2,1,0:T(8,128)S(1)} %constant_dynamic-update-slice_fusion.5.mine_ref), channel_id=1, source_target_pairs={{0,1},{1,2},{2,3},{3,4},{4,5},{5,6},{6,7},{7,8},{8,9},{9,10},{10,1... | collective-permute-start | bytes 368648 | tf_op jit(solution)/shard_map/ppermute | solution.py:434
  65.7 4.6 %collective-permute-start.25 = (f32[6,40,128]{2,1,0:T(8,128)S(1)}, f32[6,40,128]{2,1,0:T(8,128)S(1)}, u32[]{:S(2)}, u32[]{:S(2)}) collective-permute-start(f32[6,40,128]{2,1,0:T(8,128)S(1)} %constant_dynamic-update-slice_fusion.5.mine_ref), channel_id=1, source_target_pairs={{0,15},{1,0},{2,1},{3,2},{4,3},{5,4},{6,5},{7,6},{8,7},{9,8},{10,9... | collective-permute-start | bytes 368648 | tf_op jit(solution)/shard_map/ppermute | solution.py:434
  67.5 2.7 %copy-start.5 = (f32[6,40,128]{2,1,0:T(8,128)}, f32[6,40,128]{2,1,0:T(8,128)S(1)}, u32[]{:S(2)}) copy-start(f32[6,40,128]{2,1,0:T(8,128)S(1)} %collective-permute-done.24.left_ref) | copy-start | bytes 368644
  70.3 0.7 copy-start.6
  129.2 12.5 %all-to-all-start.3 = ((f32[32,1,128]{2,1,0:T(1,128)}), f32[32,1,128]{2,1,0:T(1,128)S(1)}, u32[]{:S(2)}, u32[]{:S(2)}) async-start(f32[32,1,128]{2,1,0:T(1,128)} %broadcast_in_dim.138), calls=%async_computation.3 | async-start | bytes 32768 | tf_op jit(solution)/shard_map/all_to_all | solution.py:429
  141.7 0.6 copy-start.8
  147.2 0.6 copy-start

commit v2 on v1

--- a/solution.py
+++ b/solution.py
@@ -434,6 +434,22 @@
     return lax.ppermute(array, axis, [(i, (i + by) % size) for i in range(size)])
 
 
+def wide_halo(stacked):
+    rows, cols = stacked.shape[1:]
+    above = shifted(stacked[:, rows - 4 :], GX, 1)
+    below = shifted(stacked[:, :4], GX, -1)
+    tall = jnp.concatenate([above, stacked, below], axis=1)
+    left = shifted(tall[:, 2:-2, cols - 4 :], GY, 1)
+    right = shifted(tall[:, 2:-2, :4], GY, -1)
+    around = ((0, 0), (2, 2), (0, 0))
+    padded = jnp.concatenate([jnp.pad(left, around), tall, jnp.pad(right, around)], axis=2)
+    row = lax.broadcasted_iota(jnp.int32, padded.shape[1:], 0) - 4 + lax.axis_index(GX) * rows
+    col = lax.broadcasted_iota(jnp.int32, padded.shape[1:], 1) - 4 + lax.axis_index(GY) * cols
+    inside = (row >= 0) & (row < rows * lax.axis_size(GX))
+    inside = inside & (col >= 0) & (col < cols * lax.axis_size(GY))
+    return (jnp.where(inside[None], padded, 0.0), inside)
+
+
 def momentum(fields):
     f32 = jnp.float32
     below = [shifted(fields, GX, by) for by in (2, 1)]
@@ -524,21 +540,32 @@
     grounded,
     boundary_code,
 ):
-    ice_cols = ice_mask.astype(jnp.float32)
-    bed_cols = grounded.astype(jnp.float32)
     inverse_bed, inverse_shelf = column_inverses(kappa)
     levels = enthalpy.shape[0]
-    stacked = jnp.concatenate([enthalpy, velocity_init], axis=0)
-    padded = with_halo_2(stacked, ((GX, 1), (GY, 2)), 2)
-    current = padded[:levels]
-    courant = padded[levels:]
-    for substep in range(SUBSTEPS):
-        if substep > 0:
-            current = with_halo_2(current, ((GX, 1), (GY, 2)), 2)
-        moved = advect(current, courant[0], courant[1])
-        current = diffuse(
-            moved, inverse_bed, inverse_shelf, kappa, ice_cols, bed_cols, surface_enthalpy, geo_flux
-        )
+    columns = jnp.stack(
+        [ice_mask.astype(jnp.float32), grounded.astype(jnp.float32), surface_enthalpy, geo_flux]
+    )
+    stacked = jnp.concatenate([enthalpy, velocity_init, columns], axis=0)
+    padded, inside = wide_halo(stacked)
+    courant = padded[levels : levels + 2]
+    ice_cols, bed_cols, heat, flux = padded[levels + 2 :, 2:-2, 2:-2]
+    current = advect(padded[:levels], courant[0], courant[1])
+    current = diffuse(
+        current, inverse_bed, inverse_shelf, kappa, ice_cols, bed_cols, heat, flux
+    )
+    current = jnp.where(inside[None, 2:-2, 2:-2], current, 0.0)
+    courant = courant[:, 2:-2, 2:-2]
+    current = advect(current, courant[0], courant[1])
+    current = diffuse(
+        current,
+        inverse_bed,
+        inverse_shelf,
+        kappa,
+        ice_cols[2:-2, 2:-2],
+        bed_cols[2:-2, 2:-2],
+        surface_enthalpy,
+        geo_flux,
+    )
     stiffness = jnp.exp(-soften * jnp.mean(current, axis=0))
     free_cells = (boundary_code == 0) & (ice_mask == 1)
     held_cells = free_cells | (boundary_code == 2)

time: 149 us -> 156 us (1.047)
  other arithmetic: 7.89 us -> 18.1 us
  local copies, waits for them, and re-layouts: 8.34 us -> 13.9 us
  blocking collectives: 49.6 us -> 44.7 us
  starting transfers between devices: 46.2 us -> 43.9 us
  waiting for transfers between devices: 17.6 us -> 15.3 us
    ppermute x8 -> x0, starting transfers between devices: 26.1 us -> none  [the longest x4 15.9 us: with_halo_2(): lax.ppermute(last, axis, up)]
    ppermute x6 -> x10, starting transfers between devices: 16.3 us -> 40.1 us  [shifted(): lax.ppermute(array, axis, [(i, (i + by) % size) for i in range(size)])]
    another operation x0 -> x3, other arithmetic: none -> 4.93 us  [the longest x1 3.54 us: shards(): ice_cols, bed_cols, heat, flux = padded[levels + 2:, 2:-2, 2:-2]]
    all_to_all x1, blocking collectives: 18.1 us -> 15.2 us  [over_all(): return lax.all_to_all(part, GX, 0, 0, tiled=True)]
    another operation x0 -> x4, local copies, waits for them, and re-layouts: none -> 2.49 us  [shards(): jnp.stack([ice_mask.astype(jnp.float32), grounded.astype(jnp.float32), su...]
    max x1 -> x2, other arithmetic: 1.5 us -> 3.68 us  [upwind_sweep(): positive = jnp.maximum(face_speed, 0.0)]
    all_to_all x2, blocking collectives: 31.6 us -> 29.5 us  [over_all(): part = lax.all_to_all(sums, GY, 0, 0, tiled=True)]
    ppermute x8 -> x0, waiting for transfers between devices: 1.99 us -> none  [the longest x4 1.98 us: with_halo_2(): lax.ppermute(first, axis, [(b, a) for a, b in up])]
  transfers between devices with their start and end apart: 15 -> 11, of which waited for: 5 -> 7; matrix products, arithmetic and copies ran while one was open for 2% -> 2% of each run, Pallas kernels for 1% -> 1%
where the time goes in v2:
time: 156 us; the launch traced here: 155 us
  blocking collectives  44.7 us (29%)
  starting transfers between devices  43.9 us (28%)
  other arithmetic  18.1 us (12%)
  waiting for transfers between devices  15.3 us (10%)
  local copies, waits for them, and re-layouts  13.9 us (9%)
  Pallas kernels  13.1 us (8%)
  matrix products  4.27 us (3%)
  between operations  1.82 us (1%)
    ppermute x10, starting transfers between devices, shifted(): lax.ppermute(array, axis, [(i, (i + by) % size) for i in range(size)])  40.1 us
    all_to_all x2, blocking collectives, over_all(): part = lax.all_to_all(sums, GY, 0, 0, tiled=True)  29.5 us
    all_to_all x1, blocking collectives, over_all(): return lax.all_to_all(part, GX, 0, 0, tiled=True)  15.2 us
    ppermute x10, waiting for transfers between devices, shifted(): lax.ppermute(array, axis, [(i, (i + by) % size) for i in range(size)])  7.7 us
    all_to_all x1, waiting for transfers between devices, over_all(): return lax.all_to_all(part, GX, 0, 0, tiled=True)  7.65 us
    unnamed x44, local copies, waits for them, and re-layouts  6.08 us
    pallas_call x1, Pallas kernels, momentum(): pl.pallas_call(second_picard_kernel, out_shape=(struct((2 * KRYLOV, 8, 12...  4.69 us
    add x4, other arithmetic, upwind_sweep(): face_flux + negative * (plus_one - 0.25 * (1.0 + negative) * (plus_two -...  3.97 us
  transfers between devices with their start and end apart: 11, of which 7 were waited for; matrix products, arithmetic and copies ran while one was open for 2% of the time, Pallas kernels for 1%

profile of v2, /device:TPU:1, one launch (start us, length us, event | category | flops | bytes accessed | tf_op | source)
XLA Modules:
  0.0 155.1 jit_solution(4684283378825973324)
XLA Ops:
  0.6 0.7 convert_bitcast_fusion.1
  1.6 0.7 convert_bitcast_fusion
  2.5 1.2 copy.28
  3.8 0.9 copy.29
  4.7 1.0 copy.32
  5.7 1.0 copy.33
  6.8 1.9 %concatenate.47 = f32[134,8,128]{0,2,1:T(8,128)S(1)} concatenate(f32[128,8,128]{0,2,1:T(8,128)S(1)} %copy.28, f32[2,8,128]{0,2,1:T(8,128)S(1)} %copy.29, f32[1,8,128]{0,2,1:T(8,128)S(1)} %copy.30, f32[1,8,128]{0,2,1:T(8,128)S(1)} %copy.31, f32[1,8,128]{0,2,1:T(8,128)} %copy.32, f32[1,8,128]{0,2,1:T(8,128)} %copy.33), dimensions={0} | concatenate | bytes 1097728 | tf_op jit(solution)/shard_map/concatenate | solution.py:548
  8.8 4.0 %collective-permute-start.12 = (f32[134,4,128]{0,2,1:T(8,128)S(1)}, f32[134,4,128]{0,2,1:T(8,128)S(1)}, u32[]{:S(2)}, u32[]{:S(2)}) collective-permute-start(f32[134,4,128]{0,2,1:T(8,128)S(1)} %get-tuple-element.439), channel_id=1, source_target_pairs={{0,16},{16,32},{32,48},{48,64},{64,80},{80,96},{96,112},{112,128},... | collective-permute-start | bytes 823304 | tf_op jit(solution)/shard_map/ppermute | solution.py:434
  12.8 6.0 %collective-permute-start.13 = (f32[134,4,128]{0,2,1:T(8,128)S(1)}, f32[134,4,128]{0,2,1:T(8,128)S(1)}, u32[]{:S(2)}, u32[]{:S(2)}) collective-permute-start(f32[134,4,128]{0,2,1:T(8,128)S(1)} %get-tuple-element.440), channel_id=1, source_target_pairs={{0,496},{16,0},{32,16},{48,32},{64,48},{80,64},{96,80},{112,96},{1... | collective-permute-start | bytes 823304 | tf_op jit(solution)/shard_map/ppermute | solution.py:434
  20.2 0.6 pad_maximum_fusion.13.kappa_ref
  20.8 2.7 %collective-permute-done.12 = f32[134,4,128]{0,2,1:T(8,128)S(1)} collective-permute-done((f32[134,4,128]{0,2,1:T(8,128)S(1)}, f32[134,4,128]{0,2,1:T(8,128)S(1)}, u32[]{:S(2)}, u32[]{:S(2)}) %collective-permute-start.12) | collective-permute-done | bytes 274464 | tf_op jit(solution)/shard_map/ppermute | solution.py:434
  23.4 1.5 collective-permute-done.13
  24.9 8.0 %collective-permute-start.14 = (f32[134,12,4]{0,2,1:T(4,128)S(1)}, f32[134,12,4]{0,2,1:T(4,128)S(1)}, u32[]{:S(2)}, u32[]{:S(2)}) collective-permute-start(f32[134,12,4]{0,2,1:T(4,128)S(1)} %get-tuple-element.437), channel_id=1, source_target_pairs={{0,1},{1,2},{2,3},{3,4},{4,5},{5,6},{6,7},{7,8},{8,9},{9,10},{10,1... | collective-permute-start | bytes 77192 | tf_op jit(solution)/shard_map/ppermute | solution.py:434
  32.9 2.2 %column_inverses.1 = (f32[128,128]{1,0:T(8,128)}, f32[128,128]{1,0:T(8,128)}) custom-call(f32[16,128]{1,0:T(8,128)} %pad_maximum_fusion.13.kappa_ref), custom_call_target="tpu_custom_call" | custom-call | tf_op jit(solution)/shard_map/column_inverses/pallas_call | solution.py:206
  35.2 1.3 collective-permute-done.15
  36.4 1.2 fusion.23
  37.7 0.6 slice_reduce_fusion
  38.3 2.2 %maximum_reduce_fusion = (f32[12,133]{1,0:T(8,128)S(1)}, f32[12,133]{1,0:T(8,128)S(1)}, f32[12,133]{1,0:T(8,128)S(1)}, f32[12,133]{1,0:T(8,128)S(1)}) fusion(f32[134,16,136]{0,2,1:T(8,128)S(1)} %fusion.23), kind=kLoop, calls=%fused_computation.131 | loop fusion | flops 12768 | bytes 38304 | tf_op jit(solution)/shard_map/max | solution.py:79
  40.5 3.5 %slice_reduce_fusion.2 = (f32[12,132]{1,0:T(8,128)S(1)}, f32[12,132]{1,0:T(8,128)S(1)}, f32[12,132]{1,0:T(8,128)S(1)}, f32[12,132]{1,0:T(8,128)S(1)}, f32[12,132]{1,0:T(8,128)S(1)}) fusion(f32[134,16,136]{0,2,1:T(8,128)S(1)} %fusion.23, f32[]{:T(128)} %bitcast.26), kind=kLoop, calls=%fused_computation.129 | loop fusion | flops 3168 | bytes 63364 | tf_op jit(solution)/shard_map/unstack | solution.py:551
  44.0 1.4 compare_reduce_fusion.1
  45.4 1.5 maximum_reduce_fusion.1
  47.1 1.0 fusion.28
  48.1 1.1 fusion.38
  50.7 0.8 fusion.80
  51.5 1.8 %select_select_fusion = f32[128,12,132]{0,2,1:T(8,128)S(1)} fusion(f32[128,12,132]{0,2,1:T(8,128)S(1)} %get-tuple-element.402, f32[128,12,132]{0,2,1:T(8,128)S(1)} %fusion.80, pred[12,132]{1,0:T(8,128)(4,1)S(1)} %get-tuple-element.342, pred[12,132]{1,0:T(8,128)(4,1)S(1)} %get-tuple-element.341, pred[12,132]{1,0:T(8,128)(4,1)S(1)} %slice.794, ...), kind=kOutput, calls=%fused_computation.123 | convolution fusion | flops 312035328 | bytes 3314320 | tf_op jit(solution)/shard_map/dot_general | solution.py:110
  53.4 1.0 fusion.47
  54.4 0.8 fusion.54
  55.4 0.7 fusion.62
  56.1 0.9 fusion.100
  57.0 3.4 %collective-permute-start.16 = (f32[6,8,128]{2,1,0:T(8,128)S(1)}, f32[6,8,128]{2,1,0:T(8,128)S(1)}, u32[]{:S(2)}, u32[]{:S(2)}) collective-permute-start(f32[6,8,128]{2,1,0:T(8,128)S(1)} %constant_dynamic-update-slice_fusion), channel_id=1, source_target_pairs={{0,32},{16,48},{32,64},{48,80},{64,96},{80,112},{96,128},{112,144}... | collective-permute-start | bytes 73736 | tf_op jit(solution)/shard_map/ppermute | solution.py:434
  60.4 4.6 %collective-permute-start.17 = (f32[6,8,128]{2,1,0:T(8,128)S(1)}, f32[6,8,128]{2,1,0:T(8,128)S(1)}, u32[]{:S(2)}, u32[]{:S(2)}) collective-permute-start(f32[6,8,128]{2,1,0:T(8,128)S(1)} %constant_dynamic-update-slice_fusion), channel_id=1, source_target_pairs={{0,16},{16,32},{32,48},{48,64},{64,80},{80,96},{96,112},{112,128},... | collective-permute-start | bytes 73736 | tf_op jit(solution)/shard_map/ppermute | solution.py:434
  65.0 4.0 %collective-permute-start.18 = (f32[6,8,128]{2,1,0:T(8,128)S(1)}, f32[6,8,128]{2,1,0:T(8,128)S(1)}, u32[]{:S(2)}, u32[]{:S(2)}) collective-permute-start(f32[6,8,128]{2,1,0:T(8,128)S(1)} %constant_dynamic-update-slice_fusion), channel_id=1, source_target_pairs={{0,496},{16,0},{32,16},{48,32},{64,48},{80,64},{96,80},{112,96},{1... | collective-permute-start | bytes 73736 | tf_op jit(solution)/shard_map/ppermute | solution.py:434
  69.0 3.6 %collective-permute-start.19 = (f32[6,8,128]{2,1,0:T(8,128)S(1)}, f32[6,8,128]{2,1,0:T(8,128)S(1)}, u32[]{:S(2)}, u32[]{:S(2)}) collective-permute-start(f32[6,8,128]{2,1,0:T(8,128)S(1)} %constant_dynamic-update-slice_fusion), channel_id=1, source_target_pairs={{0,480},{16,496},{32,0},{48,16},{64,32},{80,48},{96,64},{112,80},{... | collective-permute-start | bytes 73736 | tf_op jit(solution)/shard_map/ppermute | solution.py:434
  72.7 1.9 %collective-permute-done.19 = f32[6,8,128]{2,1,0:T(8,128)S(1)} collective-permute-done((f32[6,8,128]{2,1,0:T(8,128)S(1)}, f32[6,8,128]{2,1,0:T(8,128)S(1)}, u32[]{:S(2)}, u32[]{:S(2)}) %collective-permute-start.19) | collective-permute-done | bytes 24608 | tf_op jit(solution)/shard_map/ppermute | solution.py:434
  74.6 2.8 %collective-permute-start.20 = (f32[6,40,128]{2,1,0:T(8,128)S(1)}, f32[6,40,128]{2,1,0:T(8,128)S(1)}, u32[]{:S(2)}, u32[]{:S(2)}) collective-permute-start(f32[6,40,128]{2,1,0:T(8,128)S(1)} %constant_dynamic-update-slice_fusion.5.mine_ref), channel_id=1, source_target_pairs={{0,1},{1,2},{2,3},{3,4},{4,5},{5,6},{6,7},{7,8},{8,9},{9,10},{10,1... | collective-permute-start | bytes 368648 | tf_op jit(solution)/shard_map/ppermute | solution.py:434
  77.4 3.7 %collective-permute-start.21 = (f32[6,40,128]{2,1,0:T(8,128)S(1)}, f32[6,40,128]{2,1,0:T(8,128)S(1)}, u32[]{:S(2)}, u32[]{:S(2)}) collective-permute-start(f32[6,40,128]{2,1,0:T(8,128)S(1)} %constant_dynamic-update-slice_fusion.5.mine_ref), channel_id=1, source_target_pairs={{0,15},{1,0},{2,1},{3,2},{4,3},{5,4},{6,5},{7,6},{8,7},{9,8},{10,9... | collective-permute-start | bytes 368648 | tf_op jit(solution)/shard_map/ppermute | solution.py:434
  82.6 0.6 copy-done.6
  83.2 3.3 %first_picard.1 = (f32[12,24,256]{2,1,0:T(8,128)}, f32[6,24,256]{2,1,0:T(8,128)}, f32[16,128]{1,0:T(8,128)}) custom-call(s32[2]{0:T(128)} %pad_add_fusion.place_ref, s32[2]{0:T(128)} %constant.189.clone.grid_ref, f32[6,40,128]{2,1,0:T(8,128)} %copy-done.3, f32[6,40,128]{2,1,0:T(8,128)} %copy-done.5, f32[6,40,128]{2,1,0:T(8,128)} %copy-done.6), custom_call_target="tpu_custom_call" | custom-call | tf_op jit(solution)/shard_map/first_picard/pallas_call | solution.py:466
  86.5 17.3 %all_to_all.34 = f32[16,1,128]{2,1,0:T(1,128)S(1)} all-to-all(f32[16,1,128]{2,1,0:T(1,128)} %bitcast.160), channel_id=1, replica_groups=mesh['gx_0'=4,'gx_1'=8,'gy_0'=8,'gy_1'=2] {'gy_0','gy_1'}, dimensions={0} | all-to-all | bytes 16384 | tf_op jit(solution)/shard_map/all_to_all | solution.py:427
  103.8 15.2 %all_to_all.35 = f32[32,1,128]{2,1,0:T(1,128)} all-to-all(f32[32,1,128]{2,1,0:T(1,128)S(1)} %broadcast_in_dim.205), channel_id=1, replica_groups=mesh['gx_0'=4,'gx_1'=8,'gy_0'=8,'gy_1'=2] {'gx_0','gx_1'}, dimensions={0} | all-to-all | bytes 32768 | tf_op jit(solution)/shard_map/all_to_all | solution.py:429
  119.0 4.7 %second_picard.1 = (f32[12,8,128]{2,1,0:T(8,128)}, f32[2,8,128]{2,1,0:T(8,128)}, f32[16,128]{1,0:T(8,128)}, f32[8,128]{1,0:T(8,128)}) custom-call(f32[32,128]{1,0:T(8,128)} %bitcast.157, f32[12,24,256]{2,1,0:T(8,128)} %get-tuple-element.295.basis_ref, f32[6,24,256]{2,1,0:T(8,128)} %get-tuple-element.296.fixed_ref), custom_call_target="tpu_custom_call" | custom-call | tf_op jit(solution)/shard_map/second_picard/pallas_call | solution.py:477
  123.7 12.2 %all_to_all.36 = f32[16,1,128]{2,1,0:T(1,128)S(1)} all-to-all(f32[16,1,128]{2,1,0:T(1,128)} %bitcast.161), channel_id=1, replica_groups=mesh['gx_0'=4,'gx_1'=8,'gy_0'=8,'gy_1'=2] {'gy_0','gy_1'}, dimensions={0} | all-to-all | bytes 16384 | tf_op jit(solution)/shard_map/all_to_all | solution.py:427
  135.9 0.6 broadcast_in_dim.206
  136.5 3.9 %all-to-all-start.3 = ((f32[32,1,128]{2,1,0:T(1,128)}), f32[32,1,128]{2,1,0:T(1,128)S(1)}, u32[]{:S(2)}, u32[]{:S(2)}) async-start(f32[32,1,128]{2,1,0:T(1,128)} %broadcast_in_dim.206), calls=%async_computation.3 | async-start | bytes 32768 | tf_op jit(solution)/shard_map/all_to_all | solution.py:429
  140.4 1.0 copy.38
  141.4 7.6 %all-to-all-done.3 = f32[32,1,128]{2,1,0:T(1,128)S(1)} async-done(((f32[32,1,128]{2,1,0:T(1,128)}), f32[32,1,128]{2,1,0:T(1,128)S(1)}, u32[]{:S(2)}, u32[]{:S(2)}) %all-to-all-start.3) | async-done | bytes 16416 | tf_op jit(solution)/shard_map/all_to_all | solution.py:429
  149.6 3.0 %last_picard.1 = (f32[2,8,128]{2,1,0:T(8,128)S(1)}, f32[8,128]{1,0:T(8,128)}) custom-call(f32[32,128]{1,0:T(8,128)} %bitcast.156, f32[12,8,128]{2,1,0:T(8,128)} %get-tuple-element.298.basis_ref, f32[2,8,128]{2,1,0:T(8,128)} %get-tuple-element.299.velocity_ref, f32[8,128]{1,0:T(8,128)} %get-tuple-element.300.least_ref), custom_call_target="tpu_custom_call" | custom-call | tf_op jit(solution)/shard_map/last_picard/pallas_call | solution.py:487
  152.6 1.2 slice.696
  (89 shorter events, 6.5 us)
Async XLA Ops:
  0.6 4.1 %copy-start.11 = (f32[8,128]{1,0:T(8,128)S(1)}, f32[8,128]{1,0:T(8,128)}, u32[]{:S(2)}) copy-start(f32[8,128]{1,0:T(8,128)} %param.24) | copy-start | bytes 12292
  0.6 5.1 %copy-start.10 = (f32[8,128]{1,0:T(8,128)S(1)}, f32[8,128]{1,0:T(8,128)}, u32[]{:S(2)}) copy-start(f32[8,128]{1,0:T(8,128)} %param.25) | copy-start | bytes 12292
  6.7 12.1 %copy-start.16 = (f32[129]{0:T(256)S(1)}, f32[129]{0:T(256)}, u32[]{:S(2)}) copy-start(f32[129]{0:T(256)} %param.23) | copy-start | bytes 1552
  6.7 13.2 %copy-start.13 = (s32[8,128]{1,0:T(8,128)S(1)}, s32[8,128]{1,0:T(8,128)}, u32[]{:S(2)}) copy-start(s32[8,128]{1,0:T(8,128)} %param.26) | copy-start | bytes 12292
  6.7 13.2 %copy-start.14 = (s32[8,128]{1,0:T(8,128)S(1)}, s32[8,128]{1,0:T(8,128)}, u32[]{:S(2)}) copy-start(s32[8,128]{1,0:T(8,128)} %param.28) | copy-start | bytes 12292
  6.7 13.3 %copy-start.9 = (f32[2,8,128]{2,1,0:T(8,128)S(1)}, f32[2,8,128]{2,1,0:T(8,128)}, u32[]{:S(2)}) copy-start(f32[2,8,128]{2,1,0:T(8,128)} %param.19) | copy-start | bytes 24580
  6.8 13.3 %copy-start.12 = (s32[8,128]{1,0:T(8,128)S(1)}, s32[8,128]{1,0:T(8,128)}, u32[]{:S(2)}) copy-start(s32[8,128]{1,0:T(8,128)} %param.27) | copy-start | bytes 12292
  6.8 13.3 %copy-start.15 = (f32[8,128]{1,0:T(8,128)S(1)}, f32[8,128]{1,0:T(8,128)}, u32[]{:S(2)}) copy-start(f32[8,128]{1,0:T(8,128)} %param.22) | copy-start | bytes 12292
  6.8 14.0 %copy-start.4 = (f32[8,128]{1,0:T(8,128)S(1)}, f32[8,128]{1,0:T(8,128)}, u32[]{:S(2)}) copy-start(f32[8,128]{1,0:T(8,128)} %param.20) | copy-start | bytes 12292
  8.8 14.7 %collective-permute-start.12 = (f32[134,4,128]{0,2,1:T(8,128)S(1)}, f32[134,4,128]{0,2,1:T(8,128)S(1)}, u32[]{:S(2)}, u32[]{:S(2)}) collective-permute-start(f32[134,4,128]{0,2,1:T(8,128)S(1)} %get-tuple-element.439), channel_id=1, source_target_pairs={{0,16},{16,32},{32,48},{48,64},{64,80},{80,96},{96,112},{112,128},... | collective-permute-start | bytes 823304 | tf_op jit(solution)/shard_map/ppermute | solution.py:434
  12.8 12.1 %collective-permute-start.13 = (f32[134,4,128]{0,2,1:T(8,128)S(1)}, f32[134,4,128]{0,2,1:T(8,128)S(1)}, u32[]{:S(2)}, u32[]{:S(2)}) collective-permute-start(f32[134,4,128]{0,2,1:T(8,128)S(1)} %get-tuple-element.440), channel_id=1, source_target_pairs={{0,496},{16,0},{32,16},{48,32},{64,48},{80,64},{96,80},{112,96},{1... | collective-permute-start | bytes 823304 | tf_op jit(solution)/shard_map/ppermute | solution.py:434
  24.9 10.2 %collective-permute-start.14 = (f32[134,12,4]{0,2,1:T(4,128)S(1)}, f32[134,12,4]{0,2,1:T(4,128)S(1)}, u32[]{:S(2)}, u32[]{:S(2)}) collective-permute-start(f32[134,12,4]{0,2,1:T(4,128)S(1)} %get-tuple-element.437), channel_id=1, source_target_pairs={{0,1},{1,2},{2,3},{3,4},{4,5},{5,6},{6,7},{7,8},{8,9},{9,10},{10,1... | collective-permute-start | bytes 77192 | tf_op jit(solution)/shard_map/ppermute | solution.py:434
  32.9 3.5 %collective-permute-start.15 = (f32[134,12,4]{0,2,1:T(4,128)S(1)}, f32[134,12,4]{0,2,1:T(4,128)S(1)}, u32[]{:S(2)}, u32[]{:S(2)}) collective-permute-start(f32[134,12,4]{0,2,1:T(4,128)S(1)} %get-tuple-element.438), channel_id=1, source_target_pairs={{0,15},{1,0},{2,1},{3,2},{4,3},{5,4},{6,5},{7,6},{8,7},{9,8},{10,9... | collective-permute-start | bytes 77192 | tf_op jit(solution)/shard_map/ppermute | solution.py:434
  49.8 0.8 copy-start.1
  49.8 1.7 %copy-start.2 = (f32[128,128]{1,0:T(8,128)S(1)}, f32[128,128]{1,0:T(8,128)}, u32[]{:S(2)}) copy-start(f32[128,128]{1,0:T(8,128)} %get-tuple-element.293) | copy-start | bytes 196612
  55.2 1.8 %copy-start.7 = (f32[8,128]{1,0:T(8,128)S(1)}, f32[8,128]{1,0:T(8,128)}, u32[]{:S(2)}) copy-start(f32[8,128]{1,0:T(8,128)} %param.21) | copy-start | bytes 12292
  57.0 15.6 %collective-permute-start.16 = (f32[6,8,128]{2,1,0:T(8,128)S(1)}, f32[6,8,128]{2,1,0:T(8,128)S(1)}, u32[]{:S(2)}, u32[]{:S(2)}) collective-permute-start(f32[6,8,128]{2,1,0:T(8,128)S(1)} %constant_dynamic-update-slice_fusion), channel_id=1, source_target_pairs={{0,32},{16,48},{32,64},{48,80},{64,96},{80,112},{96,128},{112,144}... | collective-permute-start | bytes 73736 | tf_op jit(solution)/shard_map/ppermute | solution.py:434
  60.4 12.2 %collective-permute-start.17 = (f32[6,8,128]{2,1,0:T(8,128)S(1)}, f32[6,8,128]{2,1,0:T(8,128)S(1)}, u32[]{:S(2)}, u32[]{:S(2)}) collective-permute-start(f32[6,8,128]{2,1,0:T(8,128)S(1)} %constant_dynamic-update-slice_fusion), channel_id=1, source_target_pairs={{0,16},{16,32},{32,48},{48,64},{64,80},{80,96},{96,112},{112,128},... | collective-permute-start | bytes 73736 | tf_op jit(solution)/shard_map/ppermute | solution.py:434
  65.0 7.7 %collective-permute-start.18 = (f32[6,8,128]{2,1,0:T(8,128)S(1)}, f32[6,8,128]{2,1,0:T(8,128)S(1)}, u32[]{:S(2)}, u32[]{:S(2)}) collective-permute-start(f32[6,8,128]{2,1,0:T(8,128)S(1)} %constant_dynamic-update-slice_fusion), channel_id=1, source_target_pairs={{0,496},{16,0},{32,16},{48,32},{64,48},{80,64},{96,80},{112,96},{1... | collective-permute-start | bytes 73736 | tf_op jit(solution)/shard_map/ppermute | solution.py:434
  69.0 5.6 %collective-permute-start.19 = (f32[6,8,128]{2,1,0:T(8,128)S(1)}, f32[6,8,128]{2,1,0:T(8,128)S(1)}, u32[]{:S(2)}, u32[]{:S(2)}) collective-permute-start(f32[6,8,128]{2,1,0:T(8,128)S(1)} %constant_dynamic-update-slice_fusion), channel_id=1, source_target_pairs={{0,480},{16,496},{32,0},{48,16},{64,32},{80,48},{96,64},{112,80},{... | collective-permute-start | bytes 73736 | tf_op jit(solution)/shard_map/ppermute | solution.py:434
  74.6 7.5 %copy-start.3 = (f32[6,40,128]{2,1,0:T(8,128)}, f32[6,40,128]{2,1,0:T(8,128)S(1)}, u32[]{:S(2)}) copy-start(f32[6,40,128]{2,1,0:T(8,128)S(1)} %constant_dynamic-update-slice_fusion.5.mine_ref) | copy-start | bytes 368644
  74.6 7.3 %collective-permute-start.20 = (f32[6,40,128]{2,1,0:T(8,128)S(1)}, f32[6,40,128]{2,1,0:T(8,128)S(1)}, u32[]{:S(2)}, u32[]{:S(2)}) collective-permute-start(f32[6,40,128]{2,1,0:T(8,128)S(1)} %constant_dynamic-update-slice_fusion.5.mine_ref), channel_id=1, source_target_pairs={{0,1},{1,2},{2,3},{3,4},{4,5},{5,6},{6,7},{7,8},{8,9},{9,10},{10,1... | collective-permute-start | bytes 368648 | tf_op jit(solution)/shard_map/ppermute | solution.py:434
  77.4 4.7 %collective-permute-start.21 = (f32[6,40,128]{2,1,0:T(8,128)S(1)}, f32[6,40,128]{2,1,0:T(8,128)S(1)}, u32[]{:S(2)}, u32[]{:S(2)}) collective-permute-start(f32[6,40,128]{2,1,0:T(8,128)S(1)} %constant_dynamic-update-slice_fusion.5.mine_ref), channel_id=1, source_target_pairs={{0,15},{1,0},{2,1},{3,2},{4,3},{5,4},{6,5},{7,6},{8,7},{9,8},{10,9... | collective-permute-start | bytes 368648 | tf_op jit(solution)/shard_map/ppermute | solution.py:434
  81.9 0.7 copy-start.5
  82.6 0.6 copy-start.6
  136.5 12.5 %all-to-all-start.3 = ((f32[32,1,128]{2,1,0:T(1,128)}), f32[32,1,128]{2,1,0:T(1,128)S(1)}, u32[]{:S(2)}, u32[]{:S(2)}) async-start(f32[32,1,128]{2,1,0:T(1,128)} %broadcast_in_dim.206), calls=%async_computation.3 | async-start | bytes 32768 | tf_op jit(solution)/shard_map/all_to_all | solution.py:429
  149.0 0.6 copy-start.8
  154.5 0.6 copy-start

commit v3 on v1

--- a/solution.py
+++ b/solution.py
@@ -8,7 +8,6 @@
 from jax.sharding import Mesh
 from jax.sharding import PartitionSpec as P
 
-SUBSTEPS = 2
 PICARD = 2
 KRYLOV = 6
 TORUS = (4, 8, 8, 2)
@@ -45,75 +44,6 @@
     return functools.reduce(lax.psum, axes, shard)
 
 
-def with_halo_2(shard, sides, width):
-    edges = {}
-    for axis, dim in sides:
-        size, length = (lax.axis_size(axis), shard.shape[dim])
-        up = [(i, (i + 1) % size) for i in range(size - 1)]
-        last = lax.slice_in_dim(shard, length - width, length, axis=dim)
-        first = lax.slice_in_dim(shard, 0, width, axis=dim)
-        edges[dim] = (
-            lax.ppermute(last, axis, up),
-            lax.ppermute(first, axis, [(b, a) for a, b in up]),
-        )
-    done = []
-    for _, dim in sides:
-        low, high = edges[dim]
-        around = [(width, width) if d in done else (0, 0) for d in range(shard.ndim)]
-        shard = jnp.concatenate([jnp.pad(low, around), shard, jnp.pad(high, around)], axis=dim)
-        done.append(dim)
-    return shard
-
-
-def upwind_sweep(values, courant, axis):
-    length = values.shape[axis]
-
-    def window(array, start_cut, end_cut):
-        return lax.slice_in_dim(array, start_cut, length - end_cut, axis=axis)
-
-    face_speed = 0.5 * (window(courant, 1, 2) + window(courant, 2, 1))
-    minus_one = window(values, 0, 3)
-    here_cell = window(values, 1, 2)
-    plus_one = window(values, 2, 1)
-    plus_two = window(values, 3, 0)
-    positive = jnp.maximum(face_speed, 0.0)
-    negative = jnp.minimum(face_speed, 0.0)
-    face_flux = positive * (here_cell + 0.25 * (1.0 - positive) * (plus_one - minus_one))
-    face_flux = face_flux + negative * (plus_one - 0.25 * (1.0 + negative) * (plus_two - here_cell))
-    count = face_flux.shape[axis]
-    return lax.slice_in_dim(face_flux, 1, count, axis=axis) - lax.slice_in_dim(
-        face_flux, 0, count - 1, axis=axis
-    )
-
-
-def advect(padded, courant_x, courant_y):
-    row_count = padded.shape[1]
-    col_count = padded.shape[2]
-    along_x = upwind_sweep(
-        padded[:, :, 2 : col_count - 2], courant_x[None, :, 2 : col_count - 2], 1
-    )
-    along_y = upwind_sweep(
-        padded[:, 2 : row_count - 2, :], courant_y[None, 2 : row_count - 2, :], 2
-    )
-    return padded[:, 2 : row_count - 2, 2 : col_count - 2] - along_x - along_y
-
-
-def diffuse(moved, inverse_bed, inverse_shelf, kappa, ice_cols, bed_cols, surface_heat, heat_flux):
-    levels = moved.shape[0]
-    depth_index = lax.broadcasted_iota(jnp.int32, (levels, 1, 1), 0)
-    right_side = moved + jnp.where(depth_index == 0, kappa[0] * surface_heat[None], 0.0)
-    right_side = right_side + jnp.where(
-        depth_index == levels - 1, bed_cols[None] * heat_flux[None], 0.0
-    )
-    columns = right_side.reshape(levels, -1)
-    solved_bed = jnp.dot(inverse_bed, columns, precision=lax.Precision.HIGHEST).reshape(moved.shape)
-    solved_shelf = jnp.dot(inverse_shelf, columns, precision=lax.Precision.HIGHEST).reshape(
-        moved.shape
-    )
-    solved = jnp.where(bed_cols[None] > 0.5, solved_bed, solved_shelf)
-    return jnp.where(ice_cols[None] > 0.5, solved, moved)
-
-
 def corner_mean(array):
     return 0.25 * (array[:-1, :-1] + array[1:, :-1] + array[:-1, 1:] + array[1:, 1:])
 
@@ -167,7 +97,7 @@
     return projector * stress_image(strains(padded), weight, direction, drag_term)
 
 
-def inverse_kernel(kappa_ref, bed_ref, shelf_ref):
+def inverse_kernel(kappa_ref, out_ref):
     levels = kappa_ref.shape[1]
     above = kappa_ref[0:8, :]
     below = kappa_ref[8:16, :]
@@ -176,7 +106,7 @@
     cols = lax.broadcasted_iota(jnp.int32, (levels, levels), 1)
     floating = 1.0 + above + below
     on_bed = jnp.where(lane == levels - 1, 1.0 + above, floating)
-    for diagonal, out_ref in ((on_bed, bed_ref), (floating, shelf_ref)):
+    for k, diagonal in enumerate((on_bed, floating)):
         low = jnp.where(lane == 0, 0.0, -above)
         high = jnp.where(lane == levels - 1, 0.0, -below)
         mid = diagonal
@@ -195,17 +125,18 @@
                 + up[0:1] * pltpu.roll(right, back, 1)
             )
             step *= 2
-        out_ref[...] = right / mid[0:1]
+        out_ref[k * levels : (k + 1) * levels] = right / mid[0:1]
 
 
 def column_inverses(kappa):
     levels = kappa.shape[0] - 1
     above = jnp.broadcast_to(kappa[None, :levels], (8, levels))
     below = jnp.broadcast_to(kappa[None, 1:], (8, levels))
-    shape = jax.ShapeDtypeStruct((levels, levels), kappa.dtype)
-    return pl.pallas_call(inverse_kernel, out_shape=(shape, shape), name="column_inverses")(
-        jnp.concatenate([above, below], axis=0)
-    )
+    return pl.pallas_call(
+        inverse_kernel,
+        out_shape=jax.ShapeDtypeStruct((2 * levels, levels), kappa.dtype),
+        name="column_inverses",
+    )(jnp.concatenate([above, below], axis=0))
 
 
 def next_row(array):
@@ -434,16 +365,14 @@
     return lax.ppermute(array, axis, [(i, (i + by) % size) for i in range(size)])
 
 
-def momentum(fields):
+def momentum(fields, place, grid):
     f32 = jnp.float32
     below = [shifted(fields, GX, by) for by in (2, 1)]
     above = [shifted(fields, GX, -by) for by in (1, 2)]
     mine = jnp.concatenate(below + [fields] + above, axis=1)
     left = shifted(mine, GY, 1)
     right = shifted(mine, GY, -1)
-    gx, gy = (lax.axis_size(GX), lax.axis_size(GY))
-    place = jnp.stack([lax.axis_index(GX), lax.axis_index(GY)]).astype(jnp.int32)
-    grid = jnp.array([gx, gy], jnp.int32)
+    gy = lax.axis_size(GY)
     smem = pl.BlockSpec(memory_space=pltpu.SMEM)
     vmem = pl.BlockSpec(memory_space=pltpu.VMEM)
     struct = jax.ShapeDtypeStruct
@@ -511,6 +440,262 @@
     return lax.fori_loop(0, PICARD, picard, velocity)
 
 
+def column_tiles(planes):
+    shape = (32, 1024)
+    line = lax.broadcasted_iota(jnp.int32, shape, 0)
+    spot = lax.broadcasted_iota(jnp.int32, shape, 1)
+    within = line & 15
+    column = jnp.where(line < 16, 0, 126) + (within & 1)
+    pick = jnp.where(spot == (within >> 1) * 128 + column, 1.0, 0.0)
+    tiles = lax.dot_general(
+        pick,
+        jnp.concatenate(planes, axis=1),
+        (((1,), (1,)), ((), ())),
+        precision=lax.Precision.HIGHEST,
+        preferred_element_type=jnp.float32,
+    )
+    return (tiles[:16], tiles[16:])
+
+
+def pack_kernel(enthalpy_ref, speed_ref, low_ref, high_ref, left_ref, right_ref):
+    planes = [enthalpy_ref[pl.ds(x, 128, stride=8), :] for x in range(8)]
+    low_ref[0:128] = planes[0]
+    low_ref[128:256] = planes[1]
+    low_ref[256:264] = speed_ref[0]
+    high_ref[0:128] = planes[6]
+    high_ref[128:256] = planes[7]
+    high_ref[256:264] = speed_ref[0]
+    first, last = column_tiles(planes)
+    left_ref[0:16] = first
+    left_ref[16:24] = speed_ref[1]
+    right_ref[0:16] = last
+    right_ref[16:24] = speed_ref[1]
+
+
+def line_weights(low_face, high_face):
+    p_high, m_high = (jnp.maximum(high_face, 0.0), jnp.minimum(high_face, 0.0))
+    p_low, m_low = (jnp.maximum(low_face, 0.0), jnp.minimum(low_face, 0.0))
+    q_high, n_high = (0.25 * p_high * (1.0 - p_high), 0.25 * m_high * (1.0 + m_high))
+    q_low, n_low = (0.25 * p_low * (1.0 - p_low), 0.25 * m_low * (1.0 + m_low))
+    return (
+        -q_low,
+        q_high + (p_low + n_low),
+        (q_low + m_low) - (p_high + n_high),
+        -(q_high + m_high) - n_low,
+        n_high,
+    )
+
+
+def cell_weights(speed_ref, before_x, after_x, before_y, after_y):
+    c_x, c_y = (speed_ref[0], speed_ref[1])
+    row = lax.broadcasted_iota(jnp.int32, (8, 128), 0)
+    lane = lax.broadcasted_iota(jnp.int32, (8, 128), 1)
+    x_before = jnp.where(row == 0, pltpu.roll(before_x, 1, 0), pltpu.roll(c_x, 1, 0))
+    x_after = jnp.where(row == 7, pltpu.roll(after_x, 7, 0), pltpu.roll(c_x, 7, 0))
+    y_before = jnp.where(lane == 0, pltpu.roll(before_y, 1, 1), pltpu.roll(c_y, 1, 1))
+    y_after = jnp.where(lane == 127, pltpu.roll(after_y, 127, 1), pltpu.roll(c_y, 127, 1))
+    along_x = line_weights(0.5 * (x_before + c_x), 0.5 * (c_x + x_after))
+    along_y = line_weights(0.5 * (y_before + c_y), 0.5 * (c_y + y_after))
+    center = 1.0 + along_x[2] + along_y[2]
+    return (center,) + along_x[:2] + along_x[3:] + along_y[:2] + along_y[3:]
+
+
+def edge_products(weights, before_y, after_y):
+    line = lax.broadcasted_iota(jnp.int32, (32, 128), 0)
+    lane = lax.broadcasted_iota(jnp.int32, (32, 128), 1)
+    back_2, back_1, ahead_1, ahead_2 = weights[5:]
+    spread = []
+    for x in range(8):
+        b_2, b_1, a_1, a_2 = (w[x : x + 1] for w in (back_2, back_1, ahead_1, ahead_2))
+        far = (line == 2 * x) & (lane == 0)
+        far = far | ((line == 2 * x + 1) & (lane == 1))
+        value = jnp.where(far, b_2, 0.0)
+        value = jnp.where((line == 2 * x + 1) & (lane == 0), b_1, value)
+        far = (line == 16 + 2 * x) & (lane == 126)
+        far = far | ((line == 17 + 2 * x) & (lane == 127))
+        value = jnp.where(far, a_2, value)
+        value = jnp.where((line == 16 + 2 * x) & (lane == 127), a_1, value)
+        spread.append(value)
+    return lax.dot_general(
+        jnp.concatenate([before_y, after_y], axis=0),
+        jnp.concatenate(spread, axis=1),
+        (((0,), (0,)), ((), ())),
+        precision=lax.Precision.HIGHEST,
+        preferred_element_type=jnp.float32,
+    )
+
+
+def substep(planes, weights, edges, inverses, first_kappa, ice, bed, surface_heat, heat_flux):
+    lane = lax.broadcasted_iota(jnp.int32, (8, 128), 1)
+    center, x_b2, x_b1, x_a1, x_a2, y_b2, y_b1, y_a1, y_a2 = weights
+    y_b2 = jnp.where(lane < 2, 0.0, y_b2)
+    y_b1 = jnp.where(lane < 1, 0.0, y_b1)
+    y_a1 = jnp.where(lane > 126, 0.0, y_a1)
+    y_a2 = jnp.where(lane > 125, 0.0, y_a2)
+    level = lax.broadcasted_iota(jnp.int32, (128, 128), 0)
+    done = []
+    for x in range(0, 8, 2):
+        moved, sides = ([], [])
+        for r in (x, x + 1):
+            at = lambda w: w[r : r + 1]
+            e = planes[r + 2]
+            value = at(center) * e + edges[:, r * 128 : r * 128 + 128]
+            value = value + at(x_b2) * planes[r] + at(x_b1) * planes[r + 1]
+            value = value + at(x_a1) * planes[r + 3] + at(x_a2) * planes[r + 4]
+            value = value + at(y_b2) * pltpu.roll(e, 2, 1) + at(y_b1) * pltpu.roll(e, 1, 1)
+            value = value + at(y_a1) * pltpu.roll(e, 127, 1) + at(y_a2) * pltpu.roll(e, 126, 1)
+            moved.append(value)
+            top = first_kappa * at(surface_heat)
+            bottom = at(bed) * at(heat_flux)
+            sides.append(
+                value + jnp.where(level == 0, top, jnp.where(level == 127, bottom, 0.0))
+            )
+        solved = jnp.dot(
+            inverses,
+            jnp.concatenate(sides, axis=1),
+            precision=lax.Precision.HIGHEST,
+            preferred_element_type=jnp.float32,
+        )
+        for k, r in enumerate((x, x + 1)):
+            mine = slice(k * 128, k * 128 + 128)
+            choice = jnp.where(bed[r : r + 1] > 0.5, solved[:128, mine], solved[128:, mine])
+            done.append(jnp.where(ice[r : r + 1] > 0.5, choice, moved[k]))
+    return done
+
+
+def first_substep_kernel(
+    place_ref,
+    grid_ref,
+    kappa_ref,
+    enthalpy_ref,
+    speed_ref,
+    below_ref,
+    above_ref,
+    left_ref,
+    right_ref,
+    inverses_ref,
+    ice_ref,
+    grounded_ref,
+    surface_ref,
+    flux_ref,
+    out_ref,
+    low_ref,
+    high_ref,
+    first_ref,
+    last_ref,
+    weights_ref,
+):
+    has_below, has_above, has_left, has_right = sides_inside(place_ref, grid_ref)
+    below = jnp.where(has_below, below_ref[...], 0.0)
+    above = jnp.where(has_above, above_ref[...], 0.0)
+    left = jnp.where(has_left, left_ref[...], 0.0)
+    right = jnp.where(has_right, right_ref[...], 0.0)
+    weights = cell_weights(speed_ref, below[256:], above[256:], left[16:], right[16:])
+    for k in range(9):
+        weights_ref[k] = weights[k]
+    edges = edge_products(weights, left[:16], right[:16])
+    planes = [below[:128], below[128:256]]
+    planes += [enthalpy_ref[pl.ds(x, 128, stride=8), :] for x in range(8)]
+    planes += [above[:128], above[128:256]]
+    done = substep(
+        planes,
+        weights,
+        edges,
+        inverses_ref[...],
+        kappa_ref[0],
+        ice_ref[...].astype(jnp.float32),
+        grounded_ref[...].astype(jnp.float32),
+        surface_ref[...],
+        flux_ref[...],
+    )
+    for x in range(8):
+        out_ref[x] = done[x]
+    low_ref[0:128] = done[0]
+    low_ref[128:256] = done[1]
+    high_ref[0:128] = done[6]
+    high_ref[128:256] = done[7]
+    first_ref[...], last_ref[...] = column_tiles(done)
+
+
+def sides_inside(place_ref, grid_ref):
+    return (
+        place_ref[0] > 0,
+        place_ref[0] < grid_ref[0] - 1,
+        place_ref[1] > 0,
+        place_ref[1] < grid_ref[1] - 1,
+    )
+
+
+def second_substep_kernel(
+    place_ref,
+    grid_ref,
+    kappa_ref,
+    enthalpy_ref,
+    below_ref,
+    above_ref,
+    left_ref,
+    right_ref,
+    weights_ref,
+    inverses_ref,
+    ice_ref,
+    grounded_ref,
+    surface_ref,
+    flux_ref,
+    speed_ref,
+    thick_ref,
+    height_ref,
+    friction_ref,
+    code_ref,
+    out_ref,
+    fields_ref,
+):
+    has_below, has_above, has_left, has_right = sides_inside(place_ref, grid_ref)
+    below = jnp.where(has_below, below_ref[...], 0.0)
+    above = jnp.where(has_above, above_ref[...], 0.0)
+    left = jnp.where(has_left, left_ref[...], 0.0)
+    right = jnp.where(has_right, right_ref[...], 0.0)
+    weights = tuple(weights_ref[k] for k in range(9))
+    edges = edge_products(weights, left, right)
+    planes = [below[:128], below[128:256]]
+    planes += [enthalpy_ref[x] for x in range(8)]
+    planes += [above[:128], above[128:256]]
+    ice = ice_ref[...]
+    grounded = grounded_ref[...]
+    done = substep(
+        planes,
+        weights,
+        edges,
+        inverses_ref[...],
+        kappa_ref[0],
+        ice.astype(jnp.float32),
+        grounded.astype(jnp.float32),
+        surface_ref[...],
+        flux_ref[...],
+    )
+    means = []
+    for x in range(8):
+        out_ref[pl.ds(x, 128, stride=8), :] = done[x]
+        means.append(jnp.sum(done[x], axis=0, keepdims=True))
+    free = (code_ref[...] == 0) & (ice == 1)
+    held = free | (code_ref[...] == 2)
+    drag = jnp.where(grounded == 1, friction_ref[...], 0.0) + shelf_drag
+    fields_ref[0] = jnp.where(held, speed_ref[0], 0.0)
+    fields_ref[1] = jnp.where(held, speed_ref[1], 0.0)
+    fields_ref[2] = jnp.where(free, drag, 0.0)
+    fields_ref[3] = thick_ref[...]
+    fields_ref[4] = jnp.exp(jnp.concatenate(means, axis=0) * (-soften / 128.0))
+    fields_ref[5] = height_ref[...]
+
+
+def exchanged(low, high, left, right):
+    return (
+        shifted(high, GX, 1),
+        shifted(low, GX, -1),
+        shifted(right, GY, 1),
+        shifted(left, GY, -1),
+    )
+
+
 def shards(
     enthalpy,
     velocity_init,
@@ -524,39 +709,76 @@
     grounded,
     boundary_code,
 ):
-    ice_cols = ice_mask.astype(jnp.float32)
-    bed_cols = grounded.astype(jnp.float32)
-    inverse_bed, inverse_shelf = column_inverses(kappa)
-    levels = enthalpy.shape[0]
-    stacked = jnp.concatenate([enthalpy, velocity_init], axis=0)
-    padded = with_halo_2(stacked, ((GX, 1), (GY, 2)), 2)
-    current = padded[:levels]
-    courant = padded[levels:]
-    for substep in range(SUBSTEPS):
-        if substep > 0:
-            current = with_halo_2(current, ((GX, 1), (GY, 2)), 2)
-        moved = advect(current, courant[0], courant[1])
-        current = diffuse(
-            moved, inverse_bed, inverse_shelf, kappa, ice_cols, bed_cols, surface_enthalpy, geo_flux
-        )
-    stiffness = jnp.exp(-soften * jnp.mean(current, axis=0))
-    free_cells = (boundary_code == 0) & (ice_mask == 1)
-    held_cells = free_cells | (boundary_code == 2)
-    projector = free_cells.astype(jnp.float32)
-    drag_term = jnp.where(grounded == 1, friction, 0.0) + shelf_drag
-    velocity = jnp.where(held_cells[None], velocity_init, 0.0)
-    fields = jnp.stack(
-        [velocity[0], velocity[1], projector * drag_term, thickness, stiffness, surface]
-    )
-    quick, worst = momentum(fields)
-    velocity = lax.cond(
-        worst[0, 0] > PIVOT_FLOOR,
-        lambda: quick,
-        lambda: plain_picard(
-            velocity, thickness, stiffness, surface, drag_term, projector[None]
-        ),
-    )
-    return (current, velocity)
+    f32 = jnp.float32
+    struct = jax.ShapeDtypeStruct
+    smem = pl.BlockSpec(memory_space=pltpu.SMEM)
+    vmem = pl.BlockSpec(memory_space=pltpu.VMEM)
+    place = jnp.stack([lax.axis_index(GX), lax.axis_index(GY)]).astype(jnp.int32)
+    grid = jnp.array([lax.axis_size(GX), lax.axis_size(GY)], jnp.int32)
+    flat = enthalpy.reshape(1024, 128)
+    packed = pl.pallas_call(
+        pack_kernel,
+        out_shape=(struct((264, 128), f32),) * 2 + (struct((24, 128), f32),) * 2,
+        name="pack",
+    )(flat, velocity_init)
+    around = exchanged(*packed)
+    inverses = column_inverses(kappa)
+    current, *packed, weights = pl.pallas_call(
+        first_substep_kernel,
+        out_shape=(struct((8, 128, 128), f32),)
+        + (struct((256, 128), f32),) * 2
+        + (struct((16, 128), f32),) * 2
+        + (struct((9, 8, 128), f32),),
+        in_specs=[smem] * 3 + [vmem] * 11,
+        out_specs=(vmem,) * 6,
+        name="first_substep",
+    )(
+        place,
+        grid,
+        kappa,
+        flat,
+        velocity_init,
+        *around,
+        inverses,
+        ice_mask,
+        grounded,
+        surface_enthalpy,
+        geo_flux,
+    )
+    around = exchanged(*packed)
+    current, fields = pl.pallas_call(
+        second_substep_kernel,
+        out_shape=(struct((1024, 128), f32), struct((6, 8, 128), f32)),
+        in_specs=[smem] * 3 + [vmem] * 16,
+        out_specs=(vmem, vmem),
+        name="second_substep",
+    )(
+        place,
+        grid,
+        kappa,
+        current,
+        *around,
+        weights,
+        inverses,
+        ice_mask,
+        grounded,
+        surface_enthalpy,
+        geo_flux,
+        velocity_init,
+        thickness,
+        surface,
+        friction,
+        boundary_code,
+    )
+    quick, worst = momentum(fields, place, grid)
+
+    def plain():
+        free = ((boundary_code == 0) & (ice_mask == 1)).astype(f32)[None]
+        drag_term = jnp.where(grounded == 1, friction, 0.0) + shelf_drag
+        return plain_picard(fields[:2], thickness, fields[4], surface, drag_term, free)
+
+    velocity = lax.cond(worst[0, 0] > PIVOT_FLOOR, lambda: quick, plain)
+    return (current.reshape(enthalpy.shape), velocity)
 
 
 def solution(mesh):

time: 149 us -> 142 us (0.953)
  Pallas kernels: 13.1 us -> 23.5 us
  blocking collectives: 49.6 us -> 40.4 us
  starting transfers between devices: 46.2 us -> 53.1 us
  other arithmetic: 7.89 us -> 1.28 us
  local copies, waits for them, and re-layouts: 8.34 us -> 5.17 us
  matrix products: 3.11 us -> 0 us
  waiting for transfers between devices: 17.6 us -> 16.1 us
    ppermute x6 -> x14, starting transfers between devices: 16.3 us -> 49.3 us  [shifted(): lax.ppermute(array, axis, [(i, (i + by) % size) for i in range(size)])]
    ppermute x8 -> x0, starting transfers between devices: 26.1 us -> none  [the longest x4 15.9 us: with_halo_2(): lax.ppermute(last, axis, up)]
    pallas_call x1 -> x4, Pallas kernels: 2.17 us -> 12.6 us  [the longest x1 4.26 us: shards(): pl.pallas_call(first_substep_kernel, out_shape=(struct((8, 128, 128), f32...]
    all_to_all x1, blocking collectives: 18.1 us -> 12.2 us  [over_all(): return lax.all_to_all(part, GX, 0, 0, tiled=True)]
    all_to_all x2, blocking collectives: 31.6 us -> 28.2 us  [over_all(): part = lax.all_to_all(sums, GY, 0, 0, tiled=True)]
    add x4 -> x0, other arithmetic: 3.15 us -> none  [upwind_sweep(): face_flux + negative * (plus_one - 0.25 * (1.0 + negative) * (plus_two -...]
    dot_general x4 -> x0, matrix products: 3.11 us -> none  [the longest x2 1.64 us: diffuse(): jnp.dot(inverse_shelf, columns, precision=lax.Precision.HIGHEST)]
    unnamed x44 -> x42, local copies, waits for them, and re-layouts: 5.8 us -> 3.28 us
  transfers between devices with their start and end apart: 15 -> 15, of which waited for: 5 -> 6; matrix products, arithmetic and copies ran while one was open for 2% -> 1% of each run, Pallas kernels for 1% -> 2%
where the time goes in v3:
time: 142 us; the launch traced here: 141 us
  starting transfers between devices  53.1 us (37%)
  blocking collectives  40.4 us (28%)
  Pallas kernels  23.5 us (17%)
  waiting for transfers between devices  16.1 us (11%)
  local copies, waits for them, and re-layouts  5.17 us (4%)
  between operations  1.44 us (1%)
    ppermute x14, starting transfers between devices, shifted(): lax.ppermute(array, axis, [(i, (i + by) % size) for i in range(size)])  49.3 us
    all_to_all x2, blocking collectives, over_all(): part = lax.all_to_all(sums, GY, 0, 0, tiled=True)  28.2 us
    all_to_all x1, blocking collectives, over_all(): return lax.all_to_all(part, GX, 0, 0, tiled=True)  12.2 us
    all_to_all x1, waiting for transfers between devices, over_all(): return lax.all_to_all(part, GX, 0, 0, tiled=True)  8.67 us
    ppermute x14, waiting for transfers between devices, shifted(): lax.ppermute(array, axis, [(i, (i + by) % size) for i in range(size)])  7.43 us
    pallas_call x1, Pallas kernels, momentum(): pl.pallas_call(second_picard_kernel, out_shape=(struct((2 * KRYLOV, 8, 12...  4.7 us
    pallas_call x1, Pallas kernels, shards(): pl.pallas_call(first_substep_kernel, out_shape=(struct((8, 128, 128), f32...  4.26 us
    pallas_call x1, Pallas kernels, shards(): pl.pallas_call(second_substep_kernel, out_shape=(struct((1024, 128), f32)...  3.82 us
  transfers between devices with their start and end apart: 15, of which 6 were waited for; matrix products, arithmetic and copies ran while one was open for 1% of the time, Pallas kernels for 2%

profile of v3, /device:TPU:1, one launch (start us, length us, event | category | flops | bytes accessed | tf_op | source)
XLA Modules:
  0.0 141.0 jit_solution(4405547274920473152)
XLA Ops:
  0.6 2.3 %pack.1 = (f32[264,128]{1,0:T(8,128)}, f32[264,128]{1,0:T(8,128)}, f32[24,128]{1,0:T(8,128)}, f32[24,128]{1,0:T(8,128)}) custom-call(f32[1024,128]{1,0:T(8,128)} %bitcast.80, f32[2,8,128]{2,1,0:T(8,128)} %speed_ref.5), custom_call_target="tpu_custom_call" | custom-call | tf_op jit(solution)/shard_map/pack/pallas_call | solution.py:719
  2.9 3.5 %collective-permute-start.14 = (f32[24,128]{1,0:T(8,128)}, f32[24,128]{1,0:T(8,128)S(1)}, u32[]{:S(2)}, u32[]{:S(2)}) collective-permute-start(f32[24,128]{1,0:T(8,128)} %get-tuple-element.303), channel_id=1, source_target_pairs={{0,1},{1,2},{2,3},{3,4},{4,5},{5,6},{6,7},{7,8},{8,9},{9,10},{10,1... | collective-permute-start | bytes 36872 | tf_op jit(solution)/shard_map/ppermute | solution.py:365
  6.4 3.4 %collective-permute-start.15 = (f32[24,128]{1,0:T(8,128)}, f32[24,128]{1,0:T(8,128)S(1)}, u32[]{:S(2)}, u32[]{:S(2)}) collective-permute-start(f32[24,128]{1,0:T(8,128)} %get-tuple-element.304), channel_id=1, source_target_pairs={{0,15},{1,0},{2,1},{3,2},{4,3},{5,4},{6,5},{7,6},{8,7},{9,8},{10,9... | collective-permute-start | bytes 36872 | tf_op jit(solution)/shard_map/ppermute | solution.py:365
  9.8 2.0 %collective-permute-start.12 = (f32[264,128]{1,0:T(8,128)}, f32[264,128]{1,0:T(8,128)S(1)}, u32[]{:S(2)}, u32[]{:S(2)}) collective-permute-start(f32[264,128]{1,0:T(8,128)} %get-tuple-element.301), channel_id=1, source_target_pairs={{0,16},{16,32},{32,48},{48,64},{64,80},{80,96},{96,112},{112,128},... | collective-permute-start | bytes 405512 | tf_op jit(solution)/shard_map/ppermute | solution.py:365
  11.8 6.7 %collective-permute-start.13 = (f32[264,128]{1,0:T(8,128)}, f32[264,128]{1,0:T(8,128)S(1)}, u32[]{:S(2)}, u32[]{:S(2)}) collective-permute-start(f32[264,128]{1,0:T(8,128)} %get-tuple-element.302), channel_id=1, source_target_pairs={{0,496},{16,0},{32,16},{48,32},{64,48},{80,64},{96,80},{112,96},{1... | collective-permute-start | bytes 405512 | tf_op jit(solution)/shard_map/ppermute | solution.py:365
  18.5 0.1 fusion.29
  18.6 0.6 pad_maximum_fusion.10.kappa_ref
  19.2 0.6 pad_add_fusion.place_ref
  19.8 2.2 %column_inverses.1.inverses_ref = f32[256,128]{1,0:T(8,128)} custom-call(f32[16,128]{1,0:T(8,128)} %pad_maximum_fusion.10.kappa_ref), custom_call_target="tpu_custom_call" | custom-call | tf_op jit(solution)/shard_map/column_inverses/pallas_call | solution.py:135
  22.0 0.0 collective-permute-done.14.left_ref
  22.0 0.6 copy-done.14
  22.6 0.0 copy-done.15
  22.6 0.1 copy-done.1
  22.7 0.7 copy-done.2
  23.4 4.3 %first_substep.1 = (f32[8,128,128]{2,1,0:T(8,128)}, f32[256,128]{1,0:T(8,128)}, f32[256,128]{1,0:T(8,128)}, f32[16,128]{1,0:T(8,128)}, f32[16,128]{1,0:T(8,128)}, /*index=5*/f32[9,8,128]{2,1,0:T(8,128)}) custom-call(s32[2]{0:T(128)} %pad_add_fusion.place_ref, s32[2]{0:T(128)} %constant.145.clone.grid_ref, f32[129]{0:T(256)} %kappa_ref.3, ...), custom_call_target="tpu_custom_call" | custom-call | tf_op jit(solution)/shard_map/first_substep/pallas_call | solution.py:726
  27.6 1.9 %collective-permute-start.16 = (f32[256,128]{1,0:T(8,128)}, f32[256,128]{1,0:T(8,128)S(1)}, u32[]{:S(2)}, u32[]{:S(2)}) collective-permute-start(f32[256,128]{1,0:T(8,128)} %get-tuple-element.306), channel_id=1, source_target_pairs={{0,16},{16,32},{32,48},{48,64},{64,80},{80,96},{96,112},{112,128},... | collective-permute-start | bytes 393224 | tf_op jit(solution)/shard_map/ppermute | solution.py:365
  29.5 0.0 copy-start.8
  29.5 0.0 copy-start.7
  29.6 6.7 %collective-permute-start.17 = (f32[256,128]{1,0:T(8,128)}, f32[256,128]{1,0:T(8,128)S(1)}, u32[]{:S(2)}, u32[]{:S(2)}) collective-permute-start(f32[256,128]{1,0:T(8,128)} %get-tuple-element.307), channel_id=1, source_target_pairs={{0,496},{16,0},{32,16},{48,32},{64,48},{80,64},{96,80},{112,96},{1... | collective-permute-start | bytes 393224 | tf_op jit(solution)/shard_map/ppermute | solution.py:365
  36.2 0.1 collective-permute-start.18
  36.3 4.6 %collective-permute-start.19 = (f32[16,128]{1,0:T(8,128)}, f32[16,128]{1,0:T(8,128)S(1)}, u32[]{:S(2)}, u32[]{:S(2)}) collective-permute-start(f32[16,128]{1,0:T(8,128)} %get-tuple-element.309), channel_id=1, source_target_pairs={{0,15},{1,0},{2,1},{3,2},{4,3},{5,4},{6,5},{7,6},{8,7},{9,8},{10,9... | collective-permute-start | bytes 24584 | tf_op jit(solution)/shard_map/ppermute | solution.py:365
  40.9 0.9 collective-permute-done.18.left_ref
  41.7 0.2 collective-permute-done.19.right_ref
  41.9 0.4 copy-done.17
  42.3 0.2 copy-done.18
  42.5 0.1 copy-done.3
  42.6 0.0 copy-done.4
  42.6 3.8 %second_substep.1 = (f32[1024,128]{1,0:T(8,128)}, f32[6,8,128]{2,1,0:T(8,128)S(1)}) custom-call(s32[2]{0:T(128)} %pad_add_fusion.place_ref, s32[2]{0:T(128)} %constant.145.clone.grid_ref, f32[129]{0:T(256)} %kappa_ref.3, f32[8,128,128]{2,1,0:T(8,128)} %get-tuple-element.305.enthalpy_ref, f32[256,128]{1,0:T(8,128)} %copy-done.3, f32[256,128]{1,0:T(8,128)} %copy-done.4, ...), custom_call_target="tpu_custom_call" | custom-call | tf_op jit(solution)/shard_map/second_substep/pallas_call | solution.py:749
  46.4 1.9 %collective-permute-start.20 = (f32[6,8,128]{2,1,0:T(8,128)S(1)}, f32[6,8,128]{2,1,0:T(8,128)S(1)}, u32[]{:S(2)}, u32[]{:S(2)}) collective-permute-start(f32[6,8,128]{2,1,0:T(8,128)S(1)} %get-tuple-element.312), channel_id=1, source_target_pairs={{0,32},{16,48},{32,64},{48,80},{64,96},{80,112},{96,128},{112,144}... | collective-permute-start | bytes 73736 | tf_op jit(solution)/shard_map/ppermute | solution.py:365
  48.3 7.6 %collective-permute-start.23 = (f32[6,8,128]{2,1,0:T(8,128)S(1)}, f32[6,8,128]{2,1,0:T(8,128)S(1)}, u32[]{:S(2)}, u32[]{:S(2)}) collective-permute-start(f32[6,8,128]{2,1,0:T(8,128)S(1)} %get-tuple-element.312), channel_id=1, source_target_pairs={{0,480},{16,496},{32,0},{48,16},{64,32},{80,48},{96,64},{112,80},{... | collective-permute-start | bytes 73736 | tf_op jit(solution)/shard_map/ppermute | solution.py:365
  55.9 1.9 %collective-permute-start.22 = (f32[6,8,128]{2,1,0:T(8,128)S(1)}, f32[6,8,128]{2,1,0:T(8,128)S(1)}, u32[]{:S(2)}, u32[]{:S(2)}) collective-permute-start(f32[6,8,128]{2,1,0:T(8,128)S(1)} %get-tuple-element.312), channel_id=1, source_target_pairs={{0,496},{16,0},{32,16},{48,32},{64,48},{80,64},{96,80},{112,96},{1... | collective-permute-start | bytes 73736 | tf_op jit(solution)/shard_map/ppermute | solution.py:365
  57.9 3.4 %collective-permute-start.21 = (f32[6,8,128]{2,1,0:T(8,128)S(1)}, f32[6,8,128]{2,1,0:T(8,128)S(1)}, u32[]{:S(2)}, u32[]{:S(2)}) collective-permute-start(f32[6,8,128]{2,1,0:T(8,128)S(1)} %get-tuple-element.312), channel_id=1, source_target_pairs={{0,16},{16,32},{32,48},{48,64},{64,80},{80,96},{96,112},{112,128},... | collective-permute-start | bytes 73736 | tf_op jit(solution)/shard_map/ppermute | solution.py:365
  61.3 4.5 %collective-permute-done.21 = f32[6,8,128]{2,1,0:T(8,128)S(1)} collective-permute-done((f32[6,8,128]{2,1,0:T(8,128)S(1)}, f32[6,8,128]{2,1,0:T(8,128)S(1)}, u32[]{:S(2)}, u32[]{:S(2)}) %collective-permute-start.21) | collective-permute-done | bytes 24608 | tf_op jit(solution)/shard_map/ppermute | solution.py:365
  65.8 5.7 %collective-permute-start.25 = (f32[6,40,128]{2,1,0:T(8,128)S(1)}, f32[6,40,128]{2,1,0:T(8,128)S(1)}, u32[]{:S(2)}, u32[]{:S(2)}) collective-permute-start(f32[6,40,128]{2,1,0:T(8,128)S(1)} %constant_dynamic-update-slice_fusion.mine_ref), channel_id=1, source_target_pairs={{0,15},{1,0},{2,1},{3,2},{4,3},{5,4},{6,5},{7,6},{8,7},{9,8},{10,9... | collective-permute-start | bytes 368648 | tf_op jit(solution)/shard_map/ppermute | solution.py:365
  71.6 1.0 collective-permute-done.25.right_ref
  72.5 0.9 collective-permute-done.24.left_ref
  73.4 0.7 copy-done.6
  74.1 3.3 %first_picard.1 = (f32[12,24,256]{2,1,0:T(8,128)}, f32[6,24,256]{2,1,0:T(8,128)}, f32[16,128]{1,0:T(8,128)}) custom-call(s32[2]{0:T(128)} %pad_add_fusion.place_ref, s32[2]{0:T(128)} %constant.145.clone.grid_ref, f32[6,40,128]{2,1,0:T(8,128)} %copy-done, f32[6,40,128]{2,1,0:T(8,128)} %copy-done.6, f32[6,40,128]{2,1,0:T(8,128)} %copy-done.5), custom_call_target="tpu_custom_call" | custom-call | tf_op jit(solution)/shard_map/first_picard/pallas_call | solution.py:379
  77.4 16.0 %all_to_all.34 = f32[16,1,128]{2,1,0:T(1,128)S(1)} all-to-all(f32[16,1,128]{2,1,0:T(1,128)} %bitcast.90), channel_id=1, replica_groups=mesh['gx_0'=4,'gx_1'=8,'gy_0'=8,'gy_1'=2] {'gy_0','gy_1'}, dimensions={0} | all-to-all | bytes 16384 | tf_op jit(solution)/shard_map/all_to_all | solution.py:358
  93.5 12.2 %all_to_all.35 = f32[32,1,128]{2,1,0:T(1,128)} all-to-all(f32[32,1,128]{2,1,0:T(1,128)S(1)} %broadcast_in_dim.36), channel_id=1, replica_groups=mesh['gx_0'=4,'gx_1'=8,'gy_0'=8,'gy_1'=2] {'gx_0','gx_1'}, dimensions={0} | all-to-all | bytes 32768 | tf_op jit(solution)/shard_map/all_to_all | solution.py:360
  105.6 4.7 %second_picard.1 = (f32[12,8,128]{2,1,0:T(8,128)}, f32[2,8,128]{2,1,0:T(8,128)}, f32[16,128]{1,0:T(8,128)}, f32[8,128]{1,0:T(8,128)}) custom-call(f32[32,128]{1,0:T(8,128)} %bitcast.89, f32[12,24,256]{2,1,0:T(8,128)} %get-tuple-element.314.basis_ref, f32[6,24,256]{2,1,0:T(8,128)} %get-tuple-element.315.fixed_ref), custom_call_target="tpu_custom_call" | custom-call | tf_op jit(solution)/shard_map/second_picard/pallas_call | solution.py:390
  110.3 12.2 %all_to_all.36 = f32[16,1,128]{2,1,0:T(1,128)S(1)} all-to-all(f32[16,1,128]{2,1,0:T(1,128)} %bitcast.91), channel_id=1, replica_groups=mesh['gx_0'=4,'gx_1'=8,'gy_0'=8,'gy_1'=2] {'gy_0','gy_1'}, dimensions={0} | all-to-all | bytes 16384 | tf_op jit(solution)/shard_map/all_to_all | solution.py:358
  122.5 0.6 broadcast_in_dim.37
  123.2 3.8 %all-to-all-start.3 = ((f32[32,1,128]{2,1,0:T(1,128)}), f32[32,1,128]{2,1,0:T(1,128)S(1)}, u32[]{:S(2)}, u32[]{:S(2)}) async-start(f32[32,1,128]{2,1,0:T(1,128)} %broadcast_in_dim.37), calls=%async_computation.3 | async-start | bytes 32768 | tf_op jit(solution)/shard_map/all_to_all | solution.py:360
  126.9 8.7 %all-to-all-done.3 = f32[32,1,128]{2,1,0:T(1,128)S(1)} async-done(((f32[32,1,128]{2,1,0:T(1,128)}), f32[32,1,128]{2,1,0:T(1,128)S(1)}, u32[]{:S(2)}, u32[]{:S(2)}) %all-to-all-start.3) | async-done | bytes 16416 | tf_op jit(solution)/shard_map/all_to_all | solution.py:360
  135.6 0.6 copy-done.9
  136.2 3.0 %last_picard.1 = (f32[2,8,128]{2,1,0:T(8,128)}, f32[8,128]{1,0:T(8,128)}) custom-call(f32[32,128]{1,0:T(8,128)} %bitcast.88, f32[12,8,128]{2,1,0:T(8,128)} %get-tuple-element.317.basis_ref, f32[2,8,128]{2,1,0:T(8,128)} %get-tuple-element.318.velocity_ref, f32[8,128]{1,0:T(8,128)} %get-tuple-element.319.least_ref), custom_call_target="tpu_custom_call" | custom-call | tf_op jit(solution)/shard_map/last_picard/pallas_call | solution.py:400
  139.2 1.2 slice.466
  (46 shorter events, 0.2 us)
Async XLA Ops:
  2.9 19.1 %collective-permute-start.14 = (f32[24,128]{1,0:T(8,128)}, f32[24,128]{1,0:T(8,128)S(1)}, u32[]{:S(2)}, u32[]{:S(2)}) collective-permute-start(f32[24,128]{1,0:T(8,128)} %get-tuple-element.303), channel_id=1, source_target_pairs={{0,1},{1,2},{2,3},{3,4},{4,5},{5,6},{6,7},{7,8},{8,9},{9,10},{10,1... | collective-permute-start | bytes 36872 | tf_op jit(solution)/shard_map/ppermute | solution.py:365
  6.4 15.6 %collective-permute-start.15 = (f32[24,128]{1,0:T(8,128)}, f32[24,128]{1,0:T(8,128)S(1)}, u32[]{:S(2)}, u32[]{:S(2)}) collective-permute-start(f32[24,128]{1,0:T(8,128)} %get-tuple-element.304), channel_id=1, source_target_pairs={{0,15},{1,0},{2,1},{3,2},{4,3},{5,4},{6,5},{7,6},{8,7},{9,8},{10,9... | collective-permute-start | bytes 36872 | tf_op jit(solution)/shard_map/ppermute | solution.py:365
  9.8 8.7 %copy-start.16 = (f32[129]{0:T(256)S(1)}, f32[129]{0:T(256)}, u32[]{:S(2)}) copy-start(f32[129]{0:T(256)} %kappa_ref.3) | copy-start | bytes 1552
  9.8 12.3 %collective-permute-start.12 = (f32[264,128]{1,0:T(8,128)}, f32[264,128]{1,0:T(8,128)S(1)}, u32[]{:S(2)}, u32[]{:S(2)}) collective-permute-start(f32[264,128]{1,0:T(8,128)} %get-tuple-element.301), channel_id=1, source_target_pairs={{0,16},{16,32},{32,48},{48,64},{64,80},{80,96},{96,112},{112,128},... | collective-permute-start | bytes 405512 | tf_op jit(solution)/shard_map/ppermute | solution.py:365
  11.8 10.2 %collective-permute-start.13 = (f32[264,128]{1,0:T(8,128)}, f32[264,128]{1,0:T(8,128)S(1)}, u32[]{:S(2)}, u32[]{:S(2)}) collective-permute-start(f32[264,128]{1,0:T(8,128)} %get-tuple-element.302), channel_id=1, source_target_pairs={{0,496},{16,0},{32,16},{48,32},{64,48},{80,64},{96,80},{112,96},{1... | collective-permute-start | bytes 405512 | tf_op jit(solution)/shard_map/ppermute | solution.py:365
  19.8 3.6 %copy-start.10 = (s32[8,128]{1,0:T(8,128)S(1)}, s32[8,128]{1,0:T(8,128)}, u32[]{:S(2)}) copy-start(s32[8,128]{1,0:T(8,128)} %ice_ref.3) | copy-start | bytes 12292
  19.8 3.6 %copy-start.11 = (s32[8,128]{1,0:T(8,128)S(1)}, s32[8,128]{1,0:T(8,128)}, u32[]{:S(2)}) copy-start(s32[8,128]{1,0:T(8,128)} %grounded_ref.3) | copy-start | bytes 12292
  22.0 0.6 copy-start.14
  22.0 0.6 copy-start.15
  22.0 0.7 copy-start.1
  22.7 0.7 copy-start.2
  23.3 19.3 %copy-start.12 = (f32[8,128]{1,0:T(8,128)S(1)}, f32[8,128]{1,0:T(8,128)}, u32[]{:S(2)}) copy-start(f32[8,128]{1,0:T(8,128)} %friction_ref.1) | copy-start | bytes 12292
  23.3 19.3 %copy-start.13 = (s32[8,128]{1,0:T(8,128)S(1)}, s32[8,128]{1,0:T(8,128)}, u32[]{:S(2)}) copy-start(s32[8,128]{1,0:T(8,128)} %code_ref.1) | copy-start | bytes 12292
  27.6 14.3 %collective-permute-start.16 = (f32[256,128]{1,0:T(8,128)}, f32[256,128]{1,0:T(8,128)S(1)}, u32[]{:S(2)}, u32[]{:S(2)}) collective-permute-start(f32[256,128]{1,0:T(8,128)} %get-tuple-element.306), channel_id=1, source_target_pairs={{0,16},{16,32},{32,48},{48,64},{64,80},{80,96},{96,112},{112,128},... | collective-permute-start | bytes 393224 | tf_op jit(solution)/shard_map/ppermute | solution.py:365
  29.5 13.1 %copy-start.8 = (f32[8,128]{1,0:T(8,128)S(1)}, f32[8,128]{1,0:T(8,128)}, u32[]{:S(2)}) copy-start(f32[8,128]{1,0:T(8,128)} %height_ref.1) | copy-start | bytes 12292
  29.5 13.1 %copy-start.7 = (f32[8,128]{1,0:T(8,128)S(1)}, f32[8,128]{1,0:T(8,128)}, u32[]{:S(2)}) copy-start(f32[8,128]{1,0:T(8,128)} %thick_ref.1) | copy-start | bytes 12292
  29.6 12.4 %collective-permute-start.17 = (f32[256,128]{1,0:T(8,128)}, f32[256,128]{1,0:T(8,128)S(1)}, u32[]{:S(2)}, u32[]{:S(2)}) collective-permute-start(f32[256,128]{1,0:T(8,128)} %get-tuple-element.307), channel_id=1, source_target_pairs={{0,496},{16,0},{32,16},{48,32},{64,48},{80,64},{96,80},{112,96},{1... | collective-permute-start | bytes 393224 | tf_op jit(solution)/shard_map/ppermute | solution.py:365
  36.2 5.5 %collective-permute-start.18 = (f32[16,128]{1,0:T(8,128)}, f32[16,128]{1,0:T(8,128)S(1)}, u32[]{:S(2)}, u32[]{:S(2)}) collective-permute-start(f32[16,128]{1,0:T(8,128)} %get-tuple-element.308), channel_id=1, source_target_pairs={{0,1},{1,2},{2,3},{3,4},{4,5},{5,6},{6,7},{7,8},{8,9},{9,10},{10,1... | collective-permute-start | bytes 24584 | tf_op jit(solution)/shard_map/ppermute | solution.py:365
  36.3 5.6 %collective-permute-start.19 = (f32[16,128]{1,0:T(8,128)}, f32[16,128]{1,0:T(8,128)S(1)}, u32[]{:S(2)}, u32[]{:S(2)}) collective-permute-start(f32[16,128]{1,0:T(8,128)} %get-tuple-element.309), channel_id=1, source_target_pairs={{0,15},{1,0},{2,1},{3,2},{4,3},{5,4},{6,5},{7,6},{8,7},{9,8},{10,9... | collective-permute-start | bytes 24584 | tf_op jit(solution)/shard_map/ppermute | solution.py:365
  41.7 0.6 copy-start.17
  41.9 0.6 copy-start.18
  41.9 0.7 copy-start.3
  41.9 0.7 copy-start.4
  46.4 14.8 %collective-permute-start.20 = (f32[6,8,128]{2,1,0:T(8,128)S(1)}, f32[6,8,128]{2,1,0:T(8,128)S(1)}, u32[]{:S(2)}, u32[]{:S(2)}) collective-permute-start(f32[6,8,128]{2,1,0:T(8,128)S(1)} %get-tuple-element.312), channel_id=1, source_target_pairs={{0,32},{16,48},{32,64},{48,80},{64,96},{80,112},{96,128},{112,144}... | collective-permute-start | bytes 73736 | tf_op jit(solution)/shard_map/ppermute | solution.py:365
  48.3 17.4 %collective-permute-start.23 = (f32[6,8,128]{2,1,0:T(8,128)S(1)}, f32[6,8,128]{2,1,0:T(8,128)S(1)}, u32[]{:S(2)}, u32[]{:S(2)}) collective-permute-start(f32[6,8,128]{2,1,0:T(8,128)S(1)} %get-tuple-element.312), channel_id=1, source_target_pairs={{0,480},{16,496},{32,0},{48,16},{64,32},{80,48},{96,64},{112,80},{... | collective-permute-start | bytes 73736 | tf_op jit(solution)/shard_map/ppermute | solution.py:365
  55.9 9.8 %collective-permute-start.22 = (f32[6,8,128]{2,1,0:T(8,128)S(1)}, f32[6,8,128]{2,1,0:T(8,128)S(1)}, u32[]{:S(2)}, u32[]{:S(2)}) collective-permute-start(f32[6,8,128]{2,1,0:T(8,128)S(1)} %get-tuple-element.312), channel_id=1, source_target_pairs={{0,496},{16,0},{32,16},{48,32},{64,48},{80,64},{96,80},{112,96},{1... | collective-permute-start | bytes 73736 | tf_op jit(solution)/shard_map/ppermute | solution.py:365
  57.9 7.9 %collective-permute-start.21 = (f32[6,8,128]{2,1,0:T(8,128)S(1)}, f32[6,8,128]{2,1,0:T(8,128)S(1)}, u32[]{:S(2)}, u32[]{:S(2)}) collective-permute-start(f32[6,8,128]{2,1,0:T(8,128)S(1)} %get-tuple-element.312), channel_id=1, source_target_pairs={{0,16},{16,32},{32,48},{48,64},{64,80},{80,96},{96,112},{112,128},... | collective-permute-start | bytes 73736 | tf_op jit(solution)/shard_map/ppermute | solution.py:365
  65.8 7.6 %copy-start = (f32[6,40,128]{2,1,0:T(8,128)}, f32[6,40,128]{2,1,0:T(8,128)S(1)}, u32[]{:S(2)}) copy-start(f32[6,40,128]{2,1,0:T(8,128)S(1)} %constant_dynamic-update-slice_fusion.mine_ref) | copy-start | bytes 368644
  65.8 6.7 %collective-permute-start.25 = (f32[6,40,128]{2,1,0:T(8,128)S(1)}, f32[6,40,128]{2,1,0:T(8,128)S(1)}, u32[]{:S(2)}, u32[]{:S(2)}) collective-permute-start(f32[6,40,128]{2,1,0:T(8,128)S(1)} %constant_dynamic-update-slice_fusion.mine_ref), channel_id=1, source_target_pairs={{0,15},{1,0},{2,1},{3,2},{4,3},{5,4},{6,5},{7,6},{8,7},{9,8},{10,9... | collective-permute-start | bytes 368648 | tf_op jit(solution)/shard_map/ppermute | solution.py:365
  71.6 1.9 %collective-permute-start.24 = (f32[6,40,128]{2,1,0:T(8,128)S(1)}, f32[6,40,128]{2,1,0:T(8,128)S(1)}, u32[]{:S(2)}, u32[]{:S(2)}) collective-permute-start(f32[6,40,128]{2,1,0:T(8,128)S(1)} %constant_dynamic-update-slice_fusion.mine_ref), channel_id=1, source_target_pairs={{0,1},{1,2},{2,3},{3,4},{4,5},{5,6},{6,7},{7,8},{8,9},{9,10},{10,1... | collective-permute-start | bytes 368648 | tf_op jit(solution)/shard_map/ppermute | solution.py:365
  72.5 0.9 copy-start.5
  73.4 0.7 copy-start.6
  123.2 12.5 %all-to-all-start.3 = ((f32[32,1,128]{2,1,0:T(1,128)}), f32[32,1,128]{2,1,0:T(1,128)S(1)}, u32[]{:S(2)}, u32[]{:S(2)}) async-start(f32[32,1,128]{2,1,0:T(1,128)} %broadcast_in_dim.37), calls=%async_computation.3 | async-start | bytes 32768 | tf_op jit(solution)/shard_map/all_to_all | solution.py:360
  135.6 0.6 copy-start.9

commit v4 on v3

--- a/solution.py
+++ b/solution.py
@@ -98,9 +98,9 @@
 
 
 def inverse_kernel(kappa_ref, out_ref):
-    levels = kappa_ref.shape[1]
-    above = kappa_ref[0:8, :]
-    below = kappa_ref[8:16, :]
+    levels = out_ref.shape[1]
+    above = jnp.broadcast_to(kappa_ref[:, :levels], (8, levels))
+    below = jnp.broadcast_to(kappa_ref[:, 1:], (8, levels))
     lane = lax.broadcasted_iota(jnp.int32, (8, levels), 1)
     rows = lax.broadcasted_iota(jnp.int32, (levels, levels), 0)
     cols = lax.broadcasted_iota(jnp.int32, (levels, levels), 1)
@@ -125,18 +125,16 @@
                 + up[0:1] * pltpu.roll(right, back, 1)
             )
             step *= 2
-        out_ref[k * levels : (k + 1) * levels] = right / mid[0:1]
+        out_ref[k * levels : (k + 1) * levels] = right * (1.0 / mid)[0:1]
 
 
 def column_inverses(kappa):
     levels = kappa.shape[0] - 1
-    above = jnp.broadcast_to(kappa[None, :levels], (8, levels))
-    below = jnp.broadcast_to(kappa[None, 1:], (8, levels))
     return pl.pallas_call(
         inverse_kernel,
         out_shape=jax.ShapeDtypeStruct((2 * levels, levels), kappa.dtype),
         name="column_inverses",
-    )(jnp.concatenate([above, below], axis=0))
+    )(kappa[None])
 
 
 def next_row(array):
@@ -244,64 +242,66 @@
 
 
 def small_solve(parts):
-    sums = jnp.sum(parts, axis=0, keepdims=True)
-    at = lambda k: sums[:, k : k + 1]
-    full = {}
+    sums = jnp.broadcast_to(jnp.sum(parts, axis=0, keepdims=True), (8, 128))
+    at = lambda k: jnp.broadcast_to(sums[:, k : k + 1], (8, 128))
+    system = {}
     k = 0
     for i in range(KRYLOV):
         for j in range(i, KRYLOV):
-            full[i, j] = at(k)
+            system[i, j] = at(k)
             k += 1
-    norm = [lax.rsqrt(full[i, i]) for i in range(KRYLOV)]
-    right = [at(k + i) * norm[i] for i in range(KRYLOV)]
-    lower, pivots, least = ({}, [], None)
-    scaled = {}
-    for j in range(KRYLOV):
-        pivot = jnp.ones_like(right[0])
-        for m in range(j):
-            pivot = pivot - scaled[j, m] * lower[j, m]
-        pivots.append(pivot)
-        least = pivot if least is None else jnp.minimum(least, pivot)
-        inverse = 1.0 / pivot
-        for i in range(j + 1, KRYLOV):
-            value = full[j, i] * norm[i] * norm[j]
-            for m in range(j):
-                value = value - scaled[i, m] * lower[j, m]
-            scaled[i, j] = value
-            lower[i, j] = value * inverse
-    forward = []
-    for i in range(KRYLOV):
-        value = right[i]
-        for m in range(i):
-            value = value - lower[i, m] * forward[m]
-        forward.append(value)
+    start = [system[i, i] for i in range(KRYLOV)]
+    right = [at(k + i) for i in range(KRYLOV)]
+    least = None
+    for p in range(KRYLOV):
+        relative = system[p, p] / start[p]
+        least = relative if least is None else jnp.minimum(least, relative)
+        inverse = 1.0 / system[p, p]
+        for i in range(p + 1, KRYLOV):
+            factor = system[p, i] * inverse
+            for j in range(i, KRYLOV):
+                system[i, j] = system[i, j] - factor * system[p, j]
+            right[i] = right[i] - factor * right[p]
+        system[p, p] = inverse
     answer = [None] * KRYLOV
     for i in reversed(range(KRYLOV)):
-        value = forward[i] / pivots[i]
+        value = right[i]
         for m in range(i + 1, KRYLOV):
-            value = value - lower[m, i] * answer[m]
-        answer[i] = value
-    return ([a * n for a, n in zip(answer, norm)], least)
-
-
-def first_picard_kernel(
-    place_ref, grid_ref, mine_ref, left_ref, right_ref, basis_ref, fixed_ref, sums_ref
-):
-    rows = mine_ref.shape[1]
+            value = value - system[i, m] * answer[m]
+        answer[i] = value * system[i, i]
+    return (answer, least)
+
+
+def where_am_i():
+    place = []
+    for axes in (GX, GY):
+        major, minor = axes
+        length = lax.axis_size(minor)
+        place.append((lax.axis_index(major) * length + lax.axis_index(minor)))
+    return (place[0], place[1], lax.axis_size(GX), lax.axis_size(GY))
+
+
+def first_picard_kernel(statics_ref, left_ref, right_ref, stiff_ref, basis_ref, fixed_ref, sums_ref):
+    gx, gy, gx_size, gy_size = where_am_i()
+    rows = 40
     lane = lax.broadcasted_iota(jnp.int32, (rows, 128), 1)
-    row = lax.broadcasted_iota(jnp.int32, (rows, 128), 0) + (place_ref[0] * 8 - OWN)
-    row_in = (row >= 0) & (row < grid_ref[0] * 8)
+    row = lax.broadcasted_iota(jnp.int32, (rows, 128), 0) + (gx * 8 - OWN)
+    row_in = (row >= 0) & (row < gx_size * 8)
     from_right = lane < SIDE
-    col = place_ref[1] + jnp.where(from_right, 1, -1)
-    side_in = row_in & (col >= 0) & (col < grid_ref[1])
+    col = gy + jnp.where(from_right, 1, -1)
+    side_in = row_in & (col >= 0) & (col < gy_size)
 
     def field(k):
-        side = jnp.where(from_right, right_ref[k], left_ref[k])
+        part = slice(k * rows, k * rows + rows)
+        side = jnp.where(from_right, right_ref[part], left_ref[part])
         return jnp.concatenate(
-            [jnp.where(row_in, mine_ref[k], 0.0), jnp.where(side_in, side, 0.0)], axis=1
+            [jnp.where(row_in, statics_ref[part], 0.0), jnp.where(side_in, side, 0.0)], axis=1
         )
 
-    u, v, drag, thick, stiff, surface = (field(k) for k in range(6))
+    u, v, drag, thick, surface = (field(k) for k in range(5))
+    blocks = [stiff_ref[jnp.clip(gx + k, 0, gx_size - 1)] for k in range(-2, 3)]
+    stiff = jnp.concatenate(blocks, axis=0)
+    stiff = jnp.where(jnp.concatenate([row_in, side_in], axis=1), stiff, 0.0)
     t_sum = thick + next_col(thick)
     s_sum = stiff + next_col(stiff)
     corner_product = (1.0 / 64.0) * (t_sum + next_row(t_sum)) * (s_sum + next_row(s_sum))
@@ -327,11 +327,12 @@
     answer, least = small_solve(parts_ref[...])
     u, v = (fixed_ref[0], fixed_ref[1])
     for k in range(KRYLOV):
-        u = u + answer[k] * basis_ref[2 * k]
-        v = v + answer[k] * basis_ref[2 * k + 1]
+        scale = jnp.tile(answer[k], (3, 2))
+        u = u + scale * basis_ref[2 * k]
+        v = v + scale * basis_ref[2 * k + 1]
     velocity_ref[0] = u[8:16, :128]
     velocity_ref[1] = v[8:16, :128]
-    least_ref[...] = jnp.broadcast_to(least, least_ref.shape)
+    least_ref[...] = least
 
     def keep(k, b_u, b_v):
         next_ref[2 * k] = b_u[8:16, :128]
@@ -350,7 +351,7 @@
         v = v + answer[k] * basis_ref[2 * k + 1]
     out_ref[0] = u
     out_ref[1] = v
-    worst_ref[...] = jnp.minimum(least_ref[...], least)
+    worst_ref[0, 0] = jnp.min(jnp.minimum(least_ref[...], least))
 
 
 def over_all(sums):
@@ -365,17 +366,18 @@
     return lax.ppermute(array, axis, [(i, (i + by) % size) for i in range(size)])
 
 
-def momentum(fields, place, grid):
+def momentum(statics):
     f32 = jnp.float32
-    below = [shifted(fields, GX, by) for by in (2, 1)]
-    above = [shifted(fields, GX, -by) for by in (1, 2)]
-    mine = jnp.concatenate(below + [fields] + above, axis=1)
-    left = shifted(mine, GY, 1)
-    right = shifted(mine, GY, -1)
-    gy = lax.axis_size(GY)
+    struct = jax.ShapeDtypeStruct
     smem = pl.BlockSpec(memory_space=pltpu.SMEM)
     vmem = pl.BlockSpec(memory_space=pltpu.VMEM)
-    struct = jax.ShapeDtypeStruct
+    gx, gy = (lax.axis_size(GX), lax.axis_size(GY))
+    left = shifted(statics, GY, 1)
+    right = shifted(statics, GY, -1)
+    lane = lax.broadcasted_iota(jnp.int32, (8, 128), 1)
+    side = jnp.where(lane < SIDE, right[200:], left[200:])
+    strip = jnp.concatenate([statics[200:], side], axis=1)
+    strip = lax.all_to_all(jnp.broadcast_to(strip[None], (gx, 8, 256)), GX, 0, 0, tiled=True)
     basis, fixed, sums = pl.pallas_call(
         first_picard_kernel,
         out_shape=(
@@ -383,10 +385,8 @@
             struct((6, 24, 256), f32),
             struct((gy, 128), f32),
         ),
-        in_specs=[smem, smem, vmem, vmem, vmem],
-        out_specs=(vmem, vmem, vmem),
         name="first_picard",
-    )(place, grid, mine, left, right)
+    )(statics, left, right, strip)
     basis, velocity, sums, least = pl.pallas_call(
         second_picard_kernel,
         out_shape=(
@@ -399,7 +399,8 @@
     )(over_all(sums), basis, fixed)
     return pl.pallas_call(
         last_kernel,
-        out_shape=(struct((2, 8, 128), f32), struct((8, 128), f32)),
+        out_shape=(struct((2, 8, 128), f32), struct((1, 1), f32)),
+        out_specs=(vmem, smem),
         name="last_picard",
     )(over_all(sums), basis, velocity, least)
 
@@ -457,14 +458,37 @@
     return (tiles[:16], tiles[16:])
 
 
-def pack_kernel(enthalpy_ref, speed_ref, low_ref, high_ref, left_ref, right_ref):
+def pack_kernel(
+    enthalpy_ref,
+    speed_ref,
+    thick_ref,
+    height_ref,
+    friction_ref,
+    ice_ref,
+    grounded_ref,
+    code_ref,
+    low_ref,
+    high_ref,
+    left_ref,
+    right_ref,
+):
     planes = [enthalpy_ref[pl.ds(x, 128, stride=8), :] for x in range(8)]
-    low_ref[0:128] = planes[0]
-    low_ref[128:256] = planes[1]
-    low_ref[256:264] = speed_ref[0]
-    high_ref[0:128] = planes[6]
-    high_ref[128:256] = planes[7]
-    high_ref[256:264] = speed_ref[0]
+    free = (code_ref[...] == 0) & (ice_ref[...] == 1)
+    held = free | (code_ref[...] == 2)
+    drag = jnp.where(grounded_ref[...] == 1, friction_ref[...], 0.0) + shelf_drag
+    statics = (
+        jnp.where(held, speed_ref[0], 0.0),
+        jnp.where(held, speed_ref[1], 0.0),
+        jnp.where(free, drag, 0.0),
+        thick_ref[...],
+        height_ref[...],
+        speed_ref[0],
+    )
+    for out_ref, pair in ((low_ref, (0, 1)), (high_ref, (6, 7))):
+        out_ref[0:128] = planes[pair[0]]
+        out_ref[128:256] = planes[pair[1]]
+        for k, value in enumerate(statics):
+            out_ref[256 + 8 * k : 264 + 8 * k] = value
     first, last = column_tiles(planes)
     left_ref[0:16] = first
     left_ref[16:24] = speed_ref[1]
@@ -563,9 +587,17 @@
     return done
 
 
+def inside(below_ref, above_ref, left_ref, right_ref):
+    gx, gy, gx_size, gy_size = where_am_i()
+    return (
+        jnp.where(gx > 0, below_ref[...], 0.0),
+        jnp.where(gx < gx_size - 1, above_ref[...], 0.0),
+        jnp.where(gy > 0, left_ref[...], 0.0),
+        jnp.where(gy < gy_size - 1, right_ref[...], 0.0),
+    )
+
+
 def first_substep_kernel(
-    place_ref,
-    grid_ref,
     kappa_ref,
     enthalpy_ref,
     speed_ref,
@@ -585,12 +617,8 @@
     last_ref,
     weights_ref,
 ):
-    has_below, has_above, has_left, has_right = sides_inside(place_ref, grid_ref)
-    below = jnp.where(has_below, below_ref[...], 0.0)
-    above = jnp.where(has_above, above_ref[...], 0.0)
-    left = jnp.where(has_left, left_ref[...], 0.0)
-    right = jnp.where(has_right, right_ref[...], 0.0)
-    weights = cell_weights(speed_ref, below[256:], above[256:], left[16:], right[16:])
+    below, above, left, right = inside(below_ref, above_ref, left_ref, right_ref)
+    weights = cell_weights(speed_ref, below[296:], above[296:], left[16:], right[16:])
     for k in range(9):
         weights_ref[k] = weights[k]
     edges = edge_products(weights, left[:16], right[:16])
@@ -612,23 +640,14 @@
         out_ref[x] = done[x]
     low_ref[0:128] = done[0]
     low_ref[128:256] = done[1]
+    low_ref[256:296] = above[256:296]
     high_ref[0:128] = done[6]
     high_ref[128:256] = done[7]
+    high_ref[256:296] = below[256:296]
     first_ref[...], last_ref[...] = column_tiles(done)
 
 
-def sides_inside(place_ref, grid_ref):
-    return (
-        place_ref[0] > 0,
-        place_ref[0] < grid_ref[0] - 1,
-        place_ref[1] > 0,
-        place_ref[1] < grid_ref[1] - 1,
-    )
-
-
 def second_substep_kernel(
-    place_ref,
-    grid_ref,
     kappa_ref,
     enthalpy_ref,
     below_ref,
@@ -641,34 +660,26 @@
     grounded_ref,
     surface_ref,
     flux_ref,
-    speed_ref,
-    thick_ref,
-    height_ref,
-    friction_ref,
-    code_ref,
+    near_below_ref,
+    near_above_ref,
+    mine_ref,
     out_ref,
-    fields_ref,
+    statics_ref,
 ):
-    has_below, has_above, has_left, has_right = sides_inside(place_ref, grid_ref)
-    below = jnp.where(has_below, below_ref[...], 0.0)
-    above = jnp.where(has_above, above_ref[...], 0.0)
-    left = jnp.where(has_left, left_ref[...], 0.0)
-    right = jnp.where(has_right, right_ref[...], 0.0)
+    below, above, left, right = inside(below_ref, above_ref, left_ref, right_ref)
     weights = tuple(weights_ref[k] for k in range(9))
     edges = edge_products(weights, left, right)
     planes = [below[:128], below[128:256]]
     planes += [enthalpy_ref[x] for x in range(8)]
     planes += [above[:128], above[128:256]]
-    ice = ice_ref[...]
-    grounded = grounded_ref[...]
     done = substep(
         planes,
         weights,
         edges,
         inverses_ref[...],
         kappa_ref[0],
-        ice.astype(jnp.float32),
-        grounded.astype(jnp.float32),
+        ice_ref[...].astype(jnp.float32),
+        grounded_ref[...].astype(jnp.float32),
         surface_ref[...],
         flux_ref[...],
     )
@@ -676,15 +687,12 @@
     for x in range(8):
         out_ref[pl.ds(x, 128, stride=8), :] = done[x]
         means.append(jnp.sum(done[x], axis=0, keepdims=True))
-    free = (code_ref[...] == 0) & (ice == 1)
-    held = free | (code_ref[...] == 2)
-    drag = jnp.where(grounded == 1, friction_ref[...], 0.0) + shelf_drag
-    fields_ref[0] = jnp.where(held, speed_ref[0], 0.0)
-    fields_ref[1] = jnp.where(held, speed_ref[1], 0.0)
-    fields_ref[2] = jnp.where(free, drag, 0.0)
-    fields_ref[3] = thick_ref[...]
-    fields_ref[4] = jnp.exp(jnp.concatenate(means, axis=0) * (-soften / 128.0))
-    fields_ref[5] = height_ref[...]
+    blocks = (below_ref, near_below_ref, mine_ref, near_above_ref, above_ref)
+    for k in range(5):
+        for b, block_ref in enumerate(blocks):
+            row = 40 * k + 8 * b
+            statics_ref[row : row + 8] = block_ref[256 + 8 * k : 264 + 8 * k]
+    statics_ref[200:208] = jnp.exp(jnp.concatenate(means, axis=0) * (-soften / 128.0))
 
 
 def exchanged(low, high, left, right):
@@ -713,69 +721,45 @@
     struct = jax.ShapeDtypeStruct
     smem = pl.BlockSpec(memory_space=pltpu.SMEM)
     vmem = pl.BlockSpec(memory_space=pltpu.VMEM)
-    place = jnp.stack([lax.axis_index(GX), lax.axis_index(GY)]).astype(jnp.int32)
-    grid = jnp.array([lax.axis_size(GX), lax.axis_size(GY)], jnp.int32)
     flat = enthalpy.reshape(1024, 128)
     packed = pl.pallas_call(
         pack_kernel,
-        out_shape=(struct((264, 128), f32),) * 2 + (struct((24, 128), f32),) * 2,
+        out_shape=(struct((304, 128), f32),) * 2 + (struct((24, 128), f32),) * 2,
         name="pack",
-    )(flat, velocity_init)
-    around = exchanged(*packed)
+    )(flat, velocity_init, thickness, surface, friction, ice_mask, grounded, boundary_code)
+    mine = packed[0]
+    near = exchanged(*packed)
     inverses = column_inverses(kappa)
+    columns = (ice_mask, grounded, surface_enthalpy, geo_flux)
     current, *packed, weights = pl.pallas_call(
         first_substep_kernel,
         out_shape=(struct((8, 128, 128), f32),)
-        + (struct((256, 128), f32),) * 2
+        + (struct((296, 128), f32),) * 2
         + (struct((16, 128), f32),) * 2
         + (struct((9, 8, 128), f32),),
-        in_specs=[smem] * 3 + [vmem] * 11,
+        in_specs=[smem] + [vmem] * 11,
         out_specs=(vmem,) * 6,
         name="first_substep",
-    )(
-        place,
-        grid,
-        kappa,
-        flat,
-        velocity_init,
-        *around,
-        inverses,
-        ice_mask,
-        grounded,
-        surface_enthalpy,
-        geo_flux,
-    )
+    )(kappa, flat, velocity_init, *near, inverses, *columns)
     around = exchanged(*packed)
-    current, fields = pl.pallas_call(
+    current, statics = pl.pallas_call(
         second_substep_kernel,
-        out_shape=(struct((1024, 128), f32), struct((6, 8, 128), f32)),
-        in_specs=[smem] * 3 + [vmem] * 16,
+        out_shape=(struct((1024, 128), f32), struct((208, 128), f32)),
+        in_specs=[smem] + [vmem] * 14,
         out_specs=(vmem, vmem),
         name="second_substep",
-    )(
-        place,
-        grid,
-        kappa,
-        current,
-        *around,
-        weights,
-        inverses,
-        ice_mask,
-        grounded,
-        surface_enthalpy,
-        geo_flux,
-        velocity_init,
-        thickness,
-        surface,
-        friction,
-        boundary_code,
-    )
-    quick, worst = momentum(fields, place, grid)
+    )(kappa, current, *around, weights, inverses, *columns, near[0], near[1], mine)
+    quick, worst = momentum(statics)
 
     def plain():
-        free = ((boundary_code == 0) & (ice_mask == 1)).astype(f32)[None]
+        free_cells = (boundary_code == 0) & (ice_mask == 1)
+        held_cells = free_cells | (boundary_code == 2)
+        projector = free_cells.astype(f32)[None]
         drag_term = jnp.where(grounded == 1, friction, 0.0) + shelf_drag
-        return plain_picard(fields[:2], thickness, fields[4], surface, drag_term, free)
+        velocity = jnp.where(held_cells[None], velocity_init, 0.0)
+        return plain_picard(
+            velocity, thickness, statics[200:], surface, drag_term, projector
+        )
 
     velocity = lax.cond(worst[0, 0] > PIVOT_FLOOR, lambda: quick, plain)
     return (current.reshape(enthalpy.shape), velocity)

time: 142 us -> 137 us (0.965)
  blocking collectives: 40.4 us -> 60.5 us
  starting transfers between devices: 53.1 us -> 33 us
  Pallas kernels: 23.5 us -> 20.9 us
  local copies, waits for them, and re-layouts: 5.17 us -> 3.22 us
    ppermute x14 -> x10, starting transfers between devices: 49.3 us -> 29.1 us  [shifted(): lax.ppermute(array, axis, [(i, (i + by) % size) for i in range(size)])]
    all_to_all x0 -> x1, blocking collectives: none -> 15.5 us  [momentum(): lax.all_to_all(jnp.broadcast_to(strip[None], (gx, 8, 256)), GX, 0, 0, til...]
    all_to_all x2, blocking collectives: 28.2 us -> 32 us  [over_all(): part = lax.all_to_all(sums, GY, 0, 0, tiled=True)]
    pallas_call x1, Pallas kernels: 4.7 us -> 3.25 us  [momentum(): pl.pallas_call(second_picard_kernel, out_shape=(struct((2 * KRYLOV, 8, 12...]
    unnamed x42 -> x36, local copies, waits for them, and re-layouts: 3.28 us -> 2.57 us
    ppermute x14 -> x10, waiting for transfers between devices: 7.43 us -> 7.98 us  [shifted(): lax.ppermute(array, axis, [(i, (i + by) % size) for i in range(size)])]
  transfers between devices with their start and end apart: 15 -> 11, of which waited for: 6 -> 7; matrix products, arithmetic and copies ran while one was open for 1% -> 0% of each run, Pallas kernels for 2% -> 2%
where the time goes in v4:
time: 137 us; the launch traced here: 136 us
  blocking collectives  60.5 us (44%)
  starting transfers between devices  33 us (24%)
  Pallas kernels  20.9 us (15%)
  waiting for transfers between devices  16.7 us (12%)
  local copies, waits for them, and re-layouts  3.22 us (2%)
  between operations  1.5 us (1%)
    all_to_all x2, blocking collectives, over_all(): part = lax.all_to_all(sums, GY, 0, 0, tiled=True)  32 us
    ppermute x10, starting transfers between devices, shifted(): lax.ppermute(array, axis, [(i, (i + by) % size) for i in range(size)])  29.1 us
    all_to_all x1, blocking collectives, momentum(): lax.all_to_all(jnp.broadcast_to(strip[None], (gx, 8, 256)), GX, 0, 0, til...  15.5 us
    all_to_all x1, blocking collectives, over_all(): return lax.all_to_all(part, GX, 0, 0, tiled=True)  13 us
    all_to_all x1, waiting for transfers between devices, over_all(): return lax.all_to_all(part, GX, 0, 0, tiled=True)  8.67 us
    ppermute x10, waiting for transfers between devices, shifted(): lax.ppermute(array, axis, [(i, (i + by) % size) for i in range(size)])  7.98 us
    pallas_call x1, Pallas kernels, shards(): pl.pallas_call(first_substep_kernel, out_shape=(struct((8, 128, 128), f32...  4.32 us
    pallas_call x1, Pallas kernels, shards(): pl.pallas_call(second_substep_kernel, out_shape=(struct((1024, 128), f32)...  4 us
  transfers between devices with their start and end apart: 11, of which 7 were waited for; matrix products, arithmetic and copies ran while one was open for 0% of the time, Pallas kernels for 2%

profile of v4, /device:TPU:1, one launch (start us, length us, event | category | flops | bytes accessed | tf_op | source)
XLA Modules:
  0.0 135.9 jit_solution(17727824017902969478)
XLA Ops:
  0.6 2.3 %pack.1 = (f32[304,128]{1,0:T(8,128)}, f32[304,128]{1,0:T(8,128)}, f32[24,128]{1,0:T(8,128)}, f32[24,128]{1,0:T(8,128)}) custom-call(f32[1024,128]{1,0:T(8,128)} %bitcast.81, f32[2,8,128]{2,1,0:T(8,128)} %speed_ref.3, f32[8,128]{1,0:T(8,128)} %thick_ref.1, f32[8,128]{1,0:T(8,128)} %height_ref.1, f32[8,128]{1,0:T(8,128)} %friction_ref.1, s32[8,128]{1,0:T(8,128)} %ice_ref.5, ...), custom_call_target="tpu_custom_call" | custom-call | tf_op jit(solution)/shard_map/pack/pallas_call | solution.py:725
  3.0 8.1 %collective-permute-start.13 = (f32[304,128]{1,0:T(8,128)}, f32[304,128]{1,0:T(8,128)S(1)}, u32[]{:S(2)}, u32[]{:S(2)}) collective-permute-start(f32[304,128]{1,0:T(8,128)} %get-tuple-element.305.mine_ref), channel_id=1, source_target_pairs={{0,496},{16,0},{32,16},{48,32},{64,48},{80,64},{96,80},{112,96},{1... | collective-permute-start | bytes 466952 | tf_op jit(solution)/shard_map/ppermute | solution.py:366
  11.1 1.9 %collective-permute-start.12 = (f32[304,128]{1,0:T(8,128)}, f32[304,128]{1,0:T(8,128)S(1)}, u32[]{:S(2)}, u32[]{:S(2)}) collective-permute-start(f32[304,128]{1,0:T(8,128)} %get-tuple-element.304), channel_id=1, source_target_pairs={{0,16},{16,32},{32,48},{48,64},{64,80},{80,96},{96,112},{112,128},... | collective-permute-start | bytes 466952 | tf_op jit(solution)/shard_map/ppermute | solution.py:366
  13.0 2.9 %collective-permute-start.14 = (f32[24,128]{1,0:T(8,128)}, f32[24,128]{1,0:T(8,128)S(1)}, u32[]{:S(2)}, u32[]{:S(2)}) collective-permute-start(f32[24,128]{1,0:T(8,128)} %get-tuple-element.306), channel_id=1, source_target_pairs={{0,1},{1,2},{2,3},{3,4},{4,5},{5,6},{6,7},{7,8},{8,9},{9,10},{10,1... | collective-permute-start | bytes 36872 | tf_op jit(solution)/shard_map/ppermute | solution.py:366
  16.0 0.0 collective-permute-start.15
  16.0 2.1 %column_inverses.1.inverses_ref = f32[256,128]{1,0:T(8,128)} custom-call(f32[1,129]{1,0:T(1,128)} %bitcast.91), custom_call_target="tpu_custom_call" | custom-call | tf_op jit(solution)/shard_map/column_inverses/pallas_call | solution.py:133
  18.1 0.0 collective-permute-done.14.left_ref
  18.1 1.2 collective-permute-done.15.right_ref
  19.3 0.0 collective-permute-done.13.above_ref.near_above_ref
  19.3 1.8 %collective-permute-done.12.below_ref.near_below_ref = f32[304,128]{1,0:T(8,128)S(1)} collective-permute-done((f32[304,128]{1,0:T(8,128)}, f32[304,128]{1,0:T(8,128)S(1)}, u32[]{:S(2)}, u32[]{:S(2)}) %collective-permute-start.12) | collective-permute-done | bytes 155680 | tf_op jit(solution)/shard_map/ppermute | solution.py:366
  21.1 0.0 copy-done.14
  21.1 0.0 copy-done.15
  21.1 0.0 copy-done
  21.1 0.0 copy-start.1
  21.1 0.6 copy-done.1
  21.8 0.0 copy-done.7
  21.8 4.3 %first_substep.1 = (f32[8,128,128]{2,1,0:T(8,128)}, f32[296,128]{1,0:T(8,128)}, f32[296,128]{1,0:T(8,128)}, f32[16,128]{1,0:T(8,128)}, f32[16,128]{1,0:T(8,128)}, /*index=5*/f32[9,8,128]{2,1,0:T(8,128)}) custom-call(f32[129]{0:T(256)} %kappa_ref.3, f32[1024,128]{1,0:T(8,128)} %bitcast.82, f32[2,8,128]{2,1,0:T(8,128)S(1)} %copy-done.7, f32[304,128]{1,0:T(8,128)} %copy-done.1, ...), custom_call_target="tpu_custom_call" | custom-call | tf_op jit(solution)/shard_map/first_substep/pallas_call | solution.py:734
  26.1 1.9 %collective-permute-start.16 = (f32[296,128]{1,0:T(8,128)}, f32[296,128]{1,0:T(8,128)S(1)}, u32[]{:S(2)}, u32[]{:S(2)}) collective-permute-start(f32[296,128]{1,0:T(8,128)} %get-tuple-element.309), channel_id=1, source_target_pairs={{0,16},{16,32},{32,48},{48,64},{64,80},{80,96},{96,112},{112,128},... | collective-permute-start | bytes 454664 | tf_op jit(solution)/shard_map/ppermute | solution.py:366
  28.0 6.7 %collective-permute-start.17 = (f32[296,128]{1,0:T(8,128)}, f32[296,128]{1,0:T(8,128)S(1)}, u32[]{:S(2)}, u32[]{:S(2)}) collective-permute-start(f32[296,128]{1,0:T(8,128)} %get-tuple-element.310), channel_id=1, source_target_pairs={{0,496},{16,0},{32,16},{48,32},{64,48},{80,64},{96,80},{112,96},{1... | collective-permute-start | bytes 454664 | tf_op jit(solution)/shard_map/ppermute | solution.py:366
  34.7 4.4 %collective-permute-start.18 = (f32[16,128]{1,0:T(8,128)}, f32[16,128]{1,0:T(8,128)S(1)}, u32[]{:S(2)}, u32[]{:S(2)}) collective-permute-start(f32[16,128]{1,0:T(8,128)} %get-tuple-element.311), channel_id=1, source_target_pairs={{0,1},{1,2},{2,3},{3,4},{4,5},{5,6},{6,7},{7,8},{8,9},{9,10},{10,1... | collective-permute-start | bytes 24584 | tf_op jit(solution)/shard_map/ppermute | solution.py:366
  39.1 0.1 collective-permute-start.19
  39.2 0.9 collective-permute-done.18.left_ref
  40.1 2.3 %collective-permute-done.19.right_ref = f32[16,128]{1,0:T(8,128)S(1)} collective-permute-done((f32[16,128]{1,0:T(8,128)}, f32[16,128]{1,0:T(8,128)S(1)}, u32[]{:S(2)}, u32[]{:S(2)}) %collective-permute-start.19) | collective-permute-done | bytes 8224 | tf_op jit(solution)/shard_map/ppermute | solution.py:366
  42.4 0.0 collective-permute-done.16.below_ref
  42.4 0.0 collective-permute-done.17.above_ref
  42.4 0.0 copy-start.3
  42.4 0.0 copy-done.16
  42.4 0.6 copy-done.17
  43.0 0.1 copy-done.2
  43.0 0.1 copy-done.3
  43.1 4.0 %second_substep.1 = (f32[1024,128]{1,0:T(8,128)}, f32[208,128]{1,0:T(8,128)S(1)}) custom-call(f32[129]{0:T(256)} %kappa_ref.3, f32[8,128,128]{2,1,0:T(8,128)} %get-tuple-element.308.enthalpy_ref, f32[296,128]{1,0:T(8,128)} %copy-done.2, f32[296,128]{1,0:T(8,128)} %copy-done.3, f32[16,128]{1,0:T(8,128)} %copy-done.16, f32[16,128]{1,0:T(8,128)} %copy-done.17, ...), custom_call_target="tpu_custom_call" | custom-call | tf_op jit(solution)/shard_map/second_substep/pallas_call | solution.py:745
  47.1 0.1 collective-permute-start.20
  47.2 3.1 %collective-permute-start.21 = (f32[208,128]{1,0:T(8,128)S(1)}, f32[208,128]{1,0:T(8,128)S(1)}, u32[]{:S(2)}, u32[]{:S(2)}) collective-permute-start(f32[208,128]{1,0:T(8,128)S(1)} %get-tuple-element.315.statics_ref), channel_id=1, source_target_pairs={{0,15},{1,0},{2,1},{3,2},{4,3},{5,4},{6,5},{7,6},{8,7},{9,8},{10,9... | collective-permute-start | bytes 319496 | tf_op jit(solution)/shard_map/ppermute | solution.py:366
  50.2 0.8 collective-permute-done.20.left_ref
  51.0 0.9 collective-permute-done.21.right_ref
  52.0 0.6 copy-done.5
  52.6 15.5 %all_to_all.39.stiff_ref = f32[32,8,256]{2,1,0:T(8,128)} all-to-all(f32[32,8,256]{2,1,0:T(8,128)S(1)} %broadcast_in_dim.45), channel_id=1, replica_groups=mesh['gx_0'=4,'gx_1'=8,'gy_0'=8,'gy_1'=2] {'gx_0','gx_1'}, dimensions={0} | all-to-all | bytes 524288 | tf_op jit(solution)/shard_map/all_to_all | solution.py:380
  68.1 3.3 %first_picard.1 = (f32[12,24,256]{2,1,0:T(8,128)}, f32[6,24,256]{2,1,0:T(8,128)}, f32[16,128]{1,0:T(8,128)}) custom-call(f32[208,128]{1,0:T(8,128)S(1)} %get-tuple-element.315.statics_ref, f32[208,128]{1,0:T(8,128)} %copy-done.4, f32[208,128]{1,0:T(8,128)} %copy-done.5, f32[32,8,256]{2,1,0:T(8,128)} %all_to_all.39.stiff_ref), custom_call_target="tpu_custom_call" | custom-call | tf_op jit(solution)/shard_map/first_picard/pallas_call | solution.py:381
  71.4 19.8 %all_to_all.40 = f32[16,1,128]{2,1,0:T(1,128)S(1)} all-to-all(f32[16,1,128]{2,1,0:T(1,128)} %bitcast.93), channel_id=1, replica_groups=mesh['gx_0'=4,'gx_1'=8,'gy_0'=8,'gy_1'=2] {'gy_0','gy_1'}, dimensions={0} | all-to-all | bytes 16384 | tf_op jit(solution)/shard_map/all_to_all | solution.py:359
  91.3 13.0 %all_to_all.41 = f32[32,1,128]{2,1,0:T(1,128)} all-to-all(f32[32,1,128]{2,1,0:T(1,128)S(1)} %broadcast_in_dim.46), channel_id=1, replica_groups=mesh['gx_0'=4,'gx_1'=8,'gy_0'=8,'gy_1'=2] {'gx_0','gx_1'}, dimensions={0} | all-to-all | bytes 32768 | tf_op jit(solution)/shard_map/all_to_all | solution.py:361
  104.3 3.2 %second_picard.1 = (f32[12,8,128]{2,1,0:T(8,128)}, f32[2,8,128]{2,1,0:T(8,128)}, f32[16,128]{1,0:T(8,128)}, f32[8,128]{1,0:T(8,128)}) custom-call(f32[32,128]{1,0:T(8,128)} %bitcast.90, f32[12,24,256]{2,1,0:T(8,128)} %get-tuple-element.317.basis_ref, f32[6,24,256]{2,1,0:T(8,128)} %get-tuple-element.318.fixed_ref), custom_call_target="tpu_custom_call" | custom-call | tf_op jit(solution)/shard_map/second_picard/pallas_call | solution.py:390
  107.5 12.2 %all_to_all.42 = f32[16,1,128]{2,1,0:T(1,128)S(1)} all-to-all(f32[16,1,128]{2,1,0:T(1,128)} %bitcast.92), channel_id=1, replica_groups=mesh['gx_0'=4,'gx_1'=8,'gy_0'=8,'gy_1'=2] {'gy_0','gy_1'}, dimensions={0} | all-to-all | bytes 16384 | tf_op jit(solution)/shard_map/all_to_all | solution.py:359
  119.8 0.6 broadcast_in_dim.47
  120.4 3.8 %all-to-all-start.4 = ((f32[32,1,128]{2,1,0:T(1,128)}), f32[32,1,128]{2,1,0:T(1,128)S(1)}, u32[]{:S(2)}, u32[]{:S(2)}) async-start(f32[32,1,128]{2,1,0:T(1,128)} %broadcast_in_dim.47), calls=%async_computation.4 | async-start | bytes 32768 | tf_op jit(solution)/shard_map/all_to_all | solution.py:361
  124.2 8.7 %all-to-all-done.4 = f32[32,1,128]{2,1,0:T(1,128)S(1)} async-done(((f32[32,1,128]{2,1,0:T(1,128)}), f32[32,1,128]{2,1,0:T(1,128)S(1)}, u32[]{:S(2)}, u32[]{:S(2)}) %all-to-all-start.4) | async-done | bytes 16416 | tf_op jit(solution)/shard_map/all_to_all | solution.py:361
  132.9 0.6 copy-done.11
  133.5 1.6 %last_picard.1 = (f32[2,8,128]{2,1,0:T(8,128)}, f32[1,1]{1,0:T(1,128)}) custom-call(f32[32,128]{1,0:T(8,128)} %bitcast.89, f32[12,8,128]{2,1,0:T(8,128)} %get-tuple-element.320.basis_ref, f32[2,8,128]{2,1,0:T(8,128)} %get-tuple-element.321.velocity_ref, f32[8,128]{1,0:T(8,128)} %get-tuple-element.322.least_ref), custom_call_target="tpu_custom_call" | custom-call | tf_op jit(solution)/shard_map/last_picard/pallas_call | solution.py:400
  135.1 0.0 copy-start.6
  (31 shorter events, 0.2 us)
Async XLA Ops:
  3.0 16.3 %collective-permute-start.13 = (f32[304,128]{1,0:T(8,128)}, f32[304,128]{1,0:T(8,128)S(1)}, u32[]{:S(2)}, u32[]{:S(2)}) collective-permute-start(f32[304,128]{1,0:T(8,128)} %get-tuple-element.305.mine_ref), channel_id=1, source_target_pairs={{0,496},{16,0},{32,16},{48,32},{64,48},{80,64},{96,80},{112,96},{1... | collective-permute-start | bytes 466952 | tf_op jit(solution)/shard_map/ppermute | solution.py:366
  11.1 10.0 %collective-permute-start.12 = (f32[304,128]{1,0:T(8,128)}, f32[304,128]{1,0:T(8,128)S(1)}, u32[]{:S(2)}, u32[]{:S(2)}) collective-permute-start(f32[304,128]{1,0:T(8,128)} %get-tuple-element.304), channel_id=1, source_target_pairs={{0,16},{16,32},{32,48},{48,64},{64,80},{80,96},{96,112},{112,128},... | collective-permute-start | bytes 466952 | tf_op jit(solution)/shard_map/ppermute | solution.py:366
  13.0 5.1 %collective-permute-start.14 = (f32[24,128]{1,0:T(8,128)}, f32[24,128]{1,0:T(8,128)S(1)}, u32[]{:S(2)}, u32[]{:S(2)}) collective-permute-start(f32[24,128]{1,0:T(8,128)} %get-tuple-element.306), channel_id=1, source_target_pairs={{0,1},{1,2},{2,3},{3,4},{4,5},{5,6},{6,7},{7,8},{8,9},{9,10},{10,1... | collective-permute-start | bytes 36872 | tf_op jit(solution)/shard_map/ppermute | solution.py:366
  16.0 3.3 %collective-permute-start.15 = (f32[24,128]{1,0:T(8,128)}, f32[24,128]{1,0:T(8,128)S(1)}, u32[]{:S(2)}, u32[]{:S(2)}) collective-permute-start(f32[24,128]{1,0:T(8,128)} %get-tuple-element.307), channel_id=1, source_target_pairs={{0,15},{1,0},{2,1},{3,2},{4,3},{5,4},{6,5},{7,6},{8,7},{9,8},{10,9... | collective-permute-start | bytes 36872 | tf_op jit(solution)/shard_map/ppermute | solution.py:366
  16.0 5.8 %copy-start.7 = (f32[2,8,128]{2,1,0:T(8,128)S(1)}, f32[2,8,128]{2,1,0:T(8,128)}, u32[]{:S(2)}) copy-start(f32[2,8,128]{2,1,0:T(8,128)} %speed_ref.3) | copy-start | bytes 24580
  16.0 5.8 %copy-start.8 = (s32[8,128]{1,0:T(8,128)S(1)}, s32[8,128]{1,0:T(8,128)}, u32[]{:S(2)}) copy-start(s32[8,128]{1,0:T(8,128)} %grounded_ref.5) | copy-start | bytes 12292
  16.0 5.8 %copy-start.9 = (s32[8,128]{1,0:T(8,128)S(1)}, s32[8,128]{1,0:T(8,128)}, u32[]{:S(2)}) copy-start(s32[8,128]{1,0:T(8,128)} %ice_ref.5) | copy-start | bytes 12292
  18.1 3.1 %copy-start.14 = (f32[24,128]{1,0:T(8,128)}, f32[24,128]{1,0:T(8,128)S(1)}, u32[]{:S(2)}) copy-start(f32[24,128]{1,0:T(8,128)S(1)} %collective-permute-done.14.left_ref) | copy-start | bytes 36868
  19.3 1.8 %copy-start.15 = (f32[24,128]{1,0:T(8,128)}, f32[24,128]{1,0:T(8,128)S(1)}, u32[]{:S(2)}) copy-start(f32[24,128]{1,0:T(8,128)S(1)} %collective-permute-done.15.right_ref) | copy-start | bytes 36868
  19.3 1.8 %copy-start = (f32[304,128]{1,0:T(8,128)}, f32[304,128]{1,0:T(8,128)S(1)}, u32[]{:S(2)}) copy-start(f32[304,128]{1,0:T(8,128)S(1)} %collective-permute-done.13.above_ref.near_above_ref) | copy-start | bytes 466948
  21.1 0.7 copy-start.1
  26.1 16.3 %collective-permute-start.16 = (f32[296,128]{1,0:T(8,128)}, f32[296,128]{1,0:T(8,128)S(1)}, u32[]{:S(2)}, u32[]{:S(2)}) collective-permute-start(f32[296,128]{1,0:T(8,128)} %get-tuple-element.309), channel_id=1, source_target_pairs={{0,16},{16,32},{32,48},{48,64},{64,80},{80,96},{96,112},{112,128},... | collective-permute-start | bytes 454664 | tf_op jit(solution)/shard_map/ppermute | solution.py:366
  28.0 14.4 %collective-permute-start.17 = (f32[296,128]{1,0:T(8,128)}, f32[296,128]{1,0:T(8,128)S(1)}, u32[]{:S(2)}, u32[]{:S(2)}) collective-permute-start(f32[296,128]{1,0:T(8,128)} %get-tuple-element.310), channel_id=1, source_target_pairs={{0,496},{16,0},{32,16},{48,32},{64,48},{80,64},{96,80},{112,96},{1... | collective-permute-start | bytes 454664 | tf_op jit(solution)/shard_map/ppermute | solution.py:366
  34.7 5.4 %collective-permute-start.18 = (f32[16,128]{1,0:T(8,128)}, f32[16,128]{1,0:T(8,128)S(1)}, u32[]{:S(2)}, u32[]{:S(2)}) collective-permute-start(f32[16,128]{1,0:T(8,128)} %get-tuple-element.311), channel_id=1, source_target_pairs={{0,1},{1,2},{2,3},{3,4},{4,5},{5,6},{6,7},{7,8},{8,9},{9,10},{10,1... | collective-permute-start | bytes 24584 | tf_op jit(solution)/shard_map/ppermute | solution.py:366
  39.1 3.3 %collective-permute-start.19 = (f32[16,128]{1,0:T(8,128)}, f32[16,128]{1,0:T(8,128)S(1)}, u32[]{:S(2)}, u32[]{:S(2)}) collective-permute-start(f32[16,128]{1,0:T(8,128)} %get-tuple-element.312), channel_id=1, source_target_pairs={{0,15},{1,0},{2,1},{3,2},{4,3},{5,4},{6,5},{7,6},{8,7},{9,8},{10,9... | collective-permute-start | bytes 24584 | tf_op jit(solution)/shard_map/ppermute | solution.py:366
  40.1 2.3 %copy-start.16 = (f32[16,128]{1,0:T(8,128)}, f32[16,128]{1,0:T(8,128)S(1)}, u32[]{:S(2)}) copy-start(f32[16,128]{1,0:T(8,128)S(1)} %collective-permute-done.18.left_ref) | copy-start | bytes 24580
  42.4 0.6 copy-start.17
  42.4 0.7 copy-start.2
  42.4 0.7 copy-start.3
  47.1 3.9 %collective-permute-start.20 = (f32[208,128]{1,0:T(8,128)S(1)}, f32[208,128]{1,0:T(8,128)S(1)}, u32[]{:S(2)}, u32[]{:S(2)}) collective-permute-start(f32[208,128]{1,0:T(8,128)S(1)} %get-tuple-element.315.statics_ref), channel_id=1, source_target_pairs={{0,1},{1,2},{2,3},{3,4},{4,5},{5,6},{6,7},{7,8},{8,9},{9,10},{10,1... | collective-permute-start | bytes 319496 | tf_op jit(solution)/shard_map/ppermute | solution.py:366
  47.2 4.8 %collective-permute-start.21 = (f32[208,128]{1,0:T(8,128)S(1)}, f32[208,128]{1,0:T(8,128)S(1)}, u32[]{:S(2)}, u32[]{:S(2)}) collective-permute-start(f32[208,128]{1,0:T(8,128)S(1)} %get-tuple-element.315.statics_ref), channel_id=1, source_target_pairs={{0,15},{1,0},{2,1},{3,2},{4,3},{5,4},{6,5},{7,6},{8,7},{9,8},{10,9... | collective-permute-start | bytes 319496 | tf_op jit(solution)/shard_map/ppermute | solution.py:366
  51.0 1.0 copy-start.4
  52.0 0.6 copy-start.5
  120.4 12.5 %all-to-all-start.4 = ((f32[32,1,128]{2,1,0:T(1,128)}), f32[32,1,128]{2,1,0:T(1,128)S(1)}, u32[]{:S(2)}, u32[]{:S(2)}) async-start(f32[32,1,128]{2,1,0:T(1,128)} %broadcast_in_dim.47), calls=%async_computation.4 | async-start | bytes 32768 | tf_op jit(solution)/shard_map/all_to_all | solution.py:361
  132.9 0.6 copy-start.11
  133.5 2.3 %copy-start.10 = (f32[8,128]{1,0:T(8,128)S(1)}, f32[8,128]{1,0:T(8,128)}, u32[]{:S(2)}) copy-start(f32[8,128]{1,0:T(8,128)} %height_ref.1) | copy-start | bytes 12292
  133.5 2.3 %copy-start.12 = (s32[8,128]{1,0:T(8,128)S(1)}, s32[8,128]{1,0:T(8,128)}, u32[]{:S(2)}) copy-start(s32[8,128]{1,0:T(8,128)} %code_ref.1) | copy-start | bytes 12292
  133.5 2.4 %copy-start.13 = (f32[8,128]{1,0:T(8,128)S(1)}, f32[8,128]{1,0:T(8,128)}, u32[]{:S(2)}) copy-start(f32[8,128]{1,0:T(8,128)} %friction_ref.1) | copy-start | bytes 12292
  135.1 0.7 copy-start.6

commit v5 on v4

--- a/solution.py
+++ b/solution.py
@@ -132,9 +132,17 @@
     levels = kappa.shape[0] - 1
     return pl.pallas_call(
         inverse_kernel,
-        out_shape=jax.ShapeDtypeStruct((2 * levels, levels), kappa.dtype),
+        out_shape=kept(2 * levels, levels),
         name="column_inverses",
     )(kappa[None])
+
+
+def on_chip(array):
+    return pltpu.with_memory_space_constraint(array, pltpu.VMEM)
+
+
+def kept(*shape):
+    return pltpu.VMEM(shape, jnp.float32)
 
 
 def next_row(array):
@@ -367,8 +375,6 @@
 
 
 def momentum(statics):
-    f32 = jnp.float32
-    struct = jax.ShapeDtypeStruct
     smem = pl.BlockSpec(memory_space=pltpu.SMEM)
     vmem = pl.BlockSpec(memory_space=pltpu.VMEM)
     gx, gy = (lax.axis_size(GX), lax.axis_size(GY))
@@ -381,28 +387,31 @@
     basis, fixed, sums = pl.pallas_call(
         first_picard_kernel,
         out_shape=(
-            struct((2 * KRYLOV, 24, 256), f32),
-            struct((6, 24, 256), f32),
-            struct((gy, 128), f32),
+            kept(2 * KRYLOV, 24, 256),
+            kept(6, 24, 256),
+            kept(gy, 128),
         ),
         name="first_picard",
-    )(statics, left, right, strip)
+    )(*map(on_chip, (statics, left, right, strip)))
     basis, velocity, sums, least = pl.pallas_call(
         second_picard_kernel,
         out_shape=(
-            struct((2 * KRYLOV, 8, 128), f32),
-            struct((2, 8, 128), f32),
-            struct((gy, 128), f32),
-            struct((8, 128), f32),
+            kept(2 * KRYLOV, 8, 128),
+            kept(2, 8, 128),
+            kept(gy, 128),
+            kept(8, 128),
         ),
         name="second_picard",
-    )(over_all(sums), basis, fixed)
+    )(*map(on_chip, (over_all(sums), basis, fixed)))
     return pl.pallas_call(
         last_kernel,
-        out_shape=(struct((2, 8, 128), f32), struct((1, 1), f32)),
+        out_shape=(
+            jax.ShapeDtypeStruct((2, 8, 128), jnp.float32),
+            jax.ShapeDtypeStruct((1, 1), jnp.float32),
+        ),
         out_specs=(vmem, smem),
         name="last_picard",
-    )(over_all(sums), basis, velocity, least)
+    )(*map(on_chip, (over_all(sums), basis, velocity, least)))
 
 
 def plain_picard(velocity, thickness, stiffness, surface, drag_term, projector):
@@ -665,6 +674,7 @@
     mine_ref,
     out_ref,
     statics_ref,
+    stiff_ref,
 ):
     below, above, left, right = inside(below_ref, above_ref, left_ref, right_ref)
     weights = tuple(weights_ref[k] for k in range(9))
@@ -692,7 +702,9 @@
         for b, block_ref in enumerate(blocks):
             row = 40 * k + 8 * b
             statics_ref[row : row + 8] = block_ref[256 + 8 * k : 264 + 8 * k]
-    statics_ref[200:208] = jnp.exp(jnp.concatenate(means, axis=0) * (-soften / 128.0))
+    stiffness = jnp.exp(jnp.concatenate(means, axis=0) * (-soften / 128.0))
+    statics_ref[200:208] = stiffness
+    stiff_ref[...] = stiffness
 
 
 def exchanged(low, high, left, right):
@@ -718,37 +730,50 @@
     boundary_code,
 ):
     f32 = jnp.float32
-    struct = jax.ShapeDtypeStruct
     smem = pl.BlockSpec(memory_space=pltpu.SMEM)
     vmem = pl.BlockSpec(memory_space=pltpu.VMEM)
     flat = enthalpy.reshape(1024, 128)
     packed = pl.pallas_call(
         pack_kernel,
-        out_shape=(struct((304, 128), f32),) * 2 + (struct((24, 128), f32),) * 2,
+        out_shape=(kept(304, 128),) * 2 + (kept(24, 128),) * 2,
         name="pack",
     )(flat, velocity_init, thickness, surface, friction, ice_mask, grounded, boundary_code)
     mine = packed[0]
-    near = exchanged(*packed)
-    inverses = column_inverses(kappa)
+    near = tuple(map(on_chip, exchanged(*packed)))
+    inverses = on_chip(column_inverses(kappa))
     columns = (ice_mask, grounded, surface_enthalpy, geo_flux)
     current, *packed, weights = pl.pallas_call(
         first_substep_kernel,
-        out_shape=(struct((8, 128, 128), f32),)
-        + (struct((296, 128), f32),) * 2
-        + (struct((16, 128), f32),) * 2
-        + (struct((9, 8, 128), f32),),
+        out_shape=(kept(8, 128, 128),)
+        + (kept(296, 128),) * 2
+        + (kept(16, 128),) * 2
+        + (kept(9, 8, 128),),
         in_specs=[smem] + [vmem] * 11,
         out_specs=(vmem,) * 6,
         name="first_substep",
     )(kappa, flat, velocity_init, *near, inverses, *columns)
-    around = exchanged(*packed)
-    current, statics = pl.pallas_call(
+    around = tuple(map(on_chip, exchanged(*packed)))
+    current, statics, stiffness = pl.pallas_call(
         second_substep_kernel,
-        out_shape=(struct((1024, 128), f32), struct((208, 128), f32)),
+        out_shape=(
+            jax.ShapeDtypeStruct((1024, 128), f32),
+            kept(208, 128),
+            jax.ShapeDtypeStruct((8, 128), f32),
+        ),
         in_specs=[smem] + [vmem] * 14,
-        out_specs=(vmem, vmem),
+        out_specs=(vmem, vmem, vmem),
         name="second_substep",
-    )(kappa, current, *around, weights, inverses, *columns, near[0], near[1], mine)
+    )(
+        kappa,
+        on_chip(current),
+        *around,
+        on_chip(weights),
+        inverses,
+        *columns,
+        near[0],
+        near[1],
+        on_chip(mine),
+    )
     quick, worst = momentum(statics)
 
     def plain():
@@ -758,7 +783,7 @@
         drag_term = jnp.where(grounded == 1, friction, 0.0) + shelf_drag
         velocity = jnp.where(held_cells[None], velocity_init, 0.0)
         return plain_picard(
-            velocity, thickness, statics[200:], surface, drag_term, projector
+            velocity, thickness, stiffness, surface, drag_term, projector
         )
 
     velocity = lax.cond(worst[0, 0] > PIVOT_FLOOR, lambda: quick, plain)

time: 137 us -> 126 us (0.920)
  Pallas kernels: 20.9 us -> 14.1 us
  local copies, waits for them, and re-layouts: 3.22 us -> 0.69 us
    pallas_call x7, Pallas kernels: 20.9 us -> 14.1 us  [the longest x1 3.47 us: shards(): pl.pallas_call(first_substep_kernel, out_shape=(kept(8, 128, 128),) + (ke...]
    unnamed x36 -> x14, local copies, waits for them, and re-layouts: 2.57 us -> 0.04 us
  transfers between devices with their start and end apart: 11 -> 11, of which waited for: 7 -> 7; matrix products, arithmetic and copies ran while one was open for 0% -> 0% of each run, Pallas kernels for 2% -> 1%
where the time goes in v5:
time: 126 us
  blocking collectives  59.6 us (47%)
  starting transfers between devices  32.9 us (26%)
  waiting for transfers between devices  17 us (13%)
  Pallas kernels  14.1 us (11%)
  between operations  1.4 us (1%)
    all_to_all x2, blocking collectives, over_all(): part = lax.all_to_all(sums, GY, 0, 0, tiled=True)  31.3 us
    ppermute x10, starting transfers between devices, shifted(): lax.ppermute(array, axis, [(i, (i + by) % size) for i in range(size)])  29.1 us
    all_to_all x1, blocking collectives, momentum(): lax.all_to_all(jnp.broadcast_to(strip[None], (gx, 8, 256)), GX, 0, 0, til...  15.5 us
    all_to_all x1, blocking collectives, over_all(): return lax.all_to_all(part, GX, 0, 0, tiled=True)  12.8 us
    all_to_all x1, waiting for transfers between devices, over_all(): return lax.all_to_all(part, GX, 0, 0, tiled=True)  8.64 us
    ppermute x10, waiting for transfers between devices, shifted(): lax.ppermute(array, axis, [(i, (i + by) % size) for i in range(size)])  8.32 us
    all_to_all x1, starting transfers between devices, over_all(): return lax.all_to_all(part, GX, 0, 0, tiled=True)  3.84 us
    pallas_call x1, Pallas kernels, shards(): pl.pallas_call(first_substep_kernel, out_shape=(kept(8, 128, 128),) + (ke...  3.47 us
  transfers between devices with their start and end apart: 11, of which 7 were waited for; matrix products, arithmetic and copies ran while one was open for 0% of the time, Pallas kernels for 1%

profile of v5, /device:TPU:1, one launch (start us, length us, event | category | flops | bytes accessed | tf_op | source)
XLA Modules:
  0.0 125.8 jit_solution(7698921046002501431)
XLA Ops:
  0.6 1.7 %pack.1 = (f32[304,128]{1,0:T(8,128)S(1)}, f32[304,128]{1,0:T(8,128)S(1)}, f32[24,128]{1,0:T(8,128)S(1)}, f32[24,128]{1,0:T(8,128)S(1)}) custom-call(f32[1024,128]{1,0:T(8,128)} %bitcast.84, f32[2,8,128]{2,1,0:T(8,128)} %speed_ref.3, f32[8,128]{1,0:T(8,128)} %thick_ref.1, f32[8,128]{1,0:T(8,128)} %height_ref.1, f32[8,128]{1,0:T(8,128)} %friction_ref.1, ...), custom_call_target="tpu_custom_call" | custom-call | tf_op jit(solution)/shard_map/pack/pallas_call | solution.py:736
  2.4 8.1 %collective-permute-start.13 = (f32[304,128]{1,0:T(8,128)S(1)}, f32[304,128]{1,0:T(8,128)S(1)}, u32[]{:S(2)}, u32[]{:S(2)}) collective-permute-start(f32[304,128]{1,0:T(8,128)S(1)} %get-tuple-element.306.mine_ref), channel_id=1, source_target_pairs={{0,496},{16,0},{32,16},{48,32},{64,48},{80,64},{96,80},{112,96},{1... | collective-permute-start | bytes 466952 | tf_op jit(solution)/shard_map/ppermute | solution.py:374
  10.5 1.9 %collective-permute-start.12 = (f32[304,128]{1,0:T(8,128)S(1)}, f32[304,128]{1,0:T(8,128)S(1)}, u32[]{:S(2)}, u32[]{:S(2)}) collective-permute-start(f32[304,128]{1,0:T(8,128)S(1)} %get-tuple-element.305), channel_id=1, source_target_pairs={{0,16},{16,32},{32,48},{48,64},{64,80},{80,96},{96,112},{112,128},... | collective-permute-start | bytes 466952 | tf_op jit(solution)/shard_map/ppermute | solution.py:374
  12.4 2.9 %collective-permute-start.14 = (f32[24,128]{1,0:T(8,128)S(1)}, f32[24,128]{1,0:T(8,128)S(1)}, u32[]{:S(2)}, u32[]{:S(2)}) collective-permute-start(f32[24,128]{1,0:T(8,128)S(1)} %get-tuple-element.307), channel_id=1, source_target_pairs={{0,1},{1,2},{2,3},{3,4},{4,5},{5,6},{6,7},{7,8},{8,9},{9,10},{10,1... | collective-permute-start | bytes 36872 | tf_op jit(solution)/shard_map/ppermute | solution.py:374
  15.4 0.0 collective-permute-start.15
  15.4 0.0 copy-start.1
  15.4 0.0 copy-start.2
  15.4 0.0 copy-start.3
  15.4 1.4 %column_inverses.1.inverses_ref = f32[256,128]{1,0:T(8,128)S(1)} custom-call(f32[1,129]{1,0:T(1,128)} %bitcast.95), custom_call_target="tpu_custom_call" | custom-call | tf_op jit(solution)/shard_map/column_inverses/pallas_call | solution.py:133
  16.8 0.0 collective-permute-done.14.left_ref
  16.8 1.7 %collective-permute-done.15.right_ref = f32[24,128]{1,0:T(8,128)S(1)} collective-permute-done((f32[24,128]{1,0:T(8,128)S(1)}, f32[24,128]{1,0:T(8,128)S(1)}, u32[]{:S(2)}, u32[]{:S(2)}) %collective-permute-start.15) | collective-permute-done | bytes 12320 | tf_op jit(solution)/shard_map/ppermute | solution.py:374
  18.5 0.0 collective-permute-done.13.above_ref.near_above_ref
  18.5 1.8 %collective-permute-done.12.below_ref.near_below_ref = f32[304,128]{1,0:T(8,128)S(1)} collective-permute-done((f32[304,128]{1,0:T(8,128)S(1)}, f32[304,128]{1,0:T(8,128)S(1)}, u32[]{:S(2)}, u32[]{:S(2)}) %collective-permute-start.12) | collective-permute-done | bytes 155680 | tf_op jit(solution)/shard_map/ppermute | solution.py:374
  20.3 0.0 copy-done.1
  20.3 0.0 copy-done.2
  20.4 0.0 copy-done.3
  20.4 3.5 %first_substep.1 = (f32[8,128,128]{2,1,0:T(8,128)S(1)}, f32[296,128]{1,0:T(8,128)S(1)}, f32[296,128]{1,0:T(8,128)S(1)}, f32[16,128]{1,0:T(8,128)S(1)}, f32[16,128]{1,0:T(8,128)S(1)}, /*index=5*/f32[9,8,128]{2,1,0:T(8,128)S(1)}) custom-call(f32[129]{0:T(256)} %kappa_ref.3, f32[1024,128]{1,0:T(8,128)} %bitcast.85, f32[2,8,128]{2,1,0:T(8,128)S(1)} %copy-done.1, ...), custom_call_target="tpu_custom_call" | custom-call | tf_op jit(solution)/shard_map/first_substep/pallas_call | solution.py:745
  23.8 1.9 %collective-permute-start.16 = (f32[296,128]{1,0:T(8,128)S(1)}, f32[296,128]{1,0:T(8,128)S(1)}, u32[]{:S(2)}, u32[]{:S(2)}) collective-permute-start(f32[296,128]{1,0:T(8,128)S(1)} %get-tuple-element.310), channel_id=1, source_target_pairs={{0,16},{16,32},{32,48},{48,64},{64,80},{80,96},{96,112},{112,128},... | collective-permute-start | bytes 454664 | tf_op jit(solution)/shard_map/ppermute | solution.py:374
  25.8 6.7 %collective-permute-start.17 = (f32[296,128]{1,0:T(8,128)S(1)}, f32[296,128]{1,0:T(8,128)S(1)}, u32[]{:S(2)}, u32[]{:S(2)}) collective-permute-start(f32[296,128]{1,0:T(8,128)S(1)} %get-tuple-element.311), channel_id=1, source_target_pairs={{0,496},{16,0},{32,16},{48,32},{64,48},{80,64},{96,80},{112,96},{1... | collective-permute-start | bytes 454664 | tf_op jit(solution)/shard_map/ppermute | solution.py:374
  32.5 4.4 %collective-permute-start.18 = (f32[16,128]{1,0:T(8,128)S(1)}, f32[16,128]{1,0:T(8,128)S(1)}, u32[]{:S(2)}, u32[]{:S(2)}) collective-permute-start(f32[16,128]{1,0:T(8,128)S(1)} %get-tuple-element.312), channel_id=1, source_target_pairs={{0,1},{1,2},{2,3},{3,4},{4,5},{5,6},{6,7},{7,8},{8,9},{9,10},{10,1... | collective-permute-start | bytes 24584 | tf_op jit(solution)/shard_map/ppermute | solution.py:374
  36.8 0.0 collective-permute-start.19
  36.8 0.8 collective-permute-done.18.left_ref
  37.6 2.3 %collective-permute-done.19.right_ref = f32[16,128]{1,0:T(8,128)S(1)} collective-permute-done((f32[16,128]{1,0:T(8,128)S(1)}, f32[16,128]{1,0:T(8,128)S(1)}, u32[]{:S(2)}, u32[]{:S(2)}) %collective-permute-start.19) | collective-permute-done | bytes 8224 | tf_op jit(solution)/shard_map/ppermute | solution.py:374
  39.9 0.0 collective-permute-done.16.below_ref
  39.9 0.0 collective-permute-done.17.above_ref
  39.9 3.4 %second_substep.1 = (f32[1024,128]{1,0:T(8,128)}, f32[208,128]{1,0:T(8,128)S(1)}, f32[8,128]{1,0:T(8,128)S(1)}) custom-call(f32[129]{0:T(256)} %kappa_ref.3, f32[8,128,128]{2,1,0:T(8,128)S(1)} %get-tuple-element.309.enthalpy_ref, f32[296,128]{1,0:T(8,128)S(1)} %collective-permute-done.16.below_ref, f32[296,128]{1,0:T(8,128)S(1)} %collective-permute-done.17.above_ref, ...), custom_call_target="tpu_custom_call" | custom-call | tf_op jit(solution)/shard_map/second_substep/pallas_call | solution.py:756
  43.4 0.1 collective-permute-start.20
  43.4 3.0 %collective-permute-start.21 = (f32[208,128]{1,0:T(8,128)S(1)}, f32[208,128]{1,0:T(8,128)S(1)}, u32[]{:S(2)}, u32[]{:S(2)}) collective-permute-start(f32[208,128]{1,0:T(8,128)S(1)} %get-tuple-element.316.statics_ref), channel_id=1, source_target_pairs={{0,15},{1,0},{2,1},{3,2},{4,3},{5,4},{6,5},{7,6},{8,7},{9,8},{10,9... | collective-permute-start | bytes 319496 | tf_op jit(solution)/shard_map/ppermute | solution.py:374
  46.5 0.8 collective-permute-done.20.left_ref
  47.3 1.0 collective-permute-done.21.right_ref
  48.3 15.5 %all_to_all.39.stiff_ref = f32[32,8,256]{2,1,0:T(8,128)S(1)} all-to-all(f32[32,8,256]{2,1,0:T(8,128)S(1)} %broadcast_in_dim.45), channel_id=1, replica_groups=mesh['gx_0'=4,'gx_1'=8,'gy_0'=8,'gy_1'=2] {'gx_0','gx_1'}, dimensions={0} | all-to-all | bytes 524288 | tf_op jit(solution)/shard_map/all_to_all | solution.py:386
  63.7 1.6 %first_picard.1 = (f32[12,24,256]{2,1,0:T(8,128)S(1)}, f32[6,24,256]{2,1,0:T(8,128)S(1)}, f32[16,128]{1,0:T(8,128)S(1)}) custom-call(f32[208,128]{1,0:T(8,128)S(1)} %get-tuple-element.316.statics_ref, f32[208,128]{1,0:T(8,128)S(1)} %collective-permute-done.20.left_ref, f32[208,128]{1,0:T(8,128)S(1)} %collective-permute-done.21.right_ref, ...), custom_call_target="tpu_custom_call" | custom-call | tf_op jit(solution)/shard_map/first_picard/pallas_call | solution.py:387
  65.4 19.8 %all_to_all.40 = f32[16,1,128]{2,1,0:T(1,128)S(1)} all-to-all(f32[16,1,128]{2,1,0:T(1,128)S(1)} %bitcast.79), channel_id=1, replica_groups=mesh['gx_0'=4,'gx_1'=8,'gy_0'=8,'gy_1'=2] {'gy_0','gy_1'}, dimensions={0} | all-to-all | bytes 16384 | tf_op jit(solution)/shard_map/all_to_all | solution.py:367
  85.2 12.8 %all_to_all.41 = f32[32,1,128]{2,1,0:T(1,128)S(1)} all-to-all(f32[32,1,128]{2,1,0:T(1,128)S(1)} %broadcast_in_dim.46), channel_id=1, replica_groups=mesh['gx_0'=4,'gx_1'=8,'gy_0'=8,'gy_1'=2] {'gx_0','gx_1'}, dimensions={0} | all-to-all | bytes 32768 | tf_op jit(solution)/shard_map/all_to_all | solution.py:369
  98.0 1.6 %second_picard.1 = (f32[12,8,128]{2,1,0:T(8,128)S(1)}, f32[2,8,128]{2,1,0:T(8,128)S(1)}, f32[16,128]{1,0:T(8,128)S(1)}, f32[8,128]{1,0:T(8,128)S(1)}) custom-call(f32[32,128]{1,0:T(8,128)S(1)} %bitcast.78, f32[12,24,256]{2,1,0:T(8,128)S(1)} %get-tuple-element.318.basis_ref, f32[6,24,256]{2,1,0:T(8,128)S(1)} %get-tuple-element.319.fixed_ref), custom_call_target="tpu_custom_call" | custom-call | tf_op jit(solution)/shard_map/second_picard/pallas_call | solution.py:396
  99.6 11.6 %all_to_all.42 = f32[16,1,128]{2,1,0:T(1,128)S(1)} all-to-all(f32[16,1,128]{2,1,0:T(1,128)S(1)} %bitcast.80), channel_id=1, replica_groups=mesh['gx_0'=4,'gx_1'=8,'gy_0'=8,'gy_1'=2] {'gy_0','gy_1'}, dimensions={0} | all-to-all | bytes 16384 | tf_op jit(solution)/shard_map/all_to_all | solution.py:367
  111.2 0.6 broadcast_in_dim.47
  111.8 3.8 %all-to-all-start.4 = ((f32[32,1,128]{2,1,0:T(1,128)}), f32[32,1,128]{2,1,0:T(1,128)S(1)}, u32[]{:S(2)}, u32[]{:S(2)}) async-start(f32[32,1,128]{2,1,0:T(1,128)} %broadcast_in_dim.47), calls=%async_computation.4 | async-start | bytes 32768 | tf_op jit(solution)/shard_map/all_to_all | solution.py:369
  115.7 8.6 %all-to-all-done.4 = f32[32,1,128]{2,1,0:T(1,128)S(1)} async-done(((f32[32,1,128]{2,1,0:T(1,128)}), f32[32,1,128]{2,1,0:T(1,128)S(1)}, u32[]{:S(2)}, u32[]{:S(2)}) %all-to-all-start.4) | async-done | bytes 16416 | tf_op jit(solution)/shard_map/all_to_all | solution.py:369
  124.3 0.0 copy-start.4
  124.3 0.0 copy-start.5
  124.3 0.0 copy-start.6
  124.3 0.8 last_picard.1
  125.1 0.0 copy-start
  125.8 0.0 copy-done.4
  125.8 0.0 copy-done.5
  125.8 0.0 copy-done.6
  125.8 0.0 copy-done
  (9 shorter events, 0.1 us)
Async XLA Ops:
  2.4 16.1 %collective-permute-start.13 = (f32[304,128]{1,0:T(8,128)S(1)}, f32[304,128]{1,0:T(8,128)S(1)}, u32[]{:S(2)}, u32[]{:S(2)}) collective-permute-start(f32[304,128]{1,0:T(8,128)S(1)} %get-tuple-element.306.mine_ref), channel_id=1, source_target_pairs={{0,496},{16,0},{32,16},{48,32},{64,48},{80,64},{96,80},{112,96},{1... | collective-permute-start | bytes 466952 | tf_op jit(solution)/shard_map/ppermute | solution.py:374
  10.5 9.8 %collective-permute-start.12 = (f32[304,128]{1,0:T(8,128)S(1)}, f32[304,128]{1,0:T(8,128)S(1)}, u32[]{:S(2)}, u32[]{:S(2)}) collective-permute-start(f32[304,128]{1,0:T(8,128)S(1)} %get-tuple-element.305), channel_id=1, source_target_pairs={{0,16},{16,32},{32,48},{48,64},{64,80},{80,96},{96,112},{112,128},... | collective-permute-start | bytes 466952 | tf_op jit(solution)/shard_map/ppermute | solution.py:374
  12.4 4.4 %collective-permute-start.14 = (f32[24,128]{1,0:T(8,128)S(1)}, f32[24,128]{1,0:T(8,128)S(1)}, u32[]{:S(2)}, u32[]{:S(2)}) collective-permute-start(f32[24,128]{1,0:T(8,128)S(1)} %get-tuple-element.307), channel_id=1, source_target_pairs={{0,1},{1,2},{2,3},{3,4},{4,5},{5,6},{6,7},{7,8},{8,9},{9,10},{10,1... | collective-permute-start | bytes 36872 | tf_op jit(solution)/shard_map/ppermute | solution.py:374
  15.4 3.1 %collective-permute-start.15 = (f32[24,128]{1,0:T(8,128)S(1)}, f32[24,128]{1,0:T(8,128)S(1)}, u32[]{:S(2)}, u32[]{:S(2)}) collective-permute-start(f32[24,128]{1,0:T(8,128)S(1)} %get-tuple-element.308), channel_id=1, source_target_pairs={{0,15},{1,0},{2,1},{3,2},{4,3},{5,4},{6,5},{7,6},{8,7},{9,8},{10,9... | collective-permute-start | bytes 36872 | tf_op jit(solution)/shard_map/ppermute | solution.py:374
  15.4 5.0 %copy-start.1 = (f32[2,8,128]{2,1,0:T(8,128)S(1)}, f32[2,8,128]{2,1,0:T(8,128)}, u32[]{:S(2)}) copy-start(f32[2,8,128]{2,1,0:T(8,128)} %speed_ref.3) | copy-start | bytes 24580
  15.4 5.0 %copy-start.2 = (s32[8,128]{1,0:T(8,128)S(1)}, s32[8,128]{1,0:T(8,128)}, u32[]{:S(2)}) copy-start(s32[8,128]{1,0:T(8,128)} %grounded_ref.5) | copy-start | bytes 12292
  15.4 5.0 %copy-start.3 = (s32[8,128]{1,0:T(8,128)S(1)}, s32[8,128]{1,0:T(8,128)}, u32[]{:S(2)}) copy-start(s32[8,128]{1,0:T(8,128)} %ice_ref.5) | copy-start | bytes 12292
  23.8 16.1 %collective-permute-start.16 = (f32[296,128]{1,0:T(8,128)S(1)}, f32[296,128]{1,0:T(8,128)S(1)}, u32[]{:S(2)}, u32[]{:S(2)}) collective-permute-start(f32[296,128]{1,0:T(8,128)S(1)} %get-tuple-element.310), channel_id=1, source_target_pairs={{0,16},{16,32},{32,48},{48,64},{64,80},{80,96},{96,112},{112,128},... | collective-permute-start | bytes 454664 | tf_op jit(solution)/shard_map/ppermute | solution.py:374
  25.8 14.1 %collective-permute-start.17 = (f32[296,128]{1,0:T(8,128)S(1)}, f32[296,128]{1,0:T(8,128)S(1)}, u32[]{:S(2)}, u32[]{:S(2)}) collective-permute-start(f32[296,128]{1,0:T(8,128)S(1)} %get-tuple-element.311), channel_id=1, source_target_pairs={{0,496},{16,0},{32,16},{48,32},{64,48},{80,64},{96,80},{112,96},{1... | collective-permute-start | bytes 454664 | tf_op jit(solution)/shard_map/ppermute | solution.py:374
  32.5 5.2 %collective-permute-start.18 = (f32[16,128]{1,0:T(8,128)S(1)}, f32[16,128]{1,0:T(8,128)S(1)}, u32[]{:S(2)}, u32[]{:S(2)}) collective-permute-start(f32[16,128]{1,0:T(8,128)S(1)} %get-tuple-element.312), channel_id=1, source_target_pairs={{0,1},{1,2},{2,3},{3,4},{4,5},{5,6},{6,7},{7,8},{8,9},{9,10},{10,1... | collective-permute-start | bytes 24584 | tf_op jit(solution)/shard_map/ppermute | solution.py:374
  36.8 3.1 %collective-permute-start.19 = (f32[16,128]{1,0:T(8,128)S(1)}, f32[16,128]{1,0:T(8,128)S(1)}, u32[]{:S(2)}, u32[]{:S(2)}) collective-permute-start(f32[16,128]{1,0:T(8,128)S(1)} %get-tuple-element.313), channel_id=1, source_target_pairs={{0,15},{1,0},{2,1},{3,2},{4,3},{5,4},{6,5},{7,6},{8,7},{9,8},{10,9... | collective-permute-start | bytes 24584 | tf_op jit(solution)/shard_map/ppermute | solution.py:374
  43.4 3.9 %collective-permute-start.20 = (f32[208,128]{1,0:T(8,128)S(1)}, f32[208,128]{1,0:T(8,128)S(1)}, u32[]{:S(2)}, u32[]{:S(2)}) collective-permute-start(f32[208,128]{1,0:T(8,128)S(1)} %get-tuple-element.316.statics_ref), channel_id=1, source_target_pairs={{0,1},{1,2},{2,3},{3,4},{4,5},{5,6},{6,7},{7,8},{8,9},{9,10},{10,1... | collective-permute-start | bytes 319496 | tf_op jit(solution)/shard_map/ppermute | solution.py:374
  43.4 4.8 %collective-permute-start.21 = (f32[208,128]{1,0:T(8,128)S(1)}, f32[208,128]{1,0:T(8,128)S(1)}, u32[]{:S(2)}, u32[]{:S(2)}) collective-permute-start(f32[208,128]{1,0:T(8,128)S(1)} %get-tuple-element.316.statics_ref), channel_id=1, source_target_pairs={{0,15},{1,0},{2,1},{3,2},{4,3},{5,4},{6,5},{7,6},{8,7},{9,8},{10,9... | collective-permute-start | bytes 319496 | tf_op jit(solution)/shard_map/ppermute | solution.py:374
  111.8 12.5 %all-to-all-start.4 = ((f32[32,1,128]{2,1,0:T(1,128)}), f32[32,1,128]{2,1,0:T(1,128)S(1)}, u32[]{:S(2)}, u32[]{:S(2)}) async-start(f32[32,1,128]{2,1,0:T(1,128)} %broadcast_in_dim.47), calls=%async_computation.4 | async-start | bytes 32768 | tf_op jit(solution)/shard_map/all_to_all | solution.py:369
  124.3 1.4 %copy-start.4 = (f32[8,128]{1,0:T(8,128)S(1)}, f32[8,128]{1,0:T(8,128)}, u32[]{:S(2)}) copy-start(f32[8,128]{1,0:T(8,128)} %height_ref.1) | copy-start | bytes 12292
  124.3 1.4 %copy-start.5 = (s32[8,128]{1,0:T(8,128)S(1)}, s32[8,128]{1,0:T(8,128)}, u32[]{:S(2)}) copy-start(s32[8,128]{1,0:T(8,128)} %code_ref.1) | copy-start | bytes 12292
  124.3 1.4 %copy-start.6 = (f32[8,128]{1,0:T(8,128)S(1)}, f32[8,128]{1,0:T(8,128)}, u32[]{:S(2)}) copy-start(f32[8,128]{1,0:T(8,128)} %friction_ref.1) | copy-start | bytes 12292
  125.1 0.7 copy-start

commit v6 on v5

--- a/solution.py
+++ b/solution.py
@@ -289,26 +289,23 @@
     return (place[0], place[1], lax.axis_size(GX), lax.axis_size(GY))
 
 
-def first_picard_kernel(statics_ref, left_ref, right_ref, stiff_ref, basis_ref, fixed_ref, sums_ref):
-    gx, gy, gx_size, gy_size = where_am_i()
-    rows = 40
-    lane = lax.broadcasted_iota(jnp.int32, (rows, 128), 1)
-    row = lax.broadcasted_iota(jnp.int32, (rows, 128), 0) + (gx * 8 - OWN)
-    row_in = (row >= 0) & (row < gx_size * 8)
-    from_right = lane < SIDE
-    col = gy + jnp.where(from_right, 1, -1)
-    side_in = row_in & (col >= 0) & (col < gy_size)
-
-    def field(k):
-        part = slice(k * rows, k * rows + rows)
-        side = jnp.where(from_right, right_ref[part], left_ref[part])
-        return jnp.concatenate(
-            [jnp.where(row_in, statics_ref[part], 0.0), jnp.where(side_in, side, 0.0)], axis=1
-        )
-
-    u, v, drag, thick, surface = (field(k) for k in range(5))
-    blocks = [stiff_ref[jnp.clip(gx + k, 0, gx_size - 1)] for k in range(-2, 3)]
-    stiff = jnp.concatenate(blocks, axis=0)
+def first_picard_kernel(
+    mine_ref,
+    left_ref,
+    right_ref,
+    stiff_ref,
+    below_ref,
+    above_ref,
+    basis_ref,
+    fixed_ref,
+    sums_ref,
+):
+    row_in, side_in = inside_grid(40, -OWN)
+    fields = (mine_ref, left_ref, right_ref)
+    u, v, drag, thick, surface = (
+        wide_field(*fields, 16 + 40 * k, row_in, side_in) for k in range(5)
+    )
+    stiff = jnp.concatenate([below_ref[...], stiff_ref[0:8], above_ref[...]], axis=0)
     stiff = jnp.where(jnp.concatenate([row_in, side_in], axis=1), stiff, 0.0)
     t_sum = thick + next_col(thick)
     s_sum = stiff + next_col(stiff)
@@ -374,16 +371,10 @@
     return lax.ppermute(array, axis, [(i, (i + by) % size) for i in range(size)])
 
 
-def momentum(statics):
+def momentum(mine, sides, low, stiff):
     smem = pl.BlockSpec(memory_space=pltpu.SMEM)
     vmem = pl.BlockSpec(memory_space=pltpu.VMEM)
-    gx, gy = (lax.axis_size(GX), lax.axis_size(GY))
-    left = shifted(statics, GY, 1)
-    right = shifted(statics, GY, -1)
-    lane = lax.broadcasted_iota(jnp.int32, (8, 128), 1)
-    side = jnp.where(lane < SIDE, right[200:], left[200:])
-    strip = jnp.concatenate([statics[200:], side], axis=1)
-    strip = lax.all_to_all(jnp.broadcast_to(strip[None], (gx, 8, 256)), GX, 0, 0, tiled=True)
+    gy = lax.axis_size(GY)
     basis, fixed, sums = pl.pallas_call(
         first_picard_kernel,
         out_shape=(
@@ -392,7 +383,7 @@
             kept(gy, 128),
         ),
         name="first_picard",
-    )(*map(on_chip, (statics, left, right, strip)))
+    )(mine, *sides, low, *stiff)
     basis, velocity, sums, least = pl.pallas_call(
         second_picard_kernel,
         out_shape=(
@@ -476,6 +467,8 @@
     ice_ref,
     grounded_ref,
     code_ref,
+    surface_ref,
+    flux_ref,
     low_ref,
     high_ref,
     left_ref,
@@ -492,6 +485,11 @@
         thick_ref[...],
         height_ref[...],
         speed_ref[0],
+        speed_ref[1],
+        ice_ref[...].astype(jnp.float32),
+        grounded_ref[...].astype(jnp.float32),
+        surface_ref[...],
+        flux_ref[...],
     )
     for out_ref, pair in ((low_ref, (0, 1)), (high_ref, (6, 7))):
         out_ref[0:128] = planes[pair[0]]
@@ -606,6 +604,102 @@
     )
 
 
+def sum_weights(inverses_ref):
+    bed = jnp.sum(inverses_ref[0:128], axis=0, keepdims=True) * (1.0 / 128.0)
+    shelf = jnp.sum(inverses_ref[128:256], axis=0, keepdims=True) * (1.0 / 128.0)
+    return (bed, shelf, jnp.full((1, 128), 1.0 / 128.0, jnp.float32))
+
+
+def level_sums(planes, inverses_ref):
+    parts = sum_weights(inverses_ref)
+    sums = jnp.dot(
+        jnp.concatenate(parts + (jnp.zeros((5, 128), jnp.float32),), axis=0),
+        jnp.concatenate(planes, axis=1),
+        precision=lax.Precision.HIGHEST,
+        preferred_element_type=jnp.float32,
+    )
+    rows = [sums[k : k + 1, x * 128 : x * 128 + 128] for k in range(3) for x in range(8)]
+    return jnp.concatenate(rows, axis=0)
+
+
+def gather_kernel(
+    near_below_ref,
+    near_above_ref,
+    mine_ref,
+    below_ref,
+    above_ref,
+    sums_ref,
+    first_ref,
+    last_ref,
+    left_ref,
+    right_ref,
+):
+    left_ref[0:16] = first_ref[...]
+    right_ref[0:16] = last_ref[...]
+    blocks = (below_ref, near_below_ref, mine_ref, near_above_ref, above_ref)
+    pieces = []
+    for k in range(5):
+        pieces += [block_ref[256 + 8 * k : 264 + 8 * k] for block_ref in blocks]
+    for k in range(3):
+        part = slice(296 + 8 * k, 304 + 8 * k)
+        pieces += [block_ref[part] for block_ref in (below_ref, sums_ref, above_ref)]
+    for k in range(6):
+        part = slice(296 + 8 * k, 304 + 8 * k)
+        pieces += [block_ref[part] for block_ref in (near_below_ref, mine_ref, near_above_ref)]
+    for out_ref in (left_ref, right_ref):
+        for k, piece in enumerate(pieces):
+            out_ref[16 + 8 * k : 24 + 8 * k] = piece
+
+
+def inside_grid(rows, first_row):
+    gx, gy, gx_size, gy_size = where_am_i()
+    lane = lax.broadcasted_iota(jnp.int32, (rows, 128), 1)
+    row = lax.broadcasted_iota(jnp.int32, (rows, 128), 0) + (gx * 8 + first_row)
+    row_in = (row >= 0) & (row < gx_size * 8)
+    col = gy + jnp.where(lane < SIDE, 1, -1)
+    return (row_in, row_in & (col >= 0) & (col < gy_size))
+
+
+def wide_field(mine_ref, left_ref, right_ref, start, row_in, side_in):
+    rows = row_in.shape[0]
+    part = slice(start, start + rows)
+    lane = lax.broadcasted_iota(jnp.int32, (rows, 128), 1)
+    side = jnp.where(lane < SIDE, right_ref[part], left_ref[part])
+    return jnp.concatenate(
+        [jnp.where(row_in, mine_ref[part], 0.0), jnp.where(side_in, side, 0.0)], axis=1
+    )
+
+
+def stiffness_kernel(
+    kappa_ref, mine_ref, left_ref, right_ref, inverses_ref, low_ref, high_ref, own_ref
+):
+    where_in = inside_grid(24, -8)
+    take = lambda start: wide_field(mine_ref, left_ref, right_ref, start, *where_in)
+    sums = [take(216 + 24 * k) for k in range(3)]
+    c_x, c_y, ice, bed, heat, flux = (take(288 + 24 * k) for k in range(6))
+    along_x = line_weights(0.5 * (last_row(c_x) + c_x), 0.5 * (c_x + next_row(c_x)))
+    along_y = line_weights(0.5 * (last_col(c_y) + c_y), 0.5 * (c_y + next_col(c_y)))
+    moved = []
+    for e in sums:
+        value = (1.0 + along_x[2] + along_y[2]) * e
+        for axis, line in ((0, along_x), (1, along_y)):
+            size = e.shape[axis]
+            value = value + line[0] * pltpu.roll(e, 2, axis)
+            value = value + line[1] * pltpu.roll(e, 1, axis)
+            value = value + line[3] * pltpu.roll(e, size - 1, axis)
+            value = value + line[4] * pltpu.roll(e, size - 2, axis)
+        moved.append(value)
+    on_bed, on_shelf, _ = sum_weights(inverses_ref)
+    top = kappa_ref[0] * heat
+    grounded = moved[0] + on_bed[:, 0:1] * top + on_bed[:, 127:128] * flux
+    floating = moved[1] + on_shelf[:, 0:1] * top
+    mean = jnp.where(ice > 0.5, jnp.where(bed > 0.5, grounded, floating), moved[2])
+    stiffness = jnp.exp(mean * -soften)
+    low_ref[...] = stiffness[8:24]
+    high_ref[...] = stiffness[0:16]
+    own_ref[...] = stiffness[8:16, :128]
+
+
 def first_substep_kernel(
     kappa_ref,
     enthalpy_ref,
@@ -627,7 +721,7 @@
     weights_ref,
 ):
     below, above, left, right = inside(below_ref, above_ref, left_ref, right_ref)
-    weights = cell_weights(speed_ref, below[296:], above[296:], left[16:], right[16:])
+    weights = cell_weights(speed_ref, below[296:304], above[296:304], left[16:], right[16:])
     for k in range(9):
         weights_ref[k] = weights[k]
     edges = edge_products(weights, left[:16], right[:16])
@@ -650,6 +744,9 @@
     low_ref[0:128] = done[0]
     low_ref[128:256] = done[1]
     low_ref[256:296] = above[256:296]
+    sums = level_sums(done, inverses_ref)
+    low_ref[296:320] = sums
+    high_ref[296:320] = sums
     high_ref[0:128] = done[6]
     high_ref[128:256] = done[7]
     high_ref[256:296] = below[256:296]
@@ -669,14 +766,10 @@
     grounded_ref,
     surface_ref,
     flux_ref,
-    near_below_ref,
-    near_above_ref,
-    mine_ref,
     out_ref,
-    statics_ref,
-    stiff_ref,
 ):
-    below, above, left, right = inside(below_ref, above_ref, left_ref, right_ref)
+    sides = (below_ref.at[0:256], above_ref.at[0:256], left_ref.at[0:16], right_ref.at[0:16])
+    below, above, left, right = inside(*sides)
     weights = tuple(weights_ref[k] for k in range(9))
     edges = edge_products(weights, left, right)
     planes = [below[:128], below[128:256]]
@@ -693,27 +786,12 @@
         surface_ref[...],
         flux_ref[...],
     )
-    means = []
     for x in range(8):
         out_ref[pl.ds(x, 128, stride=8), :] = done[x]
-        means.append(jnp.sum(done[x], axis=0, keepdims=True))
-    blocks = (below_ref, near_below_ref, mine_ref, near_above_ref, above_ref)
-    for k in range(5):
-        for b, block_ref in enumerate(blocks):
-            row = 40 * k + 8 * b
-            statics_ref[row : row + 8] = block_ref[256 + 8 * k : 264 + 8 * k]
-    stiffness = jnp.exp(jnp.concatenate(means, axis=0) * (-soften / 128.0))
-    statics_ref[200:208] = stiffness
-    stiff_ref[...] = stiffness
-
-
-def exchanged(low, high, left, right):
-    return (
-        shifted(high, GX, 1),
-        shifted(low, GX, -1),
-        shifted(right, GY, 1),
-        shifted(left, GY, -1),
-    )
+
+
+def beside(low, high, axis):
+    return (on_chip(shifted(high, axis, 1)), on_chip(shifted(low, axis, -1)))
 
 
 def shards(
@@ -733,48 +811,64 @@
     smem = pl.BlockSpec(memory_space=pltpu.SMEM)
     vmem = pl.BlockSpec(memory_space=pltpu.VMEM)
     flat = enthalpy.reshape(1024, 128)
-    packed = pl.pallas_call(
+    columns = (ice_mask, grounded, surface_enthalpy, geo_flux)
+    mine, high, first, last = pl.pallas_call(
         pack_kernel,
-        out_shape=(kept(304, 128),) * 2 + (kept(24, 128),) * 2,
+        out_shape=(kept(344, 128), kept(344, 128), kept(24, 128), kept(24, 128)),
         name="pack",
-    )(flat, velocity_init, thickness, surface, friction, ice_mask, grounded, boundary_code)
-    mine = packed[0]
-    near = tuple(map(on_chip, exchanged(*packed)))
+    )(
+        flat,
+        velocity_init,
+        thickness,
+        surface,
+        friction,
+        ice_mask,
+        grounded,
+        boundary_code,
+        surface_enthalpy,
+        geo_flux,
+    )
+    near = beside(mine, high, GX)
+    near_sides = beside(first, last, GY)
     inverses = on_chip(column_inverses(kappa))
-    columns = (ice_mask, grounded, surface_enthalpy, geo_flux)
-    current, *packed, weights = pl.pallas_call(
+    current, low, high, first, last, weights = pl.pallas_call(
         first_substep_kernel,
-        out_shape=(kept(8, 128, 128),)
-        + (kept(296, 128),) * 2
-        + (kept(16, 128),) * 2
-        + (kept(9, 8, 128),),
+        out_shape=(
+            kept(8, 128, 128),
+            kept(320, 128),
+            kept(320, 128),
+            kept(16, 128),
+            kept(16, 128),
+            kept(9, 8, 128),
+        ),
         in_specs=[smem] + [vmem] * 11,
         out_specs=(vmem,) * 6,
         name="first_substep",
-    )(kappa, flat, velocity_init, *near, inverses, *columns)
-    around = tuple(map(on_chip, exchanged(*packed)))
-    current, statics, stiffness = pl.pallas_call(
+    )(kappa, flat, velocity_init, *near, *near_sides, inverses, *columns)
+    far = beside(low, high, GX)
+    mine, last = pl.pallas_call(
+        gather_kernel,
+        out_shape=(kept(432, 128), kept(432, 128)),
+        name="gather",
+    )(*near, on_chip(mine), *far, *map(on_chip, (low, first, last)))
+    mine = on_chip(mine)
+    sides = beside(mine, last, GY)
+    low, high, stiffness = pl.pallas_call(
+        stiffness_kernel,
+        out_shape=(kept(16, 256), kept(16, 256), jax.ShapeDtypeStruct((8, 128), f32)),
+        in_specs=[smem] + [vmem] * 4,
+        out_specs=(vmem,) * 3,
+        name="stiffness",
+    )(kappa, mine, *sides, inverses)
+    stiff = beside(low, high, GX)
+    current = pl.pallas_call(
         second_substep_kernel,
-        out_shape=(
-            jax.ShapeDtypeStruct((1024, 128), f32),
-            kept(208, 128),
-            jax.ShapeDtypeStruct((8, 128), f32),
-        ),
-        in_specs=[smem] + [vmem] * 14,
-        out_specs=(vmem, vmem, vmem),
+        out_shape=jax.ShapeDtypeStruct((1024, 128), f32),
+        in_specs=[smem] + [vmem] * 11,
+        out_specs=vmem,
         name="second_substep",
-    )(
-        kappa,
-        on_chip(current),
-        *around,
-        on_chip(weights),
-        inverses,
-        *columns,
-        near[0],
-        near[1],
-        on_chip(mine),
-    )
-    quick, worst = momentum(statics)
+    )(kappa, on_chip(current), *far, *sides, on_chip(weights), inverses, *columns)
+    quick, worst = momentum(mine, sides, on_chip(low), stiff)
 
     def plain():
         free_cells = (boundary_code == 0) & (ice_mask == 1)

time: 126 us -> 121 us (0.960)
  blocking collectives: 59.6 us -> 44.6 us
  starting transfers between devices: 32.9 us -> 37.8 us
  waiting for transfers between devices: 17 us -> 20.6 us
    all_to_all x1 -> x0, blocking collectives: 15.5 us -> none  [momentum(): lax.all_to_all(jnp.broadcast_to(strip[None], (gx, 8, 256)), GX, 0, 0, til...]
    ppermute x10, waiting for transfers between devices: 8.32 us -> 15.2 us  [shifted(): lax.ppermute(array, axis, [(i, (i + by) % size) for i in range(size)])]
    ppermute x10, starting transfers between devices: 29.1 us -> 34 us  [shifted(): lax.ppermute(array, axis, [(i, (i + by) % size) for i in range(size)])]
    all_to_all x1, waiting for transfers between devices: 8.64 us -> 5.37 us  [over_all(): return lax.all_to_all(part, GX, 0, 0, tiled=True)]
    all_to_all x1, blocking collectives: 12.8 us -> 15.5 us  [over_all(): return lax.all_to_all(part, GX, 0, 0, tiled=True)]
    all_to_all x2, blocking collectives: 31.3 us -> 29.2 us  [over_all(): part = lax.all_to_all(sums, GY, 0, 0, tiled=True)]
    pallas_call x3 -> x5, Pallas kernels: 8.66 us -> 9.49 us  [the longest x1 3.52 us: shards(): pl.pallas_call(first_substep_kernel, out_shape=(kept(8, 128, 128), kept(3...]
  transfers between devices with their start and end apart: 11 -> 11, of which waited for: 7 -> 8; matrix products, arithmetic and copies ran while one was open for 0% -> 0% of each run, Pallas kernels for 1% -> 4%
where the time goes in v6:
time: 121 us; the launch traced here: 120 us
  blocking collectives  44.6 us (37%)
  starting transfers between devices  37.8 us (31%)
  waiting for transfers between devices  20.6 us (17%)
  Pallas kernels  14.9 us (12%)
  between operations  1.45 us (1%)
    ppermute x10, starting transfers between devices, shifted(): lax.ppermute(array, axis, [(i, (i + by) % size) for i in range(size)])  34 us
    all_to_all x2, blocking collectives, over_all(): part = lax.all_to_all(sums, GY, 0, 0, tiled=True)  29.2 us
    all_to_all x1, blocking collectives, over_all(): return lax.all_to_all(part, GX, 0, 0, tiled=True)  15.5 us
    ppermute x10, waiting for transfers between devices, shifted(): lax.ppermute(array, axis, [(i, (i + by) % size) for i in range(size)])  15.2 us
    all_to_all x1, waiting for transfers between devices, over_all(): return lax.all_to_all(part, GX, 0, 0, tiled=True)  5.37 us
    all_to_all x1, starting transfers between devices, over_all(): return lax.all_to_all(part, GX, 0, 0, tiled=True)  3.79 us
    pallas_call x1, Pallas kernels, shards(): pl.pallas_call(first_substep_kernel, out_shape=(kept(8, 128, 128), kept(3...  3.52 us
    pallas_call x1, Pallas kernels, shards(): pl.pallas_call(second_substep_kernel, out_shape=jax.ShapeDtypeStruct((102...  3.29 us
  transfers between devices with their start and end apart: 11, of which 8 were waited for; matrix products, arithmetic and copies ran while one was open for 0% of the time, Pallas kernels for 4%

profile of v6, /device:TPU:1, one launch (start us, length us, event | category | flops | bytes accessed | tf_op | source)
XLA Modules:
  0.0 120.1 jit_solution(747850701650826355)
XLA Ops:
  0.6 1.8 %pack.1 = (f32[344,128]{1,0:T(8,128)S(1)}, f32[344,128]{1,0:T(8,128)S(1)}, f32[24,128]{1,0:T(8,128)S(1)}, f32[24,128]{1,0:T(8,128)S(1)}) custom-call(f32[1024,128]{1,0:T(8,128)} %bitcast.84, f32[2,8,128]{2,1,0:T(8,128)} %speed_ref.3, f32[8,128]{1,0:T(8,128)} %thick_ref.1, f32[8,128]{1,0:T(8,128)} %height_ref.1, f32[8,128]{1,0:T(8,128)} %friction_ref.1, ...), custom_call_target="tpu_custom_call" | custom-call | tf_op jit(solution)/shard_map/pack/pallas_call | solution.py:815
  2.4 8.1 %collective-permute-start.13 = (f32[344,128]{1,0:T(8,128)S(1)}, f32[344,128]{1,0:T(8,128)S(1)}, u32[]{:S(2)}, u32[]{:S(2)}) collective-permute-start(f32[344,128]{1,0:T(8,128)S(1)} %get-tuple-element.308.mine_ref), channel_id=1, source_target_pairs={{0,496},{16,0},{32,16},{48,32},{64,48},{80,64},{96,80},{112,96},{1... | collective-permute-start | bytes 528392 | tf_op jit(solution)/shard_map/ppermute | solution.py:371
  10.5 1.9 %collective-permute-start.12 = (f32[344,128]{1,0:T(8,128)S(1)}, f32[344,128]{1,0:T(8,128)S(1)}, u32[]{:S(2)}, u32[]{:S(2)}) collective-permute-start(f32[344,128]{1,0:T(8,128)S(1)} %get-tuple-element.307), channel_id=1, source_target_pairs={{0,16},{16,32},{32,48},{48,64},{64,80},{80,96},{96,112},{112,128},... | collective-permute-start | bytes 528392 | tf_op jit(solution)/shard_map/ppermute | solution.py:371
  12.4 2.9 %collective-permute-start.14 = (f32[24,128]{1,0:T(8,128)S(1)}, f32[24,128]{1,0:T(8,128)S(1)}, u32[]{:S(2)}, u32[]{:S(2)}) collective-permute-start(f32[24,128]{1,0:T(8,128)S(1)} %get-tuple-element.309), channel_id=1, source_target_pairs={{0,1},{1,2},{2,3},{3,4},{4,5},{5,6},{6,7},{7,8},{8,9},{9,10},{10,1... | collective-permute-start | bytes 36872 | tf_op jit(solution)/shard_map/ppermute | solution.py:371
  15.4 0.0 collective-permute-start.15
  15.4 0.0 copy-start.1
  15.4 0.0 copy-start.2
  15.4 0.0 copy-start.3
  15.4 1.4 %column_inverses.1.inverses_ref = f32[256,128]{1,0:T(8,128)S(1)} custom-call(f32[1,129]{1,0:T(1,128)} %bitcast.96), custom_call_target="tpu_custom_call" | custom-call | tf_op jit(solution)/shard_map/column_inverses/pallas_call | solution.py:133
  16.9 0.0 collective-permute-done.14.left_ref
  16.9 1.7 %collective-permute-done.15.right_ref = f32[24,128]{1,0:T(8,128)S(1)} collective-permute-done((f32[24,128]{1,0:T(8,128)S(1)}, f32[24,128]{1,0:T(8,128)S(1)}, u32[]{:S(2)}, u32[]{:S(2)}) %collective-permute-start.15) | collective-permute-done | bytes 12320 | tf_op jit(solution)/shard_map/ppermute | solution.py:371
  18.5 0.0 collective-permute-done.13.above_ref.near_above_ref
  18.5 2.3 %collective-permute-done.12.below_ref.near_below_ref = f32[344,128]{1,0:T(8,128)S(1)} collective-permute-done((f32[344,128]{1,0:T(8,128)S(1)}, f32[344,128]{1,0:T(8,128)S(1)}, u32[]{:S(2)}, u32[]{:S(2)}) %collective-permute-start.12) | collective-permute-done | bytes 176160 | tf_op jit(solution)/shard_map/ppermute | solution.py:371
  20.8 0.0 copy-done.1
  20.8 0.0 copy-done.2
  20.8 0.0 copy-done.3
  20.8 3.5 %first_substep.1 = (f32[8,128,128]{2,1,0:T(8,128)S(1)}, f32[320,128]{1,0:T(8,128)S(1)}, f32[320,128]{1,0:T(8,128)S(1)}, f32[16,128]{1,0:T(8,128)S(1)}, f32[16,128]{1,0:T(8,128)S(1)}, /*index=5*/f32[9,8,128]{2,1,0:T(8,128)S(1)}) custom-call(f32[129]{0:T(256)} %kappa_ref.5, f32[1024,128]{1,0:T(8,128)} %bitcast.85, f32[2,8,128]{2,1,0:T(8,128)S(1)} %copy-done.1, ...), custom_call_target="tpu_custom_call" | custom-call | tf_op jit(solution)/shard_map/first_substep/pallas_call | solution.py:834
  24.3 4.7 %collective-permute-start.17 = (f32[320,128]{1,0:T(8,128)S(1)}, f32[320,128]{1,0:T(8,128)S(1)}, u32[]{:S(2)}, u32[]{:S(2)}) collective-permute-start(f32[320,128]{1,0:T(8,128)S(1)} %get-tuple-element.313.sums_ref), channel_id=1, source_target_pairs={{0,496},{16,0},{32,16},{48,32},{64,48},{80,64},{96,80},{112,96},{1... | collective-permute-start | bytes 491528 | tf_op jit(solution)/shard_map/ppermute | solution.py:371
  29.0 1.9 %collective-permute-start.16 = (f32[320,128]{1,0:T(8,128)S(1)}, f32[320,128]{1,0:T(8,128)S(1)}, u32[]{:S(2)}, u32[]{:S(2)}) collective-permute-start(f32[320,128]{1,0:T(8,128)S(1)} %get-tuple-element.312), channel_id=1, source_target_pairs={{0,16},{16,32},{32,48},{48,64},{64,80},{80,96},{96,112},{112,128},... | collective-permute-start | bytes 491528 | tf_op jit(solution)/shard_map/ppermute | solution.py:371
  31.0 0.3 collective-permute-done.17.above_ref
  31.3 7.1 %collective-permute-done.16.below_ref = f32[320,128]{1,0:T(8,128)S(1)} collective-permute-done((f32[320,128]{1,0:T(8,128)S(1)}, f32[320,128]{1,0:T(8,128)S(1)}, u32[]{:S(2)}, u32[]{:S(2)}) %collective-permute-start.16) | collective-permute-done | bytes 163872 | tf_op jit(solution)/shard_map/ppermute | solution.py:371
  38.4 3.5 %collective-permute-start.18 = (f32[432,128]{1,0:T(8,128)S(1)}, f32[432,128]{1,0:T(8,128)S(1)}, u32[]{:S(2)}, u32[]{:S(2)}) collective-permute-start(f32[432,128]{1,0:T(8,128)S(1)} %get-tuple-element.316), channel_id=1, source_target_pairs={{0,1},{1,2},{2,3},{3,4},{4,5},{5,6},{6,7},{7,8},{8,9},{9,10},{10,1... | collective-permute-start | bytes 663560 | tf_op jit(solution)/shard_map/ppermute | solution.py:371
  41.9 2.4 %collective-permute-start.19 = (f32[432,128]{1,0:T(8,128)S(1)}, f32[432,128]{1,0:T(8,128)S(1)}, u32[]{:S(2)}, u32[]{:S(2)}) collective-permute-start(f32[432,128]{1,0:T(8,128)S(1)} %get-tuple-element.317.mine_ref), channel_id=1, source_target_pairs={{0,15},{1,0},{2,1},{3,2},{4,3},{5,4},{6,5},{7,6},{8,7},{9,8},{10,9... | collective-permute-start | bytes 663560 | tf_op jit(solution)/shard_map/ppermute | solution.py:371
  44.3 0.9 collective-permute-done.18.left_ref
  45.2 2.1 %collective-permute-done.19.right_ref = f32[432,128]{1,0:T(8,128)S(1)} collective-permute-done((f32[432,128]{1,0:T(8,128)S(1)}, f32[432,128]{1,0:T(8,128)S(1)}, u32[]{:S(2)}, u32[]{:S(2)}) %collective-permute-start.19) | collective-permute-done | bytes 221216 | tf_op jit(solution)/shard_map/ppermute | solution.py:371
  47.3 0.9 stiffness.1
  48.1 1.9 %collective-permute-start.20 = (f32[16,256]{1,0:T(8,128)S(1)}, f32[16,256]{1,0:T(8,128)S(1)}, u32[]{:S(2)}, u32[]{:S(2)}) collective-permute-start(f32[16,256]{1,0:T(8,128)S(1)} %get-tuple-element.320), channel_id=1, source_target_pairs={{0,16},{16,32},{32,48},{48,64},{64,80},{80,96},{96,112},{112,128},... | collective-permute-start | bytes 49160 | tf_op jit(solution)/shard_map/ppermute | solution.py:371
  50.1 6.7 %collective-permute-start.21 = (f32[16,256]{1,0:T(8,128)S(1)}, f32[16,256]{1,0:T(8,128)S(1)}, u32[]{:S(2)}, u32[]{:S(2)}) collective-permute-start(f32[16,256]{1,0:T(8,128)S(1)} %get-tuple-element.319.stiff_ref), channel_id=1, source_target_pairs={{0,496},{16,0},{32,16},{48,32},{64,48},{80,64},{96,80},{112,96},{1... | collective-permute-start | bytes 49160 | tf_op jit(solution)/shard_map/ppermute | solution.py:371
  56.8 0.0 collective-permute-done.20.below_ref
  56.8 0.8 collective-permute-done.21.above_ref
  57.6 1.6 %first_picard.1 = (f32[12,24,256]{2,1,0:T(8,128)S(1)}, f32[6,24,256]{2,1,0:T(8,128)S(1)}, f32[16,128]{1,0:T(8,128)S(1)}) custom-call(f32[432,128]{1,0:T(8,128)S(1)} %get-tuple-element.317.mine_ref, f32[432,128]{1,0:T(8,128)S(1)} %collective-permute-done.18.left_ref, f32[432,128]{1,0:T(8,128)S(1)} %collective-permute-done.19.right_ref, ...), custom_call_target="tpu_custom_call" | custom-call | tf_op jit(solution)/shard_map/first_picard/pallas_call | solution.py:378
  59.2 17.6 %all_to_all.34 = f32[16,1,128]{2,1,0:T(1,128)S(1)} all-to-all(f32[16,1,128]{2,1,0:T(1,128)S(1)} %bitcast.79), channel_id=1, replica_groups=mesh['gx_0'=4,'gx_1'=8,'gy_0'=8,'gy_1'=2] {'gy_0','gy_1'}, dimensions={0} | all-to-all | bytes 16384 | tf_op jit(solution)/shard_map/all_to_all | solution.py:364
  76.9 15.5 %all_to_all.35 = f32[32,1,128]{2,1,0:T(1,128)S(1)} all-to-all(f32[32,1,128]{2,1,0:T(1,128)S(1)} %broadcast_in_dim.39), channel_id=1, replica_groups=mesh['gx_0'=4,'gx_1'=8,'gy_0'=8,'gy_1'=2] {'gx_0','gx_1'}, dimensions={0} | all-to-all | bytes 32768 | tf_op jit(solution)/shard_map/all_to_all | solution.py:366
  92.4 1.6 %second_picard.1 = (f32[12,8,128]{2,1,0:T(8,128)S(1)}, f32[2,8,128]{2,1,0:T(8,128)S(1)}, f32[16,128]{1,0:T(8,128)S(1)}, f32[8,128]{1,0:T(8,128)S(1)}) custom-call(f32[32,128]{1,0:T(8,128)S(1)} %bitcast.78, f32[12,24,256]{2,1,0:T(8,128)S(1)} %get-tuple-element.322.basis_ref, f32[6,24,256]{2,1,0:T(8,128)S(1)} %get-tuple-element.323.fixed_ref), custom_call_target="tpu_custom_call" | custom-call | tf_op jit(solution)/shard_map/second_picard/pallas_call | solution.py:387
  94.0 11.6 %all_to_all.36 = f32[16,1,128]{2,1,0:T(1,128)S(1)} all-to-all(f32[16,1,128]{2,1,0:T(1,128)S(1)} %bitcast.80), channel_id=1, replica_groups=mesh['gx_0'=4,'gx_1'=8,'gy_0'=8,'gy_1'=2] {'gy_0','gy_1'}, dimensions={0} | all-to-all | bytes 16384 | tf_op jit(solution)/shard_map/all_to_all | solution.py:364
  105.6 0.6 broadcast_in_dim.40
  106.2 3.8 %all-to-all-start.3 = ((f32[32,1,128]{2,1,0:T(1,128)}), f32[32,1,128]{2,1,0:T(1,128)S(1)}, u32[]{:S(2)}, u32[]{:S(2)}) async-start(f32[32,1,128]{2,1,0:T(1,128)} %broadcast_in_dim.40), calls=%async_computation.3 | async-start | bytes 32768 | tf_op jit(solution)/shard_map/all_to_all | solution.py:366
  110.0 3.3 %second_substep.1 = f32[1024,128]{1,0:T(8,128)} custom-call(f32[129]{0:T(256)} %kappa_ref.5, f32[8,128,128]{2,1,0:T(8,128)S(1)} %get-tuple-element.311.enthalpy_ref, f32[320,128]{1,0:T(8,128)S(1)} %collective-permute-done.16.below_ref, f32[320,128]{1,0:T(8,128)S(1)} %collective-permute-done.17.above_ref, f32[432,128]{1,0:T(8,128)S(1)} %collective-permute-done.18.left_ref, ...), custom_call_target="tpu_custom_call" | custom-call | tf_op jit(solution)/shard_map/second_substep/pallas_call | solution.py:864
  113.3 5.4 %all-to-all-done.3 = f32[32,1,128]{2,1,0:T(1,128)S(1)} async-done(((f32[32,1,128]{2,1,0:T(1,128)}), f32[32,1,128]{2,1,0:T(1,128)S(1)}, u32[]{:S(2)}, u32[]{:S(2)}) %all-to-all-start.3) | async-done | bytes 16416 | tf_op jit(solution)/shard_map/all_to_all | solution.py:366
  118.6 0.0 copy-start.4
  118.6 0.0 copy-start.5
  118.6 0.0 copy-start.6
  118.7 0.8 last_picard.1
  119.4 0.0 copy-start
  120.1 0.0 copy-done.4
  120.1 0.0 copy-done.5
  120.1 0.0 copy-done.6
  120.1 0.0 copy-done
  (5 shorter events, 0.1 us)
Async XLA Ops:
  2.4 16.1 %collective-permute-start.13 = (f32[344,128]{1,0:T(8,128)S(1)}, f32[344,128]{1,0:T(8,128)S(1)}, u32[]{:S(2)}, u32[]{:S(2)}) collective-permute-start(f32[344,128]{1,0:T(8,128)S(1)} %get-tuple-element.308.mine_ref), channel_id=1, source_target_pairs={{0,496},{16,0},{32,16},{48,32},{64,48},{80,64},{96,80},{112,96},{1... | collective-permute-start | bytes 528392 | tf_op jit(solution)/shard_map/ppermute | solution.py:371
  10.5 10.3 %collective-permute-start.12 = (f32[344,128]{1,0:T(8,128)S(1)}, f32[344,128]{1,0:T(8,128)S(1)}, u32[]{:S(2)}, u32[]{:S(2)}) collective-permute-start(f32[344,128]{1,0:T(8,128)S(1)} %get-tuple-element.307), channel_id=1, source_target_pairs={{0,16},{16,32},{32,48},{48,64},{64,80},{80,96},{96,112},{112,128},... | collective-permute-start | bytes 528392 | tf_op jit(solution)/shard_map/ppermute | solution.py:371
  12.4 4.4 %collective-permute-start.14 = (f32[24,128]{1,0:T(8,128)S(1)}, f32[24,128]{1,0:T(8,128)S(1)}, u32[]{:S(2)}, u32[]{:S(2)}) collective-permute-start(f32[24,128]{1,0:T(8,128)S(1)} %get-tuple-element.309), channel_id=1, source_target_pairs={{0,1},{1,2},{2,3},{3,4},{4,5},{5,6},{6,7},{7,8},{8,9},{9,10},{10,1... | collective-permute-start | bytes 36872 | tf_op jit(solution)/shard_map/ppermute | solution.py:371
  15.4 3.1 %collective-permute-start.15 = (f32[24,128]{1,0:T(8,128)S(1)}, f32[24,128]{1,0:T(8,128)S(1)}, u32[]{:S(2)}, u32[]{:S(2)}) collective-permute-start(f32[24,128]{1,0:T(8,128)S(1)} %get-tuple-element.310), channel_id=1, source_target_pairs={{0,15},{1,0},{2,1},{3,2},{4,3},{5,4},{6,5},{7,6},{8,7},{9,8},{10,9... | collective-permute-start | bytes 36872 | tf_op jit(solution)/shard_map/ppermute | solution.py:371
  15.4 5.4 %copy-start.1 = (f32[2,8,128]{2,1,0:T(8,128)S(1)}, f32[2,8,128]{2,1,0:T(8,128)}, u32[]{:S(2)}) copy-start(f32[2,8,128]{2,1,0:T(8,128)} %speed_ref.3) | copy-start | bytes 24580
  15.4 5.4 %copy-start.2 = (s32[8,128]{1,0:T(8,128)S(1)}, s32[8,128]{1,0:T(8,128)}, u32[]{:S(2)}) copy-start(s32[8,128]{1,0:T(8,128)} %grounded_ref.5) | copy-start | bytes 12292
  15.4 5.4 %copy-start.3 = (s32[8,128]{1,0:T(8,128)S(1)}, s32[8,128]{1,0:T(8,128)}, u32[]{:S(2)}) copy-start(s32[8,128]{1,0:T(8,128)} %ice_ref.5) | copy-start | bytes 12292
  24.3 6.9 %collective-permute-start.17 = (f32[320,128]{1,0:T(8,128)S(1)}, f32[320,128]{1,0:T(8,128)S(1)}, u32[]{:S(2)}, u32[]{:S(2)}) collective-permute-start(f32[320,128]{1,0:T(8,128)S(1)} %get-tuple-element.313.sums_ref), channel_id=1, source_target_pairs={{0,496},{16,0},{32,16},{48,32},{64,48},{80,64},{96,80},{112,96},{1... | collective-permute-start | bytes 491528 | tf_op jit(solution)/shard_map/ppermute | solution.py:371
  29.0 9.4 %collective-permute-start.16 = (f32[320,128]{1,0:T(8,128)S(1)}, f32[320,128]{1,0:T(8,128)S(1)}, u32[]{:S(2)}, u32[]{:S(2)}) collective-permute-start(f32[320,128]{1,0:T(8,128)S(1)} %get-tuple-element.312), channel_id=1, source_target_pairs={{0,16},{16,32},{32,48},{48,64},{64,80},{80,96},{96,112},{112,128},... | collective-permute-start | bytes 491528 | tf_op jit(solution)/shard_map/ppermute | solution.py:371
  38.4 6.8 %collective-permute-start.18 = (f32[432,128]{1,0:T(8,128)S(1)}, f32[432,128]{1,0:T(8,128)S(1)}, u32[]{:S(2)}, u32[]{:S(2)}) collective-permute-start(f32[432,128]{1,0:T(8,128)S(1)} %get-tuple-element.316), channel_id=1, source_target_pairs={{0,1},{1,2},{2,3},{3,4},{4,5},{5,6},{6,7},{7,8},{8,9},{9,10},{10,1... | collective-permute-start | bytes 663560 | tf_op jit(solution)/shard_map/ppermute | solution.py:371
  41.9 5.4 %collective-permute-start.19 = (f32[432,128]{1,0:T(8,128)S(1)}, f32[432,128]{1,0:T(8,128)S(1)}, u32[]{:S(2)}, u32[]{:S(2)}) collective-permute-start(f32[432,128]{1,0:T(8,128)S(1)} %get-tuple-element.317.mine_ref), channel_id=1, source_target_pairs={{0,15},{1,0},{2,1},{3,2},{4,3},{5,4},{6,5},{7,6},{8,7},{9,8},{10,9... | collective-permute-start | bytes 663560 | tf_op jit(solution)/shard_map/ppermute | solution.py:371
  48.1 8.6 %collective-permute-start.20 = (f32[16,256]{1,0:T(8,128)S(1)}, f32[16,256]{1,0:T(8,128)S(1)}, u32[]{:S(2)}, u32[]{:S(2)}) collective-permute-start(f32[16,256]{1,0:T(8,128)S(1)} %get-tuple-element.320), channel_id=1, source_target_pairs={{0,16},{16,32},{32,48},{48,64},{64,80},{80,96},{96,112},{112,128},... | collective-permute-start | bytes 49160 | tf_op jit(solution)/shard_map/ppermute | solution.py:371
  50.1 7.5 %collective-permute-start.21 = (f32[16,256]{1,0:T(8,128)S(1)}, f32[16,256]{1,0:T(8,128)S(1)}, u32[]{:S(2)}, u32[]{:S(2)}) collective-permute-start(f32[16,256]{1,0:T(8,128)S(1)} %get-tuple-element.319.stiff_ref), channel_id=1, source_target_pairs={{0,496},{16,0},{32,16},{48,32},{64,48},{80,64},{96,80},{112,96},{1... | collective-permute-start | bytes 49160 | tf_op jit(solution)/shard_map/ppermute | solution.py:371
  106.2 12.5 %all-to-all-start.3 = ((f32[32,1,128]{2,1,0:T(1,128)}), f32[32,1,128]{2,1,0:T(1,128)S(1)}, u32[]{:S(2)}, u32[]{:S(2)}) async-start(f32[32,1,128]{2,1,0:T(1,128)} %broadcast_in_dim.40), calls=%async_computation.3 | async-start | bytes 32768 | tf_op jit(solution)/shard_map/all_to_all | solution.py:366
  118.6 1.4 %copy-start.4 = (f32[8,128]{1,0:T(8,128)S(1)}, f32[8,128]{1,0:T(8,128)}, u32[]{:S(2)}) copy-start(f32[8,128]{1,0:T(8,128)} %height_ref.1) | copy-start | bytes 12292
  118.6 1.5 %copy-start.5 = (s32[8,128]{1,0:T(8,128)S(1)}, s32[8,128]{1,0:T(8,128)}, u32[]{:S(2)}) copy-start(s32[8,128]{1,0:T(8,128)} %code_ref.1) | copy-start | bytes 12292
  118.6 1.5 %copy-start.6 = (f32[8,128]{1,0:T(8,128)S(1)}, f32[8,128]{1,0:T(8,128)}, u32[]{:S(2)}) copy-start(f32[8,128]{1,0:T(8,128)} %friction_ref.1) | copy-start | bytes 12292
  119.4 0.7 copy-start

commit v7 on v6

--- a/solution.py
+++ b/solution.py
@@ -290,23 +290,24 @@
 
 
 def first_picard_kernel(
+    kappa_ref,
     mine_ref,
     left_ref,
     right_ref,
-    stiff_ref,
-    below_ref,
-    above_ref,
+    inverses_ref,
     basis_ref,
     fixed_ref,
     sums_ref,
+    own_ref,
 ):
-    row_in, side_in = inside_grid(40, -OWN)
-    fields = (mine_ref, left_ref, right_ref)
-    u, v, drag, thick, surface = (
-        wide_field(*fields, 16 + 40 * k, row_in, side_in) for k in range(5)
-    )
-    stiff = jnp.concatenate([below_ref[...], stiff_ref[0:8], above_ref[...]], axis=0)
-    stiff = jnp.where(jnp.concatenate([row_in, side_in], axis=1), stiff, 0.0)
+    where_in = inside_grid(40, -OWN)
+    take = lambda k: wide_field(k, mine_ref, left_ref, right_ref, *where_in)
+    u, v, drag, thick, surface = (take(k) for k in range(5))
+    transport = [take(k) for k in range(5, 11)]
+    sums = [take(k) for k in range(11, 14)]
+    stiff = stiffness_of(sums, *transport, kappa_ref[0], inverses_ref)
+    stiff = jnp.where(jnp.concatenate(where_in, axis=1), stiff, 0.0)
+    own_ref[...] = stiff[OWN : OWN + 8, :128]
     t_sum = thick + next_col(thick)
     s_sum = stiff + next_col(stiff)
     corner_product = (1.0 / 64.0) * (t_sum + next_row(t_sum)) * (s_sum + next_row(s_sum))
@@ -371,19 +372,22 @@
     return lax.ppermute(array, axis, [(i, (i + by) % size) for i in range(size)])
 
 
-def momentum(mine, sides, low, stiff):
+def momentum(kappa, mine, sides, inverses):
     smem = pl.BlockSpec(memory_space=pltpu.SMEM)
     vmem = pl.BlockSpec(memory_space=pltpu.VMEM)
     gy = lax.axis_size(GY)
-    basis, fixed, sums = pl.pallas_call(
+    basis, fixed, sums, stiffness = pl.pallas_call(
         first_picard_kernel,
         out_shape=(
             kept(2 * KRYLOV, 24, 256),
             kept(6, 24, 256),
             kept(gy, 128),
+            jax.ShapeDtypeStruct((8, 128), jnp.float32),
         ),
+        in_specs=[smem] + [vmem] * 4,
+        out_specs=(vmem,) * 4,
         name="first_picard",
-    )(mine, *sides, low, *stiff)
+    )(kappa, mine, *sides, inverses)
     basis, velocity, sums, least = pl.pallas_call(
         second_picard_kernel,
         out_shape=(
@@ -394,7 +398,7 @@
         ),
         name="second_picard",
     )(*map(on_chip, (over_all(sums), basis, fixed)))
-    return pl.pallas_call(
+    velocity, worst = pl.pallas_call(
         last_kernel,
         out_shape=(
             jax.ShapeDtypeStruct((2, 8, 128), jnp.float32),
@@ -403,6 +407,7 @@
         out_specs=(vmem, smem),
         name="last_picard",
     )(*map(on_chip, (over_all(sums), basis, velocity, least)))
+    return (velocity, worst, stiffness)
 
 
 def plain_picard(velocity, thickness, stiffness, surface, drag_term, projector):
@@ -473,8 +478,11 @@
     high_ref,
     left_ref,
     right_ref,
+    planes_ref,
 ):
     planes = [enthalpy_ref[pl.ds(x, 128, stride=8), :] for x in range(8)]
+    for x in range(8):
+        planes_ref[x] = planes[x]
     free = (code_ref[...] == 0) & (ice_ref[...] == 1)
     held = free | (code_ref[...] == 2)
     drag = jnp.where(grounded_ref[...] == 1, friction_ref[...], 0.0) + shelf_drag
@@ -625,30 +633,43 @@
 def gather_kernel(
     near_below_ref,
     near_above_ref,
-    mine_ref,
+    own_ref,
     below_ref,
     above_ref,
+    far_below_ref,
+    far_above_ref,
     sums_ref,
     first_ref,
     last_ref,
+    mine_ref,
     left_ref,
     right_ref,
 ):
     left_ref[0:16] = first_ref[...]
     right_ref[0:16] = last_ref[...]
-    blocks = (below_ref, near_below_ref, mine_ref, near_above_ref, above_ref)
-    pieces = []
-    for k in range(5):
-        pieces += [block_ref[256 + 8 * k : 264 + 8 * k] for block_ref in blocks]
+    blocks = (below_ref, near_below_ref, own_ref, near_above_ref, above_ref)
+    fields = []
+    for k in range(11):
+        part = slice(256 + 8 * k, 264 + 8 * k)
+        fields.append(jnp.concatenate([block_ref[part] for block_ref in blocks], axis=0))
     for k in range(3):
-        part = slice(296 + 8 * k, 304 + 8 * k)
-        pieces += [block_ref[part] for block_ref in (below_ref, sums_ref, above_ref)]
-    for k in range(6):
-        part = slice(296 + 8 * k, 304 + 8 * k)
-        pieces += [block_ref[part] for block_ref in (near_below_ref, mine_ref, near_above_ref)]
-    for out_ref in (left_ref, right_ref):
-        for k, piece in enumerate(pieces):
-            out_ref[16 + 8 * k : 24 + 8 * k] = piece
+        end, middle = (slice(8 * k, 8 * k + 8), slice(344 + 8 * k, 352 + 8 * k))
+        pieces = [far_below_ref[end], below_ref[middle], sums_ref[end]]
+        pieces += [above_ref[middle], far_above_ref[end]]
+        fields.append(jnp.concatenate(pieces, axis=0))
+    quarter = lax.broadcasted_iota(jnp.int32, (40, 128), 1) // 32
+    for group in range(4):
+        low, high = (None, None)
+        for k, field in enumerate(fields[4 * group : 4 * group + 4]):
+            mine_ref[(4 * group + k) * 40 : (4 * group + k) * 40 + 40] = field
+            if k == 0:
+                low, high = (field, field)
+            else:
+                low = jnp.where(quarter == k, pltpu.roll(field, 32 * k, 1), low)
+                high = jnp.where(quarter == 3 - k, pltpu.roll(field, 128 - 32 * k, 1), high)
+        part = slice(16 + 40 * group, 56 + 40 * group)
+        left_ref[part] = low
+        right_ref[part] = high
 
 
 def inside_grid(rows, first_row):
@@ -660,23 +681,21 @@
     return (row_in, row_in & (col >= 0) & (col < gy_size))
 
 
-def wide_field(mine_ref, left_ref, right_ref, start, row_in, side_in):
-    rows = row_in.shape[0]
-    part = slice(start, start + rows)
-    lane = lax.broadcasted_iota(jnp.int32, (rows, 128), 1)
-    side = jnp.where(lane < SIDE, right_ref[part], left_ref[part])
+def wide_field(k, mine_ref, left_ref, right_ref, row_in, side_in):
+    part = slice(16 + 40 * (k // 4), 56 + 40 * (k // 4))
+    turn = 32 * (k % 4)
+    right, left = (right_ref[part], left_ref[part])
+    if turn:
+        right, left = (pltpu.roll(right, 128 - turn, 1), pltpu.roll(left, turn, 1))
+    lane = lax.broadcasted_iota(jnp.int32, (40, 128), 1)
+    side = jnp.where(lane < SIDE, right, left)
+    own = mine_ref[40 * k : 40 * k + 40]
     return jnp.concatenate(
-        [jnp.where(row_in, mine_ref[part], 0.0), jnp.where(side_in, side, 0.0)], axis=1
-    )
-
-
-def stiffness_kernel(
-    kappa_ref, mine_ref, left_ref, right_ref, inverses_ref, low_ref, high_ref, own_ref
-):
-    where_in = inside_grid(24, -8)
-    take = lambda start: wide_field(mine_ref, left_ref, right_ref, start, *where_in)
-    sums = [take(216 + 24 * k) for k in range(3)]
-    c_x, c_y, ice, bed, heat, flux = (take(288 + 24 * k) for k in range(6))
+        [jnp.where(row_in, own, 0.0), jnp.where(side_in, side, 0.0)], axis=1
+    )
+
+
+def stiffness_of(sums, c_x, c_y, ice, bed, heat, flux, first_kappa, inverses_ref):
     along_x = line_weights(0.5 * (last_row(c_x) + c_x), 0.5 * (c_x + next_row(c_x)))
     along_y = line_weights(0.5 * (last_col(c_y) + c_y), 0.5 * (c_y + next_col(c_y)))
     moved = []
@@ -690,14 +709,11 @@
             value = value + line[4] * pltpu.roll(e, size - 2, axis)
         moved.append(value)
     on_bed, on_shelf, _ = sum_weights(inverses_ref)
-    top = kappa_ref[0] * heat
+    top = first_kappa * heat
     grounded = moved[0] + on_bed[:, 0:1] * top + on_bed[:, 127:128] * flux
     floating = moved[1] + on_shelf[:, 0:1] * top
     mean = jnp.where(ice > 0.5, jnp.where(bed > 0.5, grounded, floating), moved[2])
-    stiffness = jnp.exp(mean * -soften)
-    low_ref[...] = stiffness[8:24]
-    high_ref[...] = stiffness[0:16]
-    own_ref[...] = stiffness[8:16, :128]
+    return jnp.exp(mean * -soften)
 
 
 def first_substep_kernel(
@@ -719,6 +735,7 @@
     first_ref,
     last_ref,
     weights_ref,
+    sums_ref,
 ):
     below, above, left, right = inside(below_ref, above_ref, left_ref, right_ref)
     weights = cell_weights(speed_ref, below[296:304], above[296:304], left[16:], right[16:])
@@ -726,7 +743,7 @@
         weights_ref[k] = weights[k]
     edges = edge_products(weights, left[:16], right[:16])
     planes = [below[:128], below[128:256]]
-    planes += [enthalpy_ref[pl.ds(x, 128, stride=8), :] for x in range(8)]
+    planes += [enthalpy_ref[x] for x in range(8)]
     planes += [above[:128], above[128:256]]
     done = substep(
         planes,
@@ -743,13 +760,14 @@
         out_ref[x] = done[x]
     low_ref[0:128] = done[0]
     low_ref[128:256] = done[1]
-    low_ref[256:296] = above[256:296]
+    low_ref[256:344] = above[256:344]
     sums = level_sums(done, inverses_ref)
-    low_ref[296:320] = sums
-    high_ref[296:320] = sums
+    low_ref[344:368] = sums
+    high_ref[344:368] = sums
+    sums_ref[...] = sums
     high_ref[0:128] = done[6]
     high_ref[128:256] = done[7]
-    high_ref[256:296] = below[256:296]
+    high_ref[256:344] = below[256:344]
     first_ref[...], last_ref[...] = column_tiles(done)
 
 
@@ -812,9 +830,15 @@
     vmem = pl.BlockSpec(memory_space=pltpu.VMEM)
     flat = enthalpy.reshape(1024, 128)
     columns = (ice_mask, grounded, surface_enthalpy, geo_flux)
-    mine, high, first, last = pl.pallas_call(
+    own, high, first, last, planes = pl.pallas_call(
         pack_kernel,
-        out_shape=(kept(344, 128), kept(344, 128), kept(24, 128), kept(24, 128)),
+        out_shape=(
+            kept(344, 128),
+            kept(344, 128),
+            kept(24, 128),
+            kept(24, 128),
+            kept(8, 128, 128),
+        ),
         name="pack",
     )(
         flat,
@@ -828,47 +852,40 @@
         surface_enthalpy,
         geo_flux,
     )
-    near = beside(mine, high, GX)
+    near = beside(own, high, GX)
     near_sides = beside(first, last, GY)
     inverses = on_chip(column_inverses(kappa))
-    current, low, high, first, last, weights = pl.pallas_call(
+    current, low, high, first, last, weights, sums = pl.pallas_call(
         first_substep_kernel,
         out_shape=(
             kept(8, 128, 128),
-            kept(320, 128),
-            kept(320, 128),
+            kept(368, 128),
+            kept(368, 128),
             kept(16, 128),
             kept(16, 128),
             kept(9, 8, 128),
+            kept(24, 128),
         ),
         in_specs=[smem] + [vmem] * 11,
-        out_specs=(vmem,) * 6,
+        out_specs=(vmem,) * 7,
         name="first_substep",
-    )(kappa, flat, velocity_init, *near, *near_sides, inverses, *columns)
-    far = beside(low, high, GX)
-    mine, last = pl.pallas_call(
+    )(kappa, on_chip(planes), velocity_init, *near, *near_sides, inverses, *columns)
+    around = beside(low, high, GX)
+    far = (on_chip(shifted(sums, GX, 2)), on_chip(shifted(sums, GX, -2)))
+    mine, first, last = pl.pallas_call(
         gather_kernel,
-        out_shape=(kept(432, 128), kept(432, 128)),
+        out_shape=(kept(560, 128), kept(176, 128), kept(176, 128)),
         name="gather",
-    )(*near, on_chip(mine), *far, *map(on_chip, (low, first, last)))
-    mine = on_chip(mine)
-    sides = beside(mine, last, GY)
-    low, high, stiffness = pl.pallas_call(
-        stiffness_kernel,
-        out_shape=(kept(16, 256), kept(16, 256), jax.ShapeDtypeStruct((8, 128), f32)),
-        in_specs=[smem] + [vmem] * 4,
-        out_specs=(vmem,) * 3,
-        name="stiffness",
-    )(kappa, mine, *sides, inverses)
-    stiff = beside(low, high, GX)
+    )(*near, on_chip(own), *around, *far, *map(on_chip, (sums, first, last)))
+    sides = beside(first, last, GY)
     current = pl.pallas_call(
         second_substep_kernel,
         out_shape=jax.ShapeDtypeStruct((1024, 128), f32),
         in_specs=[smem] + [vmem] * 11,
         out_specs=vmem,
         name="second_substep",
-    )(kappa, on_chip(current), *far, *sides, on_chip(weights), inverses, *columns)
-    quick, worst = momentum(mine, sides, on_chip(low), stiff)
+    )(kappa, on_chip(current), *around, *sides, on_chip(weights), inverses, *columns)
+    quick, worst, stiffness = momentum(kappa, on_chip(mine), sides, inverses)
 
     def plain():
         free_cells = (boundary_code == 0) & (ice_mask == 1)

time: 121 us -> 109 us (0.901)
  waiting for transfers between devices: 20.6 us -> 11.4 us
  blocking collectives: 44.6 us -> 40.1 us
  starting transfers between devices: 37.8 us -> 39.7 us
    ppermute x10, waiting for transfers between devices: 15.2 us -> 6.05 us  [shifted(): lax.ppermute(array, axis, [(i, (i + by) % size) for i in range(size)])]
    all_to_all x1, blocking collectives: 15.5 us -> 11.9 us  [over_all(): return lax.all_to_all(part, GX, 0, 0, tiled=True)]
    ppermute x10, starting transfers between devices: 34 us -> 35.9 us  [shifted(): lax.ppermute(array, axis, [(i, (i + by) % size) for i in range(size)])]
  transfers between devices with their start and end apart: 11 -> 11, of which waited for: 8 -> 4; matrix products, arithmetic and copies ran while one was open for 0% -> 0% of each run, Pallas kernels for 4% -> 4%
where the time goes in v7:
time: 109 us; the launch traced here: 108 us
  blocking collectives  40.1 us (37%)
  starting transfers between devices  39.7 us (36%)
  Pallas kernels  15 us (14%)
  waiting for transfers between devices  11.4 us (10%)
  between operations  1.46 us (1%)
    ppermute x10, starting transfers between devices, shifted(): lax.ppermute(array, axis, [(i, (i + by) % size) for i in range(size)])  35.9 us
    all_to_all x2, blocking collectives, over_all(): part = lax.all_to_all(sums, GY, 0, 0, tiled=True)  28.2 us
    all_to_all x1, blocking collectives, over_all(): return lax.all_to_all(part, GX, 0, 0, tiled=True)  11.9 us
    ppermute x10, waiting for transfers between devices, shifted(): lax.ppermute(array, axis, [(i, (i + by) % size) for i in range(size)])  6.05 us
    all_to_all x1, waiting for transfers between devices, over_all(): return lax.all_to_all(part, GX, 0, 0, tiled=True)  5.35 us
    all_to_all x1, starting transfers between devices, over_all(): return lax.all_to_all(part, GX, 0, 0, tiled=True)  3.84 us
    pallas_call x1, Pallas kernels, shards(): pl.pallas_call(second_substep_kernel, out_shape=jax.ShapeDtypeStruct((102...  3.29 us
    pallas_call x1, Pallas kernels, shards(): pl.pallas_call(first_substep_kernel, out_shape=(kept(8, 128, 128), kept(3...  3.24 us
  transfers between devices with their start and end apart: 11, of which 4 were waited for; matrix products, arithmetic and copies ran while one was open for 0% of the time, Pallas kernels for 4%

profile of v7, /device:TPU:1, one launch (start us, length us, event | category | flops | bytes accessed | tf_op | source)
XLA Modules:
  0.0 108.4 jit_solution(6931211701226937235)
XLA Ops:
  0.6 1.8 %pack.1 = (f32[344,128]{1,0:T(8,128)S(1)}, f32[344,128]{1,0:T(8,128)S(1)}, f32[24,128]{1,0:T(8,128)S(1)}, f32[24,128]{1,0:T(8,128)S(1)}, f32[8,128,128]{2,1,0:T(8,128)S(1)}) custom-call(f32[1024,128]{1,0:T(8,128)} %bitcast.85, f32[2,8,128]{2,1,0:T(8,128)} %speed_ref.3, f32[8,128]{1,0:T(8,128)} %thick_ref.1, f32[8,128]{1,0:T(8,128)} %height_ref.1, ...), custom_call_target="tpu_custom_call" | custom-call | tf_op jit(solution)/shard_map/pack/pallas_call | solution.py:833
  2.4 4.0 %collective-permute-start.12 = (f32[344,128]{1,0:T(8,128)S(1)}, f32[344,128]{1,0:T(8,128)S(1)}, u32[]{:S(2)}, u32[]{:S(2)}) collective-permute-start(f32[344,128]{1,0:T(8,128)S(1)} %get-tuple-element.309), channel_id=1, source_target_pairs={{0,16},{16,32},{32,48},{48,64},{64,80},{80,96},{96,112},{112,128},... | collective-permute-start | bytes 528392 | tf_op jit(solution)/shard_map/ppermute | solution.py:372
  6.5 6.0 %collective-permute-start.13 = (f32[344,128]{1,0:T(8,128)S(1)}, f32[344,128]{1,0:T(8,128)S(1)}, u32[]{:S(2)}, u32[]{:S(2)}) collective-permute-start(f32[344,128]{1,0:T(8,128)S(1)} %get-tuple-element.310.own_ref), channel_id=1, source_target_pairs={{0,496},{16,0},{32,16},{48,32},{64,48},{80,64},{96,80},{112,96},{1... | collective-permute-start | bytes 528392 | tf_op jit(solution)/shard_map/ppermute | solution.py:372
  12.5 2.9 %collective-permute-start.14 = (f32[24,128]{1,0:T(8,128)S(1)}, f32[24,128]{1,0:T(8,128)S(1)}, u32[]{:S(2)}, u32[]{:S(2)}) collective-permute-start(f32[24,128]{1,0:T(8,128)S(1)} %get-tuple-element.311), channel_id=1, source_target_pairs={{0,1},{1,2},{2,3},{3,4},{4,5},{5,6},{6,7},{7,8},{8,9},{9,10},{10,1... | collective-permute-start | bytes 36872 | tf_op jit(solution)/shard_map/ppermute | solution.py:372
  15.4 3.1 %collective-permute-start.15 = (f32[24,128]{1,0:T(8,128)S(1)}, f32[24,128]{1,0:T(8,128)S(1)}, u32[]{:S(2)}, u32[]{:S(2)}) collective-permute-start(f32[24,128]{1,0:T(8,128)S(1)} %get-tuple-element.312), channel_id=1, source_target_pairs={{0,15},{1,0},{2,1},{3,2},{4,3},{5,4},{6,5},{7,6},{8,7},{9,8},{10,9... | collective-permute-start | bytes 36872 | tf_op jit(solution)/shard_map/ppermute | solution.py:372
  18.5 0.0 copy-start.1
  18.5 0.0 copy-start.2
  18.5 0.0 copy-start.3
  18.5 1.4 %column_inverses.1.inverses_ref = f32[256,128]{1,0:T(8,128)S(1)} custom-call(f32[1,129]{1,0:T(1,128)} %bitcast.95), custom_call_target="tpu_custom_call" | custom-call | tf_op jit(solution)/shard_map/column_inverses/pallas_call | solution.py:133
  19.9 0.0 collective-permute-done.14.left_ref
  19.9 0.0 collective-permute-done.15.right_ref
  20.0 0.0 collective-permute-done.12.below_ref.near_below_ref
  20.0 0.0 collective-permute-done.13.above_ref.near_above_ref
  20.0 0.0 copy-done.1
  20.0 0.0 copy-done.2
  20.0 0.0 copy-done.3
  20.0 3.2 %first_substep.1 = (f32[8,128,128]{2,1,0:T(8,128)S(1)}, f32[368,128]{1,0:T(8,128)S(1)}, f32[368,128]{1,0:T(8,128)S(1)}, f32[16,128]{1,0:T(8,128)S(1)}, f32[16,12...) custom-call(f32[129]{0:T(256)} %kappa_ref.5, f32[8,128,128]{2,1,0:T(8,128)S(1)} %get-tuple-element.308.enthalpy_ref, ...), custom_call_target="tpu_custom_call" | custom-call | tf_op jit(solution)/shard_map/first_substep/pallas_call | solution.py:858
  23.2 1.9 %collective-permute-start.16 = (f32[368,128]{1,0:T(8,128)S(1)}, f32[368,128]{1,0:T(8,128)S(1)}, u32[]{:S(2)}, u32[]{:S(2)}) collective-permute-start(f32[368,128]{1,0:T(8,128)S(1)} %get-tuple-element.314), channel_id=1, source_target_pairs={{0,16},{16,32},{32,48},{48,64},{64,80},{80,96},{96,112},{112,128},... | collective-permute-start | bytes 565256 | tf_op jit(solution)/shard_map/ppermute | solution.py:372
  25.2 6.7 %collective-permute-start.17 = (f32[368,128]{1,0:T(8,128)S(1)}, f32[368,128]{1,0:T(8,128)S(1)}, u32[]{:S(2)}, u32[]{:S(2)}) collective-permute-start(f32[368,128]{1,0:T(8,128)S(1)} %get-tuple-element.315), channel_id=1, source_target_pairs={{0,496},{16,0},{32,16},{48,32},{64,48},{80,64},{96,80},{112,96},{1... | collective-permute-start | bytes 565256 | tf_op jit(solution)/shard_map/ppermute | solution.py:372
  31.9 1.9 %collective-permute-start.19 = (f32[24,128]{1,0:T(8,128)S(1)}, f32[24,128]{1,0:T(8,128)S(1)}, u32[]{:S(2)}, u32[]{:S(2)}) collective-permute-start(f32[24,128]{1,0:T(8,128)S(1)} %get-tuple-element.316.sums_ref), channel_id=1, source_target_pairs={{0,480},{16,496},{32,0},{48,16},{64,32},{80,48},{96,64},{112,80},{... | collective-permute-start | bytes 36872 | tf_op jit(solution)/shard_map/ppermute | solution.py:372
  33.8 4.3 %collective-permute-start.18 = (f32[24,128]{1,0:T(8,128)S(1)}, f32[24,128]{1,0:T(8,128)S(1)}, u32[]{:S(2)}, u32[]{:S(2)}) collective-permute-start(f32[24,128]{1,0:T(8,128)S(1)} %get-tuple-element.316.sums_ref), channel_id=1, source_target_pairs={{0,32},{16,48},{32,64},{48,80},{64,96},{80,112},{96,128},{112,144}... | collective-permute-start | bytes 36872 | tf_op jit(solution)/shard_map/ppermute | solution.py:372
  38.1 0.0 collective-permute-done.19.far_above_ref
  38.1 4.4 %collective-permute-done.18.far_below_ref = f32[24,128]{1,0:T(8,128)S(1)} collective-permute-done((f32[24,128]{1,0:T(8,128)S(1)}, f32[24,128]{1,0:T(8,128)S(1)}, u32[]{:S(2)}, u32[]{:S(2)}) %collective-permute-start.18) | collective-permute-done | bytes 12320 | tf_op jit(solution)/shard_map/ppermute | solution.py:372
  42.5 0.0 collective-permute-done.16.below_ref
  42.5 0.0 collective-permute-done.17.above_ref
  42.5 0.2 gather.1
  42.6 2.7 %collective-permute-start.20 = (f32[176,128]{1,0:T(8,128)S(1)}, f32[176,128]{1,0:T(8,128)S(1)}, u32[]{:S(2)}, u32[]{:S(2)}) collective-permute-start(f32[176,128]{1,0:T(8,128)S(1)} %get-tuple-element.319), channel_id=1, source_target_pairs={{0,1},{1,2},{2,3},{3,4},{4,5},{5,6},{6,7},{7,8},{8,9},{9,10},{10,1... | collective-permute-start | bytes 270344 | tf_op jit(solution)/shard_map/ppermute | solution.py:372
  45.4 2.3 %collective-permute-start.21 = (f32[176,128]{1,0:T(8,128)S(1)}, f32[176,128]{1,0:T(8,128)S(1)}, u32[]{:S(2)}, u32[]{:S(2)}) collective-permute-start(f32[176,128]{1,0:T(8,128)S(1)} %get-tuple-element.320), channel_id=1, source_target_pairs={{0,15},{1,0},{2,1},{3,2},{4,3},{5,4},{6,5},{7,6},{8,7},{9,8},{10,9... | collective-permute-start | bytes 270344 | tf_op jit(solution)/shard_map/ppermute | solution.py:372
  47.7 0.8 collective-permute-done.20.left_ref
  48.4 0.9 collective-permute-done.21.right_ref
  49.3 2.7 %first_picard.1 = (f32[12,24,256]{2,1,0:T(8,128)S(1)}, f32[6,24,256]{2,1,0:T(8,128)S(1)}, f32[16,128]{1,0:T(8,128)S(1)}, f32[8,128]{1,0:T(8,128)S(1)}) custom-call(f32[129]{0:T(256)} %kappa_ref.5, f32[560,128]{1,0:T(8,128)S(1)} %get-tuple-element.322.mine_ref, f32[176,128]{1,0:T(8,128)S(1)} %collective-permute-done.20.left_ref, ...), custom_call_target="tpu_custom_call" | custom-call | tf_op jit(solution)/shard_map/first_picard/pallas_call | solution.py:379
  52.1 16.7 %all_to_all.34 = f32[16,1,128]{2,1,0:T(1,128)S(1)} all-to-all(f32[16,1,128]{2,1,0:T(1,128)S(1)} %bitcast.80), channel_id=1, replica_groups=mesh['gx_0'=4,'gx_1'=8,'gy_0'=8,'gy_1'=2] {'gy_0','gy_1'}, dimensions={0} | all-to-all | bytes 16384 | tf_op jit(solution)/shard_map/all_to_all | solution.py:365
  68.8 11.9 %all_to_all.35 = f32[32,1,128]{2,1,0:T(1,128)S(1)} all-to-all(f32[32,1,128]{2,1,0:T(1,128)S(1)} %broadcast_in_dim.39), channel_id=1, replica_groups=mesh['gx_0'=4,'gx_1'=8,'gy_0'=8,'gy_1'=2] {'gx_0','gx_1'}, dimensions={0} | all-to-all | bytes 32768 | tf_op jit(solution)/shard_map/all_to_all | solution.py:367
  80.6 1.6 %second_picard.1 = (f32[12,8,128]{2,1,0:T(8,128)S(1)}, f32[2,8,128]{2,1,0:T(8,128)S(1)}, f32[16,128]{1,0:T(8,128)S(1)}, f32[8,128]{1,0:T(8,128)S(1)}) custom-call(f32[32,128]{1,0:T(8,128)S(1)} %bitcast.78, f32[12,24,256]{2,1,0:T(8,128)S(1)} %get-tuple-element.324.basis_ref, f32[6,24,256]{2,1,0:T(8,128)S(1)} %get-tuple-element.325.fixed_ref), custom_call_target="tpu_custom_call" | custom-call | tf_op jit(solution)/shard_map/second_picard/pallas_call | solution.py:391
  82.2 11.6 %all_to_all.36 = f32[16,1,128]{2,1,0:T(1,128)S(1)} all-to-all(f32[16,1,128]{2,1,0:T(1,128)S(1)} %bitcast.79), channel_id=1, replica_groups=mesh['gx_0'=4,'gx_1'=8,'gy_0'=8,'gy_1'=2] {'gy_0','gy_1'}, dimensions={0} | all-to-all | bytes 16384 | tf_op jit(solution)/shard_map/all_to_all | solution.py:365
  93.8 0.6 broadcast_in_dim.40
  94.5 3.8 %all-to-all-start.3 = ((f32[32,1,128]{2,1,0:T(1,128)}), f32[32,1,128]{2,1,0:T(1,128)S(1)}, u32[]{:S(2)}, u32[]{:S(2)}) async-start(f32[32,1,128]{2,1,0:T(1,128)} %broadcast_in_dim.40), calls=%async_computation.3 | async-start | bytes 32768 | tf_op jit(solution)/shard_map/all_to_all | solution.py:367
  98.3 3.3 %second_substep.1 = f32[1024,128]{1,0:T(8,128)} custom-call(f32[129]{0:T(256)} %kappa_ref.5, f32[8,128,128]{2,1,0:T(8,128)S(1)} %get-tuple-element.313.enthalpy_ref, f32[368,128]{1,0:T(8,128)S(1)} %collective-permute-done.16.below_ref, f32[368,128]{1,0:T(8,128)S(1)} %collective-permute-done.17.above_ref, f32[176,128]{1,0:T(8,128)S(1)} %collective-permute-done.20.left_ref, ...), custom_call_target="tpu_custom_call" | custom-call | tf_op jit(solution)/shard_map/second_substep/pallas_call | solution.py:881
  101.6 5.4 %all-to-all-done.3 = f32[32,1,128]{2,1,0:T(1,128)S(1)} async-done(((f32[32,1,128]{2,1,0:T(1,128)}), f32[32,1,128]{2,1,0:T(1,128)S(1)}, u32[]{:S(2)}, u32[]{:S(2)}) %all-to-all-start.3) | async-done | bytes 16416 | tf_op jit(solution)/shard_map/all_to_all | solution.py:367
  106.9 0.0 copy-start.4
  107.0 0.0 copy-start.5
  107.0 0.0 copy-start.6
  107.0 0.8 last_picard.1
  107.7 0.0 copy-start
  108.4 0.0 copy-done.4
  108.4 0.0 copy-done.5
  108.4 0.0 copy-done.6
  108.4 0.0 copy-done
  (4 shorter events, 0.1 us)
Async XLA Ops:
  2.4 17.5 %collective-permute-start.12 = (f32[344,128]{1,0:T(8,128)S(1)}, f32[344,128]{1,0:T(8,128)S(1)}, u32[]{:S(2)}, u32[]{:S(2)}) collective-permute-start(f32[344,128]{1,0:T(8,128)S(1)} %get-tuple-element.309), channel_id=1, source_target_pairs={{0,16},{16,32},{32,48},{48,64},{64,80},{80,96},{96,112},{112,128},... | collective-permute-start | bytes 528392 | tf_op jit(solution)/shard_map/ppermute | solution.py:372
  6.5 13.5 %collective-permute-start.13 = (f32[344,128]{1,0:T(8,128)S(1)}, f32[344,128]{1,0:T(8,128)S(1)}, u32[]{:S(2)}, u32[]{:S(2)}) collective-permute-start(f32[344,128]{1,0:T(8,128)S(1)} %get-tuple-element.310.own_ref), channel_id=1, source_target_pairs={{0,496},{16,0},{32,16},{48,32},{64,48},{80,64},{96,80},{112,96},{1... | collective-permute-start | bytes 528392 | tf_op jit(solution)/shard_map/ppermute | solution.py:372
  12.5 7.5 %collective-permute-start.14 = (f32[24,128]{1,0:T(8,128)S(1)}, f32[24,128]{1,0:T(8,128)S(1)}, u32[]{:S(2)}, u32[]{:S(2)}) collective-permute-start(f32[24,128]{1,0:T(8,128)S(1)} %get-tuple-element.311), channel_id=1, source_target_pairs={{0,1},{1,2},{2,3},{3,4},{4,5},{5,6},{6,7},{7,8},{8,9},{9,10},{10,1... | collective-permute-start | bytes 36872 | tf_op jit(solution)/shard_map/ppermute | solution.py:372
  15.4 4.5 %collective-permute-start.15 = (f32[24,128]{1,0:T(8,128)S(1)}, f32[24,128]{1,0:T(8,128)S(1)}, u32[]{:S(2)}, u32[]{:S(2)}) collective-permute-start(f32[24,128]{1,0:T(8,128)S(1)} %get-tuple-element.312), channel_id=1, source_target_pairs={{0,15},{1,0},{2,1},{3,2},{4,3},{5,4},{6,5},{7,6},{8,7},{9,8},{10,9... | collective-permute-start | bytes 36872 | tf_op jit(solution)/shard_map/ppermute | solution.py:372
  18.5 1.5 %copy-start.1 = (f32[2,8,128]{2,1,0:T(8,128)S(1)}, f32[2,8,128]{2,1,0:T(8,128)}, u32[]{:S(2)}) copy-start(f32[2,8,128]{2,1,0:T(8,128)} %speed_ref.3) | copy-start | bytes 24580
  18.5 1.5 %copy-start.2 = (s32[8,128]{1,0:T(8,128)S(1)}, s32[8,128]{1,0:T(8,128)}, u32[]{:S(2)}) copy-start(s32[8,128]{1,0:T(8,128)} %grounded_ref.5) | copy-start | bytes 12292
  18.5 1.5 %copy-start.3 = (s32[8,128]{1,0:T(8,128)S(1)}, s32[8,128]{1,0:T(8,128)}, u32[]{:S(2)}) copy-start(s32[8,128]{1,0:T(8,128)} %ice_ref.5) | copy-start | bytes 12292
  23.2 19.2 %collective-permute-start.16 = (f32[368,128]{1,0:T(8,128)S(1)}, f32[368,128]{1,0:T(8,128)S(1)}, u32[]{:S(2)}, u32[]{:S(2)}) collective-permute-start(f32[368,128]{1,0:T(8,128)S(1)} %get-tuple-element.314), channel_id=1, source_target_pairs={{0,16},{16,32},{32,48},{48,64},{64,80},{80,96},{96,112},{112,128},... | collective-permute-start | bytes 565256 | tf_op jit(solution)/shard_map/ppermute | solution.py:372
  25.2 17.3 %collective-permute-start.17 = (f32[368,128]{1,0:T(8,128)S(1)}, f32[368,128]{1,0:T(8,128)S(1)}, u32[]{:S(2)}, u32[]{:S(2)}) collective-permute-start(f32[368,128]{1,0:T(8,128)S(1)} %get-tuple-element.315), channel_id=1, source_target_pairs={{0,496},{16,0},{32,16},{48,32},{64,48},{80,64},{96,80},{112,96},{1... | collective-permute-start | bytes 565256 | tf_op jit(solution)/shard_map/ppermute | solution.py:372
  31.9 6.2 %collective-permute-start.19 = (f32[24,128]{1,0:T(8,128)S(1)}, f32[24,128]{1,0:T(8,128)S(1)}, u32[]{:S(2)}, u32[]{:S(2)}) collective-permute-start(f32[24,128]{1,0:T(8,128)S(1)} %get-tuple-element.316.sums_ref), channel_id=1, source_target_pairs={{0,480},{16,496},{32,0},{48,16},{64,32},{80,48},{96,64},{112,80},{... | collective-permute-start | bytes 36872 | tf_op jit(solution)/shard_map/ppermute | solution.py:372
  33.8 8.7 %collective-permute-start.18 = (f32[24,128]{1,0:T(8,128)S(1)}, f32[24,128]{1,0:T(8,128)S(1)}, u32[]{:S(2)}, u32[]{:S(2)}) collective-permute-start(f32[24,128]{1,0:T(8,128)S(1)} %get-tuple-element.316.sums_ref), channel_id=1, source_target_pairs={{0,32},{16,48},{32,64},{48,80},{64,96},{80,112},{96,128},{112,144}... | collective-permute-start | bytes 36872 | tf_op jit(solution)/shard_map/ppermute | solution.py:372
  42.6 5.8 %collective-permute-start.20 = (f32[176,128]{1,0:T(8,128)S(1)}, f32[176,128]{1,0:T(8,128)S(1)}, u32[]{:S(2)}, u32[]{:S(2)}) collective-permute-start(f32[176,128]{1,0:T(8,128)S(1)} %get-tuple-element.319), channel_id=1, source_target_pairs={{0,1},{1,2},{2,3},{3,4},{4,5},{5,6},{6,7},{7,8},{8,9},{9,10},{10,1... | collective-permute-start | bytes 270344 | tf_op jit(solution)/shard_map/ppermute | solution.py:372
  45.4 4.0 %collective-permute-start.21 = (f32[176,128]{1,0:T(8,128)S(1)}, f32[176,128]{1,0:T(8,128)S(1)}, u32[]{:S(2)}, u32[]{:S(2)}) collective-permute-start(f32[176,128]{1,0:T(8,128)S(1)} %get-tuple-element.320), channel_id=1, source_target_pairs={{0,15},{1,0},{2,1},{3,2},{4,3},{5,4},{6,5},{7,6},{8,7},{9,8},{10,9... | collective-permute-start | bytes 270344 | tf_op jit(solution)/shard_map/ppermute | solution.py:372
  94.5 12.5 %all-to-all-start.3 = ((f32[32,1,128]{2,1,0:T(1,128)}), f32[32,1,128]{2,1,0:T(1,128)S(1)}, u32[]{:S(2)}, u32[]{:S(2)}) async-start(f32[32,1,128]{2,1,0:T(1,128)} %broadcast_in_dim.40), calls=%async_computation.3 | async-start | bytes 32768 | tf_op jit(solution)/shard_map/all_to_all | solution.py:367
  106.9 1.4 %copy-start.4 = (f32[8,128]{1,0:T(8,128)S(1)}, f32[8,128]{1,0:T(8,128)}, u32[]{:S(2)}) copy-start(f32[8,128]{1,0:T(8,128)} %height_ref.1) | copy-start | bytes 12292
  107.0 1.4 %copy-start.5 = (s32[8,128]{1,0:T(8,128)S(1)}, s32[8,128]{1,0:T(8,128)}, u32[]{:S(2)}) copy-start(s32[8,128]{1,0:T(8,128)} %code_ref.1) | copy-start | bytes 12292
  107.0 1.4 %copy-start.6 = (f32[8,128]{1,0:T(8,128)S(1)}, f32[8,128]{1,0:T(8,128)}, u32[]{:S(2)}) copy-start(f32[8,128]{1,0:T(8,128)} %friction_ref.1) | copy-start | bytes 12292
  107.7 0.7 copy-start

commit v8 on v7

--- a/solution.py
+++ b/solution.py
@@ -540,21 +540,27 @@
 
 
 def edge_products(weights, before_y, after_y):
-    line = lax.broadcasted_iota(jnp.int32, (32, 128), 0)
-    lane = lax.broadcasted_iota(jnp.int32, (32, 128), 1)
+    line = lax.broadcasted_iota(jnp.int32, (8, 128), 0)
+    lane = lax.broadcasted_iota(jnp.int32, (8, 128), 1)
     back_2, back_1, ahead_1, ahead_2 = weights[5:]
+    before = (
+        jnp.where(lane == 0, back_2, 0.0),
+        jnp.where(lane == 0, back_1, jnp.where(lane == 1, back_2, 0.0)),
+    )
+    after = (
+        jnp.where(lane == 127, ahead_1, jnp.where(lane == 126, ahead_2, 0.0)),
+        jnp.where(lane == 127, ahead_2, 0.0),
+    )
+    nothing = jnp.zeros((8, 128), jnp.float32)
     spread = []
     for x in range(8):
-        b_2, b_1, a_1, a_2 = (w[x : x + 1] for w in (back_2, back_1, ahead_1, ahead_2))
-        far = (line == 2 * x) & (lane == 0)
-        far = far | ((line == 2 * x + 1) & (lane == 1))
-        value = jnp.where(far, b_2, 0.0)
-        value = jnp.where((line == 2 * x + 1) & (lane == 0), b_1, value)
-        far = (line == 16 + 2 * x) & (lane == 126)
-        far = far | ((line == 17 + 2 * x) & (lane == 127))
-        value = jnp.where(far, a_2, value)
-        value = jnp.where((line == 16 + 2 * x) & (lane == 127), a_1, value)
-        spread.append(value)
+        at = 2 * (x % 4)
+        tiles = []
+        for near, far in (before, after):
+            tile = jnp.where(line == at, near[x : x + 1], 0.0)
+            tile = jnp.where(line == at + 1, far[x : x + 1], tile)
+            tiles += [tile, nothing] if x < 4 else [nothing, tile]
+        spread.append(jnp.concatenate(tiles, axis=0))
     return lax.dot_general(
         jnp.concatenate([before_y, after_y], axis=0),
         jnp.concatenate(spread, axis=1),
@@ -630,6 +636,10 @@
     return jnp.concatenate(rows, axis=0)
 
 
+def tiles_kernel(planes_ref, first_ref, last_ref):
+    first_ref[...], last_ref[...] = column_tiles([planes_ref[x] for x in range(8)])
+
+
 def gather_kernel(
     near_below_ref,
     near_above_ref,
@@ -657,16 +667,16 @@
         pieces = [far_below_ref[end], below_ref[middle], sums_ref[end]]
         pieces += [above_ref[middle], far_above_ref[end]]
         fields.append(jnp.concatenate(pieces, axis=0))
-    quarter = lax.broadcasted_iota(jnp.int32, (40, 128), 1) // 32
-    for group in range(4):
+    eighth = lax.broadcasted_iota(jnp.int32, (40, 128), 1) // 16
+    for group in range(2):
         low, high = (None, None)
-        for k, field in enumerate(fields[4 * group : 4 * group + 4]):
-            mine_ref[(4 * group + k) * 40 : (4 * group + k) * 40 + 40] = field
+        for k, field in enumerate(fields[8 * group : 8 * group + 8]):
+            mine_ref[(8 * group + k) * 40 : (8 * group + k) * 40 + 40] = field
             if k == 0:
                 low, high = (field, field)
             else:
-                low = jnp.where(quarter == k, pltpu.roll(field, 32 * k, 1), low)
-                high = jnp.where(quarter == 3 - k, pltpu.roll(field, 128 - 32 * k, 1), high)
+                low = jnp.where(eighth == k, pltpu.roll(field, 16 * k, 1), low)
+                high = jnp.where(eighth == 7 - k, pltpu.roll(field, 128 - 16 * k, 1), high)
         part = slice(16 + 40 * group, 56 + 40 * group)
         left_ref[part] = low
         right_ref[part] = high
@@ -682,8 +692,8 @@
 
 
 def wide_field(k, mine_ref, left_ref, right_ref, row_in, side_in):
-    part = slice(16 + 40 * (k // 4), 56 + 40 * (k // 4))
-    turn = 32 * (k % 4)
+    part = slice(16 + 40 * (k // 8), 56 + 40 * (k // 8))
+    turn = 16 * (k % 8)
     right, left = (right_ref[part], left_ref[part])
     if turn:
         right, left = (pltpu.roll(right, 128 - turn, 1), pltpu.roll(left, turn, 1))
@@ -732,8 +742,6 @@
     out_ref,
     low_ref,
     high_ref,
-    first_ref,
-    last_ref,
     weights_ref,
     sums_ref,
 ):
@@ -768,7 +776,6 @@
     high_ref[0:128] = done[6]
     high_ref[128:256] = done[7]
     high_ref[256:344] = below[256:344]
-    first_ref[...], last_ref[...] = column_tiles(done)
 
 
 def second_substep_kernel(
@@ -855,26 +862,30 @@
     near = beside(own, high, GX)
     near_sides = beside(first, last, GY)
     inverses = on_chip(column_inverses(kappa))
-    current, low, high, first, last, weights, sums = pl.pallas_call(
+    current, low, high, weights, sums = pl.pallas_call(
         first_substep_kernel,
         out_shape=(
             kept(8, 128, 128),
             kept(368, 128),
             kept(368, 128),
-            kept(16, 128),
-            kept(16, 128),
             kept(9, 8, 128),
             kept(24, 128),
         ),
         in_specs=[smem] + [vmem] * 11,
-        out_specs=(vmem,) * 7,
+        out_specs=(vmem,) * 5,
         name="first_substep",
     )(kappa, on_chip(planes), velocity_init, *near, *near_sides, inverses, *columns)
     around = beside(low, high, GX)
     far = (on_chip(shifted(sums, GX, 2)), on_chip(shifted(sums, GX, -2)))
+    current = on_chip(current)
+    first, last = pl.pallas_call(
+        tiles_kernel,
+        out_shape=(kept(16, 128), kept(16, 128)),
+        name="tiles",
+    )(current)
     mine, first, last = pl.pallas_call(
         gather_kernel,
-        out_shape=(kept(560, 128), kept(176, 128), kept(176, 128)),
+        out_shape=(kept(560, 128), kept(96, 128), kept(96, 128)),
         name="gather",
     )(*near, on_chip(own), *around, *far, *map(on_chip, (sums, first, last)))
     sides = beside(first, last, GY)
@@ -884,7 +895,7 @@
         in_specs=[smem] + [vmem] * 11,
         out_specs=vmem,
         name="second_substep",
-    )(kappa, on_chip(current), *around, *sides, on_chip(weights), inverses, *columns)
+    )(kappa, current, *around, *sides, on_chip(weights), inverses, *columns)
     quick, worst, stiffness = momentum(kappa, on_chip(mine), sides, inverses)
 
     def plain():

time: 109 us -> 108 us (level)
  transfers between devices with their start and end apart: 11 -> 11, of which waited for: 4 -> 4; matrix products, arithmetic and copies ran while one was open for 0% -> 0% of each run, Pallas kernels for 4% -> 5%
where the time goes in v8:
time: 108 us
  blocking collectives  40.1 us (37%)
  starting transfers between devices  39.7 us (37%)
  Pallas kernels  15.3 us (14%)
  waiting for transfers between devices  10.4 us (10%)
  between operations  1.5 us (1%)
    ppermute x10, starting transfers between devices, shifted(): lax.ppermute(array, axis, [(i, (i + by) % size) for i in range(size)])  35.9 us
    all_to_all x2, blocking collectives, over_all(): part = lax.all_to_all(sums, GY, 0, 0, tiled=True)  28.2 us
    all_to_all x1, blocking collectives, over_all(): return lax.all_to_all(part, GX, 0, 0, tiled=True)  11.9 us
    all_to_all x1, waiting for transfers between devices, over_all(): return lax.all_to_all(part, GX, 0, 0, tiled=True)  5.41 us
    ppermute x10, waiting for transfers between devices, shifted(): lax.ppermute(array, axis, [(i, (i + by) % size) for i in range(size)])  5.01 us
    all_to_all x1, starting transfers between devices, over_all(): return lax.all_to_all(part, GX, 0, 0, tiled=True)  3.79 us
    pallas_call x1, Pallas kernels, shards(): pl.pallas_call(second_substep_kernel, out_shape=jax.ShapeDtypeStruct((102...  3.26 us
    pallas_call x1, Pallas kernels, shards(): pl.pallas_call(first_substep_kernel, out_shape=(kept(8, 128, 128), kept(3...  2.92 us
  transfers between devices with their start and end apart: 11, of which 4 were waited for; matrix products, arithmetic and copies ran while one was open for 0% of the time, Pallas kernels for 5%

profile of v8, /device:TPU:1, one launch (start us, length us, event | category | flops | bytes accessed | tf_op | source)
XLA Modules:
  0.0 107.7 jit_solution(18021381782407666299)
XLA Ops:
  0.6 1.8 %pack.1 = (f32[344,128]{1,0:T(8,128)S(1)}, f32[344,128]{1,0:T(8,128)S(1)}, f32[24,128]{1,0:T(8,128)S(1)}, f32[24,128]{1,0:T(8,128)S(1)}, f32[8,128,128]{2,1,0:T(8,128)S(1)}) custom-call(f32[1024,128]{1,0:T(8,128)} %bitcast.85, f32[2,8,128]{2,1,0:T(8,128)} %speed_ref.3, f32[8,128]{1,0:T(8,128)} %thick_ref.1, f32[8,128]{1,0:T(8,128)} %height_ref.1, ...), custom_call_target="tpu_custom_call" | custom-call | tf_op jit(solution)/shard_map/pack/pallas_call | solution.py:840
  2.4 4.0 %collective-permute-start.12 = (f32[344,128]{1,0:T(8,128)S(1)}, f32[344,128]{1,0:T(8,128)S(1)}, u32[]{:S(2)}, u32[]{:S(2)}) collective-permute-start(f32[344,128]{1,0:T(8,128)S(1)} %get-tuple-element.309), channel_id=1, source_target_pairs={{0,16},{16,32},{32,48},{48,64},{64,80},{80,96},{96,112},{112,128},... | collective-permute-start | bytes 528392 | tf_op jit(solution)/shard_map/ppermute | solution.py:372
  6.5 6.0 %collective-permute-start.13 = (f32[344,128]{1,0:T(8,128)S(1)}, f32[344,128]{1,0:T(8,128)S(1)}, u32[]{:S(2)}, u32[]{:S(2)}) collective-permute-start(f32[344,128]{1,0:T(8,128)S(1)} %get-tuple-element.310.own_ref), channel_id=1, source_target_pairs={{0,496},{16,0},{32,16},{48,32},{64,48},{80,64},{96,80},{112,96},{1... | collective-permute-start | bytes 528392 | tf_op jit(solution)/shard_map/ppermute | solution.py:372
  12.5 2.9 %collective-permute-start.14 = (f32[24,128]{1,0:T(8,128)S(1)}, f32[24,128]{1,0:T(8,128)S(1)}, u32[]{:S(2)}, u32[]{:S(2)}) collective-permute-start(f32[24,128]{1,0:T(8,128)S(1)} %get-tuple-element.311), channel_id=1, source_target_pairs={{0,1},{1,2},{2,3},{3,4},{4,5},{5,6},{6,7},{7,8},{8,9},{9,10},{10,1... | collective-permute-start | bytes 36872 | tf_op jit(solution)/shard_map/ppermute | solution.py:372
  15.4 3.1 %collective-permute-start.15 = (f32[24,128]{1,0:T(8,128)S(1)}, f32[24,128]{1,0:T(8,128)S(1)}, u32[]{:S(2)}, u32[]{:S(2)}) collective-permute-start(f32[24,128]{1,0:T(8,128)S(1)} %get-tuple-element.312), channel_id=1, source_target_pairs={{0,15},{1,0},{2,1},{3,2},{4,3},{5,4},{6,5},{7,6},{8,7},{9,8},{10,9... | collective-permute-start | bytes 36872 | tf_op jit(solution)/shard_map/ppermute | solution.py:372
  18.5 0.0 copy-start.1
  18.5 0.0 copy-start.2
  18.5 0.0 copy-start.3
  18.5 1.4 %column_inverses.1.inverses_ref = f32[256,128]{1,0:T(8,128)S(1)} custom-call(f32[1,129]{1,0:T(1,128)} %bitcast.95), custom_call_target="tpu_custom_call" | custom-call | tf_op jit(solution)/shard_map/column_inverses/pallas_call | solution.py:133
  19.9 0.0 collective-permute-done.14.left_ref
  19.9 0.0 collective-permute-done.15.right_ref
  20.0 0.0 collective-permute-done.12.below_ref.near_below_ref
  20.0 0.0 collective-permute-done.13.above_ref.near_above_ref
  20.0 0.0 copy-done.1
  20.0 0.0 copy-done.2
  20.0 0.0 copy-done.3
  20.0 2.9 %first_substep.1 = (f32[8,128,128]{2,1,0:T(8,128)S(1)}, f32[368,128]{1,0:T(8,128)S(1)}, f32[368,128]{1,0:T(8,128)S(1)}, f32[9,8,128]{2,1,0:T(8,128)S(1)}, f32[24,128]{1,0:T(8,128)S(1)}) custom-call(f32[129]{0:T(256)} %kappa_ref.5, f32[8,128,128]{2,1,0:T(8,128)S(1)} %get-tuple-element.308.enthalpy_ref, f32[2,8,128]{2,1,0:T(8,128)S(1)} %copy-done.1, ...), custom_call_target="tpu_custom_call" | custom-call | tf_op jit(solution)/shard_map/first_substep/pallas_call | solution.py:865
  22.9 1.9 %collective-permute-start.16 = (f32[368,128]{1,0:T(8,128)S(1)}, f32[368,128]{1,0:T(8,128)S(1)}, u32[]{:S(2)}, u32[]{:S(2)}) collective-permute-start(f32[368,128]{1,0:T(8,128)S(1)} %get-tuple-element.314), channel_id=1, source_target_pairs={{0,16},{16,32},{32,48},{48,64},{64,80},{80,96},{96,112},{112,128},... | collective-permute-start | bytes 565256 | tf_op jit(solution)/shard_map/ppermute | solution.py:372
  24.9 6.7 %collective-permute-start.17 = (f32[368,128]{1,0:T(8,128)S(1)}, f32[368,128]{1,0:T(8,128)S(1)}, u32[]{:S(2)}, u32[]{:S(2)}) collective-permute-start(f32[368,128]{1,0:T(8,128)S(1)} %get-tuple-element.315), channel_id=1, source_target_pairs={{0,496},{16,0},{32,16},{48,32},{64,48},{80,64},{96,80},{112,96},{1... | collective-permute-start | bytes 565256 | tf_op jit(solution)/shard_map/ppermute | solution.py:372
  31.5 1.9 %collective-permute-start.19 = (f32[24,128]{1,0:T(8,128)S(1)}, f32[24,128]{1,0:T(8,128)S(1)}, u32[]{:S(2)}, u32[]{:S(2)}) collective-permute-start(f32[24,128]{1,0:T(8,128)S(1)} %get-tuple-element.316.sums_ref), channel_id=1, source_target_pairs={{0,480},{16,496},{32,0},{48,16},{64,32},{80,48},{96,64},{112,80},{... | collective-permute-start | bytes 36872 | tf_op jit(solution)/shard_map/ppermute | solution.py:372
  33.5 4.3 %collective-permute-start.18 = (f32[24,128]{1,0:T(8,128)S(1)}, f32[24,128]{1,0:T(8,128)S(1)}, u32[]{:S(2)}, u32[]{:S(2)}) collective-permute-start(f32[24,128]{1,0:T(8,128)S(1)} %get-tuple-element.316.sums_ref), channel_id=1, source_target_pairs={{0,32},{16,48},{32,64},{48,80},{64,96},{80,112},{96,128},{112,144}... | collective-permute-start | bytes 36872 | tf_op jit(solution)/shard_map/ppermute | solution.py:372
  37.7 0.6 tiles.1
  38.3 0.0 collective-permute-done.19.far_above_ref
  38.4 3.8 %collective-permute-done.18.far_below_ref = f32[24,128]{1,0:T(8,128)S(1)} collective-permute-done((f32[24,128]{1,0:T(8,128)S(1)}, f32[24,128]{1,0:T(8,128)S(1)}, u32[]{:S(2)}, u32[]{:S(2)}) %collective-permute-start.18) | collective-permute-done | bytes 12320 | tf_op jit(solution)/shard_map/ppermute | solution.py:372
  42.1 0.0 collective-permute-done.16.below_ref
  42.1 0.0 collective-permute-done.17.above_ref
  42.2 0.2 gather.1
  42.3 2.7 %collective-permute-start.20 = (f32[96,128]{1,0:T(8,128)S(1)}, f32[96,128]{1,0:T(8,128)S(1)}, u32[]{:S(2)}, u32[]{:S(2)}) collective-permute-start(f32[96,128]{1,0:T(8,128)S(1)} %get-tuple-element.319), channel_id=1, source_target_pairs={{0,1},{1,2},{2,3},{3,4},{4,5},{5,6},{6,7},{7,8},{8,9},{9,10},{10,1... | collective-permute-start | bytes 147464 | tf_op jit(solution)/shard_map/ppermute | solution.py:372
  45.1 2.3 %collective-permute-start.21 = (f32[96,128]{1,0:T(8,128)S(1)}, f32[96,128]{1,0:T(8,128)S(1)}, u32[]{:S(2)}, u32[]{:S(2)}) collective-permute-start(f32[96,128]{1,0:T(8,128)S(1)} %get-tuple-element.320), channel_id=1, source_target_pairs={{0,15},{1,0},{2,1},{3,2},{4,3},{5,4},{6,5},{7,6},{8,7},{9,8},{10,9... | collective-permute-start | bytes 147464 | tf_op jit(solution)/shard_map/ppermute | solution.py:372
  47.4 0.7 collective-permute-done.20.left_ref
  48.1 0.5 collective-permute-done.21.right_ref
  48.6 2.7 %first_picard.1 = (f32[12,24,256]{2,1,0:T(8,128)S(1)}, f32[6,24,256]{2,1,0:T(8,128)S(1)}, f32[16,128]{1,0:T(8,128)S(1)}, f32[8,128]{1,0:T(8,128)S(1)}) custom-call(f32[129]{0:T(256)} %kappa_ref.5, f32[560,128]{1,0:T(8,128)S(1)} %get-tuple-element.322.mine_ref, f32[96,128]{1,0:T(8,128)S(1)} %collective-permute-done.20.left_ref, ...), custom_call_target="tpu_custom_call" | custom-call | tf_op jit(solution)/shard_map/first_picard/pallas_call | solution.py:379
  51.3 16.7 %all_to_all.34 = f32[16,1,128]{2,1,0:T(1,128)S(1)} all-to-all(f32[16,1,128]{2,1,0:T(1,128)S(1)} %bitcast.80), channel_id=1, replica_groups=mesh['gx_0'=4,'gx_1'=8,'gy_0'=8,'gy_1'=2] {'gy_0','gy_1'}, dimensions={0} | all-to-all | bytes 16384 | tf_op jit(solution)/shard_map/all_to_all | solution.py:365
  68.0 11.9 %all_to_all.35 = f32[32,1,128]{2,1,0:T(1,128)S(1)} all-to-all(f32[32,1,128]{2,1,0:T(1,128)S(1)} %broadcast_in_dim.39), channel_id=1, replica_groups=mesh['gx_0'=4,'gx_1'=8,'gy_0'=8,'gy_1'=2] {'gx_0','gx_1'}, dimensions={0} | all-to-all | bytes 32768 | tf_op jit(solution)/shard_map/all_to_all | solution.py:367
  79.9 1.6 %second_picard.1 = (f32[12,8,128]{2,1,0:T(8,128)S(1)}, f32[2,8,128]{2,1,0:T(8,128)S(1)}, f32[16,128]{1,0:T(8,128)S(1)}, f32[8,128]{1,0:T(8,128)S(1)}) custom-call(f32[32,128]{1,0:T(8,128)S(1)} %bitcast.78, f32[12,24,256]{2,1,0:T(8,128)S(1)} %get-tuple-element.324.basis_ref, f32[6,24,256]{2,1,0:T(8,128)S(1)} %get-tuple-element.325.fixed_ref), custom_call_target="tpu_custom_call" | custom-call | tf_op jit(solution)/shard_map/second_picard/pallas_call | solution.py:391
  81.5 11.6 %all_to_all.36 = f32[16,1,128]{2,1,0:T(1,128)S(1)} all-to-all(f32[16,1,128]{2,1,0:T(1,128)S(1)} %bitcast.79), channel_id=1, replica_groups=mesh['gx_0'=4,'gx_1'=8,'gy_0'=8,'gy_1'=2] {'gy_0','gy_1'}, dimensions={0} | all-to-all | bytes 16384 | tf_op jit(solution)/shard_map/all_to_all | solution.py:365
  93.1 0.6 broadcast_in_dim.40
  93.7 3.8 %all-to-all-start.3 = ((f32[32,1,128]{2,1,0:T(1,128)}), f32[32,1,128]{2,1,0:T(1,128)S(1)}, u32[]{:S(2)}, u32[]{:S(2)}) async-start(f32[32,1,128]{2,1,0:T(1,128)} %broadcast_in_dim.40), calls=%async_computation.3 | async-start | bytes 32768 | tf_op jit(solution)/shard_map/all_to_all | solution.py:367
  97.5 3.3 %second_substep.1 = f32[1024,128]{1,0:T(8,128)} custom-call(f32[129]{0:T(256)} %kappa_ref.5, f32[8,128,128]{2,1,0:T(8,128)S(1)} %get-tuple-element.313.planes_ref.enthalpy_ref, f32[368,128]{1,0:T(8,128)S(1)} %collective-permute-done.16.below_ref, f32[368,128]{1,0:T(8,128)S(1)} %collective-permute-done.17.above_ref, ...), custom_call_target="tpu_custom_call" | custom-call | tf_op jit(solution)/shard_map/second_substep/pallas_call | solution.py:892
  100.8 5.4 %all-to-all-done.3 = f32[32,1,128]{2,1,0:T(1,128)S(1)} async-done(((f32[32,1,128]{2,1,0:T(1,128)}), f32[32,1,128]{2,1,0:T(1,128)S(1)}, u32[]{:S(2)}, u32[]{:S(2)}) %all-to-all-start.3) | async-done | bytes 16416 | tf_op jit(solution)/shard_map/all_to_all | solution.py:367
  106.2 0.0 copy-start.4
  106.2 0.0 copy-start.5
  106.2 0.8 last_picard.1
  107.0 0.0 copy-start
  107.6 0.0 copy-done.4
  107.6 0.0 copy-done.5
  107.7 0.0 copy-done.6
  107.7 0.0 copy-done
  (5 shorter events, 0.1 us)
Async XLA Ops:
  2.4 17.5 %collective-permute-start.12 = (f32[344,128]{1,0:T(8,128)S(1)}, f32[344,128]{1,0:T(8,128)S(1)}, u32[]{:S(2)}, u32[]{:S(2)}) collective-permute-start(f32[344,128]{1,0:T(8,128)S(1)} %get-tuple-element.309), channel_id=1, source_target_pairs={{0,16},{16,32},{32,48},{48,64},{64,80},{80,96},{96,112},{112,128},... | collective-permute-start | bytes 528392 | tf_op jit(solution)/shard_map/ppermute | solution.py:372
  6.5 13.5 %collective-permute-start.13 = (f32[344,128]{1,0:T(8,128)S(1)}, f32[344,128]{1,0:T(8,128)S(1)}, u32[]{:S(2)}, u32[]{:S(2)}) collective-permute-start(f32[344,128]{1,0:T(8,128)S(1)} %get-tuple-element.310.own_ref), channel_id=1, source_target_pairs={{0,496},{16,0},{32,16},{48,32},{64,48},{80,64},{96,80},{112,96},{1... | collective-permute-start | bytes 528392 | tf_op jit(solution)/shard_map/ppermute | solution.py:372
  12.5 7.5 %collective-permute-start.14 = (f32[24,128]{1,0:T(8,128)S(1)}, f32[24,128]{1,0:T(8,128)S(1)}, u32[]{:S(2)}, u32[]{:S(2)}) collective-permute-start(f32[24,128]{1,0:T(8,128)S(1)} %get-tuple-element.311), channel_id=1, source_target_pairs={{0,1},{1,2},{2,3},{3,4},{4,5},{5,6},{6,7},{7,8},{8,9},{9,10},{10,1... | collective-permute-start | bytes 36872 | tf_op jit(solution)/shard_map/ppermute | solution.py:372
  15.4 4.5 %collective-permute-start.15 = (f32[24,128]{1,0:T(8,128)S(1)}, f32[24,128]{1,0:T(8,128)S(1)}, u32[]{:S(2)}, u32[]{:S(2)}) collective-permute-start(f32[24,128]{1,0:T(8,128)S(1)} %get-tuple-element.312), channel_id=1, source_target_pairs={{0,15},{1,0},{2,1},{3,2},{4,3},{5,4},{6,5},{7,6},{8,7},{9,8},{10,9... | collective-permute-start | bytes 36872 | tf_op jit(solution)/shard_map/ppermute | solution.py:372
  18.5 1.5 %copy-start.1 = (f32[2,8,128]{2,1,0:T(8,128)S(1)}, f32[2,8,128]{2,1,0:T(8,128)}, u32[]{:S(2)}) copy-start(f32[2,8,128]{2,1,0:T(8,128)} %speed_ref.3) | copy-start | bytes 24580
  18.5 1.5 %copy-start.2 = (s32[8,128]{1,0:T(8,128)S(1)}, s32[8,128]{1,0:T(8,128)}, u32[]{:S(2)}) copy-start(s32[8,128]{1,0:T(8,128)} %grounded_ref.5) | copy-start | bytes 12292
  18.5 1.5 %copy-start.3 = (s32[8,128]{1,0:T(8,128)S(1)}, s32[8,128]{1,0:T(8,128)}, u32[]{:S(2)}) copy-start(s32[8,128]{1,0:T(8,128)} %ice_ref.5) | copy-start | bytes 12292
  22.9 19.2 %collective-permute-start.16 = (f32[368,128]{1,0:T(8,128)S(1)}, f32[368,128]{1,0:T(8,128)S(1)}, u32[]{:S(2)}, u32[]{:S(2)}) collective-permute-start(f32[368,128]{1,0:T(8,128)S(1)} %get-tuple-element.314), channel_id=1, source_target_pairs={{0,16},{16,32},{32,48},{48,64},{64,80},{80,96},{96,112},{112,128},... | collective-permute-start | bytes 565256 | tf_op jit(solution)/shard_map/ppermute | solution.py:372
  24.9 17.3 %collective-permute-start.17 = (f32[368,128]{1,0:T(8,128)S(1)}, f32[368,128]{1,0:T(8,128)S(1)}, u32[]{:S(2)}, u32[]{:S(2)}) collective-permute-start(f32[368,128]{1,0:T(8,128)S(1)} %get-tuple-element.315), channel_id=1, source_target_pairs={{0,496},{16,0},{32,16},{48,32},{64,48},{80,64},{96,80},{112,96},{1... | collective-permute-start | bytes 565256 | tf_op jit(solution)/shard_map/ppermute | solution.py:372
  31.5 6.8 %collective-permute-start.19 = (f32[24,128]{1,0:T(8,128)S(1)}, f32[24,128]{1,0:T(8,128)S(1)}, u32[]{:S(2)}, u32[]{:S(2)}) collective-permute-start(f32[24,128]{1,0:T(8,128)S(1)} %get-tuple-element.316.sums_ref), channel_id=1, source_target_pairs={{0,480},{16,496},{32,0},{48,16},{64,32},{80,48},{96,64},{112,80},{... | collective-permute-start | bytes 36872 | tf_op jit(solution)/shard_map/ppermute | solution.py:372
  33.5 8.7 %collective-permute-start.18 = (f32[24,128]{1,0:T(8,128)S(1)}, f32[24,128]{1,0:T(8,128)S(1)}, u32[]{:S(2)}, u32[]{:S(2)}) collective-permute-start(f32[24,128]{1,0:T(8,128)S(1)} %get-tuple-element.316.sums_ref), channel_id=1, source_target_pairs={{0,32},{16,48},{32,64},{48,80},{64,96},{80,112},{96,128},{112,144}... | collective-permute-start | bytes 36872 | tf_op jit(solution)/shard_map/ppermute | solution.py:372
  42.3 5.7 %collective-permute-start.20 = (f32[96,128]{1,0:T(8,128)S(1)}, f32[96,128]{1,0:T(8,128)S(1)}, u32[]{:S(2)}, u32[]{:S(2)}) collective-permute-start(f32[96,128]{1,0:T(8,128)S(1)} %get-tuple-element.319), channel_id=1, source_target_pairs={{0,1},{1,2},{2,3},{3,4},{4,5},{5,6},{6,7},{7,8},{8,9},{9,10},{10,1... | collective-permute-start | bytes 147464 | tf_op jit(solution)/shard_map/ppermute | solution.py:372
  45.1 3.5 %collective-permute-start.21 = (f32[96,128]{1,0:T(8,128)S(1)}, f32[96,128]{1,0:T(8,128)S(1)}, u32[]{:S(2)}, u32[]{:S(2)}) collective-permute-start(f32[96,128]{1,0:T(8,128)S(1)} %get-tuple-element.320), channel_id=1, source_target_pairs={{0,15},{1,0},{2,1},{3,2},{4,3},{5,4},{6,5},{7,6},{8,7},{9,8},{10,9... | collective-permute-start | bytes 147464 | tf_op jit(solution)/shard_map/ppermute | solution.py:372
  93.7 12.5 %all-to-all-start.3 = ((f32[32,1,128]{2,1,0:T(1,128)}), f32[32,1,128]{2,1,0:T(1,128)S(1)}, u32[]{:S(2)}, u32[]{:S(2)}) async-start(f32[32,1,128]{2,1,0:T(1,128)} %broadcast_in_dim.40), calls=%async_computation.3 | async-start | bytes 32768 | tf_op jit(solution)/shard_map/all_to_all | solution.py:367
  106.2 1.4 %copy-start.4 = (f32[8,128]{1,0:T(8,128)S(1)}, f32[8,128]{1,0:T(8,128)}, u32[]{:S(2)}) copy-start(f32[8,128]{1,0:T(8,128)} %height_ref.1) | copy-start | bytes 12292
  106.2 1.5 %copy-start.5 = (s32[8,128]{1,0:T(8,128)S(1)}, s32[8,128]{1,0:T(8,128)}, u32[]{:S(2)}) copy-start(s32[8,128]{1,0:T(8,128)} %code_ref.1) | copy-start | bytes 12292
  106.2 1.5 %copy-start.6 = (f32[8,128]{1,0:T(8,128)S(1)}, f32[8,128]{1,0:T(8,128)}, u32[]{:S(2)}) copy-start(f32[8,128]{1,0:T(8,128)} %friction_ref.1) | copy-start | bytes 12292
  107.0 0.7 copy-start

commit v9 on v8

--- a/solution.py
+++ b/solution.py
@@ -99,6 +99,7 @@
 
 def inverse_kernel(kappa_ref, out_ref):
     levels = out_ref.shape[1]
+    out_ref[2 * levels :] = jnp.broadcast_to(kappa_ref[:, 0:1], (8, levels))
     above = jnp.broadcast_to(kappa_ref[:, :levels], (8, levels))
     below = jnp.broadcast_to(kappa_ref[:, 1:], (8, levels))
     lane = lax.broadcasted_iota(jnp.int32, (8, levels), 1)
@@ -132,7 +133,7 @@
     levels = kappa.shape[0] - 1
     return pl.pallas_call(
         inverse_kernel,
-        out_shape=kept(2 * levels, levels),
+        out_shape=kept(2 * levels + 8, levels),
         name="column_inverses",
     )(kappa[None])
 
@@ -290,7 +291,6 @@
 
 
 def first_picard_kernel(
-    kappa_ref,
     mine_ref,
     left_ref,
     right_ref,
@@ -305,7 +305,7 @@
     u, v, drag, thick, surface = (take(k) for k in range(5))
     transport = [take(k) for k in range(5, 11)]
     sums = [take(k) for k in range(11, 14)]
-    stiff = stiffness_of(sums, *transport, kappa_ref[0], inverses_ref)
+    stiff = stiffness_of(sums, *transport, inverses_ref)
     stiff = jnp.where(jnp.concatenate(where_in, axis=1), stiff, 0.0)
     own_ref[...] = stiff[OWN : OWN + 8, :128]
     t_sum = thick + next_col(thick)
@@ -372,7 +372,7 @@
     return lax.ppermute(array, axis, [(i, (i + by) % size) for i in range(size)])
 
 
-def momentum(kappa, mine, sides, inverses):
+def momentum(mine, sides, inverses):
     smem = pl.BlockSpec(memory_space=pltpu.SMEM)
     vmem = pl.BlockSpec(memory_space=pltpu.VMEM)
     gy = lax.axis_size(GY)
@@ -384,10 +384,8 @@
             kept(gy, 128),
             jax.ShapeDtypeStruct((8, 128), jnp.float32),
         ),
-        in_specs=[smem] + [vmem] * 4,
-        out_specs=(vmem,) * 4,
         name="first_picard",
-    )(kappa, mine, *sides, inverses)
+    )(mine, *sides, inverses)
     basis, velocity, sums, least = pl.pallas_call(
         second_picard_kernel,
         out_shape=(
@@ -525,8 +523,7 @@
     )
 
 
-def cell_weights(speed_ref, before_x, after_x, before_y, after_y):
-    c_x, c_y = (speed_ref[0], speed_ref[1])
+def cell_weights(c_x, c_y, before_x, after_x, before_y, after_y):
     row = lax.broadcasted_iota(jnp.int32, (8, 128), 0)
     lane = lax.broadcasted_iota(jnp.int32, (8, 128), 1)
     x_before = jnp.where(row == 0, pltpu.roll(before_x, 1, 0), pltpu.roll(c_x, 1, 0))
@@ -570,7 +567,11 @@
     )
 
 
-def substep(planes, weights, edges, inverses, first_kappa, ice, bed, surface_heat, heat_flux):
+def columns_of(own_ref):
+    return tuple(own_ref[312 + 8 * k : 320 + 8 * k] for k in range(4))
+
+
+def substep(planes, weights, edges, inverses_ref, ice, bed, surface_heat, heat_flux):
     lane = lax.broadcasted_iota(jnp.int32, (8, 128), 1)
     center, x_b2, x_b1, x_a1, x_a2, y_b2, y_b1, y_a1, y_a2 = weights
     y_b2 = jnp.where(lane < 2, 0.0, y_b2)
@@ -578,6 +579,8 @@
     y_a1 = jnp.where(lane > 126, 0.0, y_a1)
     y_a2 = jnp.where(lane > 125, 0.0, y_a2)
     level = lax.broadcasted_iota(jnp.int32, (128, 128), 0)
+    inverses = inverses_ref[0:256]
+    first_kappa = inverses_ref[256:257]
     done = []
     for x in range(0, 8, 2):
         moved, sides = ([], [])
@@ -705,7 +708,7 @@
     )
 
 
-def stiffness_of(sums, c_x, c_y, ice, bed, heat, flux, first_kappa, inverses_ref):
+def stiffness_of(sums, c_x, c_y, ice, bed, heat, flux, inverses_ref):
     along_x = line_weights(0.5 * (last_row(c_x) + c_x), 0.5 * (c_x + next_row(c_x)))
     along_y = line_weights(0.5 * (last_col(c_y) + c_y), 0.5 * (c_y + next_col(c_y)))
     moved = []
@@ -719,7 +722,7 @@
             value = value + line[4] * pltpu.roll(e, size - 2, axis)
         moved.append(value)
     on_bed, on_shelf, _ = sum_weights(inverses_ref)
-    top = first_kappa * heat
+    top = inverses_ref[256:257, 0:1] * heat
     grounded = moved[0] + on_bed[:, 0:1] * top + on_bed[:, 127:128] * flux
     floating = moved[1] + on_shelf[:, 0:1] * top
     mean = jnp.where(ice > 0.5, jnp.where(bed > 0.5, grounded, floating), moved[2])
@@ -727,18 +730,13 @@
 
 
 def first_substep_kernel(
-    kappa_ref,
     enthalpy_ref,
-    speed_ref,
+    own_ref,
     below_ref,
     above_ref,
     left_ref,
     right_ref,
     inverses_ref,
-    ice_ref,
-    grounded_ref,
-    surface_ref,
-    flux_ref,
     out_ref,
     low_ref,
     high_ref,
@@ -746,24 +744,21 @@
     sums_ref,
 ):
     below, above, left, right = inside(below_ref, above_ref, left_ref, right_ref)
-    weights = cell_weights(speed_ref, below[296:304], above[296:304], left[16:], right[16:])
+    weights = cell_weights(
+        own_ref[296:304],
+        own_ref[304:312],
+        below[296:304],
+        above[296:304],
+        left[16:],
+        right[16:],
+    )
     for k in range(9):
         weights_ref[k] = weights[k]
     edges = edge_products(weights, left[:16], right[:16])
     planes = [below[:128], below[128:256]]
     planes += [enthalpy_ref[x] for x in range(8)]
     planes += [above[:128], above[128:256]]
-    done = substep(
-        planes,
-        weights,
-        edges,
-        inverses_ref[...],
-        kappa_ref[0],
-        ice_ref[...].astype(jnp.float32),
-        grounded_ref[...].astype(jnp.float32),
-        surface_ref[...],
-        flux_ref[...],
-    )
+    done = substep(planes, weights, edges, inverses_ref, *columns_of(own_ref))
     for x in range(8):
         out_ref[x] = done[x]
     low_ref[0:128] = done[0]
@@ -779,18 +774,14 @@
 
 
 def second_substep_kernel(
-    kappa_ref,
     enthalpy_ref,
+    own_ref,
     below_ref,
     above_ref,
     left_ref,
     right_ref,
     weights_ref,
     inverses_ref,
-    ice_ref,
-    grounded_ref,
-    surface_ref,
-    flux_ref,
     out_ref,
 ):
     sides = (below_ref.at[0:256], above_ref.at[0:256], left_ref.at[0:16], right_ref.at[0:16])
@@ -800,17 +791,7 @@
     planes = [below[:128], below[128:256]]
     planes += [enthalpy_ref[x] for x in range(8)]
     planes += [above[:128], above[128:256]]
-    done = substep(
-        planes,
-        weights,
-        edges,
-        inverses_ref[...],
-        kappa_ref[0],
-        ice_ref[...].astype(jnp.float32),
-        grounded_ref[...].astype(jnp.float32),
-        surface_ref[...],
-        flux_ref[...],
-    )
+    done = substep(planes, weights, edges, inverses_ref, *columns_of(own_ref))
     for x in range(8):
         out_ref[pl.ds(x, 128, stride=8), :] = done[x]
 
@@ -833,10 +814,7 @@
     boundary_code,
 ):
     f32 = jnp.float32
-    smem = pl.BlockSpec(memory_space=pltpu.SMEM)
-    vmem = pl.BlockSpec(memory_space=pltpu.VMEM)
     flat = enthalpy.reshape(1024, 128)
-    columns = (ice_mask, grounded, surface_enthalpy, geo_flux)
     own, high, first, last, planes = pl.pallas_call(
         pack_kernel,
         out_shape=(
@@ -859,6 +837,7 @@
         surface_enthalpy,
         geo_flux,
     )
+    own = on_chip(own)
     near = beside(own, high, GX)
     near_sides = beside(first, last, GY)
     inverses = on_chip(column_inverses(kappa))
@@ -871,10 +850,8 @@
             kept(9, 8, 128),
             kept(24, 128),
         ),
-        in_specs=[smem] + [vmem] * 11,
-        out_specs=(vmem,) * 5,
         name="first_substep",
-    )(kappa, on_chip(planes), velocity_init, *near, *near_sides, inverses, *columns)
+    )(on_chip(planes), own, *near, *near_sides, inverses)
     around = beside(low, high, GX)
     far = (on_chip(shifted(sums, GX, 2)), on_chip(shifted(sums, GX, -2)))
     current = on_chip(current)
@@ -887,16 +864,14 @@
         gather_kernel,
         out_shape=(kept(560, 128), kept(96, 128), kept(96, 128)),
         name="gather",
-    )(*near, on_chip(own), *around, *far, *map(on_chip, (sums, first, last)))
+    )(*near, own, *around, *far, *map(on_chip, (sums, first, last)))
     sides = beside(first, last, GY)
     current = pl.pallas_call(
         second_substep_kernel,
         out_shape=jax.ShapeDtypeStruct((1024, 128), f32),
-        in_specs=[smem] + [vmem] * 11,
-        out_specs=vmem,
         name="second_substep",
-    )(kappa, current, *around, *sides, on_chip(weights), inverses, *columns)
-    quick, worst, stiffness = momentum(kappa, on_chip(mine), sides, inverses)
+    )(current, own, *around, *sides, on_chip(weights), inverses)
+    quick, worst, stiffness = momentum(on_chip(mine), sides, inverses)
 
     def plain():
         free_cells = (boundary_code == 0) & (ice_mask == 1)

time: 108 us -> 107 us (level)
  Pallas kernels: 15.3 us -> 13.1 us
  transfers between devices with their start and end apart: 11 -> 11, of which waited for: 4 -> 4; matrix products, arithmetic and copies ran while one was open for 0% -> 0% of each run, Pallas kernels for 5% -> 4%
where the time goes in v9:
time: 107 us; the launch traced here: 106 us
  blocking collectives  40.1 us (37%)
  starting transfers between devices  39.7 us (37%)
  Pallas kernels  13.1 us (12%)
  waiting for transfers between devices  11.1 us (10%)
  between operations  1.52 us (1%)
    ppermute x10, starting transfers between devices, shifted(): lax.ppermute(array, axis, [(i, (i + by) % size) for i in range(size)])  35.9 us
    all_to_all x2, blocking collectives, over_all(): part = lax.all_to_all(sums, GY, 0, 0, tiled=True)  28.2 us
    all_to_all x1, blocking collectives, over_all(): return lax.all_to_all(part, GX, 0, 0, tiled=True)  11.9 us
    all_to_all x1, waiting for transfers between devices, over_all(): return lax.all_to_all(part, GX, 0, 0, tiled=True)  6.08 us
    ppermute x10, waiting for transfers between devices, shifted(): lax.ppermute(array, axis, [(i, (i + by) % size) for i in range(size)])  5.01 us
    all_to_all x1, starting transfers between devices, over_all(): return lax.all_to_all(part, GX, 0, 0, tiled=True)  3.79 us
    pallas_call x1, Pallas kernels, shards(): pl.pallas_call(second_substep_kernel, out_shape=jax.ShapeDtypeStruct((102...  2.59 us
  transfers between devices with their start and end apart: 11, of which 4 were waited for; matrix products, arithmetic and copies ran while one was open for 0% of the time, Pallas kernels for 4%

profile of v9, /device:TPU:1, one launch (start us, length us, event | category | flops | bytes accessed | tf_op | source)
XLA Modules:
  0.0 106.2 jit_solution(5860564147936362707)
XLA Ops:
  0.6 1.8 %pack.1 = (f32[344,128]{1,0:T(8,128)S(1)}, f32[344,128]{1,0:T(8,128)S(1)}, f32[24,128]{1,0:T(8,128)S(1)}, f32[24,128]{1,0:T(8,128)S(1)}, f32[8,128,128]{2,1,0:T(8,128)S(1)}) custom-call(f32[1024,128]{1,0:T(8,128)} %bitcast.85, f32[2,8,128]{2,1,0:T(8,128)} %speed_ref.1, f32[8,128]{1,0:T(8,128)} %thick_ref.1, f32[8,128]{1,0:T(8,128)} %height_ref.1, ...), custom_call_target="tpu_custom_call" | custom-call | tf_op jit(solution)/shard_map/pack/pallas_call | solution.py:818
  2.4 4.0 %collective-permute-start.12 = (f32[344,128]{1,0:T(8,128)S(1)}, f32[344,128]{1,0:T(8,128)S(1)}, u32[]{:S(2)}, u32[]{:S(2)}) collective-permute-start(f32[344,128]{1,0:T(8,128)S(1)} %get-tuple-element.310), channel_id=1, source_target_pairs={{0,16},{16,32},{32,48},{48,64},{64,80},{80,96},{96,112},{112,128},... | collective-permute-start | bytes 528392 | tf_op jit(solution)/shard_map/ppermute | solution.py:372
  6.5 6.0 %collective-permute-start.13 = (f32[344,128]{1,0:T(8,128)S(1)}, f32[344,128]{1,0:T(8,128)S(1)}, u32[]{:S(2)}, u32[]{:S(2)}) collective-permute-start(f32[344,128]{1,0:T(8,128)S(1)} %get-tuple-element.309.own_ref), channel_id=1, source_target_pairs={{0,496},{16,0},{32,16},{48,32},{64,48},{80,64},{96,80},{112,96},{1... | collective-permute-start | bytes 528392 | tf_op jit(solution)/shard_map/ppermute | solution.py:372
  12.5 2.9 %collective-permute-start.14 = (f32[24,128]{1,0:T(8,128)S(1)}, f32[24,128]{1,0:T(8,128)S(1)}, u32[]{:S(2)}, u32[]{:S(2)}) collective-permute-start(f32[24,128]{1,0:T(8,128)S(1)} %get-tuple-element.311), channel_id=1, source_target_pairs={{0,1},{1,2},{2,3},{3,4},{4,5},{5,6},{6,7},{7,8},{8,9},{9,10},{10,1... | collective-permute-start | bytes 36872 | tf_op jit(solution)/shard_map/ppermute | solution.py:372
  15.4 3.1 %collective-permute-start.15 = (f32[24,128]{1,0:T(8,128)S(1)}, f32[24,128]{1,0:T(8,128)S(1)}, u32[]{:S(2)}, u32[]{:S(2)}) collective-permute-start(f32[24,128]{1,0:T(8,128)S(1)} %get-tuple-element.312), channel_id=1, source_target_pairs={{0,15},{1,0},{2,1},{3,2},{4,3},{5,4},{6,5},{7,6},{8,7},{9,8},{10,9... | collective-permute-start | bytes 36872 | tf_op jit(solution)/shard_map/ppermute | solution.py:372
  18.5 1.4 %column_inverses.1.inverses_ref = f32[264,128]{1,0:T(8,128)S(1)} custom-call(f32[1,129]{1,0:T(1,128)} %bitcast.95), custom_call_target="tpu_custom_call" | custom-call | tf_op jit(solution)/shard_map/column_inverses/pallas_call | solution.py:134
  19.9 0.0 collective-permute-done.14.left_ref
  19.9 0.0 collective-permute-done.15.right_ref
  19.9 0.0 collective-permute-done.12.below_ref.near_below_ref
  19.9 0.0 collective-permute-done.13.above_ref.near_above_ref
  19.9 2.1 %first_substep.1 = (f32[8,128,128]{2,1,0:T(8,128)S(1)}, f32[368,128]{1,0:T(8,128)S(1)}, f32[368,128]{1,0:T(8,128)S(1)}, f32[9,8,128]{2,1,0:T(8,128)S(1)}, f32[24,128]{1,0:T(8,128)S(1)}) custom-call(f32[8,128,128]{2,1,0:T(8,128)S(1)} %get-tuple-element.308.enthalpy_ref, f32[344,128]{1,0:T(8,128)S(1)} %get-tuple-element.309.own_ref, ...), custom_call_target="tpu_custom_call" | custom-call | tf_op jit(solution)/shard_map/first_substep/pallas_call | solution.py:844
  22.0 1.9 %collective-permute-start.16 = (f32[368,128]{1,0:T(8,128)S(1)}, f32[368,128]{1,0:T(8,128)S(1)}, u32[]{:S(2)}, u32[]{:S(2)}) collective-permute-start(f32[368,128]{1,0:T(8,128)S(1)} %get-tuple-element.314), channel_id=1, source_target_pairs={{0,16},{16,32},{32,48},{48,64},{64,80},{80,96},{96,112},{112,128},... | collective-permute-start | bytes 565256 | tf_op jit(solution)/shard_map/ppermute | solution.py:372
  24.0 6.7 %collective-permute-start.17 = (f32[368,128]{1,0:T(8,128)S(1)}, f32[368,128]{1,0:T(8,128)S(1)}, u32[]{:S(2)}, u32[]{:S(2)}) collective-permute-start(f32[368,128]{1,0:T(8,128)S(1)} %get-tuple-element.315), channel_id=1, source_target_pairs={{0,496},{16,0},{32,16},{48,32},{64,48},{80,64},{96,80},{112,96},{1... | collective-permute-start | bytes 565256 | tf_op jit(solution)/shard_map/ppermute | solution.py:372
  30.6 1.9 %collective-permute-start.19 = (f32[24,128]{1,0:T(8,128)S(1)}, f32[24,128]{1,0:T(8,128)S(1)}, u32[]{:S(2)}, u32[]{:S(2)}) collective-permute-start(f32[24,128]{1,0:T(8,128)S(1)} %get-tuple-element.316.sums_ref), channel_id=1, source_target_pairs={{0,480},{16,496},{32,0},{48,16},{64,32},{80,48},{96,64},{112,80},{... | collective-permute-start | bytes 36872 | tf_op jit(solution)/shard_map/ppermute | solution.py:372
  32.6 4.3 %collective-permute-start.18 = (f32[24,128]{1,0:T(8,128)S(1)}, f32[24,128]{1,0:T(8,128)S(1)}, u32[]{:S(2)}, u32[]{:S(2)}) collective-permute-start(f32[24,128]{1,0:T(8,128)S(1)} %get-tuple-element.316.sums_ref), channel_id=1, source_target_pairs={{0,32},{16,48},{32,64},{48,80},{64,96},{80,112},{96,128},{112,144}... | collective-permute-start | bytes 36872 | tf_op jit(solution)/shard_map/ppermute | solution.py:372
  36.8 0.6 tiles.1
  37.4 0.0 collective-permute-done.19.far_above_ref
  37.5 3.8 %collective-permute-done.18.far_below_ref = f32[24,128]{1,0:T(8,128)S(1)} collective-permute-done((f32[24,128]{1,0:T(8,128)S(1)}, f32[24,128]{1,0:T(8,128)S(1)}, u32[]{:S(2)}, u32[]{:S(2)}) %collective-permute-start.18) | collective-permute-done | bytes 12320 | tf_op jit(solution)/shard_map/ppermute | solution.py:372
  41.2 0.0 collective-permute-done.16.below_ref
  41.2 0.0 collective-permute-done.17.above_ref
  41.3 0.2 gather.1
  41.4 2.8 %collective-permute-start.20 = (f32[96,128]{1,0:T(8,128)S(1)}, f32[96,128]{1,0:T(8,128)S(1)}, u32[]{:S(2)}, u32[]{:S(2)}) collective-permute-start(f32[96,128]{1,0:T(8,128)S(1)} %get-tuple-element.319), channel_id=1, source_target_pairs={{0,1},{1,2},{2,3},{3,4},{4,5},{5,6},{6,7},{7,8},{8,9},{9,10},{10,1... | collective-permute-start | bytes 147464 | tf_op jit(solution)/shard_map/ppermute | solution.py:372
  44.2 2.3 %collective-permute-start.21 = (f32[96,128]{1,0:T(8,128)S(1)}, f32[96,128]{1,0:T(8,128)S(1)}, u32[]{:S(2)}, u32[]{:S(2)}) collective-permute-start(f32[96,128]{1,0:T(8,128)S(1)} %get-tuple-element.320), channel_id=1, source_target_pairs={{0,15},{1,0},{2,1},{3,2},{4,3},{5,4},{6,5},{7,6},{8,7},{9,8},{10,9... | collective-permute-start | bytes 147464 | tf_op jit(solution)/shard_map/ppermute | solution.py:372
  46.5 0.7 collective-permute-done.20.left_ref
  47.2 0.5 collective-permute-done.21.right_ref
  47.7 2.0 %first_picard.1 = (f32[12,24,256]{2,1,0:T(8,128)S(1)}, f32[6,24,256]{2,1,0:T(8,128)S(1)}, f32[16,128]{1,0:T(8,128)S(1)}, f32[8,128]{1,0:T(8,128)S(1)}) custom-call(f32[560,128]{1,0:T(8,128)S(1)} %get-tuple-element.322.mine_ref, f32[96,128]{1,0:T(8,128)S(1)} %collective-permute-done.20.left_ref, f32[96,128]{1,0:T(8,128)S(1)} %collective-permute-done.21.right_ref, ...), custom_call_target="tpu_custom_call" | custom-call | tf_op jit(solution)/shard_map/first_picard/pallas_call | solution.py:379
  49.8 16.7 %all_to_all.34 = f32[16,1,128]{2,1,0:T(1,128)S(1)} all-to-all(f32[16,1,128]{2,1,0:T(1,128)S(1)} %bitcast.80), channel_id=1, replica_groups=mesh['gx_0'=4,'gx_1'=8,'gy_0'=8,'gy_1'=2] {'gy_0','gy_1'}, dimensions={0} | all-to-all | bytes 16384 | tf_op jit(solution)/shard_map/all_to_all | solution.py:365
  66.5 11.9 %all_to_all.35 = f32[32,1,128]{2,1,0:T(1,128)S(1)} all-to-all(f32[32,1,128]{2,1,0:T(1,128)S(1)} %broadcast_in_dim.39), channel_id=1, replica_groups=mesh['gx_0'=4,'gx_1'=8,'gy_0'=8,'gy_1'=2] {'gx_0','gx_1'}, dimensions={0} | all-to-all | bytes 32768 | tf_op jit(solution)/shard_map/all_to_all | solution.py:367
  78.4 1.6 %second_picard.1 = (f32[12,8,128]{2,1,0:T(8,128)S(1)}, f32[2,8,128]{2,1,0:T(8,128)S(1)}, f32[16,128]{1,0:T(8,128)S(1)}, f32[8,128]{1,0:T(8,128)S(1)}) custom-call(f32[32,128]{1,0:T(8,128)S(1)} %bitcast.78, f32[12,24,256]{2,1,0:T(8,128)S(1)} %get-tuple-element.324.basis_ref, f32[6,24,256]{2,1,0:T(8,128)S(1)} %get-tuple-element.325.fixed_ref), custom_call_target="tpu_custom_call" | custom-call | tf_op jit(solution)/shard_map/second_picard/pallas_call | solution.py:389
  80.0 11.6 %all_to_all.36 = f32[16,1,128]{2,1,0:T(1,128)S(1)} all-to-all(f32[16,1,128]{2,1,0:T(1,128)S(1)} %bitcast.79), channel_id=1, replica_groups=mesh['gx_0'=4,'gx_1'=8,'gy_0'=8,'gy_1'=2] {'gy_0','gy_1'}, dimensions={0} | all-to-all | bytes 16384 | tf_op jit(solution)/shard_map/all_to_all | solution.py:365
  91.6 0.6 broadcast_in_dim.40
  92.2 3.8 %all-to-all-start.3 = ((f32[32,1,128]{2,1,0:T(1,128)}), f32[32,1,128]{2,1,0:T(1,128)S(1)}, u32[]{:S(2)}, u32[]{:S(2)}) async-start(f32[32,1,128]{2,1,0:T(1,128)} %broadcast_in_dim.40), calls=%async_computation.3 | async-start | bytes 32768 | tf_op jit(solution)/shard_map/all_to_all | solution.py:367
  96.0 2.6 %second_substep.1 = f32[1024,128]{1,0:T(8,128)} custom-call(f32[8,128,128]{2,1,0:T(8,128)S(1)} %get-tuple-element.313.planes_ref.enthalpy_ref, f32[344,128]{1,0:T(8,128)S(1)} %get-tuple-element.309.own_ref, f32[368,128]{1,0:T(8,128)S(1)} %collective-permute-done.16.below_ref, f32[368,128]{1,0:T(8,128)S(1)} %collective-permute-done.17.above_ref, ...), custom_call_target="tpu_custom_call" | custom-call | tf_op jit(solution)/shard_map/second_substep/pallas_call | solution.py:869
  98.6 6.1 %all-to-all-done.3 = f32[32,1,128]{2,1,0:T(1,128)S(1)} async-done(((f32[32,1,128]{2,1,0:T(1,128)}), f32[32,1,128]{2,1,0:T(1,128)S(1)}, u32[]{:S(2)}, u32[]{:S(2)}) %all-to-all-start.3) | async-done | bytes 16416 | tf_op jit(solution)/shard_map/all_to_all | solution.py:367
  104.7 0.0 copy-start.1
  104.7 0.0 copy-start.2
  104.7 0.0 copy-start.3
  104.7 0.0 copy-start.5
  104.7 0.0 copy-start.6
  104.7 0.8 last_picard.1
  105.5 0.0 copy-start
  106.1 0.0 copy-done.1
  106.1 0.0 copy-done.2
  106.2 0.0 copy-done.3
  106.2 0.0 copy-done.4
  106.2 0.0 copy-done.5
  106.2 0.0 copy-done.6
  106.2 0.0 copy-done
  (5 shorter events, 0.1 us)
Async XLA Ops:
  2.4 17.5 %collective-permute-start.12 = (f32[344,128]{1,0:T(8,128)S(1)}, f32[344,128]{1,0:T(8,128)S(1)}, u32[]{:S(2)}, u32[]{:S(2)}) collective-permute-start(f32[344,128]{1,0:T(8,128)S(1)} %get-tuple-element.310), channel_id=1, source_target_pairs={{0,16},{16,32},{32,48},{48,64},{64,80},{80,96},{96,112},{112,128},... | collective-permute-start | bytes 528392 | tf_op jit(solution)/shard_map/ppermute | solution.py:372
  6.5 13.5 %collective-permute-start.13 = (f32[344,128]{1,0:T(8,128)S(1)}, f32[344,128]{1,0:T(8,128)S(1)}, u32[]{:S(2)}, u32[]{:S(2)}) collective-permute-start(f32[344,128]{1,0:T(8,128)S(1)} %get-tuple-element.309.own_ref), channel_id=1, source_target_pairs={{0,496},{16,0},{32,16},{48,32},{64,48},{80,64},{96,80},{112,96},{1... | collective-permute-start | bytes 528392 | tf_op jit(solution)/shard_map/ppermute | solution.py:372
  12.5 7.4 %collective-permute-start.14 = (f32[24,128]{1,0:T(8,128)S(1)}, f32[24,128]{1,0:T(8,128)S(1)}, u32[]{:S(2)}, u32[]{:S(2)}) collective-permute-start(f32[24,128]{1,0:T(8,128)S(1)} %get-tuple-element.311), channel_id=1, source_target_pairs={{0,1},{1,2},{2,3},{3,4},{4,5},{5,6},{6,7},{7,8},{8,9},{9,10},{10,1... | collective-permute-start | bytes 36872 | tf_op jit(solution)/shard_map/ppermute | solution.py:372
  15.4 4.5 %collective-permute-start.15 = (f32[24,128]{1,0:T(8,128)S(1)}, f32[24,128]{1,0:T(8,128)S(1)}, u32[]{:S(2)}, u32[]{:S(2)}) collective-permute-start(f32[24,128]{1,0:T(8,128)S(1)} %get-tuple-element.312), channel_id=1, source_target_pairs={{0,15},{1,0},{2,1},{3,2},{4,3},{5,4},{6,5},{7,6},{8,7},{9,8},{10,9... | collective-permute-start | bytes 36872 | tf_op jit(solution)/shard_map/ppermute | solution.py:372
  22.0 19.2 %collective-permute-start.16 = (f32[368,128]{1,0:T(8,128)S(1)}, f32[368,128]{1,0:T(8,128)S(1)}, u32[]{:S(2)}, u32[]{:S(2)}) collective-permute-start(f32[368,128]{1,0:T(8,128)S(1)} %get-tuple-element.314), channel_id=1, source_target_pairs={{0,16},{16,32},{32,48},{48,64},{64,80},{80,96},{96,112},{112,128},... | collective-permute-start | bytes 565256 | tf_op jit(solution)/shard_map/ppermute | solution.py:372
  24.0 17.3 %collective-permute-start.17 = (f32[368,128]{1,0:T(8,128)S(1)}, f32[368,128]{1,0:T(8,128)S(1)}, u32[]{:S(2)}, u32[]{:S(2)}) collective-permute-start(f32[368,128]{1,0:T(8,128)S(1)} %get-tuple-element.315), channel_id=1, source_target_pairs={{0,496},{16,0},{32,16},{48,32},{64,48},{80,64},{96,80},{112,96},{1... | collective-permute-start | bytes 565256 | tf_op jit(solution)/shard_map/ppermute | solution.py:372
  30.6 6.8 %collective-permute-start.19 = (f32[24,128]{1,0:T(8,128)S(1)}, f32[24,128]{1,0:T(8,128)S(1)}, u32[]{:S(2)}, u32[]{:S(2)}) collective-permute-start(f32[24,128]{1,0:T(8,128)S(1)} %get-tuple-element.316.sums_ref), channel_id=1, source_target_pairs={{0,480},{16,496},{32,0},{48,16},{64,32},{80,48},{96,64},{112,80},{... | collective-permute-start | bytes 36872 | tf_op jit(solution)/shard_map/ppermute | solution.py:372
  32.6 8.7 %collective-permute-start.18 = (f32[24,128]{1,0:T(8,128)S(1)}, f32[24,128]{1,0:T(8,128)S(1)}, u32[]{:S(2)}, u32[]{:S(2)}) collective-permute-start(f32[24,128]{1,0:T(8,128)S(1)} %get-tuple-element.316.sums_ref), channel_id=1, source_target_pairs={{0,32},{16,48},{32,64},{48,80},{64,96},{80,112},{96,128},{112,144}... | collective-permute-start | bytes 36872 | tf_op jit(solution)/shard_map/ppermute | solution.py:372
  41.4 5.8 %collective-permute-start.20 = (f32[96,128]{1,0:T(8,128)S(1)}, f32[96,128]{1,0:T(8,128)S(1)}, u32[]{:S(2)}, u32[]{:S(2)}) collective-permute-start(f32[96,128]{1,0:T(8,128)S(1)} %get-tuple-element.319), channel_id=1, source_target_pairs={{0,1},{1,2},{2,3},{3,4},{4,5},{5,6},{6,7},{7,8},{8,9},{9,10},{10,1... | collective-permute-start | bytes 147464 | tf_op jit(solution)/shard_map/ppermute | solution.py:372
  44.2 3.5 %collective-permute-start.21 = (f32[96,128]{1,0:T(8,128)S(1)}, f32[96,128]{1,0:T(8,128)S(1)}, u32[]{:S(2)}, u32[]{:S(2)}) collective-permute-start(f32[96,128]{1,0:T(8,128)S(1)} %get-tuple-element.320), channel_id=1, source_target_pairs={{0,15},{1,0},{2,1},{3,2},{4,3},{5,4},{6,5},{7,6},{8,7},{9,8},{10,9... | collective-permute-start | bytes 147464 | tf_op jit(solution)/shard_map/ppermute | solution.py:372
  92.2 12.5 %all-to-all-start.3 = ((f32[32,1,128]{2,1,0:T(1,128)}), f32[32,1,128]{2,1,0:T(1,128)S(1)}, u32[]{:S(2)}, u32[]{:S(2)}) async-start(f32[32,1,128]{2,1,0:T(1,128)} %broadcast_in_dim.40), calls=%async_computation.3 | async-start | bytes 32768 | tf_op jit(solution)/shard_map/all_to_all | solution.py:367
  104.7 1.5 %copy-start.1 = (f32[8,128]{1,0:T(8,128)S(1)}, f32[8,128]{1,0:T(8,128)}, u32[]{:S(2)}) copy-start(f32[8,128]{1,0:T(8,128)} %height_ref.1) | copy-start | bytes 12292
  104.7 1.5 %copy-start.2 = (s32[8,128]{1,0:T(8,128)S(1)}, s32[8,128]{1,0:T(8,128)}, u32[]{:S(2)}) copy-start(s32[8,128]{1,0:T(8,128)} %code_ref.1) | copy-start | bytes 12292
  104.7 1.5 %copy-start.3 = (f32[2,8,128]{2,1,0:T(8,128)S(1)}, f32[2,8,128]{2,1,0:T(8,128)}, u32[]{:S(2)}) copy-start(f32[2,8,128]{2,1,0:T(8,128)} %speed_ref.1) | copy-start | bytes 24580
  104.7 1.5 %copy-start.4 = (f32[8,128]{1,0:T(8,128)S(1)}, f32[8,128]{1,0:T(8,128)}, u32[]{:S(2)}) copy-start(f32[8,128]{1,0:T(8,128)} %friction_ref.1) | copy-start | bytes 12292
  104.7 1.5 %copy-start.5 = (s32[8,128]{1,0:T(8,128)S(1)}, s32[8,128]{1,0:T(8,128)}, u32[]{:S(2)}) copy-start(s32[8,128]{1,0:T(8,128)} %grounded_ref.1) | copy-start | bytes 12292
  104.7 1.5 %copy-start.6 = (s32[8,128]{1,0:T(8,128)S(1)}, s32[8,128]{1,0:T(8,128)}, u32[]{:S(2)}) copy-start(s32[8,128]{1,0:T(8,128)} %ice_ref.1) | copy-start | bytes 12292
  105.5 0.7 copy-start

commit v10 on v9

--- a/solution.py
+++ b/solution.py
@@ -22,7 +22,7 @@
 
 MIDDLE = 17.0
 RADIUS = 17.0
-PIVOT_FLOOR = 2e-4
+PIVOT_FLOOR = 1e-2
 OWN = 16
 SIDE = 64
 
@@ -474,8 +474,6 @@
     flux_ref,
     low_ref,
     high_ref,
-    left_ref,
-    right_ref,
     planes_ref,
 ):
     planes = [enthalpy_ref[pl.ds(x, 128, stride=8), :] for x in range(8)]
@@ -502,11 +500,6 @@
         out_ref[128:256] = planes[pair[1]]
         for k, value in enumerate(statics):
             out_ref[256 + 8 * k : 264 + 8 * k] = value
-    first, last = column_tiles(planes)
-    left_ref[0:16] = first
-    left_ref[16:24] = speed_ref[1]
-    right_ref[0:16] = last
-    right_ref[16:24] = speed_ref[1]
 
 
 def line_weights(low_face, high_face):
@@ -639,8 +632,19 @@
     return jnp.concatenate(rows, axis=0)
 
 
-def tiles_kernel(planes_ref, first_ref, last_ref):
-    first_ref[...], last_ref[...] = column_tiles([planes_ref[x] for x in range(8)])
+def tiles_kernel(planes_ref, own_ref, first_ref, last_ref):
+    tiles = column_tiles([planes_ref[x] for x in range(8)])
+    for out_ref, tile in zip((first_ref, last_ref), tiles):
+        out_ref[0:16] = tile
+        out_ref[16:24] = own_ref[304:312]
+
+
+def edge_columns(planes, own):
+    return pl.pallas_call(
+        tiles_kernel,
+        out_shape=(kept(24, 128), kept(24, 128)),
+        name="tiles",
+    )(planes, own)
 
 
 def gather_kernel(
@@ -658,8 +662,8 @@
     left_ref,
     right_ref,
 ):
-    left_ref[0:16] = first_ref[...]
-    right_ref[0:16] = last_ref[...]
+    left_ref[0:16] = first_ref[0:16]
+    right_ref[0:16] = last_ref[0:16]
     blocks = (below_ref, near_below_ref, own_ref, near_above_ref, above_ref)
     fields = []
     for k in range(11):
@@ -815,13 +819,11 @@
 ):
     f32 = jnp.float32
     flat = enthalpy.reshape(1024, 128)
-    own, high, first, last, planes = pl.pallas_call(
+    own, high, planes = pl.pallas_call(
         pack_kernel,
         out_shape=(
             kept(344, 128),
             kept(344, 128),
-            kept(24, 128),
-            kept(24, 128),
             kept(8, 128, 128),
         ),
         name="pack",
@@ -837,9 +839,9 @@
         surface_enthalpy,
         geo_flux,
     )
-    own = on_chip(own)
+    own, planes = (on_chip(own), on_chip(planes))
     near = beside(own, high, GX)
-    near_sides = beside(first, last, GY)
+    near_sides = beside(*edge_columns(planes, own), GY)
     inverses = on_chip(column_inverses(kappa))
     current, low, high, weights, sums = pl.pallas_call(
         first_substep_kernel,
@@ -851,15 +853,11 @@
             kept(24, 128),
         ),
         name="first_substep",
-    )(on_chip(planes), own, *near, *near_sides, inverses)
+    )(planes, own, *near, *near_sides, inverses)
     around = beside(low, high, GX)
     far = (on_chip(shifted(sums, GX, 2)), on_chip(shifted(sums, GX, -2)))
     current = on_chip(current)
-    first, last = pl.pallas_call(
-        tiles_kernel,
-        out_shape=(kept(16, 128), kept(16, 128)),
-        name="tiles",
-    )(current)
+    first, last = edge_columns(current, own)
     mine, first, last = pl.pallas_call(
         gather_kernel,
         out_shape=(kept(560, 128), kept(96, 128), kept(96, 128)),

time: 107 us -> 106 us (level)
  transfers between devices with their start and end apart: 11 -> 11, of which waited for: 4 -> 4; matrix products, arithmetic and copies ran while one was open for 0% -> 0% of each run, Pallas kernels for 4% -> 5%
where the time goes in v10:
time: 106 us
  blocking collectives  40 us (38%)
  starting transfers between devices  39.5 us (37%)
  Pallas kernels  13 us (12%)
  waiting for transfers between devices  10.8 us (10%)
  between operations  1.43 us (1%)
    ppermute x10, starting transfers between devices, shifted(): lax.ppermute(array, axis, [(i, (i + by) % size) for i in range(size)])  35.7 us
    all_to_all x2, blocking collectives, over_all(): part = lax.all_to_all(sums, GY, 0, 0, tiled=True)  28.1 us
    all_to_all x1, blocking collectives, over_all(): return lax.all_to_all(part, GX, 0, 0, tiled=True)  11.9 us
    all_to_all x1, waiting for transfers between devices, over_all(): return lax.all_to_all(part, GX, 0, 0, tiled=True)  6.12 us
    ppermute x10, waiting for transfers between devices, shifted(): lax.ppermute(array, axis, [(i, (i + by) % size) for i in range(size)])  4.69 us
    all_to_all x1, starting transfers between devices, over_all(): return lax.all_to_all(part, GX, 0, 0, tiled=True)  3.78 us
    pallas_call x1, Pallas kernels, shards(): pl.pallas_call(second_substep_kernel, out_shape=jax.ShapeDtypeStruct((102...  2.55 us
  transfers between devices with their start and end apart: 11, of which 4 were waited for; matrix products, arithmetic and copies ran while one was open for 0% of the time, Pallas kernels for 5%

profile of v10, /device:TPU:1, one launch (start us, length us, event | category | flops | bytes accessed | tf_op | source)
XLA Modules:
  0.0 105.6 jit_solution(5212583127990019494)
XLA Ops:
  0.6 1.2 %pack.1 = (f32[344,128]{1,0:T(8,128)S(1)}, f32[344,128]{1,0:T(8,128)S(1)}, f32[8,128,128]{2,1,0:T(8,128)S(1)}) custom-call(f32[1024,128]{1,0:T(8,128)} %bitcast.85, f32[2,8,128]{2,1,0:T(8,128)} %speed_ref.1, f32[8,128]{1,0:T(8,128)} %thick_ref.1, f32[8,128]{1,0:T(8,128)} %height_ref.1, f32[8,128]{1,0:T(8,128)} %friction_ref.1, s32[8,128]{1,0:T(8,128)} %ice_ref.1, ...), custom_call_target="tpu_custom_call" | custom-call | tf_op jit(solution)/shard_map/pack/pallas_call | solution.py:822
  1.9 4.0 %collective-permute-start.12 = (f32[344,128]{1,0:T(8,128)S(1)}, f32[344,128]{1,0:T(8,128)S(1)}, u32[]{:S(2)}, u32[]{:S(2)}) collective-permute-start(f32[344,128]{1,0:T(8,128)S(1)} %get-tuple-element.310), channel_id=1, source_target_pairs={{0,16},{16,32},{32,48},{48,64},{64,80},{80,96},{96,112},{112,128},... | collective-permute-start | bytes 528392 | tf_op jit(solution)/shard_map/ppermute | solution.py:372
  5.9 6.0 %collective-permute-start.13 = (f32[344,128]{1,0:T(8,128)S(1)}, f32[344,128]{1,0:T(8,128)S(1)}, u32[]{:S(2)}, u32[]{:S(2)}) collective-permute-start(f32[344,128]{1,0:T(8,128)S(1)} %get-tuple-element.309.own_ref), channel_id=1, source_target_pairs={{0,496},{16,0},{32,16},{48,32},{64,48},{80,64},{96,80},{112,96},{1... | collective-permute-start | bytes 528392 | tf_op jit(solution)/shard_map/ppermute | solution.py:372
  11.9 0.6 tiles.2
  12.5 3.0 %collective-permute-start.14 = (f32[24,128]{1,0:T(8,128)S(1)}, f32[24,128]{1,0:T(8,128)S(1)}, u32[]{:S(2)}, u32[]{:S(2)}) collective-permute-start(f32[24,128]{1,0:T(8,128)S(1)} %get-tuple-element.311), channel_id=1, source_target_pairs={{0,1},{1,2},{2,3},{3,4},{4,5},{5,6},{6,7},{7,8},{8,9},{9,10},{10,1... | collective-permute-start | bytes 36872 | tf_op jit(solution)/shard_map/ppermute | solution.py:372
  15.5 3.0 %collective-permute-start.15 = (f32[24,128]{1,0:T(8,128)S(1)}, f32[24,128]{1,0:T(8,128)S(1)}, u32[]{:S(2)}, u32[]{:S(2)}) collective-permute-start(f32[24,128]{1,0:T(8,128)S(1)} %get-tuple-element.312), channel_id=1, source_target_pairs={{0,15},{1,0},{2,1},{3,2},{4,3},{5,4},{6,5},{7,6},{8,7},{9,8},{10,9... | collective-permute-start | bytes 36872 | tf_op jit(solution)/shard_map/ppermute | solution.py:372
  18.5 1.4 %column_inverses.1.inverses_ref = f32[264,128]{1,0:T(8,128)S(1)} custom-call(f32[1,129]{1,0:T(1,128)} %bitcast.95), custom_call_target="tpu_custom_call" | custom-call | tf_op jit(solution)/shard_map/column_inverses/pallas_call | solution.py:134
  19.9 0.0 collective-permute-done.14.left_ref
  19.9 0.0 collective-permute-done.15.right_ref
  19.9 0.0 collective-permute-done.12.below_ref.near_below_ref
  19.9 0.0 collective-permute-done.13.above_ref.near_above_ref
  20.0 2.1 %first_substep.1 = (f32[8,128,128]{2,1,0:T(8,128)S(1)}, f32[368,128]{1,0:T(8,128)S(1)}, f32[368,128]{1,0:T(8,128)S(1)}, f32[9,8,128]{2,1,0:T(8,128)S(1)}, f32[24,128]{1,0:T(8,128)S(1)}) custom-call(f32[8,128,128]{2,1,0:T(8,128)S(1)} %get-tuple-element.308.planes_ref.enthalpy_ref, f32[344,128]{1,0:T(8,128)S(1)} %get-tuple-element.309.own_ref, ...), custom_call_target="tpu_custom_call" | custom-call | tf_op jit(solution)/shard_map/first_substep/pallas_call | solution.py:846
  22.0 1.9 %collective-permute-start.16 = (f32[368,128]{1,0:T(8,128)S(1)}, f32[368,128]{1,0:T(8,128)S(1)}, u32[]{:S(2)}, u32[]{:S(2)}) collective-permute-start(f32[368,128]{1,0:T(8,128)S(1)} %get-tuple-element.314), channel_id=1, source_target_pairs={{0,16},{16,32},{32,48},{48,64},{64,80},{80,96},{96,112},{112,128},... | collective-permute-start | bytes 565256 | tf_op jit(solution)/shard_map/ppermute | solution.py:372
  24.0 6.7 %collective-permute-start.17 = (f32[368,128]{1,0:T(8,128)S(1)}, f32[368,128]{1,0:T(8,128)S(1)}, u32[]{:S(2)}, u32[]{:S(2)}) collective-permute-start(f32[368,128]{1,0:T(8,128)S(1)} %get-tuple-element.315), channel_id=1, source_target_pairs={{0,496},{16,0},{32,16},{48,32},{64,48},{80,64},{96,80},{112,96},{1... | collective-permute-start | bytes 565256 | tf_op jit(solution)/shard_map/ppermute | solution.py:372
  30.6 1.9 %collective-permute-start.19 = (f32[24,128]{1,0:T(8,128)S(1)}, f32[24,128]{1,0:T(8,128)S(1)}, u32[]{:S(2)}, u32[]{:S(2)}) collective-permute-start(f32[24,128]{1,0:T(8,128)S(1)} %get-tuple-element.316.sums_ref), channel_id=1, source_target_pairs={{0,480},{16,496},{32,0},{48,16},{64,32},{80,48},{96,64},{112,80},{... | collective-permute-start | bytes 36872 | tf_op jit(solution)/shard_map/ppermute | solution.py:372
  32.6 4.3 %collective-permute-start.18 = (f32[24,128]{1,0:T(8,128)S(1)}, f32[24,128]{1,0:T(8,128)S(1)}, u32[]{:S(2)}, u32[]{:S(2)}) collective-permute-start(f32[24,128]{1,0:T(8,128)S(1)} %get-tuple-element.316.sums_ref), channel_id=1, source_target_pairs={{0,32},{16,48},{32,64},{48,80},{64,96},{80,112},{96,128},{112,144}... | collective-permute-start | bytes 36872 | tf_op jit(solution)/shard_map/ppermute | solution.py:372
  36.8 0.6 tiles.3
  37.4 0.0 collective-permute-done.19.far_above_ref
  37.5 3.8 %collective-permute-done.18.far_below_ref = f32[24,128]{1,0:T(8,128)S(1)} collective-permute-done((f32[24,128]{1,0:T(8,128)S(1)}, f32[24,128]{1,0:T(8,128)S(1)}, u32[]{:S(2)}, u32[]{:S(2)}) %collective-permute-start.18) | collective-permute-done | bytes 12320 | tf_op jit(solution)/shard_map/ppermute | solution.py:372
  41.2 0.0 collective-permute-done.16.below_ref
  41.2 0.0 collective-permute-done.17.above_ref
  41.2 0.2 gather.1
  41.4 2.2 %collective-permute-start.20 = (f32[96,128]{1,0:T(8,128)S(1)}, f32[96,128]{1,0:T(8,128)S(1)}, u32[]{:S(2)}, u32[]{:S(2)}) collective-permute-start(f32[96,128]{1,0:T(8,128)S(1)} %get-tuple-element.319), channel_id=1, source_target_pairs={{0,1},{1,2},{2,3},{3,4},{4,5},{5,6},{6,7},{7,8},{8,9},{9,10},{10,1... | collective-permute-start | bytes 147464 | tf_op jit(solution)/shard_map/ppermute | solution.py:372
  43.6 2.7 %collective-permute-start.21 = (f32[96,128]{1,0:T(8,128)S(1)}, f32[96,128]{1,0:T(8,128)S(1)}, u32[]{:S(2)}, u32[]{:S(2)}) collective-permute-start(f32[96,128]{1,0:T(8,128)S(1)} %get-tuple-element.320), channel_id=1, source_target_pairs={{0,15},{1,0},{2,1},{3,2},{4,3},{5,4},{6,5},{7,6},{8,7},{9,8},{10,9... | collective-permute-start | bytes 147464 | tf_op jit(solution)/shard_map/ppermute | solution.py:372
  46.4 0.7 collective-permute-done.20.left_ref
  47.1 0.2 collective-permute-done.21.right_ref
  47.2 2.0 %first_picard.1 = (f32[12,24,256]{2,1,0:T(8,128)S(1)}, f32[6,24,256]{2,1,0:T(8,128)S(1)}, f32[16,128]{1,0:T(8,128)S(1)}, f32[8,128]{1,0:T(8,128)S(1)}) custom-call(f32[560,128]{1,0:T(8,128)S(1)} %get-tuple-element.322.mine_ref, f32[96,128]{1,0:T(8,128)S(1)} %collective-permute-done.20.left_ref, f32[96,128]{1,0:T(8,128)S(1)} %collective-permute-done.21.right_ref, ...), custom_call_target="tpu_custom_call" | custom-call | tf_op jit(solution)/shard_map/first_picard/pallas_call | solution.py:379
  49.3 16.6 %all_to_all.34 = f32[16,1,128]{2,1,0:T(1,128)S(1)} all-to-all(f32[16,1,128]{2,1,0:T(1,128)S(1)} %bitcast.80), channel_id=1, replica_groups=mesh['gx_0'=4,'gx_1'=8,'gy_0'=8,'gy_1'=2] {'gy_0','gy_1'}, dimensions={0} | all-to-all | bytes 16384 | tf_op jit(solution)/shard_map/all_to_all | solution.py:365
  65.9 11.9 %all_to_all.35 = f32[32,1,128]{2,1,0:T(1,128)S(1)} all-to-all(f32[32,1,128]{2,1,0:T(1,128)S(1)} %broadcast_in_dim.39), channel_id=1, replica_groups=mesh['gx_0'=4,'gx_1'=8,'gy_0'=8,'gy_1'=2] {'gx_0','gx_1'}, dimensions={0} | all-to-all | bytes 32768 | tf_op jit(solution)/shard_map/all_to_all | solution.py:367
  77.8 1.6 %second_picard.1 = (f32[12,8,128]{2,1,0:T(8,128)S(1)}, f32[2,8,128]{2,1,0:T(8,128)S(1)}, f32[16,128]{1,0:T(8,128)S(1)}, f32[8,128]{1,0:T(8,128)S(1)}) custom-call(f32[32,128]{1,0:T(8,128)S(1)} %bitcast.78, f32[12,24,256]{2,1,0:T(8,128)S(1)} %get-tuple-element.324.basis_ref, f32[6,24,256]{2,1,0:T(8,128)S(1)} %get-tuple-element.325.fixed_ref), custom_call_target="tpu_custom_call" | custom-call | tf_op jit(solution)/shard_map/second_picard/pallas_call | solution.py:389
  79.4 11.6 %all_to_all.36 = f32[16,1,128]{2,1,0:T(1,128)S(1)} all-to-all(f32[16,1,128]{2,1,0:T(1,128)S(1)} %bitcast.79), channel_id=1, replica_groups=mesh['gx_0'=4,'gx_1'=8,'gy_0'=8,'gy_1'=2] {'gy_0','gy_1'}, dimensions={0} | all-to-all | bytes 16384 | tf_op jit(solution)/shard_map/all_to_all | solution.py:365
  91.0 0.6 broadcast_in_dim.40
  91.6 3.8 %all-to-all-start.3 = ((f32[32,1,128]{2,1,0:T(1,128)}), f32[32,1,128]{2,1,0:T(1,128)S(1)}, u32[]{:S(2)}, u32[]{:S(2)}) async-start(f32[32,1,128]{2,1,0:T(1,128)} %broadcast_in_dim.40), calls=%async_computation.3 | async-start | bytes 32768 | tf_op jit(solution)/shard_map/all_to_all | solution.py:367
  95.4 2.5 %second_substep.1 = f32[1024,128]{1,0:T(8,128)} custom-call(f32[8,128,128]{2,1,0:T(8,128)S(1)} %get-tuple-element.313.planes_ref.enthalpy_ref, f32[344,128]{1,0:T(8,128)S(1)} %get-tuple-element.309.own_ref, f32[368,128]{1,0:T(8,128)S(1)} %collective-permute-done.16.below_ref, f32[368,128]{1,0:T(8,128)S(1)} %collective-permute-done.17.above_ref, ...), custom_call_target="tpu_custom_call" | custom-call | tf_op jit(solution)/shard_map/second_substep/pallas_call | solution.py:867
  97.9 6.1 %all-to-all-done.3 = f32[32,1,128]{2,1,0:T(1,128)S(1)} async-done(((f32[32,1,128]{2,1,0:T(1,128)}), f32[32,1,128]{2,1,0:T(1,128)S(1)}, u32[]{:S(2)}, u32[]{:S(2)}) %all-to-all-start.3) | async-done | bytes 16416 | tf_op jit(solution)/shard_map/all_to_all | solution.py:367
  104.1 0.0 copy-start.2
  104.1 0.0 copy-start.3
  104.1 0.0 copy-start.5
  104.1 0.0 copy-start.6
  104.1 0.8 last_picard.1
  104.9 0.0 copy-start
  105.5 0.0 copy-done.1
  105.5 0.0 copy-done.2
  105.5 0.0 copy-done.3
  105.5 0.0 copy-done.4
  105.5 0.0 copy-done.5
  105.5 0.0 copy-done.6
  105.5 0.0 copy-done
  (6 shorter events, 0.1 us)
Async XLA Ops:
  1.9 18.1 %collective-permute-start.12 = (f32[344,128]{1,0:T(8,128)S(1)}, f32[344,128]{1,0:T(8,128)S(1)}, u32[]{:S(2)}, u32[]{:S(2)}) collective-permute-start(f32[344,128]{1,0:T(8,128)S(1)} %get-tuple-element.310), channel_id=1, source_target_pairs={{0,16},{16,32},{32,48},{48,64},{64,80},{80,96},{96,112},{112,128},... | collective-permute-start | bytes 528392 | tf_op jit(solution)/shard_map/ppermute | solution.py:372
  5.9 14.1 %collective-permute-start.13 = (f32[344,128]{1,0:T(8,128)S(1)}, f32[344,128]{1,0:T(8,128)S(1)}, u32[]{:S(2)}, u32[]{:S(2)}) collective-permute-start(f32[344,128]{1,0:T(8,128)S(1)} %get-tuple-element.309.own_ref), channel_id=1, source_target_pairs={{0,496},{16,0},{32,16},{48,32},{64,48},{80,64},{96,80},{112,96},{1... | collective-permute-start | bytes 528392 | tf_op jit(solution)/shard_map/ppermute | solution.py:372
  12.5 7.4 %collective-permute-start.14 = (f32[24,128]{1,0:T(8,128)S(1)}, f32[24,128]{1,0:T(8,128)S(1)}, u32[]{:S(2)}, u32[]{:S(2)}) collective-permute-start(f32[24,128]{1,0:T(8,128)S(1)} %get-tuple-element.311), channel_id=1, source_target_pairs={{0,1},{1,2},{2,3},{3,4},{4,5},{5,6},{6,7},{7,8},{8,9},{9,10},{10,1... | collective-permute-start | bytes 36872 | tf_op jit(solution)/shard_map/ppermute | solution.py:372
  15.5 4.5 %collective-permute-start.15 = (f32[24,128]{1,0:T(8,128)S(1)}, f32[24,128]{1,0:T(8,128)S(1)}, u32[]{:S(2)}, u32[]{:S(2)}) collective-permute-start(f32[24,128]{1,0:T(8,128)S(1)} %get-tuple-element.312), channel_id=1, source_target_pairs={{0,15},{1,0},{2,1},{3,2},{4,3},{5,4},{6,5},{7,6},{8,7},{9,8},{10,9... | collective-permute-start | bytes 36872 | tf_op jit(solution)/shard_map/ppermute | solution.py:372
  22.0 19.2 %collective-permute-start.16 = (f32[368,128]{1,0:T(8,128)S(1)}, f32[368,128]{1,0:T(8,128)S(1)}, u32[]{:S(2)}, u32[]{:S(2)}) collective-permute-start(f32[368,128]{1,0:T(8,128)S(1)} %get-tuple-element.314), channel_id=1, source_target_pairs={{0,16},{16,32},{32,48},{48,64},{64,80},{80,96},{96,112},{112,128},... | collective-permute-start | bytes 565256 | tf_op jit(solution)/shard_map/ppermute | solution.py:372
  24.0 17.3 %collective-permute-start.17 = (f32[368,128]{1,0:T(8,128)S(1)}, f32[368,128]{1,0:T(8,128)S(1)}, u32[]{:S(2)}, u32[]{:S(2)}) collective-permute-start(f32[368,128]{1,0:T(8,128)S(1)} %get-tuple-element.315), channel_id=1, source_target_pairs={{0,496},{16,0},{32,16},{48,32},{64,48},{80,64},{96,80},{112,96},{1... | collective-permute-start | bytes 565256 | tf_op jit(solution)/shard_map/ppermute | solution.py:372
  30.6 6.8 %collective-permute-start.19 = (f32[24,128]{1,0:T(8,128)S(1)}, f32[24,128]{1,0:T(8,128)S(1)}, u32[]{:S(2)}, u32[]{:S(2)}) collective-permute-start(f32[24,128]{1,0:T(8,128)S(1)} %get-tuple-element.316.sums_ref), channel_id=1, source_target_pairs={{0,480},{16,496},{32,0},{48,16},{64,32},{80,48},{96,64},{112,80},{... | collective-permute-start | bytes 36872 | tf_op jit(solution)/shard_map/ppermute | solution.py:372
  32.6 8.7 %collective-permute-start.18 = (f32[24,128]{1,0:T(8,128)S(1)}, f32[24,128]{1,0:T(8,128)S(1)}, u32[]{:S(2)}, u32[]{:S(2)}) collective-permute-start(f32[24,128]{1,0:T(8,128)S(1)} %get-tuple-element.316.sums_ref), channel_id=1, source_target_pairs={{0,32},{16,48},{32,64},{48,80},{64,96},{80,112},{96,128},{112,144}... | collective-permute-start | bytes 36872 | tf_op jit(solution)/shard_map/ppermute | solution.py:372
  41.4 5.6 %collective-permute-start.20 = (f32[96,128]{1,0:T(8,128)S(1)}, f32[96,128]{1,0:T(8,128)S(1)}, u32[]{:S(2)}, u32[]{:S(2)}) collective-permute-start(f32[96,128]{1,0:T(8,128)S(1)} %get-tuple-element.319), channel_id=1, source_target_pairs={{0,1},{1,2},{2,3},{3,4},{4,5},{5,6},{6,7},{7,8},{8,9},{9,10},{10,1... | collective-permute-start | bytes 147464 | tf_op jit(solution)/shard_map/ppermute | solution.py:372
  43.6 3.6 %collective-permute-start.21 = (f32[96,128]{1,0:T(8,128)S(1)}, f32[96,128]{1,0:T(8,128)S(1)}, u32[]{:S(2)}, u32[]{:S(2)}) collective-permute-start(f32[96,128]{1,0:T(8,128)S(1)} %get-tuple-element.320), channel_id=1, source_target_pairs={{0,15},{1,0},{2,1},{3,2},{4,3},{5,4},{6,5},{7,6},{8,7},{9,8},{10,9... | collective-permute-start | bytes 147464 | tf_op jit(solution)/shard_map/ppermute | solution.py:372
  91.6 12.5 %all-to-all-start.3 = ((f32[32,1,128]{2,1,0:T(1,128)}), f32[32,1,128]{2,1,0:T(1,128)S(1)}, u32[]{:S(2)}, u32[]{:S(2)}) async-start(f32[32,1,128]{2,1,0:T(1,128)} %broadcast_in_dim.40), calls=%async_computation.3 | async-start | bytes 32768 | tf_op jit(solution)/shard_map/all_to_all | solution.py:367
  104.1 1.4 %copy-start.1 = (f32[8,128]{1,0:T(8,128)S(1)}, f32[8,128]{1,0:T(8,128)}, u32[]{:S(2)}) copy-start(f32[8,128]{1,0:T(8,128)} %height_ref.1) | copy-start | bytes 12292
  104.1 1.4 %copy-start.2 = (s32[8,128]{1,0:T(8,128)S(1)}, s32[8,128]{1,0:T(8,128)}, u32[]{:S(2)}) copy-start(s32[8,128]{1,0:T(8,128)} %code_ref.1) | copy-start | bytes 12292
  104.1 1.4 %copy-start.3 = (f32[2,8,128]{2,1,0:T(8,128)S(1)}, f32[2,8,128]{2,1,0:T(8,128)}, u32[]{:S(2)}) copy-start(f32[2,8,128]{2,1,0:T(8,128)} %speed_ref.1) | copy-start | bytes 24580
  104.1 1.4 %copy-start.4 = (f32[8,128]{1,0:T(8,128)S(1)}, f32[8,128]{1,0:T(8,128)}, u32[]{:S(2)}) copy-start(f32[8,128]{1,0:T(8,128)} %friction_ref.1) | copy-start | bytes 12292
  104.1 1.4 %copy-start.5 = (s32[8,128]{1,0:T(8,128)S(1)}, s32[8,128]{1,0:T(8,128)}, u32[]{:S(2)}) copy-start(s32[8,128]{1,0:T(8,128)} %grounded_ref.1) | copy-start | bytes 12292
  104.1 1.4 %copy-start.6 = (s32[8,128]{1,0:T(8,128)S(1)}, s32[8,128]{1,0:T(8,128)}, u32[]{:S(2)}) copy-start(s32[8,128]{1,0:T(8,128)} %ice_ref.1) | copy-start | bytes 12292
  104.9 0.7 copy-start

commit v11 on v10

--- a/solution.py
+++ b/solution.py
@@ -630,6 +630,14 @@
     )
     rows = [sums[k : k + 1, x * 128 : x * 128 + 128] for k in range(3) for x in range(8)]
     return jnp.concatenate(rows, axis=0)
+
+
+def rows_kernel(planes_ref, below_ref, above_ref, sums_ref, low_ref, high_ref):
+    for out_ref, first, behind_ref in ((low_ref, 0, above_ref), (high_ref, 6, below_ref)):
+        out_ref[0:128] = planes_ref[first]
+        out_ref[128:256] = planes_ref[first + 1]
+        out_ref[256:344] = behind_ref[256:344]
+        out_ref[344:368] = sums_ref[...]
 
 
 def tiles_kernel(planes_ref, own_ref, first_ref, last_ref):
@@ -742,8 +750,6 @@
     right_ref,
     inverses_ref,
     out_ref,
-    low_ref,
-    high_ref,
     weights_ref,
     sums_ref,
 ):
@@ -765,16 +771,7 @@
     done = substep(planes, weights, edges, inverses_ref, *columns_of(own_ref))
     for x in range(8):
         out_ref[x] = done[x]
-    low_ref[0:128] = done[0]
-    low_ref[128:256] = done[1]
-    low_ref[256:344] = above[256:344]
-    sums = level_sums(done, inverses_ref)
-    low_ref[344:368] = sums
-    high_ref[344:368] = sums
-    sums_ref[...] = sums
-    high_ref[0:128] = done[6]
-    high_ref[128:256] = done[7]
-    high_ref[256:344] = below[256:344]
+    sums_ref[...] = level_sums(done, inverses_ref)
 
 
 def second_substep_kernel(
@@ -843,26 +840,29 @@
     near = beside(own, high, GX)
     near_sides = beside(*edge_columns(planes, own), GY)
     inverses = on_chip(column_inverses(kappa))
-    current, low, high, weights, sums = pl.pallas_call(
+    current, weights, sums = pl.pallas_call(
         first_substep_kernel,
         out_shape=(
             kept(8, 128, 128),
-            kept(368, 128),
-            kept(368, 128),
             kept(9, 8, 128),
             kept(24, 128),
         ),
         name="first_substep",
     )(planes, own, *near, *near_sides, inverses)
+    current, sums = (on_chip(current), on_chip(sums))
+    far = (on_chip(shifted(sums, GX, 2)), on_chip(shifted(sums, GX, -2)))
+    low, high = pl.pallas_call(
+        rows_kernel,
+        out_shape=(kept(368, 128), kept(368, 128)),
+        name="rows",
+    )(current, *near, sums)
     around = beside(low, high, GX)
-    far = (on_chip(shifted(sums, GX, 2)), on_chip(shifted(sums, GX, -2)))
-    current = on_chip(current)
     first, last = edge_columns(current, own)
     mine, first, last = pl.pallas_call(
         gather_kernel,
         out_shape=(kept(560, 128), kept(96, 128), kept(96, 128)),
         name="gather",
-    )(*near, own, *around, *far, *map(on_chip, (sums, first, last)))
+    )(*near, own, *around, *far, sums, *map(on_chip, (first, last)))
     sides = beside(first, last, GY)
     current = pl.pallas_call(
         second_substep_kernel,

time: 106 us -> 114 us (1.075)
  blocking collectives: 40 us -> 44.6 us
  waiting for transfers between devices: 10.8 us -> 13.2 us
    all_to_all x1, blocking collectives: 11.9 us -> 16.4 us  [over_all(): return lax.all_to_all(part, GX, 0, 0, tiled=True)]
    ppermute x10, waiting for transfers between devices: 4.69 us -> 7.11 us  [shifted(): lax.ppermute(array, axis, [(i, (i + by) % size) for i in range(size)])]
  transfers between devices with their start and end apart: 11 -> 11, of which waited for: 4 -> 6; matrix products, arithmetic and copies ran while one was open for 0% -> 0% of each run, Pallas kernels for 5% -> 5%
where the time goes in v11:
time: 114 us; the launch traced here: 113 us
  blocking collectives  44.6 us (39%)
  starting transfers between devices  40.4 us (35%)
  waiting for transfers between devices  13.2 us (12%)
  Pallas kernels  13 us (11%)
  between operations  1.5 us (1%)
    ppermute x10, starting transfers between devices, shifted(): lax.ppermute(array, axis, [(i, (i + by) % size) for i in range(size)])  36.6 us
    all_to_all x2, blocking collectives, over_all(): part = lax.all_to_all(sums, GY, 0, 0, tiled=True)  28.2 us
    all_to_all x1, blocking collectives, over_all(): return lax.all_to_all(part, GX, 0, 0, tiled=True)  16.4 us
    ppermute x10, waiting for transfers between devices, shifted(): lax.ppermute(array, axis, [(i, (i + by) % size) for i in range(size)])  7.11 us
    all_to_all x1, waiting for transfers between devices, over_all(): return lax.all_to_all(part, GX, 0, 0, tiled=True)  6.09 us
    all_to_all x1, starting transfers between devices, over_all(): return lax.all_to_all(part, GX, 0, 0, tiled=True)  3.81 us
    pallas_call x1, Pallas kernels, shards(): pl.pallas_call(second_substep_kernel, out_shape=jax.ShapeDtypeStruct((102...  2.55 us
  transfers between devices with their start and end apart: 11, of which 6 were waited for; matrix products, arithmetic and copies ran while one was open for 0% of the time, Pallas kernels for 5%

profile of v11, /device:TPU:1, one launch (start us, length us, event | category | flops | bytes accessed | tf_op | source)
XLA Modules:
  0.0 113.5 jit_solution(9066225253238909378)
XLA Ops:
  0.6 1.2 %pack.1 = (f32[344,128]{1,0:T(8,128)S(1)}, f32[344,128]{1,0:T(8,128)S(1)}, f32[8,128,128]{2,1,0:T(8,128)S(1)}) custom-call(f32[1024,128]{1,0:T(8,128)} %bitcast.85, f32[2,8,128]{2,1,0:T(8,128)} %speed_ref.1, f32[8,128]{1,0:T(8,128)} %thick_ref.1, f32[8,128]{1,0:T(8,128)} %height_ref.1, f32[8,128]{1,0:T(8,128)} %friction_ref.1, s32[8,128]{1,0:T(8,128)} %ice_ref.1, ...), custom_call_target="tpu_custom_call" | custom-call | tf_op jit(solution)/shard_map/pack/pallas_call | solution.py:819
  1.9 8.1 %collective-permute-start.13 = (f32[344,128]{1,0:T(8,128)S(1)}, f32[344,128]{1,0:T(8,128)S(1)}, u32[]{:S(2)}, u32[]{:S(2)}) collective-permute-start(f32[344,128]{1,0:T(8,128)S(1)} %get-tuple-element.309.own_ref), channel_id=1, source_target_pairs={{0,496},{16,0},{32,16},{48,32},{64,48},{80,64},{96,80},{112,96},{1... | collective-permute-start | bytes 528392 | tf_op jit(solution)/shard_map/ppermute | solution.py:372
  10.0 1.9 %collective-permute-start.12 = (f32[344,128]{1,0:T(8,128)S(1)}, f32[344,128]{1,0:T(8,128)S(1)}, u32[]{:S(2)}, u32[]{:S(2)}) collective-permute-start(f32[344,128]{1,0:T(8,128)S(1)} %get-tuple-element.310), channel_id=1, source_target_pairs={{0,16},{16,32},{32,48},{48,64},{64,80},{80,96},{96,112},{112,128},... | collective-permute-start | bytes 528392 | tf_op jit(solution)/shard_map/ppermute | solution.py:372
  11.9 0.6 tiles.2
  12.5 3.0 %collective-permute-start.14 = (f32[24,128]{1,0:T(8,128)S(1)}, f32[24,128]{1,0:T(8,128)S(1)}, u32[]{:S(2)}, u32[]{:S(2)}) collective-permute-start(f32[24,128]{1,0:T(8,128)S(1)} %get-tuple-element.311), channel_id=1, source_target_pairs={{0,1},{1,2},{2,3},{3,4},{4,5},{5,6},{6,7},{7,8},{8,9},{9,10},{10,1... | collective-permute-start | bytes 36872 | tf_op jit(solution)/shard_map/ppermute | solution.py:372
  15.5 0.0 collective-permute-start.15
  15.5 1.4 %column_inverses.1.inverses_ref = f32[264,128]{1,0:T(8,128)S(1)} custom-call(f32[1,129]{1,0:T(1,128)} %bitcast.95), custom_call_target="tpu_custom_call" | custom-call | tf_op jit(solution)/shard_map/column_inverses/pallas_call | solution.py:134
  16.9 0.0 collective-permute-done.14.left_ref
  16.9 1.7 %collective-permute-done.15.right_ref = f32[24,128]{1,0:T(8,128)S(1)} collective-permute-done((f32[24,128]{1,0:T(8,128)S(1)}, f32[24,128]{1,0:T(8,128)S(1)}, u32[]{:S(2)}, u32[]{:S(2)}) %collective-permute-start.15) | collective-permute-done | bytes 12320 | tf_op jit(solution)/shard_map/ppermute | solution.py:372
  18.6 0.0 collective-permute-done.13.above_ref.near_above_ref
  18.6 1.7 %collective-permute-done.12.below_ref.near_below_ref = f32[344,128]{1,0:T(8,128)S(1)} collective-permute-done((f32[344,128]{1,0:T(8,128)S(1)}, f32[344,128]{1,0:T(8,128)S(1)}, u32[]{:S(2)}, u32[]{:S(2)}) %collective-permute-start.12) | collective-permute-done | bytes 176160 | tf_op jit(solution)/shard_map/ppermute | solution.py:372
  20.3 2.1 %first_substep.1 = (f32[8,128,128]{2,1,0:T(8,128)S(1)}, f32[9,8,128]{2,1,0:T(8,128)S(1)}, f32[24,128]{1,0:T(8,128)S(1)}) custom-call(f32[8,128,128]{2,1,0:T(8,128)S(1)} %get-tuple-element.308.planes_ref.enthalpy_ref, f32[344,128]{1,0:T(8,128)S(1)} %get-tuple-element.309.own_ref, f32[344,128]{1,0:T(8,128)S(1)} %collective-permute-done.12.below_ref.near_below_ref, ...), custom_call_target="tpu_custom_call" | custom-call | tf_op jit(solution)/shard_map/first_substep/pallas_call | solution.py:843
  22.3 1.9 %collective-permute-start.16 = (f32[368,128]{1,0:T(8,128)S(1)}, f32[368,128]{1,0:T(8,128)S(1)}, u32[]{:S(2)}, u32[]{:S(2)}) collective-permute-start(f32[368,128]{1,0:T(8,128)S(1)} %get-tuple-element.315), channel_id=1, source_target_pairs={{0,16},{16,32},{32,48},{48,64},{64,80},{80,96},{96,112},{112,128},... | collective-permute-start | bytes 565256 | tf_op jit(solution)/shard_map/ppermute | solution.py:372
  24.3 6.7 %collective-permute-start.17 = (f32[368,128]{1,0:T(8,128)S(1)}, f32[368,128]{1,0:T(8,128)S(1)}, u32[]{:S(2)}, u32[]{:S(2)}) collective-permute-start(f32[368,128]{1,0:T(8,128)S(1)} %get-tuple-element.316), channel_id=1, source_target_pairs={{0,496},{16,0},{32,16},{48,32},{64,48},{80,64},{96,80},{112,96},{1... | collective-permute-start | bytes 565256 | tf_op jit(solution)/shard_map/ppermute | solution.py:372
  31.0 1.9 %collective-permute-start.18 = (f32[24,128]{1,0:T(8,128)S(1)}, f32[24,128]{1,0:T(8,128)S(1)}, u32[]{:S(2)}, u32[]{:S(2)}) collective-permute-start(f32[24,128]{1,0:T(8,128)S(1)} %get-tuple-element.314.sums_ref), channel_id=1, source_target_pairs={{0,32},{16,48},{32,64},{48,80},{64,96},{80,112},{96,128},{112,144}... | collective-permute-start | bytes 36872 | tf_op jit(solution)/shard_map/ppermute | solution.py:372
  32.9 7.6 %collective-permute-start.19 = (f32[24,128]{1,0:T(8,128)S(1)}, f32[24,128]{1,0:T(8,128)S(1)}, u32[]{:S(2)}, u32[]{:S(2)}) collective-permute-start(f32[24,128]{1,0:T(8,128)S(1)} %get-tuple-element.314.sums_ref), channel_id=1, source_target_pairs={{0,480},{16,496},{32,0},{48,16},{64,32},{80,48},{96,64},{112,80},{... | collective-permute-start | bytes 36872 | tf_op jit(solution)/shard_map/ppermute | solution.py:372
  40.5 0.6 tiles.3
  41.1 0.0 collective-permute-done.18.far_below_ref
  41.1 0.2 collective-permute-done.19.far_above_ref
  41.3 0.0 collective-permute-done.16.below_ref
  41.3 0.0 collective-permute-done.17.above_ref
  41.3 0.2 gather.1
  41.5 5.5 %collective-permute-start.20 = (f32[96,128]{1,0:T(8,128)S(1)}, f32[96,128]{1,0:T(8,128)S(1)}, u32[]{:S(2)}, u32[]{:S(2)}) collective-permute-start(f32[96,128]{1,0:T(8,128)S(1)} %get-tuple-element.319), channel_id=1, source_target_pairs={{0,1},{1,2},{2,3},{3,4},{4,5},{5,6},{6,7},{7,8},{8,9},{9,10},{10,1... | collective-permute-start | bytes 147464 | tf_op jit(solution)/shard_map/ppermute | solution.py:372
  47.0 0.0 collective-permute-start.21
  47.0 1.2 %collective-permute-done.20.left_ref = f32[96,128]{1,0:T(8,128)S(1)} collective-permute-done((f32[96,128]{1,0:T(8,128)S(1)}, f32[96,128]{1,0:T(8,128)S(1)}, u32[]{:S(2)}, u32[]{:S(2)}) %collective-permute-start.20) | collective-permute-done | bytes 49184 | tf_op jit(solution)/shard_map/ppermute | solution.py:372
  48.2 2.3 %collective-permute-done.21.right_ref = f32[96,128]{1,0:T(8,128)S(1)} collective-permute-done((f32[96,128]{1,0:T(8,128)S(1)}, f32[96,128]{1,0:T(8,128)S(1)}, u32[]{:S(2)}, u32[]{:S(2)}) %collective-permute-start.21) | collective-permute-done | bytes 49184 | tf_op jit(solution)/shard_map/ppermute | solution.py:372
  50.5 2.0 %first_picard.1 = (f32[12,24,256]{2,1,0:T(8,128)S(1)}, f32[6,24,256]{2,1,0:T(8,128)S(1)}, f32[16,128]{1,0:T(8,128)S(1)}, f32[8,128]{1,0:T(8,128)S(1)}) custom-call(f32[560,128]{1,0:T(8,128)S(1)} %get-tuple-element.322.mine_ref, f32[96,128]{1,0:T(8,128)S(1)} %collective-permute-done.20.left_ref, f32[96,128]{1,0:T(8,128)S(1)} %collective-permute-done.21.right_ref, ...), custom_call_target="tpu_custom_call" | custom-call | tf_op jit(solution)/shard_map/first_picard/pallas_call | solution.py:379
  52.5 16.7 %all_to_all.34 = f32[16,1,128]{2,1,0:T(1,128)S(1)} all-to-all(f32[16,1,128]{2,1,0:T(1,128)S(1)} %bitcast.80), channel_id=1, replica_groups=mesh['gx_0'=4,'gx_1'=8,'gy_0'=8,'gy_1'=2] {'gy_0','gy_1'}, dimensions={0} | all-to-all | bytes 16384 | tf_op jit(solution)/shard_map/all_to_all | solution.py:365
  69.2 16.4 %all_to_all.35 = f32[32,1,128]{2,1,0:T(1,128)S(1)} all-to-all(f32[32,1,128]{2,1,0:T(1,128)S(1)} %broadcast_in_dim.39), channel_id=1, replica_groups=mesh['gx_0'=4,'gx_1'=8,'gy_0'=8,'gy_1'=2] {'gx_0','gx_1'}, dimensions={0} | all-to-all | bytes 32768 | tf_op jit(solution)/shard_map/all_to_all | solution.py:367
  85.6 1.6 %second_picard.1 = (f32[12,8,128]{2,1,0:T(8,128)S(1)}, f32[2,8,128]{2,1,0:T(8,128)S(1)}, f32[16,128]{1,0:T(8,128)S(1)}, f32[8,128]{1,0:T(8,128)S(1)}) custom-call(f32[32,128]{1,0:T(8,128)S(1)} %bitcast.78, f32[12,24,256]{2,1,0:T(8,128)S(1)} %get-tuple-element.324.basis_ref, f32[6,24,256]{2,1,0:T(8,128)S(1)} %get-tuple-element.325.fixed_ref), custom_call_target="tpu_custom_call" | custom-call | tf_op jit(solution)/shard_map/second_picard/pallas_call | solution.py:389
  87.2 11.6 %all_to_all.36 = f32[16,1,128]{2,1,0:T(1,128)S(1)} all-to-all(f32[16,1,128]{2,1,0:T(1,128)S(1)} %bitcast.79), channel_id=1, replica_groups=mesh['gx_0'=4,'gx_1'=8,'gy_0'=8,'gy_1'=2] {'gy_0','gy_1'}, dimensions={0} | all-to-all | bytes 16384 | tf_op jit(solution)/shard_map/all_to_all | solution.py:365
  98.8 0.6 broadcast_in_dim.40
  99.4 3.8 %all-to-all-start.3 = ((f32[32,1,128]{2,1,0:T(1,128)}), f32[32,1,128]{2,1,0:T(1,128)S(1)}, u32[]{:S(2)}, u32[]{:S(2)}) async-start(f32[32,1,128]{2,1,0:T(1,128)} %broadcast_in_dim.40), calls=%async_computation.3 | async-start | bytes 32768 | tf_op jit(solution)/shard_map/all_to_all | solution.py:367
  103.3 2.6 %second_substep.1 = f32[1024,128]{1,0:T(8,128)} custom-call(f32[8,128,128]{2,1,0:T(8,128)S(1)} %get-tuple-element.313.planes_ref.enthalpy_ref, f32[344,128]{1,0:T(8,128)S(1)} %get-tuple-element.309.own_ref, f32[368,128]{1,0:T(8,128)S(1)} %collective-permute-done.16.below_ref, f32[368,128]{1,0:T(8,128)S(1)} %collective-permute-done.17.above_ref, ...), custom_call_target="tpu_custom_call" | custom-call | tf_op jit(solution)/shard_map/second_substep/pallas_call | solution.py:867
  105.8 6.1 %all-to-all-done.3 = f32[32,1,128]{2,1,0:T(1,128)S(1)} async-done(((f32[32,1,128]{2,1,0:T(1,128)}), f32[32,1,128]{2,1,0:T(1,128)S(1)}, u32[]{:S(2)}, u32[]{:S(2)}) %all-to-all-start.3) | async-done | bytes 16416 | tf_op jit(solution)/shard_map/all_to_all | solution.py:367
  111.9 0.0 copy-start.1
  111.9 0.0 copy-start.2
  111.9 0.0 copy-start.5
  111.9 0.0 copy-start.6
  111.9 0.8 last_picard.1
  112.7 0.0 copy-start
  113.4 0.0 copy-done.1
  113.4 0.0 copy-done.2
  113.4 0.0 copy-done.3
  113.4 0.0 copy-done.4
  113.4 0.0 copy-done.5
  113.4 0.0 copy-done.6
  113.4 0.0 copy-done
  (7 shorter events, 0.1 us)
Async XLA Ops:
  1.9 16.7 %collective-permute-start.13 = (f32[344,128]{1,0:T(8,128)S(1)}, f32[344,128]{1,0:T(8,128)S(1)}, u32[]{:S(2)}, u32[]{:S(2)}) collective-permute-start(f32[344,128]{1,0:T(8,128)S(1)} %get-tuple-element.309.own_ref), channel_id=1, source_target_pairs={{0,496},{16,0},{32,16},{48,32},{64,48},{80,64},{96,80},{112,96},{1... | collective-permute-start | bytes 528392 | tf_op jit(solution)/shard_map/ppermute | solution.py:372
  10.0 10.3 %collective-permute-start.12 = (f32[344,128]{1,0:T(8,128)S(1)}, f32[344,128]{1,0:T(8,128)S(1)}, u32[]{:S(2)}, u32[]{:S(2)}) collective-permute-start(f32[344,128]{1,0:T(8,128)S(1)} %get-tuple-element.310), channel_id=1, source_target_pairs={{0,16},{16,32},{32,48},{48,64},{64,80},{80,96},{96,112},{112,128},... | collective-permute-start | bytes 528392 | tf_op jit(solution)/shard_map/ppermute | solution.py:372
  12.5 4.4 %collective-permute-start.14 = (f32[24,128]{1,0:T(8,128)S(1)}, f32[24,128]{1,0:T(8,128)S(1)}, u32[]{:S(2)}, u32[]{:S(2)}) collective-permute-start(f32[24,128]{1,0:T(8,128)S(1)} %get-tuple-element.311), channel_id=1, source_target_pairs={{0,1},{1,2},{2,3},{3,4},{4,5},{5,6},{6,7},{7,8},{8,9},{9,10},{10,1... | collective-permute-start | bytes 36872 | tf_op jit(solution)/shard_map/ppermute | solution.py:372
  15.5 3.1 %collective-permute-start.15 = (f32[24,128]{1,0:T(8,128)S(1)}, f32[24,128]{1,0:T(8,128)S(1)}, u32[]{:S(2)}, u32[]{:S(2)}) collective-permute-start(f32[24,128]{1,0:T(8,128)S(1)} %get-tuple-element.312), channel_id=1, source_target_pairs={{0,15},{1,0},{2,1},{3,2},{4,3},{5,4},{6,5},{7,6},{8,7},{9,8},{10,9... | collective-permute-start | bytes 36872 | tf_op jit(solution)/shard_map/ppermute | solution.py:372
  22.3 18.9 %collective-permute-start.16 = (f32[368,128]{1,0:T(8,128)S(1)}, f32[368,128]{1,0:T(8,128)S(1)}, u32[]{:S(2)}, u32[]{:S(2)}) collective-permute-start(f32[368,128]{1,0:T(8,128)S(1)} %get-tuple-element.315), channel_id=1, source_target_pairs={{0,16},{16,32},{32,48},{48,64},{64,80},{80,96},{96,112},{112,128},... | collective-permute-start | bytes 565256 | tf_op jit(solution)/shard_map/ppermute | solution.py:372
  24.3 17.0 %collective-permute-start.17 = (f32[368,128]{1,0:T(8,128)S(1)}, f32[368,128]{1,0:T(8,128)S(1)}, u32[]{:S(2)}, u32[]{:S(2)}) collective-permute-start(f32[368,128]{1,0:T(8,128)S(1)} %get-tuple-element.316), channel_id=1, source_target_pairs={{0,496},{16,0},{32,16},{48,32},{64,48},{80,64},{96,80},{112,96},{1... | collective-permute-start | bytes 565256 | tf_op jit(solution)/shard_map/ppermute | solution.py:372
  31.0 10.1 %collective-permute-start.18 = (f32[24,128]{1,0:T(8,128)S(1)}, f32[24,128]{1,0:T(8,128)S(1)}, u32[]{:S(2)}, u32[]{:S(2)}) collective-permute-start(f32[24,128]{1,0:T(8,128)S(1)} %get-tuple-element.314.sums_ref), channel_id=1, source_target_pairs={{0,32},{16,48},{32,64},{48,80},{64,96},{80,112},{96,128},{112,144}... | collective-permute-start | bytes 36872 | tf_op jit(solution)/shard_map/ppermute | solution.py:372
  32.9 8.4 %collective-permute-start.19 = (f32[24,128]{1,0:T(8,128)S(1)}, f32[24,128]{1,0:T(8,128)S(1)}, u32[]{:S(2)}, u32[]{:S(2)}) collective-permute-start(f32[24,128]{1,0:T(8,128)S(1)} %get-tuple-element.314.sums_ref), channel_id=1, source_target_pairs={{0,480},{16,496},{32,0},{48,16},{64,32},{80,48},{96,64},{112,80},{... | collective-permute-start | bytes 36872 | tf_op jit(solution)/shard_map/ppermute | solution.py:372
  41.5 6.7 %collective-permute-start.20 = (f32[96,128]{1,0:T(8,128)S(1)}, f32[96,128]{1,0:T(8,128)S(1)}, u32[]{:S(2)}, u32[]{:S(2)}) collective-permute-start(f32[96,128]{1,0:T(8,128)S(1)} %get-tuple-element.319), channel_id=1, source_target_pairs={{0,1},{1,2},{2,3},{3,4},{4,5},{5,6},{6,7},{7,8},{8,9},{9,10},{10,1... | collective-permute-start | bytes 147464 | tf_op jit(solution)/shard_map/ppermute | solution.py:372
  47.0 3.5 %collective-permute-start.21 = (f32[96,128]{1,0:T(8,128)S(1)}, f32[96,128]{1,0:T(8,128)S(1)}, u32[]{:S(2)}, u32[]{:S(2)}) collective-permute-start(f32[96,128]{1,0:T(8,128)S(1)} %get-tuple-element.320), channel_id=1, source_target_pairs={{0,15},{1,0},{2,1},{3,2},{4,3},{5,4},{6,5},{7,6},{8,7},{9,8},{10,9... | collective-permute-start | bytes 147464 | tf_op jit(solution)/shard_map/ppermute | solution.py:372
  99.4 12.5 %all-to-all-start.3 = ((f32[32,1,128]{2,1,0:T(1,128)}), f32[32,1,128]{2,1,0:T(1,128)S(1)}, u32[]{:S(2)}, u32[]{:S(2)}) async-start(f32[32,1,128]{2,1,0:T(1,128)} %broadcast_in_dim.40), calls=%async_computation.3 | async-start | bytes 32768 | tf_op jit(solution)/shard_map/all_to_all | solution.py:367
  111.9 1.5 %copy-start.1 = (f32[8,128]{1,0:T(8,128)S(1)}, f32[8,128]{1,0:T(8,128)}, u32[]{:S(2)}) copy-start(f32[8,128]{1,0:T(8,128)} %height_ref.1) | copy-start | bytes 12292
  111.9 1.5 %copy-start.2 = (s32[8,128]{1,0:T(8,128)S(1)}, s32[8,128]{1,0:T(8,128)}, u32[]{:S(2)}) copy-start(s32[8,128]{1,0:T(8,128)} %code_ref.1) | copy-start | bytes 12292
  111.9 1.5 %copy-start.3 = (f32[2,8,128]{2,1,0:T(8,128)S(1)}, f32[2,8,128]{2,1,0:T(8,128)}, u32[]{:S(2)}) copy-start(f32[2,8,128]{2,1,0:T(8,128)} %speed_ref.1) | copy-start | bytes 24580
  111.9 1.5 %copy-start.4 = (f32[8,128]{1,0:T(8,128)S(1)}, f32[8,128]{1,0:T(8,128)}, u32[]{:S(2)}) copy-start(f32[8,128]{1,0:T(8,128)} %friction_ref.1) | copy-start | bytes 12292
  111.9 1.5 %copy-start.5 = (s32[8,128]{1,0:T(8,128)S(1)}, s32[8,128]{1,0:T(8,128)}, u32[]{:S(2)}) copy-start(s32[8,128]{1,0:T(8,128)} %grounded_ref.1) | copy-start | bytes 12292
  111.9 1.5 %copy-start.6 = (s32[8,128]{1,0:T(8,128)S(1)}, s32[8,128]{1,0:T(8,128)}, u32[]{:S(2)}) copy-start(s32[8,128]{1,0:T(8,128)} %ice_ref.1) | copy-start | bytes 12292
  112.7 0.7 copy-start
